TPU v7x, 32 devices: a whole 2x2x4 slice. The times are simulated.
32 devices in a mesh: section: 2 (over core), dp: 4 (over z), seq: 4 (over y, x).
Axes of the slice: x: 2, y: 2, z: 4, core: 2. Of those that a mesh axis runs over, the one named last changes fastest.
Arguments:
- signal: bfloat16 [8, 1024, 1024], P('dp', 'seq'), may hold values from -6 to 6
- frame_segment_index: int32 [8, 1024], P('dp'), may hold values from 0 to 3, as said below
- conv_weight: float32 [8192, 1024], P(('section', 'dp', 'seq')), may hold values from -0.25 to 0.25
- conv_bias: float32 [1024], P(('section', 'dp', 'seq')), may hold values from -3 to 3
- norm1_gain: float32 [2, 1024], P('section', ('dp', 'seq')), may hold values from 0.1 to 1.9
- qkv_weight: float32 [2, 1024, 3072], P('section', ('dp', 'seq')), may hold values from -0.1875 to 0.1875
- out_weight: float32 [2, 1024, 1024], P('section', ('dp', 'seq')), may hold values from -2 to 2
- norm2_gain: float32 [2, 1024], P('section', ('dp', 'seq')), may hold values from 0.1 to 1.9
- up_weight: float32 [2, 1024, 4096], P('section', ('dp', 'seq')), may hold values from -0.1875 to 0.1875
- down_weight: float32 [2, 4096, 1024], P('section', ('dp', 'seq')), may hold values from -0.09375 to 0.09375
- cotangent: bfloat16 [8, 1024, 1024], P('dp', 'seq'), may hold values from -6 to 6
Outputs:
- ends: float32 [2, 8, 1024, 1024], P('section', 'dp', 'seq')
- conv_weight_grad: float32 [8192, 1024], P(('section', 'dp', 'seq'))
- conv_bias_grad: float32 [1024], P(('section', 'dp', 'seq'))
- norm1_gain_grad: float32 [2, 1024], P('section', ('dp', 'seq'))
- qkv_weight_grad: float32 [2, 1024, 3072], P('section', ('dp', 'seq'))
- out_weight_grad: float32 [2, 1024, 1024], P('section', ('dp', 'seq'))
- norm2_gain_grad: float32 [2, 1024], P('section', ('dp', 'seq'))
- up_weight_grad: float32 [2, 1024, 4096], P('section', ('dp', 'seq'))
- down_weight_grad: float32 [2, 4096, 1024], P('section', ('dp', 'seq'))
Inputs may be any that keep to these rules, and one draw needn't show every extreme that they name: `frame_segment_index`: in each row the segment ids start at 0 and never fall, each segment covering consecutive frames. In each aligned block of 2 rows (the rows of one index of dp) one row, drawn from the seed, is a single segment; every other row has exactly 4 segments.
All inputs are finite; a program needn't handle non-finite values.
Results may differ from a plain program's by a relative error of at most 0.018.
Values may be sent and summed in bfloat16 or wider, within the bound.
A program may use at most 832 MiB of HBM per device.

v0:
```python
import math

import jax
import jax.numpy as jnp
from jax import lax
from jax.sharding import PartitionSpec as P

HEAD_DIM = 64
GROUPS = 16
TAPS = 128


EPS = 1e-05
NEG = -1e30


def padded_2(block, sides, width):
    for axis, dim in sides:
        count = lax.axis_size(axis)
        forward = [(i, i + 1) for i in range(count - 1)]
        backward = [(target, source) for source, target in forward]
        low = lax.ppermute(
            lax.slice_in_dim(block, block.shape[dim] - width, None, axis=dim), axis, forward
        )
        high = lax.ppermute(lax.slice_in_dim(block, 0, width, axis=dim), axis, backward)
        block = jnp.concatenate([low, block, high], axis=dim)
    return block


def from_behind(value, axis, steps):
    count = lax.axis_size(axis)
    first, last = (max(0, -steps), min(count, count - steps))
    return lax.ppermute(value, axis, [(source, source + steps) for source in range(first, last)])


def normalize(values, gain):
    average = jnp.mean(values, axis=-1, keepdims=True)
    centred = values - average
    spread = jnp.mean(centred * centred, axis=-1, keepdims=True)
    return centred * lax.rsqrt(spread + EPS) * gain


def smooth(values):
    return jax.nn.gelu(values, approximate=False)


def conv_taps(padded, kernel, frames):
    width_all = padded.shape[1]
    per_group = width_all // GROUPS
    tap_step = math.gcd(TAPS, 16)
    weight_view = kernel.reshape(TAPS, per_group, GROUPS, per_group)
    running = jnp.zeros((frames, GROUPS, per_group), jnp.float32)
    for first_tap in range(0, TAPS, tap_step):
        windows = jnp.stack(
            [padded[first_tap + offset : first_tap + offset + frames] for offset in range(tap_step)]
        )
        windows = windows.reshape(tap_step, frames, GROUPS, per_group)
        running = running + jnp.einsum(
            "jtgc,jcgo->tgo",
            windows,
            weight_view[first_tap : first_tap + tap_step],
            preferred_element_type=jnp.float32,
        )
    return running.reshape(frames, width_all)


def conv_input_grad(grad_pad, kernel, frames):
    width_all = grad_pad.shape[1]
    per_group = width_all // GROUPS
    tap_step = math.gcd(TAPS, 16)
    weight_view = kernel.reshape(TAPS, per_group, GROUPS, per_group)
    running = jnp.zeros((frames, GROUPS, per_group), jnp.float32)
    for first_tap in range(0, TAPS, tap_step):
        back_windows = jnp.stack(
            [
                grad_pad[TAPS - first_tap - offset : TAPS - first_tap - offset + frames]
                for offset in range(tap_step)
            ]
        )
        back_windows = back_windows.reshape(tap_step, frames, GROUPS, per_group)
        running = running + jnp.einsum(
            "jtgo,jcgo->tgc",
            back_windows,
            weight_view[first_tap : first_tap + tap_step],
            preferred_element_type=jnp.float32,
        )
    return running.reshape(frames, width_all)


def conv_kernel_grad(padded_all, grad_all):
    step_count, frames, width_all = grad_all.shape
    per_group = width_all // GROUPS
    tap_step = math.gcd(TAPS, 16)
    grad_view = grad_all.reshape(step_count * frames, GROUPS, per_group)
    kernel_parts = []
    for first_tap in range(0, TAPS, tap_step):
        windows = jnp.stack(
            [
                padded_all[:, first_tap + offset : first_tap + offset + frames]
                for offset in range(tap_step)
            ]
        )
        windows = windows.reshape(tap_step, step_count * frames, GROUPS, per_group)
        kernel_parts.append(
            jnp.einsum("jtgc,tgo->jcgo", windows, grad_view, preferred_element_type=jnp.float32)
        )
    return jnp.concatenate(kernel_parts, axis=0).reshape(TAPS * per_group, width_all)


def score_block(query_heads, key_block, query_segs, key_segs, factor):
    scores = (
        jnp.einsum("qhd,khd->hqk", query_heads, key_block, preferred_element_type=jnp.float32)
        * factor
    )
    allowed = (query_segs[:, None] == key_segs[None, :])[None]
    return (scores, allowed)


def front(layer_in, weights, kernel, conv_shift, first_section):
    frames, width_all = layer_in.shape
    padded = padded_2(layer_in, (("seq", 0),), TAPS // 2)
    conv_pre = lax.cond(
        first_section,
        lambda: conv_taps(padded, kernel, frames) + conv_shift.astype(jnp.float32),
        lambda: jnp.zeros((frames, width_all), jnp.float32),
    )
    conv_val, conv_pull = jax.vjp(smooth, conv_pre)
    resid_one = layer_in.astype(jnp.float32) + conv_val
    normed_val, norm_pull = jax.vjp(normalize, resid_one, weights[0].astype(jnp.float32))
    normed_one = normed_val.astype(jnp.bfloat16)
    packed = jnp.dot(normed_one, weights[1], preferred_element_type=jnp.float32).astype(
        jnp.bfloat16
    )
    return (padded, conv_pull, resid_one, norm_pull, normed_one, packed)


def tail(resid_one, attn_low, weights):
    resid_two = resid_one + jnp.dot(attn_low, weights[2], preferred_element_type=jnp.float32)
    normed_val, norm_pull = jax.vjp(normalize, resid_two, weights[3].astype(jnp.float32))
    normed_two = normed_val.astype(jnp.bfloat16)
    hidden_pre = jnp.dot(normed_two, weights[4], preferred_element_type=jnp.float32)
    hidden_val, gelu_pull = jax.vjp(smooth, hidden_pre)
    hidden_low = hidden_val.astype(jnp.bfloat16)
    result = resid_two + jnp.dot(hidden_low, weights[5], preferred_element_type=jnp.float32)
    return (result, norm_pull, normed_two, gelu_pull, hidden_low)


def key_loop(keys_all, values_all, segment_row, head_count, visit, initial):
    total_rows = keys_all.shape[0]
    block_rows = math.gcd(total_rows, 512)

    def one_block(block_index, running):
        offset = block_index * block_rows
        key_block = lax.dynamic_slice_in_dim(keys_all, offset, block_rows, 0).reshape(
            block_rows, head_count, HEAD_DIM
        )
        value_block = lax.dynamic_slice_in_dim(values_all, offset, block_rows, 0).reshape(
            block_rows, head_count, HEAD_DIM
        )
        key_segs = lax.dynamic_slice_in_dim(segment_row, offset, block_rows, 0)
        return visit(running, key_block, value_block, key_segs)

    return lax.fori_loop(0, total_rows // block_rows, one_block, initial)


def layer_forward(
    layer_in, segment_row, weights, kernel, conv_shift, first_section, my_start, factor
):
    frames, width_all = layer_in.shape
    head_count = width_all // HEAD_DIM
    padded, conv_pull, resid_one, norm_pull, normed_one, packed = front(
        layer_in, weights, kernel, conv_shift, first_section
    )
    query_heads = packed[:, :width_all].reshape(frames, head_count, HEAD_DIM)
    query_segs = lax.dynamic_slice_in_dim(segment_row, my_start, frames, 0)
    initial = (
        jnp.full((head_count, frames), NEG, jnp.float32),
        jnp.zeros((head_count, frames), jnp.float32),
        jnp.zeros((head_count, frames, HEAD_DIM), jnp.float32),
    )
    key_piece = lax.all_gather(packed[:, width_all : 2 * width_all], "seq", axis=0, tiled=True)
    value_piece = lax.all_gather(packed[:, 2 * width_all :], "seq", axis=0, tiled=True)
    piece_rows = key_piece.shape[0]
    block_rows = math.gcd(piece_rows, 512)

    def one_block(block_index, running):
        run_max, run_sum, run_acc = running
        offset = block_index * block_rows
        key_block = lax.dynamic_slice_in_dim(key_piece, offset, block_rows, 0).reshape(
            block_rows, head_count, HEAD_DIM
        )
        value_block = lax.dynamic_slice_in_dim(value_piece, offset, block_rows, 0).reshape(
            block_rows, head_count, HEAD_DIM
        )
        key_segs = lax.dynamic_slice_in_dim(segment_row, offset, block_rows, 0)
        scores, allowed = score_block(query_heads, key_block, query_segs, key_segs, factor)
        masked = jnp.where(allowed, scores, NEG)
        new_max = jnp.maximum(run_max, jnp.max(masked, axis=-1))
        weights_now = jnp.where(allowed, jnp.exp(masked - new_max[..., None]), 0.0)
        rescale = jnp.exp(run_max - new_max)
        run_sum = run_sum * rescale + jnp.sum(weights_now, axis=-1)
        run_acc = run_acc * rescale[..., None] + jnp.einsum(
            "hqk,khd->hqd",
            weights_now.astype(jnp.bfloat16),
            value_block,
            preferred_element_type=jnp.float32,
        )
        return (new_max, run_sum, run_acc)

    run_max, run_sum, run_acc = lax.fori_loop(0, piece_rows // block_rows, one_block, initial)
    log_total = run_max + jnp.log(run_sum)
    mixture = run_acc / run_sum[..., None]
    attn_low = jnp.transpose(mixture, (1, 0, 2)).reshape(frames, width_all).astype(jnp.bfloat16)
    result, norm_two_pull, normed_two, gelu_pull, hidden_low = tail(resid_one, attn_low, weights)
    kept = (
        padded,
        conv_pull,
        norm_pull,
        normed_one,
        packed,
        log_total,
        mixture,
        attn_low,
        norm_two_pull,
        normed_two,
        gelu_pull,
        hidden_low,
        segment_row,
    )
    return (result, kept)


def layer_backward(kept, grad_out, weights, kernel, first_section, my_start, factor):
    (
        padded,
        conv_pull,
        norm_one_pull,
        normed_one,
        packed,
        log_total,
        mixture,
        attn_low,
        norm_two_pull,
        normed_two,
        gelu_pull,
        hidden_low,
        segment_row,
    ) = kept
    frames, width_all = normed_one.shape
    head_count = width_all // HEAD_DIM
    query_heads = packed[:, :width_all].reshape(frames, head_count, HEAD_DIM)
    key_local = packed[:, width_all : 2 * width_all]
    value_local = packed[:, 2 * width_all :]
    query_segs = lax.dynamic_slice_in_dim(segment_row, my_start, frames, 0)
    keys_all, values_all = (
        lax.all_gather(key_local, "seq", axis=0, tiled=True),
        lax.all_gather(value_local, "seq", axis=0, tiled=True),
    )

    def chances_for(key_block, key_segs):
        scores, allowed = score_block(query_heads, key_block, query_segs, key_segs, factor)
        return jnp.where(
            allowed, jnp.exp(jnp.where(allowed, scores, NEG) - log_total[..., None]), 0.0
        )

    branch_grad = grad_out.astype(jnp.bfloat16)
    hidden_grad = jnp.einsum(
        "to,io->ti", branch_grad, weights[5], preferred_element_type=jnp.float32
    )
    pre_grad = gelu_pull(hidden_grad)[0].astype(jnp.bfloat16)
    normed_two_grad = jnp.einsum(
        "tf,if->ti", pre_grad, weights[4], preferred_element_type=jnp.float32
    )
    resid_two_grad, grad_gain_two = norm_two_pull(normed_two_grad)
    resid_two_grad = resid_two_grad + grad_out
    attn_branch_grad = resid_two_grad.astype(jnp.bfloat16)
    attended_grad = jnp.einsum(
        "to,io->ti", attn_branch_grad, weights[2], preferred_element_type=jnp.float32
    ).astype(jnp.bfloat16)
    dout_heads = attended_grad.reshape(frames, head_count, HEAD_DIM)
    delta_rows = jnp.einsum("qhd,hqd->hq", dout_heads.astype(jnp.float32), mixture)

    def visit_query(running, key_block, value_block, key_segs):
        chances = chances_for(key_block, key_segs)
        prob_grad = jnp.einsum(
            "qhd,khd->hqk", dout_heads, value_block, preferred_element_type=jnp.float32
        )
        score_grad = (chances * (prob_grad - delta_rows[..., None])).astype(jnp.bfloat16)
        return running + jnp.einsum(
            "hqk,khd->qhd", score_grad, key_block, preferred_element_type=jnp.float32
        )

    grad_query = (
        key_loop(
            keys_all,
            values_all,
            segment_row,
            head_count,
            visit_query,
            jnp.zeros((frames, head_count, HEAD_DIM), jnp.float32),
        )
        * factor
    )
    row_stats = (
        lax.all_gather(log_total, "seq", axis=1, tiled=True),
        lax.all_gather(delta_rows, "seq", axis=1, tiled=True),
    )
    key_heads = key_local.reshape(frames, head_count, HEAD_DIM)
    value_heads = value_local.reshape(frames, head_count, HEAD_DIM)
    start_acc = (
        jnp.zeros((frames, head_count, HEAD_DIM), jnp.float32),
        jnp.zeros((frames, head_count, HEAD_DIM), jnp.float32),
    )
    query_piece = lax.all_gather(packed[:, :width_all], "seq", axis=0, tiled=True)
    dout_piece = lax.all_gather(attended_grad, "seq", axis=0, tiled=True)
    piece_rows = query_piece.shape[0]
    block_rows = math.gcd(piece_rows, 512)

    def one_block(block_index, running):
        key_acc, value_acc = running
        offset = block_index * block_rows
        query_block = lax.dynamic_slice_in_dim(query_piece, offset, block_rows, 0).reshape(
            block_rows, head_count, HEAD_DIM
        )
        dout_block = lax.dynamic_slice_in_dim(dout_piece, offset, block_rows, 0).reshape(
            block_rows, head_count, HEAD_DIM
        )
        seg_block = lax.dynamic_slice_in_dim(segment_row, offset, block_rows, 0)
        total_block = lax.dynamic_slice_in_dim(row_stats[0], offset, block_rows, 1)
        delta_block = lax.dynamic_slice_in_dim(row_stats[1], offset, block_rows, 1)
        scores, allowed = score_block(query_block, key_heads, seg_block, query_segs, factor)
        chances = jnp.where(
            allowed, jnp.exp(jnp.where(allowed, scores, NEG) - total_block[..., None]), 0.0
        )
        prob_grad = jnp.einsum(
            "qhd,khd->hqk", dout_block, value_heads, preferred_element_type=jnp.float32
        )
        score_grad = (chances * (prob_grad - delta_block[..., None])).astype(jnp.bfloat16)
        key_acc = (
            key_acc
            + jnp.einsum(
                "hqk,qhd->khd", score_grad, query_block, preferred_element_type=jnp.float32
            )
            * factor
        )
        value_acc = value_acc + jnp.einsum(
            "hqk,qhd->khd",
            chances.astype(jnp.bfloat16),
            dout_block,
            preferred_element_type=jnp.float32,
        )
        return (key_acc, value_acc)

    key_acc, value_acc = lax.fori_loop(0, piece_rows // block_rows, one_block, start_acc)
    grad_key = key_acc.reshape(frames, width_all)
    grad_value = value_acc.reshape(frames, width_all)
    packed_grad = jnp.concatenate(
        [grad_query.reshape(frames, width_all), grad_key, grad_value], axis=1
    ).astype(jnp.bfloat16)
    normed_one_grad = jnp.einsum(
        "tj,ij->ti", packed_grad, weights[1], preferred_element_type=jnp.float32
    )
    resid_one_grad, grad_gain_one = norm_one_pull(normed_one_grad)
    resid_one_grad = resid_one_grad + resid_two_grad
    conv_grad = jnp.where(first_section, conv_pull(resid_one_grad)[0], 0.0).astype(jnp.bfloat16)
    grad_pad = padded_2(conv_grad, (("seq", 0),), TAPS // 2)
    back_sum = lax.cond(
        first_section,
        lambda: conv_input_grad(grad_pad, kernel, frames),
        lambda: jnp.zeros((frames, width_all), jnp.float32),
    )
    grad_in = resid_one_grad + back_sum
    products = (
        normed_one,
        packed_grad,
        attn_low,
        attn_branch_grad,
        normed_two,
        pre_grad,
        hidden_low,
        branch_grad,
        padded,
        conv_grad,
    )
    return (grad_in, (grad_gain_one, grad_gain_two), products)


def per_device(
    signal,
    frame_segment_index,
    conv_weight,
    conv_bias,
    norm1_gain,
    qkv_weight,
    out_weight,
    norm2_gain,
    up_weight,
    down_weight,
    cotangent,
):
    micro_count, frames, width_all = signal.shape
    factor = 1.0 / math.sqrt(HEAD_DIM)
    first_section = lax.axis_index("section") == 0
    my_start = lax.axis_index("seq") * frames
    gathered = (
        lax.all_gather(norm1_gain.astype(jnp.bfloat16), ("dp", "seq"), axis=1, tiled=True),
        lax.all_gather(qkv_weight.astype(jnp.bfloat16), ("dp", "seq"), axis=1, tiled=True),
        lax.all_gather(out_weight.astype(jnp.bfloat16), ("dp", "seq"), axis=1, tiled=True),
        lax.all_gather(norm2_gain.astype(jnp.bfloat16), ("dp", "seq"), axis=1, tiled=True),
        lax.all_gather(up_weight.astype(jnp.bfloat16), ("dp", "seq"), axis=1, tiled=True),
        lax.all_gather(down_weight.astype(jnp.bfloat16), ("dp", "seq"), axis=1, tiled=True),
    )
    weights = tuple((member[0] for member in gathered))
    kernel, conv_shift = (
        lax.all_gather(
            conv_weight.astype(jnp.bfloat16), ("section", "dp", "seq"), axis=0, tiled=True
        ),
        lax.all_gather(
            conv_bias.astype(jnp.bfloat16), ("section", "dp", "seq"), axis=0, tiled=True
        ),
    )
    received = jnp.zeros((frames, width_all), jnp.bfloat16)
    saved = []
    forward_outs = []
    for step_index in range(micro_count + 1):
        own_index = min(step_index, micro_count - 1)
        prior_index = max(step_index - 1, 0)
        layer_in = jnp.where(first_section, signal[own_index], received)
        segment_row = jnp.where(
            first_section, frame_segment_index[own_index], frame_segment_index[prior_index]
        )
        result, kept = layer_forward(
            layer_in, segment_row, weights, kernel, conv_shift, first_section, my_start, factor
        )
        saved.append(kept)
        forward_outs.append(result)
        if step_index < micro_count:
            received = from_behind(result.astype(jnp.bfloat16), "section", 1)
    received_back = jnp.zeros((frames, width_all), jnp.bfloat16)
    input_grads = []
    gain_totals = None
    product_list = []
    for step_index in range(micro_count + 1):
        kept = saved[micro_count - step_index]
        if step_index < micro_count:
            top_grad = cotangent[micro_count - 1 - step_index].astype(jnp.float32)
        else:
            top_grad = jnp.zeros((frames, width_all), jnp.float32)
        incoming = jnp.where(first_section, received_back.astype(jnp.float32), top_grad)
        grad_in, gain_grads, products = layer_backward(
            kept, incoming, weights, kernel, first_section, my_start, factor
        )
        input_grads.append(grad_in)
        product_list.append(products)
        if gain_totals is None:
            gain_totals = gain_grads
        else:
            gain_totals = (gain_totals[0] + gain_grads[0], gain_totals[1] + gain_grads[1])
        if step_index < micro_count:
            received_back = from_behind(grad_in.astype(jnp.bfloat16), "section", -1)

    def joined(position):
        return jnp.concatenate([member[position] for member in product_list], axis=0)

    grad_qkv = jnp.einsum("ti,tj->ij", joined(0), joined(1), preferred_element_type=jnp.float32)
    grad_out_weight = jnp.einsum(
        "ti,to->io", joined(2), joined(3), preferred_element_type=jnp.float32
    )
    grad_up = jnp.einsum("ti,tf->if", joined(4), joined(5), preferred_element_type=jnp.float32)
    grad_down = jnp.einsum("ti,to->io", joined(6), joined(7), preferred_element_type=jnp.float32)
    padded_all = jnp.stack([member[8] for member in product_list])
    conv_grad_all = jnp.stack([member[9] for member in product_list])
    kernel_grad = conv_kernel_grad(padded_all, conv_grad_all)
    bias_grad = jnp.sum(joined(9).astype(jnp.float32), axis=0)
    ends = jnp.stack(
        [
            jnp.where(
                first_section, input_grads[micro_count - mb_index], forward_outs[mb_index + 1]
            )
            for mb_index in range(micro_count)
        ]
    )[None]
    layer_sums = (
        lax.psum_scatter(gain_totals[0][None], ("dp", "seq"), scatter_dimension=1, tiled=True),
        lax.psum_scatter(grad_qkv[None], ("dp", "seq"), scatter_dimension=1, tiled=True),
        lax.psum_scatter(grad_out_weight[None], ("dp", "seq"), scatter_dimension=1, tiled=True),
        lax.psum_scatter(gain_totals[1][None], ("dp", "seq"), scatter_dimension=1, tiled=True),
        lax.psum_scatter(grad_up[None], ("dp", "seq"), scatter_dimension=1, tiled=True),
        lax.psum_scatter(grad_down[None], ("dp", "seq"), scatter_dimension=1, tiled=True),
    )
    conv_sums = (
        lax.psum_scatter(kernel_grad, ("section", "dp", "seq"), scatter_dimension=0, tiled=True),
        lax.psum_scatter(bias_grad, ("section", "dp", "seq"), scatter_dimension=0, tiled=True),
    )
    return (
        ends,
        conv_sums[0],
        conv_sums[1],
        layer_sums[0],
        layer_sums[1],
        layer_sums[2],
        layer_sums[3],
        layer_sums[4],
        layer_sums[5],
    )


def solution(mesh):
    placed = (
        P("dp", "seq", None),
        P("dp", None),
        P(("section", "dp", "seq"), None),
        P(("section", "dp", "seq")),
        P("section", ("dp", "seq")),
        P("section", ("dp", "seq"), None),
        P("section", ("dp", "seq"), None),
        P("section", ("dp", "seq")),
        P("section", ("dp", "seq"), None),
        P("section", ("dp", "seq"), None),
        P("dp", "seq", None),
    )
    return jax.shard_map(
        per_device,
        mesh=mesh,
        in_specs=placed,
        out_specs=(
            P("section", "dp", "seq", None),
            P(("section", "dp", "seq"), None),
            P(("section", "dp", "seq")),
            P("section", ("dp", "seq")),
            P("section", ("dp", "seq"), None),
            P("section", ("dp", "seq"), None),
            P("section", ("dp", "seq")),
            P("section", ("dp", "seq"), None),
            P("section", ("dp", "seq"), None),
        ),
        check_vma=False,
    )
```

profile of v0, /device:TPU:17, one launch (start us, length us, event | category | flops | bytes accessed | tf_op | source)
XLA Modules:
  0.0 5210.9 jit_solution(5016122026054794831)
XLA Ops:
  48.0 57.4 %all-reduce = bf16[1024]{0:T(1024)(128)(2,1)S(1)} all-reduce(bf16[1024]{0:T(1024)(128)(2,1)S(1)} %dynamic-update-slice), channel_id=1, replica_groups=mesh['section'=2,'dp'=4,'seq'=4] {'section','dp','seq'}, use_global_device_ids=true, to_apply=%add | all-reduce | flops 1024 | bytes 4096
  144.0 78.6 %all-gather.20.cloned.1.call-done = bf16[1,1024,3072]{2,1,0:T(8,128)(2,1)} async-done(((bf16[1,64,3072]{2,1,0:T(8,128)(2,1)}), bf16[1,1024,3072]{2,1,0:T(8,128)(2,1)}) %all-gather.20.cloned.1.call-update) | async-done | bytes 6291472 | tf_op jit(solution)/shard_map/all_gather | solution.py:407
  233.8 217.6 %all-gather.22.cloned.1.call-done = bf16[1024,1024]{1,0:T(8,128)(2,1)} async-done(((bf16[256,1024]{1,0:T(8,128)(2,1)}), bf16[1024,1024]{1,0:T(8,128)(2,1)}) %all-gather.22.cloned.1.call-update) | async-done | bytes 2097168 | tf_op jit(solution)/shard_map/all_gather | solution.py:256
  454.3 34.2 all-gather.24.cloned.1.call-done
  492.4 35.5 while.144
  556.0 109.8 %all-gather.28.cloned.1.call-done = bf16[1,1024,4096]{2,1,0:T(8,128)(2,1)} async-done(((bf16[1,64,4096]{2,1,0:T(8,128)(2,1)}), bf16[1,1024,4096]{2,1,0:T(8,128)(2,1)}) %all-gather.28.cloned.1.call-update) | async-done | bytes 8388624 | tf_op jit(solution)/shard_map/all_gather | solution.py:410
  681.8 97.9 %all-gather.30.cloned.1.call-done = bf16[1,4096,1024]{2,1,0:T(8,128)(2,1)} async-done(((bf16[1,256,1024]{2,1,0:T(8,128)(2,1)}), bf16[1,4096,1024]{2,1,0:T(8,128)(2,1)}) %all-gather.30.cloned.1.call-update) | async-done | bytes 8388624 | tf_op jit(solution)/shard_map/all_gather | solution.py:411
  821.6 304.0 %all-gather.32.cloned.1.call-done = bf16[1024,1024]{1,0:T(8,128)(2,1)} async-done(((bf16[256,1024]{1,0:T(8,128)(2,1)}), bf16[1024,1024]{1,0:T(8,128)(2,1)}) %all-gather.32.cloned.1.call-update) | async-done | bytes 2097168 | tf_op jit(solution)/shard_map/all_gather | solution.py:256
  1128.5 34.3 all-gather.34.cloned.1.call-done
  1166.7 35.3 while.145
  1264.6 303.8 %all-gather.36.cloned.1.call-done = bf16[1024,1024]{1,0:T(8,128)(2,1)} async-done(((bf16[256,1024]{1,0:T(8,128)(2,1)}), bf16[1024,1024]{1,0:T(8,128)(2,1)}) %all-gather.36.cloned.1.call-update) | async-done | bytes 2097168 | tf_op jit(solution)/shard_map/all_gather | solution.py:256
  1571.4 34.7 all-gather.38.cloned.1.call-done
  1610.1 37.6 while.146
  1699.7 33.5 while.147
  1735.4 46.9 while.148
  1815.3 272.6 %collective-permute-start.10 = (bf16[256,1024]{1,0:T(8,128)(2,1)}, bf16[256,1024]{1,0:T(8,128)(2,1)S(1)}, u32[]{:S(2)}, u32[]{:S(2)}) collective-permute-start(bf16[256,1024]{1,0:T(8,128)(2,1)} %add_convert_fusion.3), channel_id=1, source_target_pairs={{16,0},{17,1},{18,2},{19,3},{20,4},{21,5},{22,6},{23,7},{24,8},{25... | collective-permute-start | bytes 1572872 | tf_op jit(solution)/shard_map/ppermute | solution.py:33
  2167.1 47.0 while.150
  2245.1 265.1 %collective-permute-start.13 = (bf16[256,1024]{1,0:T(8,128)(2,1)S(1)}, bf16[256,1024]{1,0:T(8,128)(2,1)S(1)}, u32[]{:S(2)}, u32[]{:S(2)}) collective-permute-start(bf16[256,1024]{1,0:T(8,128)(2,1)S(1)} %add_convert_fusion.4), channel_id=1, source_target_pairs={{16,0},{17,1},{18,2},{19,3},{20,4},{21,5},{22,6},{23,7},{24,8},{25... | collective-permute-start | bytes 1572872 | tf_op jit(solution)/shard_map/ppermute | solution.py:33
  2555.2 33.7 while.151
  2591.4 47.3 while.152
  4366.2 69.0 %copy.932 = f32[128,64,16,64]{3,2,1,0:T(8,128)} copy(f32[128,64,16,64]{1,3,0,2:T(8,128)} %bitcast_dynamic-update-slice_fusion) | data formatting | bytes 67108864 | tf_op jit(solution)/shard_map/concatenate | solution.py:107
  4435.2 55.5 %reshape.2647 = f32[8192,1024]{1,0:T(8,128)} reshape(f32[128,64,16,64]{3,2,1,0:T(8,128)} %copy.932) | data formatting | bytes 67108864 | tf_op jit(solution)/shard_map/reshape | solution.py:107
  4508.2 52.7 %all-reduce.3 = f32[1024]{0:T(1024)S(1)} all-reduce(f32[1024]{0:T(1024)S(1)} %convert_reduce_fusion), channel_id=3, replica_groups=mesh['section'=2,'dp'=4,'seq'=4] {'section','dp','seq'}, use_global_device_ids=true, to_apply=%region_62.63.clone | all-reduce | flops 1024 | bytes 8192
  4571.3 632.3 %reduce-scatter.12.cloned.1.call-done = f32[256,1024]{1,0:T(8,128)} async-done(((f32[8192,1024]{1,0:T(8,128)}), f32[256,1024]{1,0:T(8,128)}) %reduce-scatter.12.cloned.1.call-update) | async-done | bytes 1048592 | tf_op jit(solution)/shard_map/reduce_scatter | solution.py:492
  (1489 shorter events, 2611.6 us)
Async XLA Ops:
  7.2 121.1 %all-gather.18.cloned.1.call-start = ((), (), s32[]{:S(2)}) async-start(), calls=%async_computation.7 | async-start | bytes 17301504 | tf_op jit(solution)/shard_map/all_gather | solution.py:415
  9.3 213.3 %all-gather.20.cloned.1.call-start = ((), (), s32[]{:S(2)}) async-start(), calls=%async_computation.8 | async-start | bytes 6684672 | tf_op jit(solution)/shard_map/all_gather | solution.py:407
  11.4 440.1 %all-gather.22.cloned.1.call-start = ((), (), s32[]{:S(2)}) async-start(), calls=%async_computation.9 | async-start | bytes 2621440 | tf_op jit(solution)/shard_map/all_gather | solution.py:256
  228.4 260.0 %all-gather.24.cloned.1.call-start = ((), (), s32[]{:S(2)}) async-start(), calls=%async_computation.10 | async-start | bytes 2621440 | tf_op jit(solution)/shard_map/all_gather | solution.py:257
  229.0 322.3 %all-gather.26.cloned.1.call-start = ((), (), s32[]{:S(2)}) async-start(), calls=%async_computation.11 | async-start | bytes 2228224 | tf_op jit(solution)/shard_map/all_gather | solution.py:408
  229.8 436.1 %all-gather.28.cloned.1.call-start = ((), (), s32[]{:S(2)}) async-start(), calls=%async_computation.12 | async-start | bytes 8912896 | tf_op jit(solution)/shard_map/all_gather | solution.py:410
  230.7 549.0 %all-gather.30.cloned.1.call-start = ((), (), s32[]{:S(2)}) async-start(), calls=%async_computation.13 | async-start | bytes 8912896 | tf_op jit(solution)/shard_map/all_gather | solution.py:411
  232.9 892.7 %all-gather.32.cloned.1.call-start = ((), (), s32[]{:S(2)}) async-start(), calls=%async_computation.14 | async-start | bytes 2621440 | tf_op jit(solution)/shard_map/all_gather | solution.py:256
  820.5 342.3 %all-gather.34.cloned.1.call-start = ((), (), s32[]{:S(2)}) async-start(), calls=%async_computation.15 | async-start | bytes 2621440 | tf_op jit(solution)/shard_map/all_gather | solution.py:257
  821.2 747.2 %all-gather.36.cloned.1.call-start = ((), (), s32[]{:S(2)}) async-start(), calls=%async_computation.16 | async-start | bytes 2621440 | tf_op jit(solution)/shard_map/all_gather | solution.py:256
  1258.5 347.6 %all-gather.38.cloned.1.call-start = ((), (), s32[]{:S(2)}) async-start(), calls=%async_computation.17 | async-start | bytes 2621440 | tf_op jit(solution)/shard_map/all_gather | solution.py:257
  1259.2 476.2 %all-gather.40.cloned.1.call-start = ((), (), s32[]{:S(2)}) async-start(), calls=%async_computation.18 | async-start | bytes 2621440 | tf_op jit(solution)/shard_map/all_gather | solution.py:314
  1264.5 470.9 %all-gather.42.cloned.1.call-start = ((), (), s32[]{:S(2)}) async-start(), calls=%async_computation.19 | async-start | bytes 2621440 | tf_op jit(solution)/shard_map/all_gather | solution.py:315
  1692.7 474.5 %all-gather.44.cloned.1.call-start = ((), (), s32[]{:S(2)}) async-start(), calls=%async_computation.20 | async-start | bytes 2621440 | tf_op jit(solution)/shard_map/all_gather | solution.py:314
  1815.3 285.6 %collective-permute-start.10 = (bf16[256,1024]{1,0:T(8,128)(2,1)}, bf16[256,1024]{1,0:T(8,128)(2,1)S(1)}, u32[]{:S(2)}, u32[]{:S(2)}) collective-permute-start(bf16[256,1024]{1,0:T(8,128)(2,1)} %add_convert_fusion.3), channel_id=1, source_target_pairs={{16,0},{17,1},{18,2},{19,3},{20,4},{21,5},{22,6},{23,7},{24,8},{25... | collective-permute-start | bytes 1572872 | tf_op jit(solution)/shard_map/ppermute | solution.py:33
  2124.8 466.6 %all-gather.48.cloned.1.call-start = ((), (), s32[]{:S(2)}) async-start(), calls=%async_computation.22 | async-start | bytes 2621440 | tf_op jit(solution)/shard_map/all_gather | solution.py:314
  2245.1 278.7 %collective-permute-start.13 = (bf16[256,1024]{1,0:T(8,128)(2,1)S(1)}, bf16[256,1024]{1,0:T(8,128)(2,1)S(1)}, u32[]{:S(2)}, u32[]{:S(2)}) collective-permute-start(bf16[256,1024]{1,0:T(8,128)(2,1)S(1)} %add_convert_fusion.4), channel_id=1, source_target_pairs={{16,0},{17,1},{18,2},{19,3},{20,4},{21,5},{22,6},{23,7},{24,8},{25... | collective-permute-start | bytes 1572872 | tf_op jit(solution)/shard_map/ppermute | solution.py:33
  2547.3 1958.1 %reduce-scatter.24.cloned.1.call-start = ((), (), s32[]{:S(2)}) async-start(), calls=%async_computation.30 | async-start | bytes 557056
  2591.0 1970.5 %reduce-scatter.22.cloned.1.call-start = ((), (), s32[]{:S(2)}) async-start(), calls=%async_computation.29 | async-start | bytes 557056
  2649.5 1921.7 %reduce-scatter.16.cloned.1.call-start = ((), (), s32[]{:S(2)}) async-start(), calls=%async_computation.26 | async-start | bytes 4456448 | tf_op jit(solution)/shard_map/reduce_scatter | solution.py:486
  2654.9 1916.4 %reduce-scatter.14.cloned.1.call-start = ((), (), s32[]{:S(2)}) async-start(), calls=%async_computation.25 | async-start | bytes 13369344 | tf_op jit(solution)/shard_map/reduce_scatter | solution.py:485
  2673.8 1897.5 %reduce-scatter.18.cloned.1.call-start = ((), (), s32[]{:S(2)}) async-start(), calls=%async_computation.27 | async-start | bytes 17825792 | tf_op jit(solution)/shard_map/reduce_scatter | solution.py:488
  2687.3 1884.0 %reduce-scatter.20.cloned.1.call-start = ((), (), s32[]{:S(2)}) async-start(), calls=%async_computation.28 | async-start | bytes 17825792 | tf_op jit(solution)/shard_map/reduce_scatter | solution.py:489
  4053.0 1150.6 %reduce-scatter.12.cloned.1.call-start = ((), (), s32[]{:S(2)}) async-start(), calls=%async_computation.24 | async-start | bytes 34603008 | tf_op jit(solution)/shard_map/reduce_scatter | solution.py:492
  (337 other events, 6198.2 us)
Sparse Core Ops, SparseCore 0:
  11.6 116.6 all-gather.17
  131.0 91.5 all-gather.19
  228.6 222.8 all-gather.21
  453.1 35.2 all-gather.23
  491.6 59.6 all-gather.25
  554.5 111.2 all-gather.27
  668.6 111.0 all-gather.29
  820.6 304.9 all-gather.31
  1127.5 35.2 all-gather.33
  1258.6 309.6 all-gather.35
  1570.8 35.2 all-gather.37
  1607.8 35.2 all-gather.39
  1692.8 37.5 all-gather.41
  2088.0 37.7 all-gather.43
  2127.5 35.2 all-gather.45
  2510.4 38.2 all-gather.47
  2551.0 35.2 all-gather.49
  2591.1 56.8 reduce-scatter.23
  2650.4 73.1 reduce-scatter.21
  2726.4 111.5 reduce-scatter.15
  2844.2 205.6 reduce-scatter.13
  3052.9 346.4 reduce-scatter.17
  4053.1 349.0 reduce-scatter.19
  4490.9 712.6 reduce-scatter.11
where the time goes:
time: 5250 us; the launch traced here: 5210 us
  waiting for transfers between devices  1910 us (36%)
  local copies, waits for them, and re-layouts  1770 us (34%)
  matrix products  614 us (12%)
  starting transfers between devices  574 us (11%)
  blocking collectives  177 us (3%)
  other arithmetic  120 us (2%)
    another operation x264, local copies, waits for them, and re-layouts, conv_kernel_grad(): jnp.stack([padded_all[:, first_tap + offset:first_tap + offset + frames]...  1280 us
    all_gather x3, waiting for transfers between devices, layer_backward(): lax.all_gather(key_local, 'seq', axis=0, tiled=True)  825 us
    reduce_scatter x1, waiting for transfers between devices, per_device(): lax.psum_scatter(kernel_grad, ('section', 'dp', 'seq'), scatter_dimension...  632 us
    ppermute x4, starting transfers between devices, from_behind(): lax.ppermute(value, axis, [(source, source + steps) for source in range(f...  540 us
    unnamed x744, local copies, waits for them, and re-layouts  200 us
    dot_general x8, matrix products, conv_kernel_grad(): jnp.einsum('jtgc,tgo->jcgo', windows, grad_view, preferred_element_type=j...  150 us
    unnamed x3, blocking collectives  136 us
    all_gather x1, waiting for transfers between devices, per_device(): lax.all_gather(up_weight.astype(jnp.bfloat16), ('dp', 'seq'), axis=1, til...  110 us
  transfers between devices with their start and end apart: 40, of which 22 were waited for; matrix products, arithmetic and copies ran while one was open for 43% of the time, Pallas kernels for 0%

commit v1 on v0

--- a/solution.py
+++ b/solution.py
@@ -1,8 +1,11 @@
+import functools
 import math
 
 import jax
 import jax.numpy as jnp
 from jax import lax
+from jax.experimental import pallas as pl
+from jax.experimental.pallas import tpu as pltpu
 from jax.sharding import PartitionSpec as P
 
 HEAD_DIM = 64
@@ -505,6 +508,554 @@
     )
 
 
+def swap_section(value):
+    return lax.ppermute(value, "section", [(0, 1), (1, 0)])
+
+
+def swap_x(value):
+    return lax.ppermute(value, "seq", [(q, q ^ 1) for q in range(4)])
+
+
+def pair_sum(value):
+    low = value.astype(jnp.bfloat16)
+    return low.astype(jnp.float32) + swap_x(low).astype(jnp.float32)
+
+
+def choose(flag, first, second):
+    return jnp.where(flag, first, second), jnp.where(flag, second, first)
+
+
+def y_groups():
+    return [[d * 4 + y * 2 + x for d in range(lax.axis_size("dp")) for y in range(2)] for x in range(2)]
+
+
+def gather_yz(value):
+    return lax.all_gather(value, ("dp", "seq"), axis=0, tiled=False, axis_index_groups=y_groups())
+
+
+def scatter_yz(value):
+    return lax.psum_scatter(
+        value, ("dp", "seq"), scatter_dimension=0, tiled=False, axis_index_groups=y_groups()
+    )
+
+
+def norm_stats(values):
+    average = jnp.mean(values, axis=-1, keepdims=True)
+    centred = values - average
+    spread = jnp.mean(centred * centred, axis=-1, keepdims=True)
+    return centred, lax.rsqrt(spread + EPS)
+
+
+def norm_back(values, gain, grad):
+    centred, inv = norm_stats(values)
+    unit = centred * inv
+    gain_grad = jnp.sum(grad * unit, axis=0)
+    f = grad * gain
+    mean_f = jnp.mean(f, axis=-1, keepdims=True)
+    mean_fu = jnp.mean(f * unit, axis=-1, keepdims=True)
+    return (f - mean_f - unit * mean_fu) * inv, gain_grad
+
+
+def gelu_slope(values):
+    cdf = 0.5 * (1.0 + lax.erf(values * (1.0 / math.sqrt(2.0))))
+    pdf = jnp.exp(-0.5 * values * values) * (1.0 / math.sqrt(2.0 * math.pi))
+    return cdf + values * pdf
+
+
+def attention_forward_kernel(factor, q_ref, k_ref, v_ref, qs_ref, ks_ref, o_ref, lse_ref):
+    queries = q_ref[...]
+    lane = lax.broadcasted_iota(jnp.int32, queries.shape, 1)
+    allowed = qs_ref[...] == ks_ref[...]
+    keys = k_ref[...]
+    values = v_ref[...]
+    outs = []
+    for head in range(2):
+        mine = (lane < HEAD_DIM) if head == 0 else (lane >= HEAD_DIM)
+        own = jnp.where(mine, queries, jnp.zeros_like(queries))
+        scores = lax.dot_general(
+            own, keys, (((1,), (1,)), ((), ())), preferred_element_type=jnp.float32
+        ) * factor
+        scores = jnp.where(allowed, scores, NEG)
+        top = jnp.max(scores, axis=-1, keepdims=True)
+        raised = jnp.exp(scores - top)
+        total = jnp.sum(raised, axis=-1, keepdims=True)
+        chances = (raised * (1.0 / total)).astype(jnp.bfloat16)
+        outs.append(jnp.dot(chances, values, preferred_element_type=jnp.float32))
+        lse_ref[0, head] = top + jnp.log(total)
+    o_ref[...] = jnp.where(lane < HEAD_DIM, outs[0], outs[1]).astype(o_ref.dtype)
+
+
+def attention_forward(packed, kv_all, query_segs, key_segs, factor):
+    frames = packed.shape[0]
+    keys = kv_all.shape[0]
+    width = packed.shape[1] // 3
+    pairs = width // 128
+    rows = math.gcd(frames, 256)
+    return pl.pallas_call(
+        functools.partial(attention_forward_kernel, factor),
+        grid=(pairs, frames // rows),
+        in_specs=[
+            pl.BlockSpec((rows, 128), lambda h, i: (i, h)),
+            pl.BlockSpec((keys, 128), lambda h, i: (0, h)),
+            pl.BlockSpec((keys, 128), lambda h, i: (0, pairs + h)),
+            pl.BlockSpec((rows, 1), lambda h, i: (i, 0)),
+            pl.BlockSpec((1, keys), lambda h, i: (0, 0)),
+        ],
+        out_specs=[
+            pl.BlockSpec((rows, 128), lambda h, i: (i, h)),
+            pl.BlockSpec((1, 2, rows, 1), lambda h, i: (h, 0, i, 0)),
+        ],
+        out_shape=[
+            jax.ShapeDtypeStruct((frames, width), jnp.bfloat16),
+            jax.ShapeDtypeStruct((pairs, 2, frames, 1), jnp.float32),
+        ],
+        compiler_params=pltpu.CompilerParams(vmem_limit_bytes=40 * 1024 * 1024),
+        cost_estimate=pl.CostEstimate(
+            flops=4 * frames * keys * width * 2,
+            bytes_accessed=2 * (frames * width * 2 + keys * width * 2),
+            transcendentals=frames * keys * (width // HEAD_DIM),
+        ),
+        name="attention_forward",
+    )(packed, kv_all, kv_all, query_segs[:, None], key_segs[None, :])
+
+
+def attention_backward_kernel(
+    factor, q_ref, k_ref, v_ref, g_ref, o_ref, lse_ref, qs_ref, ks_ref, dq_ref, dk_ref, dv_ref
+):
+    step = pl.program_id(1)
+
+    @pl.when(step == 0)
+    def _():
+        dk_ref[...] = jnp.zeros_like(dk_ref)
+        dv_ref[...] = jnp.zeros_like(dv_ref)
+
+    queries = q_ref[...]
+    grads = g_ref[...]
+    keys = k_ref[...]
+    values = v_ref[...]
+    lane = lax.broadcasted_iota(jnp.int32, queries.shape, 1)
+    key_lane = lax.broadcasted_iota(jnp.int32, keys.shape, 1)
+    allowed = qs_ref[...] == ks_ref[...]
+    product = grads.astype(jnp.float32) * o_ref[...].astype(jnp.float32)
+    dq = None
+    for head in range(2):
+        mine = (lane < HEAD_DIM) if head == 0 else (lane >= HEAD_DIM)
+        key_mine = (key_lane < HEAD_DIM) if head == 0 else (key_lane >= HEAD_DIM)
+        own_q = jnp.where(mine, queries, jnp.zeros_like(queries))
+        own_g = jnp.where(mine, grads, jnp.zeros_like(grads))
+        own_k = jnp.where(key_mine, keys, jnp.zeros_like(keys))
+        delta = jnp.sum(jnp.where(mine, product, 0.0), axis=-1, keepdims=True)
+        scores = lax.dot_general(
+            own_q, keys, (((1,), (1,)), ((), ())), preferred_element_type=jnp.float32
+        ) * factor
+        chances = jnp.exp(jnp.where(allowed, scores, NEG) - lse_ref[0, head])
+        prob_grad = lax.dot_general(
+            own_g, values, (((1,), (1,)), ((), ())), preferred_element_type=jnp.float32
+        )
+        score_grad = (chances * (prob_grad - delta)).astype(jnp.bfloat16)
+        part = jnp.dot(score_grad, own_k, preferred_element_type=jnp.float32)
+        dq = part if dq is None else dq + part
+        dk_ref[...] += lax.dot_general(
+            score_grad, own_q, (((0,), (0,)), ((), ())), preferred_element_type=jnp.float32
+        ) * factor
+        dv_ref[...] += lax.dot_general(
+            chances.astype(jnp.bfloat16), own_g, (((0,), (0,)), ((), ())),
+            preferred_element_type=jnp.float32,
+        )
+    dq_ref[...] = (dq * factor).astype(dq_ref.dtype)
+
+
+def attention_backward(packed, kv_all, grads, attended, lse, query_segs, key_segs, factor):
+    frames = packed.shape[0]
+    keys = kv_all.shape[0]
+    width = packed.shape[1] // 3
+    pairs = width // 128
+    rows = math.gcd(frames, 256)
+    return pl.pallas_call(
+        functools.partial(attention_backward_kernel, factor),
+        grid=(pairs, frames // rows),
+        in_specs=[
+            pl.BlockSpec((rows, 128), lambda h, i: (i, h)),
+            pl.BlockSpec((keys, 128), lambda h, i: (0, h)),
+            pl.BlockSpec((keys, 128), lambda h, i: (0, pairs + h)),
+            pl.BlockSpec((rows, 128), lambda h, i: (i, h)),
+            pl.BlockSpec((rows, 128), lambda h, i: (i, h)),
+            pl.BlockSpec((1, 2, rows, 1), lambda h, i: (h, 0, i, 0)),
+            pl.BlockSpec((rows, 1), lambda h, i: (i, 0)),
+            pl.BlockSpec((1, keys), lambda h, i: (0, 0)),
+        ],
+        out_specs=[
+            pl.BlockSpec((rows, 128), lambda h, i: (i, h)),
+            pl.BlockSpec((keys, 128), lambda h, i: (0, h)),
+            pl.BlockSpec((keys, 128), lambda h, i: (0, h)),
+        ],
+        out_shape=[
+            jax.ShapeDtypeStruct((frames, width), jnp.bfloat16),
+            jax.ShapeDtypeStruct((keys, width), jnp.float32),
+            jax.ShapeDtypeStruct((keys, width), jnp.float32),
+        ],
+        compiler_params=pltpu.CompilerParams(vmem_limit_bytes=48 * 1024 * 1024),
+        cost_estimate=pl.CostEstimate(
+            flops=10 * frames * keys * width * 2,
+            bytes_accessed=4 * (frames * width * 2 + keys * width * 2),
+            transcendentals=frames * keys * (width // HEAD_DIM),
+        ),
+        name="attention_backward",
+    )(packed, kv_all, kv_all, grads, attended, lse, query_segs[:, None], key_segs[None, :])
+
+
+CONV_STEP = 4
+
+
+def conv_bands(kernel, per_group):
+    groups = kernel.shape[1] // per_group
+    steps = TAPS // CONV_STEP + 1
+    bands = []
+    for group in range(groups):
+        own = kernel[:, group * per_group : (group + 1) * per_group]
+        shifted = [
+            jnp.pad(own, ((shift * per_group, (CONV_STEP - shift) * per_group), (0, 0)))
+            for shift in range(CONV_STEP)
+        ]
+        band = jnp.concatenate(shifted, axis=1)
+        bands.append(band.reshape(steps, CONV_STEP * per_group, CONV_STEP * per_group))
+    return bands
+
+
+def group_view(values, per_group):
+    rows, frames, width = values.shape
+    return [
+        values[:, :, g * per_group : (g + 1) * per_group].reshape(
+            rows, frames // CONV_STEP, CONV_STEP * per_group
+        )
+        for g in range(width // per_group)
+    ]
+
+
+def ungroup(parts, per_group):
+    rows, blocks, _ = parts[0].shape
+    return jnp.concatenate(
+        [part.reshape(rows, blocks * CONV_STEP, per_group) for part in parts], axis=2
+    )
+
+
+CONV_DIMS = ("NWC", "WIO", "NWC")
+
+
+def conv_forward(views, bands):
+    half = TAPS // 2 // CONV_STEP
+    return [
+        lax.conv_general_dilated(
+            view, band, (1,), [(half, half)], dimension_numbers=CONV_DIMS,
+            preferred_element_type=jnp.float32,
+        )
+        for view, band in zip(views, bands)
+    ]
+
+
+def conv_back(grad_views, bands):
+    half = TAPS // 2 // CONV_STEP
+    return [
+        lax.conv_general_dilated(
+            view, jnp.transpose(band[::-1], (0, 2, 1)), (1,), [(half, half)],
+            dimension_numbers=CONV_DIMS, preferred_element_type=jnp.float32,
+        )
+        for view, band in zip(grad_views, bands)
+    ]
+
+
+def conv_taps_grad(views, grad_views, per_group):
+    half = TAPS // 2 // CONV_STEP
+    results = []
+    for view, grad in zip(views, grad_views):
+        band = lax.conv_general_dilated(
+            view, grad, (1,), [(half, half)],
+            dimension_numbers=("CWN", "IWO", "WNC"),
+            preferred_element_type=jnp.float32,
+        )
+        flat = band.reshape(-1, CONV_STEP, per_group)
+        total = None
+        for shift in range(CONV_STEP):
+            part = flat[shift * per_group : (shift + TAPS) * per_group, shift]
+            total = part if total is None else total + part
+        results.append(total)
+    return jnp.concatenate(results, axis=1)
+
+
+def to_column(vector, width):
+    return jnp.pad(vector[:, None], ((0, 0), (0, width - 1)))
+
+
+def per_device_pairs(
+    signal, frame_segment_index, conv_weight, conv_bias, norm1_gain, qkv_weight, out_weight,
+    norm2_gain, up_weight, down_weight, cotangent,
+):
+    micro_count, frames, width = signal.shape
+    bf16, f32 = jnp.bfloat16, jnp.float32
+    per_group = width // GROUPS
+    dp_count = lax.axis_size("dp")
+    factor = 1.0 / math.sqrt(HEAD_DIM)
+    sec = lax.axis_index("section")
+    dp = lax.axis_index("dp")
+    seq = lax.axis_index("seq")
+    x, y = seq % 2, seq // 2
+    sec0, x0 = sec == 0, x == 0
+    row_frames = 4 * frames
+    half_frames = 2 * frames
+    both = ("section", "seq")
+
+    block_width = width // 8
+    rows_here = conv_weight.shape[0]
+    conv_low = conv_weight.astype(bf16).reshape(rows_here, 8, block_width)
+    bias_low = jnp.pad(conv_bias.astype(bf16), (0, block_width - conv_bias.shape[0]))
+    bias_rows = jnp.pad(
+        jnp.broadcast_to(bias_low[None, None, :], (1, 8, block_width)), ((0, 15), (0, 0), (0, 0))
+    )
+    conv_send = jnp.transpose(jnp.concatenate([conv_low, bias_rows], axis=0), (1, 0, 2))
+    conv_got = lax.all_to_all(conv_send, both, 0, 0, tiled=True)
+
+    own_half = jnp.where(sec0, signal[:, :, : width // 2], signal[:, :, width // 2 :])
+    sig_send = jnp.transpose(own_half.reshape(micro_count, frames, 4, block_width), (2, 0, 1, 3))
+    sig_got = lax.all_to_all(sig_send, "seq", 0, 0, tiled=True)
+    sig_all = jnp.transpose(sig_got, (1, 0, 2, 3)).reshape(micro_count, row_frames, block_width)
+
+    up_chain = [(i, i + 1) for i in range(dp_count - 1)]
+    down_chain = [(i + 1, i) for i in range(dp_count - 1)]
+    from_low, from_high = conv_got, conv_got
+    pieces = [conv_got]
+    lows, highs = [], []
+    for _ in range(dp_count - 1):
+        from_low = lax.ppermute(from_low, "dp", up_chain)
+        from_high = lax.ppermute(from_high, "dp", down_chain)
+        lows.append(from_low)
+        highs.append(from_high)
+    ordered = []
+    for source in range(dp_count):
+        value = conv_got
+        for distance in range(1, dp_count):
+            if source - distance >= 0 or source + distance < dp_count:
+                if source + distance < dp_count:
+                    value = jnp.where(dp == source + distance, lows[distance - 1], value)
+                if source - distance >= 0:
+                    value = jnp.where(dp == source - distance, highs[distance - 1], value)
+        ordered.append(value)
+    conv_all = jnp.stack(ordered)
+    conv_all = conv_all.reshape(dp_count, 2, 4, rows_here + 16, block_width)
+    conv_all = jnp.transpose(conv_all, (1, 0, 2, 3, 4))
+    bias_all = conv_all[:, :, :, rows_here, : conv_bias.shape[0]].reshape(width)
+    bias_own = lax.dynamic_slice_in_dim(bias_all, (sec * 4 + seq) * block_width, block_width, 0)
+    kernel_own = conv_all[:, :, :, :rows_here].reshape(TAPS * per_group, block_width)
+    bands = conv_bands(kernel_own, per_group)
+
+    def exchange_columns(weight, gain, unit):
+        rows, columns = weight.shape
+        view = weight.astype(bf16).reshape(rows, columns // (2 * unit), 2, unit)
+        keep, send = choose(x0, view[:, :, 0], view[:, :, 1])
+        gain_part = to_column(gain.astype(bf16), 128)
+        keep = jnp.concatenate([keep.reshape(rows, columns // 2), gain_part], axis=1)
+        send = jnp.concatenate([send.reshape(rows, columns // 2), gain_part], axis=1)
+        got = swap_x(send)
+        return choose(x0, keep, got)
+
+    qkv_halves = exchange_columns(qkv_weight[0], norm1_gain[0], HEAD_DIM)
+    up_halves = exchange_columns(up_weight[0], norm2_gain[0], down_weight.shape[1])
+    out_rows = out_weight.shape[1] // 2
+    out_low = out_weight[0].astype(bf16)
+    down_rows = down_weight.shape[1] // 2
+    down_low = down_weight[0].astype(bf16)
+    halves = (
+        qkv_halves,
+        (out_low[:out_rows], out_low[out_rows:]),
+        up_halves,
+        (down_low[:down_rows], down_low[down_rows:]),
+    )
+    own_parts = []
+    for first, second in halves:
+        keep, send = choose(sec0, first, second)
+        got = swap_section(send)
+        own_parts.append(choose(sec0, keep, got))
+    layer_weights = []
+    for layer in range(2):
+        full = []
+        for part in own_parts:
+            mine = gather_yz(part[layer])
+            other = swap_section(mine)
+            first, second = choose(sec0, mine, other)
+            joined = jnp.stack([first, second], axis=1)
+            full.append(joined.reshape(-1, joined.shape[-1]))
+        w_qkv, w_out, w_up, w_down = full
+        gain_one = w_qkv[:, -128].astype(f32)[None, :]
+        gain_two = w_up[:, -128].astype(f32)[None, :]
+        layer_weights.append((gain_one, w_qkv[:, :-128], w_out, gain_two, w_up[:, :-128], w_down))
+
+    picked = jnp.where(sec0, cotangent[0], cotangent[1])
+    across = [(s * 4 + 2 * yy + xx, yy * 4 + 2 * s + xx) for s in range(2) for yy in range(2) for xx in range(2)]
+    cot_own = lax.ppermute(picked, both, across)
+    cot_other = swap_x(cot_own)
+    cot_pair = choose(x0, cot_own, cot_other)
+    top_grad = jnp.concatenate(cot_pair, axis=0).astype(f32)
+
+    segment_row = jnp.where(y == 0, frame_segment_index[0], frame_segment_index[1])
+    seg_pair = choose(sec0, segment_row[:half_frames], segment_row[half_frames:])
+    query_segs = seg_pair[0]
+    key_segs = jnp.concatenate(seg_pair)
+
+    sig_views = group_view(sig_all, per_group)
+    conv_pre = ungroup(conv_forward(sig_views, bands), per_group) + bias_own.astype(f32)
+    stream = (sig_all.astype(f32) + smooth(conv_pre)).astype(bf16)
+    slope = gelu_slope(conv_pre).astype(bf16)
+    stream_send = stream.reshape(2, 2, half_frames, block_width)
+    stream_send = jnp.transpose(stream_send, (1, 0, 2, 3))
+    stream_send = jnp.repeat(stream_send.reshape(4, half_frames, block_width), 2, axis=0)
+    stream_got = lax.all_to_all(stream_send, both, 0, 0, tiled=True)
+    layer_in = jnp.transpose(stream_got, (1, 0, 2)).reshape(half_frames, width).astype(f32)
+
+    kept = []
+    for layer in range(2):
+        gain_one, w_qkv, w_out, gain_two, w_up, w_down = layer_weights[layer]
+        centred, inv = norm_stats(layer_in)
+        normed_one = (centred * inv * gain_one).astype(bf16)
+        packed = jnp.dot(normed_one, w_qkv, preferred_element_type=f32).astype(bf16)
+        kv_own = packed[:, width // 2 :]
+        kv_all = jnp.concatenate([kv_own, swap_section(kv_own)], axis=0)
+        attended, lse = attention_forward(packed, kv_all, query_segs, key_segs, factor)
+        resid_two = layer_in + pair_sum(jnp.dot(attended, w_out, preferred_element_type=f32))
+        centred, inv = norm_stats(resid_two)
+        normed_two = (centred * inv * gain_two).astype(bf16)
+        hidden_pre = jnp.dot(normed_two, w_up, preferred_element_type=f32)
+        hidden = smooth(hidden_pre).astype(bf16)
+        hidden_slope = gelu_slope(hidden_pre).astype(bf16)
+        result = resid_two + pair_sum(jnp.dot(hidden, w_down, preferred_element_type=f32))
+        kept.append(
+            (layer_in, normed_one, packed, kv_all, attended, lse, resid_two, normed_two, hidden, hidden_slope)
+        )
+        layer_in = result.astype(bf16).astype(f32)
+    output = result
+
+    grad_out = top_grad
+    reduced = [None, None]
+    for layer in (1, 0):
+        gain_one, w_qkv, w_out, gain_two, w_up, w_down = layer_weights[layer]
+        (layer_in, normed_one, packed, kv_all, attended, lse, resid_two, normed_two, hidden, hidden_slope) = kept[layer]
+        branch = grad_out.astype(bf16)
+        hidden_grad = lax.dot_general(
+            branch, w_down, (((1,), (1,)), ((), ())), preferred_element_type=f32
+        )
+        pre_grad = (hidden_grad * hidden_slope.astype(f32)).astype(bf16)
+        part = lax.dot_general(
+            pre_grad, w_up, (((1,), (1,)), ((), ())), preferred_element_type=f32
+        )
+        normed_grad = pair_sum(part)
+        grad_down = lax.dot_general(
+            hidden, branch, (((0,), (0,)), ((), ())), preferred_element_type=f32
+        ).astype(bf16)
+        grad_up = lax.dot_general(
+            normed_two, pre_grad, (((0,), (0,)), ((), ())), preferred_element_type=f32
+        ).astype(bf16)
+        resid_grad, gain_two_grad = norm_back(resid_two, gain_two, normed_grad)
+        resid_grad = resid_grad + grad_out
+        attn_branch = resid_grad.astype(bf16)
+        attended_grad = lax.dot_general(
+            attn_branch, w_out, (((1,), (1,)), ((), ())), preferred_element_type=f32
+        ).astype(bf16)
+        dq, dk, dv = attention_backward(
+            packed, kv_all, attended_grad, attended, lse, query_segs, key_segs, factor
+        )
+        dkv = jnp.concatenate([dk, dv], axis=1)
+        other_dkv = swap_section(dkv[half_frames:].astype(bf16))
+        dkv_own = (dkv[:half_frames] + other_dkv.astype(f32)).astype(bf16)
+        packed_grad = jnp.concatenate([dq, dkv_own], axis=1)
+        part = lax.dot_general(
+            packed_grad, w_qkv, (((1,), (1,)), ((), ())), preferred_element_type=f32
+        )
+        normed_grad = pair_sum(part)
+        grad_out_weight = lax.dot_general(
+            attended, attn_branch, (((0,), (0,)), ((), ())), preferred_element_type=f32
+        ).astype(bf16)
+        grad_qkv = lax.dot_general(
+            normed_one, packed_grad, (((0,), (0,)), ((), ())), preferred_element_type=f32
+        ).astype(bf16)
+        in_grad, gain_one_grad = norm_back(layer_in, gain_one, normed_grad)
+        grad_in = resid_grad + in_grad
+        grad_up = jnp.concatenate([grad_up, to_column(gain_two_grad.astype(bf16), 128)], axis=1)
+        grad_qkv = jnp.concatenate([grad_qkv, to_column(gain_one_grad.astype(bf16), 128)], axis=1)
+        sums = []
+        for member in (grad_qkv, grad_out_weight, grad_up, grad_down):
+            blocks = member.reshape(2 * dp_count, 2, -1, member.shape[-1])
+            keep, send = choose(sec0, blocks[:, 0], blocks[:, 1])
+            total = (keep.astype(f32) + swap_section(send).astype(f32)).astype(bf16)
+            sums.append(scatter_yz(total))
+        reduced[layer] = sums
+        grad_out = grad_in.astype(bf16).astype(f32)
+    grad_in_low = grad_in.astype(bf16)
+
+    lig_send = jnp.transpose(grad_in_low.reshape(half_frames, 8, block_width), (1, 0, 2))
+    lig_got = lax.all_to_all(lig_send, both, 0, 0, tiled=True).reshape(2, 2, 2, half_frames, block_width)
+    lig = jnp.transpose(lig_got[:, :, 0], (1, 0, 2, 3)).reshape(micro_count, row_frames, block_width)
+    conv_grad = (lig.astype(f32) * slope.astype(f32)).astype(bf16)
+    grad_views = group_view(conv_grad, per_group)
+    back = ungroup(conv_back(grad_views, bands), per_group)
+    grad_signal = (lig.astype(f32) + back).astype(bf16)
+    gs_send = jnp.transpose(
+        grad_signal.reshape(micro_count, 4, frames, block_width), (1, 0, 2, 3)
+    )
+    gs_send = jnp.concatenate([gs_send, gs_send], axis=0)
+    gs_got = lax.all_to_all(gs_send, both, 0, 0, tiled=True)
+    gs_rows = jnp.transpose(gs_got, (1, 2, 0, 3)).reshape(micro_count, frames, width).astype(f32)
+
+    taps_grad = conv_taps_grad(sig_views, grad_views, per_group)
+    bias_grad = jnp.sum(conv_grad.astype(f32), axis=(0, 1))
+    taps_view = jnp.transpose(
+        taps_grad.reshape(2, dp_count, 4, rows_here, block_width), (1, 0, 2, 3, 4)
+    ).astype(bf16)
+    bias_view = jnp.pad(
+        jnp.broadcast_to(bias_grad.astype(bf16), (dp_count, 2, 4, 1, block_width)),
+        ((0, 0), (0, 0), (0, 0), (0, 15), (0, 0)),
+    )
+    taps_send = jnp.concatenate([taps_view, bias_view], axis=3)
+    taps_sum = lax.psum_scatter(taps_send, "dp", scatter_dimension=0, tiled=False)
+    taps_got = lax.all_to_all(
+        taps_sum.reshape(8, rows_here + 16, block_width), both, 0, 0, tiled=True
+    )
+    conv_weight_grad = jnp.transpose(taps_got[:, :rows_here], (1, 0, 2)).reshape(rows_here, width).astype(f32)
+    bias_count = conv_bias.shape[0]
+    conv_bias_grad = lax.dynamic_slice_in_dim(
+        taps_got[:, rows_here].reshape(width),
+        ((sec * dp_count + dp) * 4 + seq) * bias_count,
+        bias_count,
+        0,
+    ).astype(f32)
+
+    own_block = jnp.where(x0, output[:frames], output[frames:])
+    row_block = lax.ppermute(own_block, both, across)
+    other_row = swap_section(row_block)
+    output_rows = jnp.stack(choose(sec0, row_block, other_row))
+    ends = jnp.where(sec0, gs_rows, output_rows)[None]
+
+    own_layer = []
+    for first, second in zip(reduced[0], reduced[1]):
+        keep, send = choose(sec0, first, second)
+        got = swap_section(send)
+        own_layer.append(choose(sec0, keep, got))
+
+    def finish_columns(pair, unit):
+        keep, send = choose(x0, pair[0], pair[1])
+        rows = keep.shape[0]
+        columns = keep.shape[1] - 128
+        gain_grad = keep[:, columns].astype(f32)
+        got = swap_x(send)
+        shape = (rows, columns // unit, unit)
+        parity = choose(x0, keep[:, :columns].reshape(shape), got[:, :columns].reshape(shape))
+        joined = jnp.stack(parity, axis=2).reshape(rows, 2 * columns)
+        return joined.astype(f32)[None], gain_grad[None]
+
+    qkv_grad, norm1_grad = finish_columns(own_layer[0], HEAD_DIM)
+    up_grad, norm2_grad = finish_columns(own_layer[2], down_weight.shape[1])
+    out_grad = jnp.concatenate(own_layer[1], axis=0).astype(f32)[None]
+    down_grad = jnp.concatenate(own_layer[3], axis=0).astype(f32)[None]
+    return (ends, conv_weight_grad, conv_bias_grad, norm1_grad, qkv_grad, out_grad, norm2_grad, up_grad, down_grad)
+
+
 def solution(mesh):
     placed = (
         P("dp", "seq", None),
@@ -519,8 +1070,13 @@
         P("section", ("dp", "seq"), None),
         P("dp", "seq", None),
     )
+
+    def step(*arrays):
+        pairs = mesh.shape["seq"] == 4 and mesh.shape["section"] == 2 and arrays[0].shape[0] == 2
+        return (per_device_pairs if pairs else per_device)(*arrays)
+
     return jax.shard_map(
-        per_device,
+        step,
         mesh=mesh,
         in_specs=placed,
         out_specs=(

time: 5250 us -> 1260 us (0.24)
  local copies, waits for them, and re-layouts: 1770 us -> 105 us
  waiting for transfers between devices: 1910 us -> 632 us
  matrix products: 614 us -> 118 us
  starting transfers between devices: 574 us -> 101 us
  blocking collectives: 177 us -> 79.7 us
  Pallas kernels: 0 us -> 63.8 us
    another operation x274 -> x7, local copies, waits for them, and re-layouts: 1290 us -> 4.02 us  [the longest x6 3.94 us: per_device_pairs(): joined = jnp.stack([first, second], axis=1)]
    all_gather x17 -> x6, waiting for transfers between devices: 1260 us -> 90.2 us  [gather_yz(): lax.all_gather(value, ('dp', 'seq'), axis=0, tiled=False, axis_index_grou...]
    dot_general x78 -> x24, matrix products: 614 us -> 78.6 us  [the longest x2 24.1 us: per_device_pairs(): hidden_pre = jnp.dot(normed_two, w_up, preferred_element_type=f32)]
    ppermute x16 -> x50, starting transfers between devices: 572 us -> 75.2 us  [the longest x29 35.6 us: swap_section(): return lax.ppermute(value, 'section', [(0, 1), (1, 0)])]
    reduce_scatter x5 -> x9, waiting for transfers between devices: 632 us -> 300 us  [the longest x8 258 us: scatter_yz(): lax.psum_scatter(value, ('dp', 'seq'), scatter_dimension=0, tiled=False,...]
    ppermute x16 -> x50, waiting for transfers between devices: 13.7 us -> 225 us  [the longest x13 159 us: swap_x(): return lax.ppermute(value, 'seq', [(q, q ^ 1) for q in range(4)])]
    unnamed x744 -> x233, local copies, waits for them, and re-layouts: 200 us -> 20.2 us
    unnamed x3 -> x0, blocking collectives: 136 us -> none
  transfers between devices with their start and end apart: 40 -> 70, of which waited for: 22 -> 30; matrix products, arithmetic and copies ran while one was open for 43% -> 25% of each run, Pallas kernels for 0% -> 4%
where the time goes in v1:
time: 1260 us; the launch traced here: 1250 us
  waiting for transfers between devices  632 us (50%)
  other arithmetic  135 us (11%)
  matrix products  118 us (9%)
  local copies, waits for them, and re-layouts  105 us (8%)
  starting transfers between devices  101 us (8%)
  blocking collectives  79.7 us (6%)
  Pallas kernels  63.8 us (5%)
  between operations  17 us (1%)
    reduce_scatter x8, waiting for transfers between devices, scatter_yz(): lax.psum_scatter(value, ('dp', 'seq'), scatter_dimension=0, tiled=False,...  258 us
    ppermute x13, waiting for transfers between devices, swap_x(): return lax.ppermute(value, 'seq', [(q, q ^ 1) for q in range(4)])  159 us
    all_gather x6, waiting for transfers between devices, gather_yz(): lax.all_gather(value, ('dp', 'seq'), axis=0, tiled=False, axis_index_grou...  90.2 us
    all_gather x2, blocking collectives, gather_yz(): lax.all_gather(value, ('dp', 'seq'), axis=0, tiled=False, axis_index_grou...  65.9 us
    reduce_scatter x1, waiting for transfers between devices, per_device_pairs(): lax.psum_scatter(taps_send, 'dp', scatter_dimension=0, tiled=False)  41 us
    pallas_call x2, Pallas kernels, attention_backward(): pl.pallas_call(functools.partial(attention_backward_kernel, factor), grid...  37.5 us
    ppermute x29, starting transfers between devices, swap_section(): return lax.ppermute(value, 'section', [(0, 1), (1, 0)])  35.6 us
    pallas_call x2, Pallas kernels, attention_forward(): pl.pallas_call(functools.partial(attention_forward_kernel, factor), grid=...  26.3 us
  transfers between devices with their start and end apart: 70, of which 30 were waited for; matrix products, arithmetic and copies ran while one was open for 25% of the time, Pallas kernels for 4%

profile of v1, /device:TPU:17, one launch (start us, length us, event | category | flops | bytes accessed | tf_op | source)
XLA Modules:
  0.0 1250.8 jit_solution(5604123344083706591)
XLA Ops:
  37.5 13.8 %all_to_all.30 = bf16[8,272,128]{2,1,0:T(8,128)(2,1)S(1)} all-to-all(bf16[8,272,128]{2,1,0:T(8,128)(2,1)S(1)} %fusion.148), channel_id=1, replica_groups=mesh['section'=2,'dp'=4,'seq'=4] {'section','seq'}, dimensions={0} | all-to-all | bytes 1114112 | tf_op jit(solution)/shard_map/all_to_all | solution.py:815
  57.5 18.6 %collective-permute-done.7 = bf16[8,272,128]{2,1,0:T(8,128)(2,1)S(1)} collective-permute-done((bf16[8,272,128]{2,1,0:T(8,128)(2,1)S(1)}, bf16[8,272,128]{2,1,0:T(8,128)(2,1)S(1)}, u32[]{:S(2)}, u32[]{:S(2)}) %collective-permute-start.7) | collective-permute-done | bytes 557088 | tf_op jit(solution)/shard_map/ppermute | solution.py:829
  113.0 20.6 %collective-permute-done.6 = bf16[8,272,128]{2,1,0:T(8,128)(2,1)} collective-permute-done((bf16[8,272,128]{2,1,0:T(8,128)(2,1)}, bf16[8,272,128]{2,1,0:T(8,128)(2,1)}, u32[]{:S(2)}, u32[]{:S(2)}) %collective-permute-start.6) | collective-permute-done | bytes 557088 | tf_op jit(solution)/shard_map/ppermute | solution.py:828
  169.0 38.6 %all-gather.2 = bf16[256,1024]{1,0:T(8,128)(2,1)S(1)} all-gather(bf16[32,1024]{1,0:T(8,128)(2,1)S(1)} %copy-done.85), channel_id=4, replica_groups={{0,2,4,6,8,10,12,14},{1,3,5,7,9,11,13,15},{16,18,20,22,24,26,28,30},{17..., dimensions={0}, use_global_device_ids=true | all-gather | bytes 589824 | tf_op jit(solution)/shard_map/all_gather | solution.py:533
  213.7 27.3 %all-gather.6 = bf16[256,1024]{1,0:T(8,128)(2,1)S(1)} all-gather(bf16[32,1024]{1,0:T(8,128)(2,1)S(1)} %get-tuple-element.133), channel_id=8, replica_groups={{0,2,4,6,8,10,12,14},{1,3,5,7,9,11,13,15},{16,18,20,22,24,26,28,30},{17..., dimensions={0}, use_global_device_ids=true | all-gather | bytes 589824 | tf_op jit(solution)/shard_map/all_gather | solution.py:533
  259.3 45.0 %all-gather.15.cloned.1.call-done = bf16[1024,1024]{1,0:T(8,128)(2,1)} async-done(((bf16[128,1024]{1,0:T(8,128)(2,1)}), bf16[1024,1024]{1,0:T(8,128)(2,1)}) %all-gather.15.cloned.1.call-update) | async-done | bytes 2097168 | tf_op jit(solution)/shard_map/all_gather | solution.py:533
  310.8 45.2 %all-gather.25.cloned.1.call-done = bf16[512,2176]{1,0:T(8,128)(2,1)} async-done(((bf16[64,2176]{1,0:T(8,128)(2,1)}), bf16[512,2176]{1,0:T(8,128)(2,1)}) %all-gather.25.cloned.1.call-update) | async-done | bytes 2228240 | tf_op jit(solution)/shard_map/all_gather | solution.py:533
  359.0 13.0 %attention_forward.2 = (bf16[512,512]{1,0:T(8,128)(2,1)S(1)}, f32[4,2,512,1]{3,2,1,0:T(8,128)S(1)}) custom-call(bf16[512,1536]{1,0:T(8,128)(2,1)S(1)} %convolution_convert_fusion.7.q_ref, bf16[1024,1024]{1,0:T(8,128)(2,1)S(1)} %pad_maximum_fusion.6.k_ref.v_ref, bf16[1024,1024]{1,0:T(8,128)(2,1)S(1)} %pad_maximum_fusion.6.k_ref.v_ref, ...), custom_call_target="tpu_custom_call" | custom-call | flops 2147483648 | bytes 3145728 | tf_op jit(solution)/shard_map/attention_forward/pallas_call | solution.py:594
  377.7 19.9 %collective-permute-done.16 = bf16[512,1024]{1,0:T(8,128)(2,1)S(1)} collective-permute-done((bf16[512,1024]{1,0:T(8,128)(2,1)S(1)}, bf16[512,1024]{1,0:T(8,128)(2,1)S(1)}, u32[]{:S(2)}, u32[]{:S(2)}) %collective-permute-start.16) | collective-permute-done | bytes 1048608 | tf_op jit(solution)/shard_map/ppermute | solution.py:516
  398.6 13.0 %fusion.27 = (bf16[512,2048]{1,0:T(8,128)(2,1)S(1)}, f32[512,2048]{1,0:T(8,128)}) fusion(bf16[1024,2176]{1,0:T(8,128)(2,1)S(1)} %bitcast.453, f32[512,1024]{1,0:T(8,128)S(1)} %get-tuple-element.70, f32[1024]{0:T(1024)S(1)} %convert_reduce_fusion.4, f32[512]{0:T(512)S(1)} %add_rsqrt_fusion.2, f32[512]{0:T(512)S(1)} %broadcast_multiply_fusion.10), kind=kOutput, calls=%fused_computation.44 | convolution fusion | flops 2217738240 | bytes 12591104 | tf_op jit(solution)/shard_map/dot_general | solution.py:925
  417.8 20.1 %collective-permute-done.21 = bf16[512,1024]{1,0:T(8,128)(2,1)S(1)} collective-permute-done((bf16[512,1024]{1,0:T(8,128)(2,1)S(1)}, bf16[512,1024]{1,0:T(8,128)(2,1)S(1)}, u32[]{:S(2)}, u32[]{:S(2)}) %collective-permute-start.21) | collective-permute-done | bytes 1048608 | tf_op jit(solution)/shard_map/ppermute | solution.py:516
  449.2 13.3 %attention_forward.3 = (bf16[512,512]{1,0:T(8,128)(2,1)S(1)}, f32[4,2,512,1]{3,2,1,0:T(8,128)S(1)}) custom-call(bf16[512,1536]{1,0:T(8,128)(2,1)S(1)} %convolution_convert_fusion.6.q_ref, bf16[1024,1024]{1,0:T(8,128)(2,1)S(1)} %pad_maximum_fusion.7.k_ref.v_ref, bf16[1024,1024]{1,0:T(8,128)(2,1)S(1)} %pad_maximum_fusion.7.k_ref.v_ref, ...), custom_call_target="tpu_custom_call" | custom-call | flops 2147483648 | bytes 3145728 | tf_op jit(solution)/shard_map/attention_forward/pallas_call | solution.py:594
  468.0 19.1 %collective-permute-done.25 = bf16[512,1024]{1,0:T(8,128)(2,1)S(1)} collective-permute-done((bf16[512,1024]{1,0:T(8,128)(2,1)S(1)}, bf16[512,1024]{1,0:T(8,128)(2,1)S(1)}, u32[]{:S(2)}, u32[]{:S(2)}) %collective-permute-start.25) | collective-permute-done | bytes 1048608 | tf_op jit(solution)/shard_map/ppermute | solution.py:516
  509.7 18.9 %collective-permute-done.27 = bf16[512,1024]{1,0:T(8,128)(2,1)S(1)} collective-permute-done((bf16[512,1024]{1,0:T(8,128)(2,1)S(1)}, bf16[512,1024]{1,0:T(8,128)(2,1)S(1)}, u32[]{:S(2)}, u32[]{:S(2)}) %collective-permute-start.27) | collective-permute-done | bytes 1048608 | tf_op jit(solution)/shard_map/ppermute | solution.py:516
  529.6 21.5 %collective-permute-done.33 = bf16[512,1024]{1,0:T(8,128)(2,1)S(1)} collective-permute-done((bf16[512,1024]{1,0:T(8,128)(2,1)S(1)}, bf16[512,1024]{1,0:T(8,128)(2,1)S(1)}, u32[]{:S(2)}, u32[]{:S(2)}) %collective-permute-start.33) | collective-permute-done | bytes 1048608 | tf_op jit(solution)/shard_map/ppermute | solution.py:516
  554.5 18.7 %attention_backward.2 = (bf16[512,512]{1,0:T(8,128)(2,1)S(1)}, f32[1024,512]{1,0:T(8,128)S(1)}, f32[1024,512]{1,0:T(8,128)}) custom-call(bf16[512,1536]{1,0:T(8,128)(2,1)S(1)} %convolution_convert_fusion.6.q_ref, bf16[1024,1024]{1,0:T(8,128)(2,1)} %copy-done.1, bf16[1024,1024]{1,0:T(8,128)(2,1)} %copy-done.1, ...), custom_call_target="tpu_custom_call" | custom-call | flops 5368709120 | bytes 6291456 | tf_op jit(solution)/shard_map/attention_backward/pallas_call | solution.py:674
  585.3 21.6 %collective-permute-done.29 = bf16[512,1024]{1,0:T(8,128)(2,1)S(1)} collective-permute-done((bf16[512,1024]{1,0:T(8,128)(2,1)S(1)}, bf16[512,1024]{1,0:T(8,128)(2,1)S(1)}, u32[]{:S(2)}, u32[]{:S(2)}) %collective-permute-start.29) | collective-permute-done | bytes 1048608 | tf_op jit(solution)/shard_map/ppermute | solution.py:516
  625.9 14.3 %collective-permute-done.30 = bf16[512,1024]{1,0:T(8,128)(2,1)} collective-permute-done((bf16[512,1024]{1,0:T(8,128)(2,1)S(1)}, bf16[512,1024]{1,0:T(8,128)(2,1)}, u32[]{:S(2)}, u32[]{:S(2)}) %collective-permute-start.30) | collective-permute-done | bytes 1048608 | tf_op jit(solution)/shard_map/ppermute | solution.py:516
  709.3 18.8 %attention_backward.3 = (bf16[512,512]{1,0:T(8,128)(2,1)S(1)}, f32[1024,512]{1,0:T(8,128)S(1)}, f32[1024,512]{1,0:T(8,128)}) custom-call(bf16[512,1536]{1,0:T(8,128)(2,1)S(1)} %convolution_convert_fusion.7.q_ref, bf16[1024,1024]{1,0:T(8,128)(2,1)} %copy-done, bf16[1024,1024]{1,0:T(8,128)(2,1)} %copy-done, ...), custom_call_target="tpu_custom_call" | custom-call | flops 5368709120 | bytes 6291456 | tf_op jit(solution)/shard_map/attention_backward/pallas_call | solution.py:674
  913.2 58.3 %reduce-scatter.22.cloned.1.call-done = bf16[1,64,2176]{2,1,0:T(8,128)(2,1)} async-done(((bf16[8,64,2176]{2,1,0:T(8,128)(2,1)}), bf16[1,64,2176]{2,1,0:T(8,128)(2,1)}) %reduce-scatter.22.cloned.1.call-update) | async-done | bytes 278544 | tf_op jit(solution)/shard_map/reduce_scatter | solution.py:537
  971.5 70.9 %reduce-scatter.20.cloned.1.call-done = bf16[1,64,2176]{2,1,0:T(8,128)(2,1)} async-done(((bf16[8,64,2176]{2,1,0:T(8,128)(2,1)}), bf16[1,64,2176]{2,1,0:T(8,128)(2,1)}) %reduce-scatter.20.cloned.1.call-update) | async-done | bytes 278544 | tf_op jit(solution)/shard_map/reduce_scatter | solution.py:537
  1049.4 61.0 %reduce-scatter.14.cloned.1.call-done = bf16[1,64,1664]{2,1,0:T(8,128)(2,1)} async-done(((bf16[8,64,1664]{2,1,0:T(8,128)(2,1)}), bf16[1,64,1664]{2,1,0:T(8,128)(2,1)}) %reduce-scatter.14.cloned.1.call-update) | async-done | bytes 213008 | tf_op jit(solution)/shard_map/reduce_scatter | solution.py:537
  1110.4 68.2 %reduce-scatter.12.cloned.1.call-done = bf16[1,64,1664]{2,1,0:T(8,128)(2,1)} async-done(((bf16[8,64,1664]{2,1,0:T(8,128)(2,1)}), bf16[1,64,1664]{2,1,0:T(8,128)(2,1)}) %reduce-scatter.12.cloned.1.call-update) | async-done | bytes 213008 | tf_op jit(solution)/shard_map/reduce_scatter | solution.py:537
  1186.5 41.0 %reduce-scatter.10.cloned.1.call-done = bf16[1,2,4,272,128]{4,3,2,1,0:T(8,128)(2,1)} async-done(((bf16[4,2,4,272,128]{4,3,2,1,0:T(8,128)(2,1)}), bf16[1,2,4,272,128]{4,3,2,1,0:T(8,128)(2,1)}) %reduce-scatter.10.cloned.1.call-update) | async-done | bytes 557072 | tf_op jit(solution)/shard_map/reduce_scatter | solution.py:1016
  (622 shorter events, 513.1 us)
Async XLA Ops:
  7.2 161.6 %all-gather.17.cloned.1.call-start = ((), (), s32[]{:S(2)}) async-start(), calls=%async_computation.25 | async-start | bytes 1916928 | tf_op jit(solution)/shard_map/all_gather | solution.py:533
  21.1 227.4 %all-gather.21.cloned.1.call-start = ((), (), s32[]{:S(2)}) async-start(), calls=%async_computation.27 | async-start | bytes 2359296 | tf_op jit(solution)/shard_map/all_gather | solution.py:533
  23.7 225.1 %all-gather.19.cloned.1.call-start = ((), (), s32[]{:S(2)}) async-start(), calls=%async_computation.26 | async-start | bytes 2506752 | tf_op jit(solution)/shard_map/all_gather | solution.py:533
  36.7 222.3 %all-gather.23.cloned.1.call-start = ((), (), s32[]{:S(2)}) async-start(), calls=%async_computation.28 | async-start | bytes 1916928 | tf_op jit(solution)/shard_map/all_gather | solution.py:533
  83.1 162.9 %collective-permute-start = (bf16[256,1024]{1,0:T(8,128)(2,1)}, bf16[256,1024]{1,0:T(8,128)(2,1)}, u32[]{:S(2)}, u32[]{:S(2)}) collective-permute-start(bf16[256,1024]{1,0:T(8,128)(2,1)} %select_bitcast_fusion.26), channel_id=1, source_target_pairs={{0,0},{1,1},{2,16},{3,17},{16,2},{17,3},{18,18},{19,19},{4,4},{5,5... | collective-permute-start | bytes 1572872 | tf_op jit(solution)/shard_map/ppermute | solution.py:893
  93.0 211.3 %all-gather.15.cloned.1.call-start = ((), (), s32[]{:S(2)}) async-start(), calls=%async_computation.24 | async-start | bytes 2359296 | tf_op jit(solution)/shard_map/all_gather | solution.py:533
  168.8 187.2 %all-gather.25.cloned.1.call-start = ((), (), s32[]{:S(2)}) async-start(), calls=%async_computation.29 | async-start | bytes 2506752 | tf_op jit(solution)/shard_map/all_gather | solution.py:533
  213.7 534.1 %reduce-scatter.18.cloned.1.call-start = ((), (), s32[]{:S(2)}) async-start(), calls=%async_computation.19 | async-start | bytes 589824 | tf_op jit(solution)/shard_map/reduce_scatter | solution.py:537
  246.0 197.0 %collective-permute-start.1 = (bf16[256,1024]{1,0:T(8,128)(2,1)}, bf16[256,1024]{1,0:T(8,128)(2,1)}, u32[]{:S(2)}, u32[]{:S(2)}) collective-permute-start(bf16[256,1024]{1,0:T(8,128)(2,1)} %collective-permute-done), channel_id=1, source_target_pairs={{0,1},{1,0},{2,3},{3,2},{4,5},{5,4},{6,7},{7,6},{8,9},{9,8},{10,11... | collective-permute-start | bytes 1572872 | tf_op jit(solution)/shard_map/ppermute | solution.py:516
  248.8 124.0 %collective-permute-start.19 = (bf16[8,64,2176]{2,1,0:T(8,128)(2,1)}, bf16[8,64,2176]{2,1,0:T(8,128)(2,1)}, u32[]{:S(2)}, u32[]{:S(2)}) collective-permute-start(bf16[8,64,2176]{2,1,0:T(8,128)(2,1)} %bitcast.485), channel_id=1, source_target_pairs={{0,16},{16,0},{1,17},{17,1},{2,18},{18,2},{3,19},{19,3},{4,20},{20... | collective-permute-start | bytes 6684680 | tf_op jit(solution)/shard_map/ppermute | solution.py:512
  255.4 100.7 %collective-permute-start.13 = (bf16[512,1024]{1,0:T(8,128)(2,1)}, bf16[512,1024]{1,0:T(8,128)(2,1)}, u32[]{:S(2)}, u32[]{:S(2)}) collective-permute-start(bf16[512,1024]{1,0:T(8,128)(2,1)} %slice.316), channel_id=1, source_target_pairs={{0,16},{16,0},{1,17},{17,1},{2,18},{18,2},{3,19},{19,3},{4,20},{20... | collective-permute-start | bytes 3145736 | tf_op jit(solution)/shard_map/ppermute | solution.py:512
  259.0 156.3 %collective-permute-start.22 = (bf16[8,64,1664]{2,1,0:T(8,128)(2,1)}, bf16[8,64,1664]{2,1,0:T(8,128)(2,1)}, u32[]{:S(2)}, u32[]{:S(2)}) collective-permute-start(bf16[8,64,1664]{2,1,0:T(8,128)(2,1)} %bitcast.503), channel_id=1, source_target_pairs={{0,16},{16,0},{1,17},{17,1},{2,18},{18,2},{3,19},{19,3},{4,20},{20... | collective-permute-start | bytes 5111816 | tf_op jit(solution)/shard_map/ppermute | solution.py:512
  304.3 140.1 %collective-permute-start.3 = (bf16[8,128,1024]{2,1,0:T(8,128)(2,1)}, bf16[8,128,1024]{2,1,0:T(8,128)(2,1)}, u32[]{:S(2)}, u32[]{:S(2)}) collective-permute-start(bf16[8,128,1024]{2,1,0:T(8,128)(2,1)} %bitcast.501), channel_id=1, source_target_pairs={{0,16},{16,0},{1,17},{17,1},{2,18},{18,2},{3,19},{19,3},{4,20},{20... | collective-permute-start | bytes 6291464 | tf_op jit(solution)/shard_map/ppermute | solution.py:512
  356.0 108.5 %collective-permute-start.26 = (bf16[8,64,2176]{2,1,0:T(8,128)(2,1)}, bf16[8,64,2176]{2,1,0:T(8,128)(2,1)}, u32[]{:S(2)}, u32[]{:S(2)}) collective-permute-start(bf16[8,64,2176]{2,1,0:T(8,128)(2,1)} %bitcast.487), channel_id=1, source_target_pairs={{0,16},{16,0},{1,17},{17,1},{2,18},{18,2},{3,19},{19,3},{4,20},{20... | collective-permute-start | bytes 6684680 | tf_op jit(solution)/shard_map/ppermute | solution.py:512
  625.5 122.4 %reduce-scatter.16.cloned.1.call-start = ((), (), s32[]{:S(2)}) async-start(), calls=%async_computation.18 | async-start | bytes 589824 | tf_op jit(solution)/shard_map/reduce_scatter | solution.py:537
  651.8 260.4 %reduce-scatter.26.cloned.1.call-start = ((), (), s32[]{:S(2)}) async-start(), calls=%async_computation.23 | async-start | bytes 2359296 | tf_op jit(solution)/shard_map/reduce_scatter | solution.py:537
  657.6 254.5 %reduce-scatter.24.cloned.1.call-start = ((), (), s32[]{:S(2)}) async-start(), calls=%async_computation.22 | async-start | bytes 2359296 | tf_op jit(solution)/shard_map/reduce_scatter | solution.py:537
  671.9 299.6 %reduce-scatter.22.cloned.1.call-start = ((), (), s32[]{:S(2)}) async-start(), calls=%async_computation.21 | async-start | bytes 2506752 | tf_op jit(solution)/shard_map/reduce_scatter | solution.py:537
  683.7 358.7 %reduce-scatter.20.cloned.1.call-start = ((), (), s32[]{:S(2)}) async-start(), calls=%async_computation.20 | async-start | bytes 2506752 | tf_op jit(solution)/shard_map/reduce_scatter | solution.py:537
  693.9 416.5 %reduce-scatter.14.cloned.1.call-start = ((), (), s32[]{:S(2)}) async-start(), calls=%async_computation.17 | async-start | bytes 1916928 | tf_op jit(solution)/shard_map/reduce_scatter | solution.py:537
  838.0 340.7 %reduce-scatter.12.cloned.1.call-start = ((), (), s32[]{:S(2)}) async-start(), calls=%async_computation.16 | async-start | bytes 1916928 | tf_op jit(solution)/shard_map/reduce_scatter | solution.py:537
  862.2 365.4 %reduce-scatter.10.cloned.1.call-start = ((), (), s32[]{:S(2)}) async-start(), calls=%async_computation.15 | async-start | bytes 2785280 | tf_op jit(solution)/shard_map/reduce_scatter | solution.py:1016
  913.1 132.2 %collective-permute-start.49 = (bf16[128,1024]{1,0:T(8,128)(2,1)S(1)}, bf16[128,1024]{1,0:T(8,128)(2,1)S(1)}, u32[]{:S(2)}, u32[]{:S(2)}) collective-permute-start(bf16[128,1024]{1,0:T(8,128)(2,1)S(1)} %select_bitcast_fusion.28), channel_id=1, source_target_pairs={{0,16},{16,0},{1,17},{17,1},{2,18},{18,2},{3,19},{19,3},{4,20},{20... | collective-permute-start | bytes 786440 | tf_op jit(solution)/shard_map/ppermute | solution.py:512
  1047.6 134.1 %collective-permute-start.46 = (bf16[64,2176]{1,0:T(8,128)(2,1)S(1)}, bf16[64,2176]{1,0:T(8,128)(2,1)S(1)}, u32[]{:S(2)}, u32[]{:S(2)}) collective-permute-start(bf16[64,2176]{1,0:T(8,128)(2,1)S(1)} %get-tuple-element.59), channel_id=1, source_target_pairs={{0,1},{1,0},{2,3},{3,2},{4,5},{5,4},{6,7},{7,6},{8,9},{9,8},{10,11... | collective-permute-start | bytes 835592 | tf_op jit(solution)/shard_map/ppermute | solution.py:516
  (156 other events, 2491.4 us)
Sparse Core Ops, SparseCore 0:
  21.2 51.4 all-gather.16
  75.4 58.7 all-gather.20
  136.9 65.7 all-gather.18
  204.8 49.7 all-gather.22
  256.5 47.6 all-gather.14
  306.9 49.0 all-gather.24
  625.6 56.6 reduce-scatter.17
  686.0 60.8 reduce-scatter.15
  750.4 73.4 reduce-scatter.25
  827.4 72.7 reduce-scatter.23
  903.7 67.8 reduce-scatter.21
  974.8 67.5 reduce-scatter.19
  1045.8 64.5 reduce-scatter.13
  1114.1 64.5 reduce-scatter.11
  1180.8 46.6 reduce-scatter.9

commit v2 on v1

--- a/solution.py
+++ b/solution.py
@@ -525,17 +525,70 @@
     return jnp.where(flag, first, second), jnp.where(flag, second, first)
 
 
-def y_groups():
-    return [[d * 4 + y * 2 + x for d in range(lax.axis_size("dp")) for y in range(2)] for x in range(2)]
-
-
-def gather_yz(value):
-    return lax.all_gather(value, ("dp", "seq"), axis=0, tiled=False, axis_index_groups=y_groups())
-
-
-def scatter_yz(value):
+def chain_steps(value):
+    count = lax.axis_size("dp")
+    upward = [(i, i + 1) for i in range(count - 1)]
+    downward = [(i + 1, i) for i in range(count - 1)]
+    low, high = value, value
+    lows, highs = [], []
+    for _ in range(count - 1):
+        low = lax.ppermute(low, "dp", upward)
+        high = lax.ppermute(high, "dp", downward)
+        lows.append(low)
+        highs.append(high)
+    return lows, highs
+
+
+def place_dp(value, dp):
+    count = lax.axis_size("dp")
+    lows, highs = chain_steps(value)
+    whole = jnp.zeros((count, *value.shape), value.dtype)
+    whole = lax.dynamic_update_index_in_dim(whole, value, dp, 0)
+    for turn in range(1, count):
+        piece = jnp.where(dp + turn < count, highs[turn - 1], lows[count - turn - 1])
+        whole = lax.dynamic_update_index_in_dim(whole, piece, (dp + turn) % count, 0)
+    return whole
+
+
+def sum_dp(blocks, dp):
+    count = lax.axis_size("dp")
+    f32, bf16 = jnp.float32, jnp.bfloat16
+
+    def block(index):
+        return lax.dynamic_index_in_dim(blocks, jnp.clip(index, 0, count - 1), 0, keepdims=False)
+
+    total = block(dp).astype(f32)
+    for sign in (1, -1):
+        pairs = [(i, i + sign) for i in range(count) if 0 <= i + sign < count]
+        running = None
+        for distance in range(count - 1, 0, -1):
+            own = block(dp + sign * distance)
+            if running is not None:
+                own = (own.astype(f32) + running.astype(f32)).astype(bf16)
+            live = [(a, b) for a, b in pairs if 0 <= a + sign * distance < count]
+            running = lax.ppermute(own, "dp", live)
+        total = total + running.astype(f32)
+    return total.astype(bf16)
+
+
+def line_groups():
+    count = lax.axis_size("dp")
+    return [
+        [(s * count + d) * 4 + 2 * y + x for d in range(count) for y in range(2) for s in range(2)]
+        for x in range(2)
+    ]
+
+
+def gather_rows(piece):
+    return lax.all_gather(
+        piece, ("section", "dp", "seq"), axis=0, tiled=True, axis_index_groups=line_groups()
+    )
+
+
+def scatter_rows(partial):
     return lax.psum_scatter(
-        value, ("dp", "seq"), scatter_dimension=0, tiled=False, axis_index_groups=y_groups()
+        partial, ("section", "dp", "seq"), scatter_dimension=0, tiled=True,
+        axis_index_groups=line_groups(),
     )
 
 
@@ -773,10 +826,13 @@
             dimension_numbers=("CWN", "IWO", "WNC"),
             preferred_element_type=jnp.float32,
         )
-        flat = band.reshape(-1, CONV_STEP, per_group)
+        flat = band.reshape(-1, CONV_STEP * per_group)
         total = None
         for shift in range(CONV_STEP):
-            part = flat[shift * per_group : (shift + TAPS) * per_group, shift]
+            part = flat[
+                shift * per_group : (shift + TAPS) * per_group,
+                shift * per_group : (shift + 1) * per_group,
+            ]
             total = part if total is None else total + part
         results.append(total)
     return jnp.concatenate(results, axis=1)
@@ -819,27 +875,7 @@
     sig_got = lax.all_to_all(sig_send, "seq", 0, 0, tiled=True)
     sig_all = jnp.transpose(sig_got, (1, 0, 2, 3)).reshape(micro_count, row_frames, block_width)
 
-    up_chain = [(i, i + 1) for i in range(dp_count - 1)]
-    down_chain = [(i + 1, i) for i in range(dp_count - 1)]
-    from_low, from_high = conv_got, conv_got
-    pieces = [conv_got]
-    lows, highs = [], []
-    for _ in range(dp_count - 1):
-        from_low = lax.ppermute(from_low, "dp", up_chain)
-        from_high = lax.ppermute(from_high, "dp", down_chain)
-        lows.append(from_low)
-        highs.append(from_high)
-    ordered = []
-    for source in range(dp_count):
-        value = conv_got
-        for distance in range(1, dp_count):
-            if source - distance >= 0 or source + distance < dp_count:
-                if source + distance < dp_count:
-                    value = jnp.where(dp == source + distance, lows[distance - 1], value)
-                if source - distance >= 0:
-                    value = jnp.where(dp == source - distance, highs[distance - 1], value)
-        ordered.append(value)
-    conv_all = jnp.stack(ordered)
+    conv_all = place_dp(conv_got, dp)
     conv_all = conv_all.reshape(dp_count, 2, 4, rows_here + 16, block_width)
     conv_all = jnp.transpose(conv_all, (1, 0, 2, 3, 4))
     bias_all = conv_all[:, :, :, rows_here, : conv_bias.shape[0]].reshape(width)
@@ -847,46 +883,54 @@
     kernel_own = conv_all[:, :, :, :rows_here].reshape(TAPS * per_group, block_width)
     bands = conv_bands(kernel_own, per_group)
 
-    def exchange_columns(weight, gain, unit):
-        rows, columns = weight.shape
-        view = weight.astype(bf16).reshape(rows, columns // (2 * unit), 2, unit)
-        keep, send = choose(x0, view[:, :, 0], view[:, :, 1])
-        gain_part = to_column(gain.astype(bf16), 128)
-        keep = jnp.concatenate([keep.reshape(rows, columns // 2), gain_part], axis=1)
-        send = jnp.concatenate([send.reshape(rows, columns // 2), gain_part], axis=1)
-        got = swap_x(send)
-        return choose(x0, keep, got)
-
-    qkv_halves = exchange_columns(qkv_weight[0], norm1_gain[0], HEAD_DIM)
-    up_halves = exchange_columns(up_weight[0], norm2_gain[0], down_weight.shape[1])
-    out_rows = out_weight.shape[1] // 2
+    in_rows = qkv_weight.shape[1]
+    unit = down_weight.shape[1] // 4
+    qkv_view = qkv_weight[0].astype(bf16).reshape(in_rows, -1, 2, HEAD_DIM)
+    qkv_parity = [qkv_view[:, :, p].reshape(in_rows, -1) for p in range(2)]
+    up_view = up_weight[0].astype(bf16).reshape(in_rows, -1, 2, 2, 2, unit)
+    up_parity = [
+        jnp.transpose(up_view[:, :, p], (0, 3, 1, 2, 4)).reshape(in_rows, -1) for p in range(2)
+    ]
+    qkv_cols, up_cols = qkv_parity[0].shape[1], up_parity[0].shape[1]
+    col_one = to_column(norm1_gain[0].astype(bf16), 128)
+    col_two = to_column(norm2_gain[0].astype(bf16), 128)
+    cut = qkv_cols + 128
+    keep_cols, send_cols = [
+        jnp.concatenate([a, col_one, b, col_two], axis=1)
+        for a, b in zip(choose(x0, *qkv_parity), choose(x0, *up_parity))
+    ]
+    row_sets = choose(x0, keep_cols, swap_x(send_cols))
     out_low = out_weight[0].astype(bf16)
-    down_rows = down_weight.shape[1] // 2
-    down_low = down_weight[0].astype(bf16)
-    halves = (
-        qkv_halves,
-        (out_low[:out_rows], out_low[out_rows:]),
-        up_halves,
-        (down_low[:down_rows], down_low[down_rows:]),
-    )
-    own_parts = []
-    for first, second in halves:
-        keep, send = choose(sec0, first, second)
-        got = swap_section(send)
-        own_parts.append(choose(sec0, keep, got))
+    down_low = down_weight[0].astype(bf16).reshape(2, 2, unit, width)
+    out_at, up_at = cut, cut + width // 2
+    two_at = up_at + up_cols
+    down_at = two_at + 128
+    row_parts = [
+        jnp.concatenate(
+            [
+                row_sets[h][:, :cut],
+                out_low[:, h * width // 2 : (h + 1) * width // 2],
+                row_sets[h][:, cut:],
+                down_low[h, 0],
+                down_low[h, 1],
+            ],
+            axis=1,
+        )
+        for h in range(2)
+    ]
+    keep, send = choose(sec0, *row_parts)
+    layer_pieces = choose(sec0, keep, swap_section(send))
     layer_weights = []
     for layer in range(2):
-        full = []
-        for part in own_parts:
-            mine = gather_yz(part[layer])
-            other = swap_section(mine)
-            first, second = choose(sec0, mine, other)
-            joined = jnp.stack([first, second], axis=1)
-            full.append(joined.reshape(-1, joined.shape[-1]))
-        w_qkv, w_out, w_up, w_down = full
-        gain_one = w_qkv[:, -128].astype(f32)[None, :]
-        gain_two = w_up[:, -128].astype(f32)[None, :]
-        layer_weights.append((gain_one, w_qkv[:, :-128], w_out, gain_two, w_up[:, :-128], w_down))
+        whole = gather_rows(layer_pieces[layer])
+        w_out = jnp.transpose(
+            whole[:, out_at:up_at].reshape(-1, 2, in_rows, width // 2), (0, 2, 1, 3)
+        ).reshape(-1, width)
+        gain_one = whole[:, qkv_cols].astype(f32)[None, :]
+        gain_two = whole[:, two_at].astype(f32)[None, :]
+        w_up = [whole[:, up_at + part * width : up_at + (part + 1) * width] for part in range(2)]
+        w_down = [whole[:, down_at + part * width : down_at + (part + 1) * width] for part in range(2)]
+        layer_weights.append((gain_one, whole[:, :qkv_cols], w_out, gain_two, w_up, w_down))
 
     picked = jnp.where(sec0, cotangent[0], cotangent[1])
     across = [(s * 4 + 2 * yy + xx, yy * 4 + 2 * s + xx) for s in range(2) for yy in range(2) for xx in range(2)]
@@ -922,10 +966,15 @@
         resid_two = layer_in + pair_sum(jnp.dot(attended, w_out, preferred_element_type=f32))
         centred, inv = norm_stats(resid_two)
         normed_two = (centred * inv * gain_two).astype(bf16)
-        hidden_pre = jnp.dot(normed_two, w_up, preferred_element_type=f32)
-        hidden = smooth(hidden_pre).astype(bf16)
-        hidden_slope = gelu_slope(hidden_pre).astype(bf16)
-        result = resid_two + pair_sum(jnp.dot(hidden, w_down, preferred_element_type=f32))
+        hidden, hidden_slope, down_sum = [], [], None
+        for part in range(2):
+            hidden_pre = jnp.dot(normed_two, w_up[part], preferred_element_type=f32)
+            hidden.append(smooth(hidden_pre).astype(bf16))
+            hidden_slope.append(gelu_slope(hidden_pre).astype(bf16))
+        for part in range(2):
+            term = jnp.dot(hidden[part], w_down[part], preferred_element_type=f32)
+            down_sum = term if down_sum is None else down_sum + term
+        result = resid_two + pair_sum(down_sum)
         kept.append(
             (layer_in, normed_one, packed, kv_all, attended, lse, resid_two, normed_two, hidden, hidden_slope)
         )
@@ -938,20 +987,18 @@
         gain_one, w_qkv, w_out, gain_two, w_up, w_down = layer_weights[layer]
         (layer_in, normed_one, packed, kv_all, attended, lse, resid_two, normed_two, hidden, hidden_slope) = kept[layer]
         branch = grad_out.astype(bf16)
-        hidden_grad = lax.dot_general(
-            branch, w_down, (((1,), (1,)), ((), ())), preferred_element_type=f32
-        )
-        pre_grad = (hidden_grad * hidden_slope.astype(f32)).astype(bf16)
-        part = lax.dot_general(
-            pre_grad, w_up, (((1,), (1,)), ((), ())), preferred_element_type=f32
-        )
-        normed_grad = pair_sum(part)
-        grad_down = lax.dot_general(
-            hidden, branch, (((0,), (0,)), ((), ())), preferred_element_type=f32
-        ).astype(bf16)
-        grad_up = lax.dot_general(
-            normed_two, pre_grad, (((0,), (0,)), ((), ())), preferred_element_type=f32
-        ).astype(bf16)
+        pre_grad, part_sum = [], None
+        for part in range(2):
+            hidden_grad = lax.dot_general(
+                branch, w_down[part], (((1,), (1,)), ((), ())), preferred_element_type=f32
+            )
+            pre_grad.append((hidden_grad * hidden_slope[part].astype(f32)).astype(bf16))
+        for part in range(2):
+            term = lax.dot_general(
+                pre_grad[part], w_up[part], (((1,), (1,)), ((), ())), preferred_element_type=f32
+            )
+            part_sum = term if part_sum is None else part_sum + term
+        normed_grad = pair_sum(part_sum)
         resid_grad, gain_two_grad = norm_back(resid_two, gain_two, normed_grad)
         resid_grad = resid_grad + grad_out
         attn_branch = resid_grad.astype(bf16)
@@ -969,23 +1016,30 @@
             packed_grad, w_qkv, (((1,), (1,)), ((), ())), preferred_element_type=f32
         )
         normed_grad = pair_sum(part)
-        grad_out_weight = lax.dot_general(
-            attended, attn_branch, (((0,), (0,)), ((), ())), preferred_element_type=f32
-        ).astype(bf16)
-        grad_qkv = lax.dot_general(
-            normed_one, packed_grad, (((0,), (0,)), ((), ())), preferred_element_type=f32
-        ).astype(bf16)
         in_grad, gain_one_grad = norm_back(layer_in, gain_one, normed_grad)
         grad_in = resid_grad + in_grad
-        grad_up = jnp.concatenate([grad_up, to_column(gain_two_grad.astype(bf16), 128)], axis=1)
-        grad_qkv = jnp.concatenate([grad_qkv, to_column(gain_one_grad.astype(bf16), 128)], axis=1)
-        sums = []
-        for member in (grad_qkv, grad_out_weight, grad_up, grad_down):
-            blocks = member.reshape(2 * dp_count, 2, -1, member.shape[-1])
-            keep, send = choose(sec0, blocks[:, 0], blocks[:, 1])
-            total = (keep.astype(f32) + swap_section(send).astype(f32)).astype(bf16)
-            sums.append(scatter_yz(total))
-        reduced[layer] = sums
+        def outer(left, right):
+            return lax.dot_general(
+                left, right, (((0,), (0,)), ((), ())), preferred_element_type=f32
+            ).astype(bf16)
+
+        grad_out_weight = jnp.transpose(
+            outer(attended, attn_branch).reshape(-1, in_rows, 2, width // 2), (0, 2, 1, 3)
+        ).reshape(-1, width // 2)
+        partial = jnp.concatenate(
+            [
+                outer(normed_one, packed_grad),
+                to_column(gain_one_grad.astype(bf16), 128),
+                grad_out_weight,
+                outer(normed_two, pre_grad[0]),
+                outer(normed_two, pre_grad[1]),
+                to_column(gain_two_grad.astype(bf16), 128),
+                outer(hidden[0], branch),
+                outer(hidden[1], branch),
+            ],
+            axis=1,
+        )
+        reduced[layer] = scatter_rows(partial)
         grad_out = grad_in.astype(bf16).astype(f32)
     grad_in_low = grad_in.astype(bf16)
 
@@ -1013,7 +1067,7 @@
         ((0, 0), (0, 0), (0, 0), (0, 15), (0, 0)),
     )
     taps_send = jnp.concatenate([taps_view, bias_view], axis=3)
-    taps_sum = lax.psum_scatter(taps_send, "dp", scatter_dimension=0, tiled=False)
+    taps_sum = sum_dp(taps_send, dp)
     taps_got = lax.all_to_all(
         taps_sum.reshape(8, rows_here + 16, block_width), both, 0, 0, tiled=True
     )
@@ -1032,27 +1086,32 @@
     output_rows = jnp.stack(choose(sec0, row_block, other_row))
     ends = jnp.where(sec0, gs_rows, output_rows)[None]
 
-    own_layer = []
-    for first, second in zip(reduced[0], reduced[1]):
-        keep, send = choose(sec0, first, second)
-        got = swap_section(send)
-        own_layer.append(choose(sec0, keep, got))
-
-    def finish_columns(pair, unit):
-        keep, send = choose(x0, pair[0], pair[1])
-        rows = keep.shape[0]
-        columns = keep.shape[1] - 128
-        gain_grad = keep[:, columns].astype(f32)
-        got = swap_x(send)
-        shape = (rows, columns // unit, unit)
-        parity = choose(x0, keep[:, :columns].reshape(shape), got[:, :columns].reshape(shape))
-        joined = jnp.stack(parity, axis=2).reshape(rows, 2 * columns)
-        return joined.astype(f32)[None], gain_grad[None]
-
-    qkv_grad, norm1_grad = finish_columns(own_layer[0], HEAD_DIM)
-    up_grad, norm2_grad = finish_columns(own_layer[2], down_weight.shape[1])
-    out_grad = jnp.concatenate(own_layer[1], axis=0).astype(f32)[None]
-    down_grad = jnp.concatenate(own_layer[3], axis=0).astype(f32)[None]
+    keep, send = choose(sec0, reduced[0], reduced[1])
+    half_sets = choose(sec0, keep, swap_section(send))
+    out_grad = jnp.concatenate([member[:, out_at:up_at] for member in half_sets], axis=1).astype(f32)[None]
+    down_grad = jnp.concatenate(
+        [member[:, at : at + width] for member in half_sets for at in (down_at, down_at + width)],
+        axis=0,
+    ).astype(f32)[None]
+    col_first, col_second = [
+        jnp.concatenate([member[:, :cut], member[:, up_at:down_at]], axis=1) for member in half_sets
+    ]
+    keep, send = choose(x0, col_first, col_second)
+    norm1_grad = keep[:, qkv_cols].astype(f32)[None]
+    norm2_grad = keep[:, cut + up_cols].astype(f32)[None]
+    first, second = choose(x0, keep, swap_x(send))
+    qkv_grad = jnp.stack(
+        [member[:, :qkv_cols].reshape(in_rows, -1, HEAD_DIM) for member in (first, second)], axis=2
+    ).reshape(in_rows, -1).astype(f32)[None]
+    up_grad = jnp.stack(
+        [
+            jnp.transpose(
+                member[:, cut : cut + up_cols].reshape(in_rows, 2, -1, 2, unit), (0, 2, 3, 1, 4)
+            )
+            for member in (first, second)
+        ],
+        axis=2,
+    ).reshape(in_rows, -1).astype(f32)[None]
     return (ends, conv_weight_grad, conv_bias_grad, norm1_grad, qkv_grad, out_grad, norm2_grad, up_grad, down_grad)
 
 

time: 1260 us -> 899 us (0.71)
  waiting for transfers between devices: 632 us -> 385 us
  other arithmetic: 135 us -> 80.1 us
  blocking collectives: 79.7 us -> 35.6 us
  matrix products: 118 us -> 147 us
  local copies, waits for them, and re-layouts: 105 us -> 76 us
  starting transfers between devices: 101 us -> 82.8 us
    reduce_scatter x9 -> x2, waiting for transfers between devices: 300 us -> 55.9 us  [scatter_rows(): lax.psum_scatter(partial, ('section', 'dp', 'seq'), scatter_dimension=0,...]
    all_gather x6 -> x2, waiting for transfers between devices: 90.2 us -> 0.02 us  [gather_rows(): lax.all_gather(piece, ('section', 'dp', 'seq'), axis=0, tiled=True, axis_...]
    ppermute x6 -> x12, waiting for transfers between devices: 49.7 us -> 131 us  [the longest x3 71.2 us: chain_steps(): low = lax.ppermute(low, 'dp', upward)]
    all_gather x2 -> x0, blocking collectives: 65.9 us -> none  [gather_yz(): lax.all_gather(value, ('dp', 'seq'), axis=0, tiled=False, axis_index_grou...]
    ppermute x29 -> x7, starting transfers between devices: 35.6 us -> 7.38 us  [swap_section(): return lax.ppermute(value, 'section', [(0, 1), (1, 0)])]
    another operation x18 -> x2, other arithmetic: 30.6 us -> 5.93 us  [the longest x16 21.1 us: per_device_pairs(): joined = jnp.stack([first, second], axis=1)]
    all_to_all x0 -> x1, blocking collectives: none -> 22.1 us  [per_device_pairs(): stream_got = lax.all_to_all(stream_send, both, 0, 0, tiled=True)]
    conv_general_dilated x2 -> x0, local copies, waits for them, and re-layouts: 21.2 us -> none  [conv_taps_grad(): lax.conv_general_dilated(view, grad, (1,), [(half, half)], dimension_numb...]
  transfers between devices with their start and end apart: 70 -> 40, of which waited for: 30 -> 24; matrix products, arithmetic and copies ran while one was open for 25% -> 25% of each run, Pallas kernels for 4% -> 5%
where the time goes in v2:
time: 899 us; the launch traced here: 886 us
  waiting for transfers between devices  385 us (43%)
  matrix products  147 us (16%)
  starting transfers between devices  82.8 us (9%)
  other arithmetic  80.1 us (9%)
  local copies, waits for them, and re-layouts  76 us (8%)
  Pallas kernels  62.7 us (7%)
  blocking collectives  35.6 us (4%)
  between operations  17 us (2%)
    ppermute x11, waiting for transfers between devices, swap_x(): return lax.ppermute(value, 'seq', [(q, q ^ 1) for q in range(4)])  173 us
    ppermute x3, waiting for transfers between devices, chain_steps(): low = lax.ppermute(low, 'dp', upward)  71.2 us
    reduce_scatter x2, waiting for transfers between devices, scatter_rows(): lax.psum_scatter(partial, ('section', 'dp', 'seq'), scatter_dimension=0,...  55.9 us
    ppermute x6, waiting for transfers between devices, sum_dp(): running = lax.ppermute(own, 'dp', live)  43.2 us
    pallas_call x2, Pallas kernels, attention_backward(): pl.pallas_call(functools.partial(attention_backward_kernel, factor), grid...  36.9 us
    dot_general x12, matrix products, outer(): lax.dot_general(left, right, (((0,), (0,)), ((), ())), preferred_element_...  33.9 us
    dot_general x4, matrix products, per_device_pairs(): hidden_pre = jnp.dot(normed_two, w_up[part], preferred_element_type=f32)  27.8 us
    pallas_call x2, Pallas kernels, attention_forward(): pl.pallas_call(functools.partial(attention_forward_kernel, factor), grid=...  25.7 us
  transfers between devices with their start and end apart: 40, of which 24 were waited for; matrix products, arithmetic and copies ran while one was open for 25% of the time, Pallas kernels for 5%

profile of v2, /device:TPU:17, one launch (start us, length us, event | category | flops | bytes accessed | tf_op | source)
XLA Modules:
  0.0 886.2 jit_solution(1751255551689125490)
XLA Ops:
  17.9 10.3 %collective-permute-done.2 = bf16[64,3840]{1,0:T(8,128)(2,1)S(1)} collective-permute-done((bf16[64,3840]{1,0:T(8,128)(2,1)}, bf16[64,3840]{1,0:T(8,128)(2,1)S(1)}, u32[]{:S(2)}, u32[]{:S(2)}) %collective-permute-start.2) | collective-permute-done | bytes 491552 | tf_op jit(solution)/shard_map/ppermute | solution.py:516
  35.1 13.5 %all_to_all.30 = bf16[8,272,128]{2,1,0:T(8,128)(2,1)S(1)} all-to-all(bf16[8,272,128]{2,1,0:T(8,128)(2,1)S(1)} %copy.356), channel_id=1, replica_groups=mesh['section'=2,'dp'=4,'seq'=4] {'section','seq'}, dimensions={0} | all-to-all | bytes 1114112 | tf_op jit(solution)/shard_map/all_to_all | solution.py:871
  54.5 28.6 %collective-permute-done.5 = bf16[8,272,128]{2,1,0:T(8,128)(2,1)} collective-permute-done((bf16[8,272,128]{2,1,0:T(8,128)(2,1)S(1)}, bf16[8,272,128]{2,1,0:T(8,128)(2,1)}, u32[]{:S(2)}, u32[]{:S(2)}) %collective-permute-start.5) | collective-permute-done | bytes 557088 | tf_op jit(solution)/shard_map/ppermute | solution.py:535
  92.9 22.0 %collective-permute-done.6 = bf16[8,272,128]{2,1,0:T(8,128)(2,1)S(1)} collective-permute-done((bf16[8,272,128]{2,1,0:T(8,128)(2,1)}, bf16[8,272,128]{2,1,0:T(8,128)(2,1)S(1)}, u32[]{:S(2)}, u32[]{:S(2)}) %collective-permute-start.6) | collective-permute-done | bytes 557088 | tf_op jit(solution)/shard_map/ppermute | solution.py:535
  132.7 20.6 %collective-permute-done.7 = bf16[8,272,128]{2,1,0:T(8,128)(2,1)} collective-permute-done((bf16[8,272,128]{2,1,0:T(8,128)(2,1)S(1)}, bf16[8,272,128]{2,1,0:T(8,128)(2,1)}, u32[]{:S(2)}, u32[]{:S(2)}) %collective-permute-start.7) | collective-permute-done | bytes 557088 | tf_op jit(solution)/shard_map/ppermute | solution.py:535
  154.8 9.3 %collective-permute-done.9 = bf16[8,272,128]{2,1,0:T(8,128)(2,1)S(1)} collective-permute-done((bf16[8,272,128]{2,1,0:T(8,128)(2,1)}, bf16[8,272,128]{2,1,0:T(8,128)(2,1)S(1)}, u32[]{:S(2)}, u32[]{:S(2)}) %collective-permute-start.9) | collective-permute-done | bytes 557088 | tf_op jit(solution)/shard_map/ppermute | solution.py:536
  180.8 18.4 %fusion.228 = f32[2,256,256]{2,0,1:T(2,128)S(1)} fusion(bf16[33,256,256]{2,1,0:T(8,128)(2,1)} %bitcast.279, bf16[2,256,256]{2,1,0:T(8,128)(2,1)S(1)} %reshape.548), kind=kOutput, calls=%fused_computation.411 | convolution fusion | flops 2143289344 | bytes 5111808 | tf_op jit(solution)/shard_map/conv_general_dilated | solution.py:801
  202.6 22.1 %all_to_all.31 = bf16[8,512,128]{2,1,0:T(8,128)(2,1)S(1)} all-to-all(bf16[8,512,128]{2,1,0:T(8,128)(2,1)S(1)} %bitcast.295), channel_id=1, replica_groups=mesh['section'=2,'dp'=4,'seq'=4] {'section','seq'}, dimensions={0} | all-to-all | bytes 2097152 | tf_op jit(solution)/shard_map/all_to_all | solution.py:954
  236.8 12.9 %attention_forward.2 = (bf16[512,512]{1,0:T(8,128)(2,1)S(1)}, f32[4,2,512,1]{3,2,1,0:T(8,128)S(1)}) custom-call(bf16[512,1536]{1,0:T(8,128)(2,1)S(1)} %convolution_convert_fusion.3.q_ref, bf16[1024,1024]{1,0:T(8,128)(2,1)S(1)} %pad_maximum_fusion.k_ref.v_ref, bf16[1024,1024]{1,0:T(8,128)(2,1)S(1)} %pad_maximum_fusion.k_ref.v_ref, ...), custom_call_target="tpu_custom_call" | custom-call | flops 2147483648 | bytes 3145728 | tf_op jit(solution)/shard_map/attention_forward/pallas_call | solution.py:647
  252.5 23.4 %collective-permute-done.11 = bf16[512,1024]{1,0:T(8,128)(2,1)S(1)} collective-permute-done((bf16[512,1024]{1,0:T(8,128)(2,1)S(1)}, bf16[512,1024]{1,0:T(8,128)(2,1)S(1)}, u32[]{:S(2)}, u32[]{:S(2)}) %collective-permute-start.11) | collective-permute-done | bytes 1048608 | tf_op jit(solution)/shard_map/ppermute | solution.py:516
  296.6 21.7 %collective-permute-done.12 = bf16[512,1024]{1,0:T(8,128)(2,1)} collective-permute-done((bf16[512,1024]{1,0:T(8,128)(2,1)S(1)}, bf16[512,1024]{1,0:T(8,128)(2,1)}, u32[]{:S(2)}, u32[]{:S(2)}) %collective-permute-start.12) | collective-permute-done | bytes 1048608 | tf_op jit(solution)/shard_map/ppermute | solution.py:516
  331.5 12.9 %attention_forward.3 = (bf16[512,512]{1,0:T(8,128)(2,1)S(1)}, f32[4,2,512,1]{3,2,1,0:T(8,128)S(1)}) custom-call(bf16[512,1536]{1,0:T(8,128)(2,1)S(1)} %convolution_convert_fusion.2.q_ref, bf16[1024,1024]{1,0:T(8,128)(2,1)S(1)} %pad_maximum_fusion.1.k_ref.v_ref, bf16[1024,1024]{1,0:T(8,128)(2,1)S(1)} %pad_maximum_fusion.1.k_ref.v_ref, ...), custom_call_target="tpu_custom_call" | custom-call | flops 2147483648 | bytes 3145728 | tf_op jit(solution)/shard_map/attention_forward/pallas_call | solution.py:647
  346.7 33.8 %collective-permute-done.1 = bf16[256,1024]{1,0:T(8,128)(2,1)S(1)} collective-permute-done((bf16[256,1024]{1,0:T(8,128)(2,1)S(1)}, bf16[256,1024]{1,0:T(8,128)(2,1)S(1)}, u32[]{:S(2)}, u32[]{:S(2)}) %collective-permute-start.1) | collective-permute-done | bytes 524320 | tf_op jit(solution)/shard_map/ppermute | solution.py:516
  407.3 16.3 %collective-permute-done.21 = bf16[512,1024]{1,0:T(8,128)(2,1)S(1)} collective-permute-done((bf16[512,1024]{1,0:T(8,128)(2,1)S(1)}, bf16[512,1024]{1,0:T(8,128)(2,1)S(1)}, u32[]{:S(2)}, u32[]{:S(2)}) %collective-permute-start.21) | collective-permute-done | bytes 1048608 | tf_op jit(solution)/shard_map/ppermute | solution.py:516
  423.6 22.5 %collective-permute-done.15 = bf16[512,1024]{1,0:T(8,128)(2,1)S(1)} collective-permute-done((bf16[512,1024]{1,0:T(8,128)(2,1)S(1)}, bf16[512,1024]{1,0:T(8,128)(2,1)S(1)}, u32[]{:S(2)}, u32[]{:S(2)}) %collective-permute-start.15) | collective-permute-done | bytes 1048608 | tf_op jit(solution)/shard_map/ppermute | solution.py:516
  450.2 18.5 %attention_backward.2 = (bf16[512,512]{1,0:T(8,128)(2,1)S(1)}, f32[1024,512]{1,0:T(8,128)S(1)}, f32[1024,512]{1,0:T(8,128)}) custom-call(bf16[512,1536]{1,0:T(8,128)(2,1)S(1)} %convolution_convert_fusion.2.q_ref, bf16[1024,1024]{1,0:T(8,128)(2,1)} %copy-done.1, bf16[1024,1024]{1,0:T(8,128)(2,1)} %copy-done.1, ...), custom_call_target="tpu_custom_call" | custom-call | flops 5368709120 | bytes 6291456 | tf_op jit(solution)/shard_map/attention_backward/pallas_call | solution.py:727
  490.5 13.3 %collective-permute-done.17 = bf16[512,1024]{1,0:T(8,128)(2,1)} collective-permute-done((bf16[512,1024]{1,0:T(8,128)(2,1)}, bf16[512,1024]{1,0:T(8,128)(2,1)}, u32[]{:S(2)}, u32[]{:S(2)}) %collective-permute-start.17) | collective-permute-done | bytes 1048608 | tf_op jit(solution)/shard_map/ppermute | solution.py:516
  538.2 21.7 %collective-permute-done.18 = bf16[512,1024]{1,0:T(8,128)(2,1)S(1)} collective-permute-done((bf16[512,1024]{1,0:T(8,128)(2,1)S(1)}, bf16[512,1024]{1,0:T(8,128)(2,1)S(1)}, u32[]{:S(2)}, u32[]{:S(2)}) %collective-permute-start.18) | collective-permute-done | bytes 1048608 | tf_op jit(solution)/shard_map/ppermute | solution.py:516
  563.6 18.5 %attention_backward.3 = (bf16[512,512]{1,0:T(8,128)(2,1)S(1)}, f32[1024,512]{1,0:T(8,128)S(1)}, f32[1024,512]{1,0:T(8,128)}) custom-call(bf16[512,1536]{1,0:T(8,128)(2,1)S(1)} %convolution_convert_fusion.3.q_ref, bf16[1024,1024]{1,0:T(8,128)(2,1)} %copy-done, bf16[1024,1024]{1,0:T(8,128)(2,1)} %copy-done, ...), custom_call_target="tpu_custom_call" | custom-call | flops 5368709120 | bytes 6291456 | tf_op jit(solution)/shard_map/attention_backward/pallas_call | solution.py:727
  598.9 11.8 %collective-permute-done.22 = f32[256,1024]{1,0:T(8,128)} collective-permute-done((f32[256,1024]{1,0:T(8,128)}, f32[256,1024]{1,0:T(8,128)}, u32[]{:S(2)}, u32[]{:S(2)}) %collective-permute-start.22) | collective-permute-done | bytes 1048608 | tf_op jit(solution)/shard_map/ppermute | solution.py:1084
  697.0 34.9 %collective-permute-done.25 = bf16[2,4,272,128]{3,2,1,0:T(8,128)(2,1)S(1)} collective-permute-done((bf16[2,4,272,128]{3,2,1,0:T(8,128)(2,1)S(1)}, bf16[2,4,272,128]{3,2,1,0:T(8,128)(2,1)S(1)}, u32[]{:S(2)}, u32[]{:S(2)}) %collective-permute-start.25) | collective-permute-done | bytes 557088 | tf_op jit(solution)/shard_map/ppermute | solution.py:569
  751.8 12.2 %all-to-all-start.4 = ((bf16[8,2,256,128]{3,2,1,0:T(8,128)(2,1)}), bf16[8,2,256,128]{3,2,1,0:T(8,128)(2,1)S(1)}, u32[]{:S(2)}, u32[]{:S(2)}) async-start(bf16[8,2,256,128]{3,2,1,0:T(8,128)(2,1)} %copy.381), calls=%async_computation.4 | async-start | bytes 2097152 | tf_op jit(solution)/shard_map/all_to_all | solution.py:1057
  775.2 55.9 %reduce-scatter.3.cloned.1.call-done = bf16[64,6400]{1,0:T(8,128)(2,1)} async-done(((bf16[1024,6400]{1,0:T(8,128)(2,1)}), bf16[64,6400]{1,0:T(8,128)(2,1)}) %reduce-scatter.3.cloned.1.call-update) | async-done | bytes 819216 | tf_op jit(solution)/shard_map/reduce_scatter | solution.py:589
  858.0 10.3 %collective-permute-done.31 = bf16[64,3840]{1,0:T(8,128)(2,1)S(1)} collective-permute-done((bf16[64,3840]{1,0:T(8,128)(2,1)S(1)}, bf16[64,3840]{1,0:T(8,128)(2,1)S(1)}, u32[]{:S(2)}, u32[]{:S(2)}) %collective-permute-start.31) | collective-permute-done | bytes 491552 | tf_op jit(solution)/shard_map/ppermute | solution.py:516
  (578 shorter events, 383.9 us)
Async XLA Ops:
  7.2 218.2 %all-gather.5.cloned.1.call-start = ((), (), s32[]{:S(2)}) async-start(), calls=%async_computation.9 | async-start | bytes 13926400 | tf_op jit(solution)/shard_map/all_gather | solution.py:583
  33.5 261.8 %all-gather.3.cloned.1.call-start = ((), (), s32[]{:S(2)}) async-start(), calls=%async_computation.8 | async-start | bytes 13926400 | tf_op jit(solution)/shard_map/all_gather | solution.py:583
  48.7 34.4 %collective-permute-start.5 = (bf16[8,272,128]{2,1,0:T(8,128)(2,1)S(1)}, bf16[8,272,128]{2,1,0:T(8,128)(2,1)}, u32[]{:S(2)}, u32[]{:S(2)}) collective-permute-start(bf16[8,272,128]{2,1,0:T(8,128)(2,1)S(1)} %all_to_all.30), channel_id=1, source_target_pairs={{0,4},{4,8},{8,12},{1,5},{5,9},{9,13},{2,6},{6,10},{10,14},{3,7},{... | collective-permute-start | bytes 1671176 | tf_op jit(solution)/shard_map/ppermute | solution.py:535
  52.0 38.9 %collective-permute-start.4 = (bf16[8,272,128]{2,1,0:T(8,128)(2,1)S(1)}, bf16[8,272,128]{2,1,0:T(8,128)(2,1)}, u32[]{:S(2)}, u32[]{:S(2)}) collective-permute-start(bf16[8,272,128]{2,1,0:T(8,128)(2,1)S(1)} %all_to_all.30), channel_id=1, source_target_pairs={{4,0},{8,4},{12,8},{5,1},{9,5},{13,9},{6,2},{10,6},{14,10},{7,3},{... | collective-permute-start | bytes 1671176 | tf_op jit(solution)/shard_map/ppermute | solution.py:536
  83.1 31.8 %collective-permute-start.6 = (bf16[8,272,128]{2,1,0:T(8,128)(2,1)}, bf16[8,272,128]{2,1,0:T(8,128)(2,1)S(1)}, u32[]{:S(2)}, u32[]{:S(2)}) collective-permute-start(bf16[8,272,128]{2,1,0:T(8,128)(2,1)} %collective-permute-done.5), channel_id=1, source_target_pairs={{0,4},{4,8},{8,12},{1,5},{5,9},{9,13},{2,6},{6,10},{10,14},{3,7},{... | collective-permute-start | bytes 1671176 | tf_op jit(solution)/shard_map/ppermute | solution.py:535
  87.4 29.8 %all-to-all-start = ((bf16[4,2,256,128]{2,3,1,0:T(8,128)(2,1)}), bf16[4,2,256,128]{2,3,1,0:T(8,128)(2,1)S(1)}, u32[]{:S(2)}, u32[]{:S(2)}) async-start(bf16[4,2,256,128]{2,3,1,0:T(8,128)(2,1)} %copy.353), calls=%async_computation | async-start | bytes 1048576 | tf_op jit(solution)/shard_map/all_to_all | solution.py:875
  90.9 684.4 %reduce-scatter.5.cloned.1.call-start = ((), (), s32[]{:S(2)}) async-start(), calls=%async_computation.11 | async-start | bytes 13926400 | tf_op jit(solution)/shard_map/reduce_scatter | solution.py:589
  90.9 34.4 %collective-permute-start.8 = (bf16[8,272,128]{2,1,0:T(8,128)(2,1)}, bf16[8,272,128]{2,1,0:T(8,128)(2,1)}, u32[]{:S(2)}, u32[]{:S(2)}) collective-permute-start(bf16[8,272,128]{2,1,0:T(8,128)(2,1)} %collective-permute-done.4), channel_id=1, source_target_pairs={{4,0},{8,4},{12,8},{5,1},{9,5},{13,9},{6,2},{10,6},{14,10},{7,3},{... | collective-permute-start | bytes 1671176 | tf_op jit(solution)/shard_map/ppermute | solution.py:536
  114.9 38.4 %collective-permute-start.7 = (bf16[8,272,128]{2,1,0:T(8,128)(2,1)S(1)}, bf16[8,272,128]{2,1,0:T(8,128)(2,1)}, u32[]{:S(2)}, u32[]{:S(2)}) collective-permute-start(bf16[8,272,128]{2,1,0:T(8,128)(2,1)S(1)} %collective-permute-done.6), channel_id=1, source_target_pairs={{0,4},{4,8},{8,12},{1,5},{5,9},{9,13},{2,6},{6,10},{10,14},{3,7},{... | collective-permute-start | bytes 1671176 | tf_op jit(solution)/shard_map/ppermute | solution.py:535
  125.4 38.7 %collective-permute-start.9 = (bf16[8,272,128]{2,1,0:T(8,128)(2,1)}, bf16[8,272,128]{2,1,0:T(8,128)(2,1)S(1)}, u32[]{:S(2)}, u32[]{:S(2)}) collective-permute-start(bf16[8,272,128]{2,1,0:T(8,128)(2,1)} %collective-permute-done.8), channel_id=1, source_target_pairs={{4,0},{8,4},{12,8},{5,1},{9,5},{13,9},{6,2},{10,6},{14,10},{7,3},{... | collective-permute-start | bytes 1671176 | tf_op jit(solution)/shard_map/ppermute | solution.py:536
  250.5 25.4 %collective-permute-start.11 = (bf16[512,1024]{1,0:T(8,128)(2,1)S(1)}, bf16[512,1024]{1,0:T(8,128)(2,1)S(1)}, u32[]{:S(2)}, u32[]{:S(2)}) collective-permute-start(bf16[512,1024]{1,0:T(8,128)(2,1)S(1)} %convolution_convert_fusion.7), channel_id=1, source_target_pairs={{0,1},{1,0},{2,3},{3,2},{4,5},{5,4},{6,7},{7,6},{8,9},{9,8},{10,11... | collective-permute-start | bytes 3145736 | tf_op jit(solution)/shard_map/ppermute | solution.py:516
  345.1 35.5 %collective-permute-start.14 = (bf16[512,1024]{1,0:T(8,128)(2,1)S(1)}, bf16[512,1024]{1,0:T(8,128)(2,1)S(1)}, u32[]{:S(2)}, u32[]{:S(2)}) collective-permute-start(bf16[512,1024]{1,0:T(8,128)(2,1)S(1)} %convolution_convert_fusion.6), channel_id=1, source_target_pairs={{0,1},{1,0},{2,3},{3,2},{4,5},{5,4},{6,7},{7,6},{8,9},{9,8},{10,11... | collective-permute-start | bytes 3145736 | tf_op jit(solution)/shard_map/ppermute | solution.py:516
  346.3 34.2 %collective-permute-start.1 = (bf16[256,1024]{1,0:T(8,128)(2,1)S(1)}, bf16[256,1024]{1,0:T(8,128)(2,1)S(1)}, u32[]{:S(2)}, u32[]{:S(2)}) collective-permute-start(bf16[256,1024]{1,0:T(8,128)(2,1)S(1)} %collective-permute-done), channel_id=1, source_target_pairs={{0,1},{1,0},{2,3},{3,2},{4,5},{5,4},{6,7},{7,6},{8,9},{9,8},{10,11... | collective-permute-start | bytes 1572872 | tf_op jit(solution)/shard_map/ppermute | solution.py:516
  398.7 25.0 %collective-permute-start.21 = (bf16[512,1024]{1,0:T(8,128)(2,1)S(1)}, bf16[512,1024]{1,0:T(8,128)(2,1)S(1)}, u32[]{:S(2)}, u32[]{:S(2)}) collective-permute-start(bf16[512,1024]{1,0:T(8,128)(2,1)S(1)} %add_convert_fusion), channel_id=1, source_target_pairs={{0,1},{1,0},{2,3},{3,2},{4,5},{5,4},{6,7},{7,6},{8,9},{9,8},{10,11... | collective-permute-start | bytes 3145736 | tf_op jit(solution)/shard_map/ppermute | solution.py:516
  406.9 39.2 %collective-permute-start.15 = (bf16[512,1024]{1,0:T(8,128)(2,1)S(1)}, bf16[512,1024]{1,0:T(8,128)(2,1)S(1)}, u32[]{:S(2)}, u32[]{:S(2)}) collective-permute-start(bf16[512,1024]{1,0:T(8,128)(2,1)S(1)} %add_convert_fusion.3), channel_id=1, source_target_pairs={{0,1},{1,0},{2,3},{3,2},{4,5},{5,4},{6,7},{7,6},{8,9},{9,8},{10,11... | collective-permute-start | bytes 3145736 | tf_op jit(solution)/shard_map/ppermute | solution.py:516
  479.1 24.7 %collective-permute-start.17 = (bf16[512,1024]{1,0:T(8,128)(2,1)}, bf16[512,1024]{1,0:T(8,128)(2,1)}, u32[]{:S(2)}, u32[]{:S(2)}) collective-permute-start(bf16[512,1024]{1,0:T(8,128)(2,1)} %fusion.159), channel_id=1, source_target_pairs={{0,1},{1,0},{2,3},{3,2},{4,5},{5,4},{6,7},{7,6},{8,9},{9,8},{10,11... | collective-permute-start | bytes 3145736 | tf_op jit(solution)/shard_map/ppermute | solution.py:516
  595.4 27.6 %collective-permute-start.20 = (bf16[512,1024]{1,0:T(8,128)(2,1)}, bf16[512,1024]{1,0:T(8,128)(2,1)}, u32[]{:S(2)}, u32[]{:S(2)}) collective-permute-start(bf16[512,1024]{1,0:T(8,128)(2,1)} %fusion.156), channel_id=1, source_target_pairs={{0,1},{1,0},{2,3},{3,2},{4,5},{5,4},{6,7},{7,6},{8,9},{9,8},{10,11... | collective-permute-start | bytes 3145736 | tf_op jit(solution)/shard_map/ppermute | solution.py:516
  610.7 67.0 %collective-permute-start.23 = (f32[256,1024]{1,0:T(8,128)}, f32[256,1024]{1,0:T(8,128)}, u32[]{:S(2)}, u32[]{:S(2)}) collective-permute-start(f32[256,1024]{1,0:T(8,128)} %collective-permute-done.22), channel_id=1, source_target_pairs={{0,16},{16,0},{1,17},{17,1},{2,18},{18,2},{3,19},{19,3},{4,20},{20... | collective-permute-start | bytes 3145736 | tf_op jit(solution)/shard_map/ppermute | solution.py:512
  633.7 197.4 %reduce-scatter.3.cloned.1.call-start = ((), (), s32[]{:S(2)}) async-start(), calls=%async_computation.10 | async-start | bytes 13926400 | tf_op jit(solution)/shard_map/reduce_scatter | solution.py:589
  684.9 47.0 %collective-permute-start.25 = (bf16[2,4,272,128]{3,2,1,0:T(8,128)(2,1)S(1)}, bf16[2,4,272,128]{3,2,1,0:T(8,128)(2,1)S(1)}, u32[]{:S(2)}, u32[]{:S(2)}) collective-permute-start(bf16[2,4,272,128]{3,2,1,0:T(8,128)(2,1)S(1)} %fusion.174), channel_id=1, source_target_pairs={{0,4},{4,8},{1,5},{5,9},{2,6},{6,10},{3,7},{7,11},{16,20},{20,24},... | collective-permute-start | bytes 1671176 | tf_op jit(solution)/shard_map/ppermute | solution.py:569
  733.2 35.9 %collective-permute-start.28 = (bf16[2,4,272,128]{3,2,1,0:T(8,128)(2,1)}, bf16[2,4,272,128]{3,2,1,0:T(8,128)(2,1)}, u32[]{:S(2)}, u32[]{:S(2)}) collective-permute-start(bf16[2,4,272,128]{3,2,1,0:T(8,128)(2,1)} %get-tuple-element.87), channel_id=1, source_target_pairs={{8,4},{12,8},{9,5},{13,9},{10,6},{14,10},{11,7},{15,11},{24,20},{2... | collective-permute-start | bytes 1671176 | tf_op jit(solution)/shard_map/ppermute | solution.py:569
  751.8 84.3 %all-to-all-start.4 = ((bf16[8,2,256,128]{3,2,1,0:T(8,128)(2,1)}), bf16[8,2,256,128]{3,2,1,0:T(8,128)(2,1)S(1)}, u32[]{:S(2)}, u32[]{:S(2)}) async-start(bf16[8,2,256,128]{3,2,1,0:T(8,128)(2,1)} %copy.381), calls=%async_computation.4 | async-start | bytes 2097152 | tf_op jit(solution)/shard_map/all_to_all | solution.py:1057
  764.0 69.8 %collective-permute-start.26 = (bf16[2,4,272,128]{3,2,1,0:T(8,128)(2,1)}, bf16[2,4,272,128]{3,2,1,0:T(8,128)(2,1)}, u32[]{:S(2)}, u32[]{:S(2)}) collective-permute-start(bf16[2,4,272,128]{3,2,1,0:T(8,128)(2,1)} %get-tuple-element.86), channel_id=1, source_target_pairs={{0,4},{4,8},{8,12},{1,5},{5,9},{9,13},{2,6},{6,10},{10,14},{3,7},{... | collective-permute-start | bytes 1671176 | tf_op jit(solution)/shard_map/ppermute | solution.py:569
  771.1 62.8 %collective-permute-start.29 = (bf16[2,4,272,128]{3,2,1,0:T(8,128)(2,1)}, bf16[2,4,272,128]{3,2,1,0:T(8,128)(2,1)}, u32[]{:S(2)}, u32[]{:S(2)}) collective-permute-start(bf16[2,4,272,128]{3,2,1,0:T(8,128)(2,1)} %fusion.173), channel_id=1, source_target_pairs={{4,0},{8,4},{12,8},{5,1},{9,5},{13,9},{6,2},{10,6},{14,10},{7,3},{... | collective-permute-start | bytes 1671176 | tf_op jit(solution)/shard_map/ppermute | solution.py:569
  (140 other events, 1580.0 us)
Sparse Core Ops, SparseCore 0:
  33.6 137.6 all-gather.4
  173.6 105.5 all-gather.2
  520.1 147.3 reduce-scatter.4
  672.0 159.0 reduce-scatter.2

commit v3 on v2

--- a/solution.py
+++ b/solution.py
@@ -516,9 +516,12 @@
     return lax.ppermute(value, "seq", [(q, q ^ 1) for q in range(4)])
 
 
-def pair_sum(value):
-    low = value.astype(jnp.bfloat16)
+def pair_sum(low):
     return low.astype(jnp.float32) + swap_x(low).astype(jnp.float32)
+
+
+def after(first, second):
+    return lax.optimization_barrier((first, second))
 
 
 def choose(flag, first, second):
@@ -673,14 +676,15 @@
 
 
 def attention_backward_kernel(
-    factor, q_ref, k_ref, v_ref, g_ref, o_ref, lse_ref, qs_ref, ks_ref, dq_ref, dk_ref, dv_ref
+    factor, q_ref, k_ref, v_ref, g_ref, o_ref, lse_ref, qs_ref, ks_ref, *rest
 ):
+    *begin, dq_ref, dk_ref, dv_ref = rest
     step = pl.program_id(1)
 
     @pl.when(step == 0)
     def _():
-        dk_ref[...] = jnp.zeros_like(dk_ref)
-        dv_ref[...] = jnp.zeros_like(dv_ref)
+        for index, total_ref in enumerate((dk_ref, dv_ref)):
+            total_ref[...] = begin[index][...] if begin else jnp.zeros_like(total_ref)
 
     queries = q_ref[...]
     grads = g_ref[...]
@@ -718,7 +722,7 @@
     dq_ref[...] = (dq * factor).astype(dq_ref.dtype)
 
 
-def attention_backward(packed, kv_all, grads, attended, lse, query_segs, key_segs, factor):
+def attention_backward(packed, kv_all, grads, attended, lse, query_segs, key_segs, factor, begin=None):
     frames = packed.shape[0]
     keys = kv_all.shape[0]
     width = packed.shape[1] // 3
@@ -736,7 +740,8 @@
             pl.BlockSpec((1, 2, rows, 1), lambda h, i: (h, 0, i, 0)),
             pl.BlockSpec((rows, 1), lambda h, i: (i, 0)),
             pl.BlockSpec((1, keys), lambda h, i: (0, 0)),
-        ],
+        ]
+        + [pl.BlockSpec((keys, 128), lambda h, i: (0, h))] * (2 if begin else 0),
         out_specs=[
             pl.BlockSpec((rows, 128), lambda h, i: (i, h)),
             pl.BlockSpec((keys, 128), lambda h, i: (0, h)),
@@ -754,7 +759,7 @@
             transcendentals=frames * keys * (width // HEAD_DIM),
         ),
         name="attention_backward",
-    )(packed, kv_all, kv_all, grads, attended, lse, query_segs[:, None], key_segs[None, :])
+    )(packed, kv_all, kv_all, grads, attended, lse, query_segs[:, None], key_segs[None, :], *(begin or ()))
 
 
 CONV_STEP = 4
@@ -920,9 +925,9 @@
     ]
     keep, send = choose(sec0, *row_parts)
     layer_pieces = choose(sec0, keep, swap_section(send))
-    layer_weights = []
-    for layer in range(2):
-        whole = gather_rows(layer_pieces[layer])
+    gathered = [gather_rows(layer_pieces[layer]) for layer in range(2)]
+
+    def views(whole):
         w_out = jnp.transpose(
             whole[:, out_at:up_at].reshape(-1, 2, in_rows, width // 2), (0, 2, 1, 3)
         ).reshape(-1, width)
@@ -930,7 +935,9 @@
         gain_two = whole[:, two_at].astype(f32)[None, :]
         w_up = [whole[:, up_at + part * width : up_at + (part + 1) * width] for part in range(2)]
         w_down = [whole[:, down_at + part * width : down_at + (part + 1) * width] for part in range(2)]
-        layer_weights.append((gain_one, whole[:, :qkv_cols], w_out, gain_two, w_up, w_down))
+        return gain_one, whole[:, :qkv_cols], w_out, gain_two, w_up, w_down
+
+    layer_weights = []
 
     picked = jnp.where(sec0, cotangent[0], cotangent[1])
     across = [(s * 4 + 2 * yy + xx, yy * 4 + 2 * s + xx) for s in range(2) for yy in range(2) for xx in range(2)]
@@ -954,94 +961,153 @@
     stream_got = lax.all_to_all(stream_send, both, 0, 0, tiled=True)
     layer_in = jnp.transpose(stream_got, (1, 0, 2)).reshape(half_frames, width).astype(f32)
 
+    chunks = 2
+    rows = half_frames // chunks
+    layer_in = [layer_in[c * rows : (c + 1) * rows] for c in range(chunks)]
+    chunk_segs = [query_segs[c * rows : (c + 1) * rows] for c in range(chunks)]
     kept = []
     for layer in range(2):
+        layer_in, whole = after(layer_in, gathered[layer])
+        layer_weights.append(views(whole))
         gain_one, w_qkv, w_out, gain_two, w_up, w_down = layer_weights[layer]
-        centred, inv = norm_stats(layer_in)
-        normed_one = (centred * inv * gain_one).astype(bf16)
-        packed = jnp.dot(normed_one, w_qkv, preferred_element_type=f32).astype(bf16)
-        kv_own = packed[:, width // 2 :]
-        kv_all = jnp.concatenate([kv_own, swap_section(kv_own)], axis=0)
-        attended, lse = attention_forward(packed, kv_all, query_segs, key_segs, factor)
-        resid_two = layer_in + pair_sum(jnp.dot(attended, w_out, preferred_element_type=f32))
-        centred, inv = norm_stats(resid_two)
-        normed_two = (centred * inv * gain_two).astype(bf16)
-        hidden, hidden_slope, down_sum = [], [], None
-        for part in range(2):
-            hidden_pre = jnp.dot(normed_two, w_up[part], preferred_element_type=f32)
-            hidden.append(smooth(hidden_pre).astype(bf16))
-            hidden_slope.append(gelu_slope(hidden_pre).astype(bf16))
-        for part in range(2):
-            term = jnp.dot(hidden[part], w_down[part], preferred_element_type=f32)
-            down_sum = term if down_sum is None else down_sum + term
-        result = resid_two + pair_sum(down_sum)
-        kept.append(
-            (layer_in, normed_one, packed, kv_all, attended, lse, resid_two, normed_two, hidden, hidden_slope)
-        )
-        layer_in = result.astype(bf16).astype(f32)
-    output = result
-
-    grad_out = top_grad
-    reduced = [None, None]
+        normed_one, packed, kv_own, kv_other = [], [], [], []
+        for c in range(chunks):
+            centred, inv = norm_stats(layer_in[c])
+            normed_one.append((centred * inv * gain_one).astype(bf16))
+            packed.append(jnp.dot(normed_one[c], w_qkv, preferred_element_type=f32).astype(bf16))
+            kv_own.append(packed[c][:, width // 2 :])
+            kv_other.append(swap_section(kv_own[c]))
+        kv_all = jnp.concatenate(kv_own + kv_other, axis=0)
+        attended, lse, resid_two, normed_two, hidden, hidden_slope, result = [], [], [], [], [], [], []
+        low = None
+        for c in range(chunks):
+            own = packed[c]
+            if low is not None:
+                low, own = after(low, own)
+                resid_two.append(layer_in[c - 1] + pair_sum(low))
+            mixed, log_total = attention_forward(own, kv_all, chunk_segs[c], key_segs, factor)
+            attended.append(mixed)
+            lse.append(log_total)
+            low = jnp.dot(mixed, w_out, preferred_element_type=f32).astype(bf16)
+        resid_two.append(layer_in[-1] + pair_sum(low))
+        low, lows = None, []
+        for c in range(chunks):
+            values = resid_two[c]
+            if low is not None:
+                low, values = after(low, values)
+                lows.append(low)
+            centred, inv = norm_stats(values)
+            normed_two.append((centred * inv * gain_two).astype(bf16))
+            down_sum, own_hidden, own_slope = None, [], []
+            for part in range(2):
+                hidden_pre = jnp.dot(normed_two[c], w_up[part], preferred_element_type=f32)
+                own_hidden.append(smooth(hidden_pre).astype(bf16))
+                own_slope.append(gelu_slope(hidden_pre).astype(bf16))
+            for part in range(2):
+                term = jnp.dot(own_hidden[part], w_down[part], preferred_element_type=f32)
+                down_sum = term if down_sum is None else down_sum + term
+            hidden.append(own_hidden)
+            hidden_slope.append(own_slope)
+            low = down_sum.astype(bf16)
+        lows.append(low)
+
+        def joined(members):
+            return jnp.concatenate(members, axis=0)
+
+        resid_two_last = resid_two
+        kept.append((layer_in, normed_one, packed, kv_all, attended, lse, resid_two, normed_two, hidden, hidden_slope))
+        if layer == 0:
+            result = [member + pair_sum(low) for member, low in zip(resid_two, lows)]
+            layer_in = [member.astype(bf16).astype(f32) for member in result]
+
+    def outer(left, right):
+        return lax.dot_general(
+            left, right, (((0,), (0,)), ((), ())), preferred_element_type=f32
+        ).astype(bf16)
+
+    def back(left, right):
+        return lax.dot_general(left, right, (((1,), (1,)), ((), ())), preferred_element_type=f32)
+
+    grad_out = [top_grad[c * rows : (c + 1) * rows] for c in range(chunks)]
+    attn_members, scattered = [], []
     for layer in (1, 0):
         gain_one, w_qkv, w_out, gain_two, w_up, w_down = layer_weights[layer]
         (layer_in, normed_one, packed, kv_all, attended, lse, resid_two, normed_two, hidden, hidden_slope) = kept[layer]
-        branch = grad_out.astype(bf16)
-        pre_grad, part_sum = [], None
-        for part in range(2):
-            hidden_grad = lax.dot_general(
-                branch, w_down[part], (((1,), (1,)), ((), ())), preferred_element_type=f32
+        branch = [member.astype(bf16) for member in grad_out]
+        pre_grad, sums, low = [], [], None
+        for c in range(chunks):
+            own = branch[c]
+            if low is not None:
+                low, own = after(low, own)
+                sums.append(pair_sum(low))
+            own_pre, part_sum = [], None
+            for part in range(2):
+                own_pre.append((back(own, w_down[part]) * hidden_slope[c][part].astype(f32)).astype(bf16))
+            for part in range(2):
+                term = back(own_pre[part], w_up[part])
+                part_sum = term if part_sum is None else part_sum + term
+            pre_grad.append(own_pre)
+            low = part_sum.astype(bf16)
+        sums.append(pair_sum(low))
+        whole_pre = [jnp.concatenate([pre_grad[c][p] for c in range(chunks)]) for p in range(2)]
+        whole_hidden = [jnp.concatenate([hidden[c][p] for c in range(chunks)]) for p in range(2)]
+        whole_branch, whole_two = jnp.concatenate(branch), jnp.concatenate(normed_two)
+        ff_members = [
+            outer(whole_two, whole_pre[0]), outer(whole_two, whole_pre[1]),
+            outer(whole_hidden[0], whole_branch), outer(whole_hidden[1], whole_branch),
+        ]
+        if layer == 1:
+            ff_members.append(jnp.zeros((width, 128), bf16))
+        partial = jnp.concatenate(attn_members + ff_members, axis=1)
+        if layer == 0:
+            sums, partial = after(sums, partial)
+        scattered.append(scatter_rows(partial))
+        resid_grad, attn_branch, dq, gain_two_grad = [], [], [], None
+        dkv = None
+        for c in range(chunks):
+            in_part, gain_part = norm_back(resid_two[c], gain_two, sums[c])
+            gain_two_grad = gain_part if gain_two_grad is None else gain_two_grad + gain_part
+            resid_grad.append(in_part + grad_out[c])
+            attn_branch.append(resid_grad[c].astype(bf16))
+            attended_grad = back(attn_branch[c], w_out).astype(bf16)
+            own_dq, *dkv = attention_backward(
+                packed[c], kv_all, attended_grad, attended[c], lse[c], chunk_segs[c], key_segs, factor,
+                None if c == 0 else dkv,
             )
-            pre_grad.append((hidden_grad * hidden_slope[part].astype(f32)).astype(bf16))
-        for part in range(2):
-            term = lax.dot_general(
-                pre_grad[part], w_up[part], (((1,), (1,)), ((), ())), preferred_element_type=f32
-            )
-            part_sum = term if part_sum is None else part_sum + term
-        normed_grad = pair_sum(part_sum)
-        resid_grad, gain_two_grad = norm_back(resid_two, gain_two, normed_grad)
-        resid_grad = resid_grad + grad_out
-        attn_branch = resid_grad.astype(bf16)
-        attended_grad = lax.dot_general(
-            attn_branch, w_out, (((1,), (1,)), ((), ())), preferred_element_type=f32
-        ).astype(bf16)
-        dq, dk, dv = attention_backward(
-            packed, kv_all, attended_grad, attended, lse, query_segs, key_segs, factor
-        )
-        dkv = jnp.concatenate([dk, dv], axis=1)
+            dq.append(own_dq)
+        if layer == 0:
+            dkv, scattered[0] = after(dkv, scattered[0])
+        dkv = jnp.concatenate(dkv, axis=1)
         other_dkv = swap_section(dkv[half_frames:].astype(bf16))
         dkv_own = (dkv[:half_frames] + other_dkv.astype(f32)).astype(bf16)
-        packed_grad = jnp.concatenate([dq, dkv_own], axis=1)
-        part = lax.dot_general(
-            packed_grad, w_qkv, (((1,), (1,)), ((), ())), preferred_element_type=f32
-        )
-        normed_grad = pair_sum(part)
-        in_grad, gain_one_grad = norm_back(layer_in, gain_one, normed_grad)
-        grad_in = resid_grad + in_grad
-        def outer(left, right):
-            return lax.dot_general(
-                left, right, (((0,), (0,)), ((), ())), preferred_element_type=f32
-            ).astype(bf16)
-
+        packed_grad, sums, low = [], [], None
+        for c in range(chunks):
+            packed_grad.append(jnp.concatenate([dq[c], dkv_own[c * rows : (c + 1) * rows]], axis=1))
+            own = packed_grad[c]
+            if low is not None:
+                low, own = after(low, own)
+                sums.append(pair_sum(low))
+            low = back(own, w_qkv).astype(bf16)
+        sums.append(pair_sum(low))
+        next_grad, gain_one_grad = [], None
+        for c in range(chunks):
+            in_part, gain_part = norm_back(layer_in[c], gain_one, sums[c])
+            gain_one_grad = gain_part if gain_one_grad is None else gain_one_grad + gain_part
+            next_grad.append((resid_grad[c] + in_part).astype(bf16))
+        whole_one, whole_pg, whole_att, whole_ab = [
+            jnp.concatenate(m) for m in (normed_one, packed_grad, attended, attn_branch)
+        ]
         grad_out_weight = jnp.transpose(
-            outer(attended, attn_branch).reshape(-1, in_rows, 2, width // 2), (0, 2, 1, 3)
+            outer(whole_att, whole_ab).reshape(-1, in_rows, 2, width // 2), (0, 2, 1, 3)
         ).reshape(-1, width // 2)
-        partial = jnp.concatenate(
-            [
-                outer(normed_one, packed_grad),
-                to_column(gain_one_grad.astype(bf16), 128),
-                grad_out_weight,
-                outer(normed_two, pre_grad[0]),
-                outer(normed_two, pre_grad[1]),
-                to_column(gain_two_grad.astype(bf16), 128),
-                outer(hidden[0], branch),
-                outer(hidden[1], branch),
-            ],
-            axis=1,
-        )
-        reduced[layer] = scatter_rows(partial)
-        grad_out = grad_in.astype(bf16).astype(f32)
-    grad_in_low = grad_in.astype(bf16)
+        gain_grads = jnp.stack([gain_one_grad, gain_two_grad], axis=1).astype(bf16)
+        gain_grads = jnp.pad(gain_grads, ((0, 0), (0, 126)))
+        attn_members = [outer(whole_one, whole_pg), gain_grads, grad_out_weight]
+        grad_out = [member.astype(f32) for member in next_grad]
+    grad_in_low = jnp.concatenate(next_grad)
+    scattered.append(scatter_rows(jnp.concatenate(attn_members, axis=1)))
+    grad_in_low, lows = after(grad_in_low, lows)
+    output = jnp.concatenate([member + pair_sum(low) for member, low in zip(resid_two_last, lows)])
 
     lig_send = jnp.transpose(grad_in_low.reshape(half_frames, 8, block_width), (1, 0, 2))
     lig_got = lax.all_to_all(lig_send, both, 0, 0, tiled=True).reshape(2, 2, 2, half_frames, block_width)
@@ -1067,6 +1133,7 @@
         ((0, 0), (0, 0), (0, 0), (0, 15), (0, 0)),
     )
     taps_send = jnp.concatenate([taps_view, bias_view], axis=3)
+    taps_send, scattered[1] = after(taps_send, scattered[1])
     taps_sum = sum_dp(taps_send, dp)
     taps_got = lax.all_to_all(
         taps_sum.reshape(8, rows_here + 16, block_width), both, 0, 0, tiled=True
@@ -1086,29 +1153,35 @@
     output_rows = jnp.stack(choose(sec0, row_block, other_row))
     ends = jnp.where(sec0, gs_rows, output_rows)[None]
 
-    keep, send = choose(sec0, reduced[0], reduced[1])
-    half_sets = choose(sec0, keep, swap_section(send))
-    out_grad = jnp.concatenate([member[:, out_at:up_at] for member in half_sets], axis=1).astype(f32)[None]
+    attn_cols = up_at
+    attn_sums = (scattered[2], scattered[1][:, :attn_cols])
+    ff_sums = (scattered[1][:, attn_cols:], scattered[0][:, :-128])
+    half_sets = []
+    for sums in (attn_sums, ff_sums):
+        keep, send = choose(sec0, *sums)
+        half_sets.append(choose(sec0, keep, swap_section(send)))
+    attn_sets, ff_sets = half_sets
+    out_grad = jnp.concatenate([member[:, out_at:up_at] for member in attn_sets], axis=1).astype(f32)[None]
     down_grad = jnp.concatenate(
-        [member[:, at : at + width] for member in half_sets for at in (down_at, down_at + width)],
+        [member[:, up_cols + at : up_cols + at + width] for member in ff_sets for at in (0, width)],
         axis=0,
     ).astype(f32)[None]
-    col_first, col_second = [
-        jnp.concatenate([member[:, :cut], member[:, up_at:down_at]], axis=1) for member in half_sets
-    ]
-    keep, send = choose(x0, col_first, col_second)
-    norm1_grad = keep[:, qkv_cols].astype(f32)[None]
-    norm2_grad = keep[:, cut + up_cols].astype(f32)[None]
-    first, second = choose(x0, keep, swap_x(send))
+
+    def finish_columns(first, second, gains):
+        keep, send = choose(x0, first, second)
+        return keep[:, : keep.shape[1] - gains], keep[:, keep.shape[1] - gains :], choose(x0, keep, swap_x(send))
+
+    qkv_own, gain_own, qkv_sets = finish_columns(attn_sets[0][:, :cut], attn_sets[1][:, :cut], 128)
+    _, _, up_sets = finish_columns(ff_sets[0][:, :up_cols], ff_sets[1][:, :up_cols], 0)
+    norm1_grad = gain_own[:, 0].astype(f32)[None]
+    norm2_grad = gain_own[:, 1].astype(f32)[None]
     qkv_grad = jnp.stack(
-        [member[:, :qkv_cols].reshape(in_rows, -1, HEAD_DIM) for member in (first, second)], axis=2
+        [member[:, :qkv_cols].reshape(in_rows, -1, HEAD_DIM) for member in qkv_sets], axis=2
     ).reshape(in_rows, -1).astype(f32)[None]
     up_grad = jnp.stack(
         [
-            jnp.transpose(
-                member[:, cut : cut + up_cols].reshape(in_rows, 2, -1, 2, unit), (0, 2, 3, 1, 4)
-            )
-            for member in (first, second)
+            jnp.transpose(member.reshape(in_rows, 2, -1, 2, unit), (0, 2, 3, 1, 4))
+            for member in up_sets
         ],
         axis=2,
     ).reshape(in_rows, -1).astype(f32)[None]

time: 899 us -> 870 us (0.968)
  waiting for transfers between devices: 385 us -> 305 us
  blocking collectives: 35.6 us -> 13.5 us
  matrix products: 147 us -> 169 us
  other arithmetic: 80.1 us -> 98.8 us
  starting transfers between devices: 82.8 us -> 101 us
    ppermute x11 -> x20, waiting for transfers between devices: 173 us -> 142 us  [swap_x(): return lax.ppermute(value, 'seq', [(q, q ^ 1) for q in range(4)])]
    dot_general x24 -> x48, matrix products: 72.2 us -> 101 us  [the longest x24 39.4 us: back(): lax.dot_general(left, right, (((1,), (1,)), ((), ())), preferred_element_...]
    reduce_scatter x2 -> x3, waiting for transfers between devices: 55.9 us -> 28.4 us  [scatter_rows(): lax.psum_scatter(partial, ('section', 'dp', 'seq'), scatter_dimension=0,...]
    all_to_all x1 -> x0, blocking collectives: 22.1 us -> none  [per_device_pairs(): stream_got = lax.all_to_all(stream_send, both, 0, 0, tiled=True)]
    ppermute x6, waiting for transfers between devices: 43.2 us -> 28.6 us  [sum_dp(): running = lax.ppermute(own, 'dp', live)]
    conv_general_dilated x2, matrix products: 24.6 us -> 12.3 us  [conv_forward(): lax.conv_general_dilated(view, band, (1,), [(half, half)], dimension_numb...]
    ppermute x1, waiting for transfers between devices: 11.8 us -> 0.01 us  [per_device_pairs(): row_block = lax.ppermute(own_block, both, across)]
    all_to_all x0 -> x1, waiting for transfers between devices: none -> 10.3 us  [per_device_pairs(): stream_got = lax.all_to_all(stream_send, both, 0, 0, tiled=True)]
  transfers between devices with their start and end apart: 40 -> 54, of which waited for: 24 -> 31; matrix products, arithmetic and copies ran while one was open for 25% -> 34% of each run, Pallas kernels for 5% -> 7%
where the time goes in v3:
time: 870 us; the launch traced here: 858 us
  waiting for transfers between devices  305 us (35%)
  matrix products  169 us (19%)
  starting transfers between devices  101 us (12%)
  other arithmetic  98.8 us (11%)
  local copies, waits for them, and re-layouts  84.6 us (10%)
  Pallas kernels  68.3 us (8%)
  between operations  18.2 us (2%)
  blocking collectives  13.5 us (2%)
    ppermute x20, waiting for transfers between devices, swap_x(): return lax.ppermute(value, 'seq', [(q, q ^ 1) for q in range(4)])  142 us
    ppermute x3, waiting for transfers between devices, chain_steps(): low = lax.ppermute(low, 'dp', upward)  71.4 us
    pallas_call x4, Pallas kernels, attention_backward(): pl.pallas_call(functools.partial(attention_backward_kernel, factor), grid...  41.4 us
    dot_general x24, matrix products, back(): lax.dot_general(left, right, (((1,), (1,)), ((), ())), preferred_element_...  39.4 us
    dot_general x8, matrix products, per_device_pairs(): hidden_pre = jnp.dot(normed_two[c], w_up[part], preferred_element_type=f32)  34 us
    dot_general x12, matrix products, outer(): lax.dot_general(left, right, (((0,), (0,)), ((), ())), preferred_element_...  31.3 us
    ppermute x6, waiting for transfers between devices, sum_dp(): running = lax.ppermute(own, 'dp', live)  28.6 us
    reduce_scatter x3, waiting for transfers between devices, scatter_rows(): lax.psum_scatter(partial, ('section', 'dp', 'seq'), scatter_dimension=0,...  28.4 us
  transfers between devices with their start and end apart: 54, of which 31 were waited for; matrix products, arithmetic and copies ran while one was open for 34% of the time, Pallas kernels for 7%

profile of v3, /device:TPU:17, one launch (start us, length us, event | category | flops | bytes accessed | tf_op | source)
XLA Modules:
  0.0 858.1 jit_solution(13396138907148096208)
XLA Ops:
  18.4 10.3 %collective-permute-done.8 = bf16[64,3840]{1,0:T(8,128)(2,1)S(1)} collective-permute-done((bf16[64,3840]{1,0:T(8,128)(2,1)}, bf16[64,3840]{1,0:T(8,128)(2,1)S(1)}, u32[]{:S(2)}, u32[]{:S(2)}) %collective-permute-start.8) | collective-permute-done | bytes 491552 | tf_op jit(solution)/shard_map/ppermute | solution.py:516
  35.6 13.5 %all_to_all.30 = bf16[8,272,128]{2,1,0:T(8,128)(2,1)S(1)} all-to-all(bf16[8,272,128]{2,1,0:T(8,128)(2,1)S(1)} %copy.370), channel_id=1, replica_groups=mesh['section'=2,'dp'=4,'seq'=4] {'section','seq'}, dimensions={0} | all-to-all | bytes 1114112 | tf_op jit(solution)/shard_map/all_to_all | solution.py:876
  55.0 28.6 %collective-permute-done.3 = bf16[8,272,128]{2,1,0:T(8,128)(2,1)} collective-permute-done((bf16[8,272,128]{2,1,0:T(8,128)(2,1)S(1)}, bf16[8,272,128]{2,1,0:T(8,128)(2,1)}, u32[]{:S(2)}, u32[]{:S(2)}) %collective-permute-start.3) | collective-permute-done | bytes 557088 | tf_op jit(solution)/shard_map/ppermute | solution.py:538
  93.3 22.1 %collective-permute-done.4 = bf16[8,272,128]{2,1,0:T(8,128)(2,1)S(1)} collective-permute-done((bf16[8,272,128]{2,1,0:T(8,128)(2,1)}, bf16[8,272,128]{2,1,0:T(8,128)(2,1)S(1)}, u32[]{:S(2)}, u32[]{:S(2)}) %collective-permute-start.4) | collective-permute-done | bytes 557088 | tf_op jit(solution)/shard_map/ppermute | solution.py:538
  133.2 20.7 %collective-permute-done.5 = bf16[8,272,128]{2,1,0:T(8,128)(2,1)} collective-permute-done((bf16[8,272,128]{2,1,0:T(8,128)(2,1)S(1)}, bf16[8,272,128]{2,1,0:T(8,128)(2,1)}, u32[]{:S(2)}, u32[]{:S(2)}) %collective-permute-start.5) | collective-permute-done | bytes 557088 | tf_op jit(solution)/shard_map/ppermute | solution.py:538
  155.3 9.3 %collective-permute-done.7 = bf16[8,272,128]{2,1,0:T(8,128)(2,1)S(1)} collective-permute-done((bf16[8,272,128]{2,1,0:T(8,128)(2,1)}, bf16[8,272,128]{2,1,0:T(8,128)(2,1)S(1)}, u32[]{:S(2)}, u32[]{:S(2)}) %collective-permute-start.7) | collective-permute-done | bytes 557088 | tf_op jit(solution)/shard_map/ppermute | solution.py:539
  204.3 10.3 %all-to-all-done.2 = bf16[8,512,128]{2,1,0:T(8,128)(2,1)S(1)} async-done(((bf16[8,512,128]{2,1,0:T(8,128)(2,1)}), bf16[8,512,128]{2,1,0:T(8,128)(2,1)S(1)}, u32[]{:S(2)}, u32[]{:S(2)}) %all-to-all-start.2) | async-done | bytes 1048608 | tf_op jit(solution)/shard_map/all_to_all | solution.py:961
  254.3 20.5 %collective-permute-done.13 = bf16[256,1024]{1,0:T(8,128)(2,1)S(1)} collective-permute-done((bf16[256,1024]{1,0:T(8,128)(2,1)S(1)}, bf16[256,1024]{1,0:T(8,128)(2,1)S(1)}, u32[]{:S(2)}, u32[]{:S(2)}) %collective-permute-start.13) | collective-permute-done | bytes 524320 | tf_op jit(solution)/shard_map/ppermute | solution.py:516
  301.4 11.3 %collective-permute-done.15 = bf16[256,1024]{1,0:T(8,128)(2,1)S(1)} collective-permute-done((bf16[256,1024]{1,0:T(8,128)(2,1)S(1)}, bf16[256,1024]{1,0:T(8,128)(2,1)S(1)}, u32[]{:S(2)}, u32[]{:S(2)}) %collective-permute-start.15) | collective-permute-done | bytes 524320 | tf_op jit(solution)/shard_map/ppermute | solution.py:516
  368.4 8.9 %collective-permute-done.19 = bf16[256,1024]{1,0:T(8,128)(2,1)} collective-permute-done((bf16[256,1024]{1,0:T(8,128)(2,1)}, bf16[256,1024]{1,0:T(8,128)(2,1)}, u32[]{:S(2)}, u32[]{:S(2)}) %collective-permute-start.19) | collective-permute-done | bytes 524320 | tf_op jit(solution)/shard_map/ppermute | solution.py:516
  406.5 10.6 %collective-permute-done.21 = bf16[256,1024]{1,0:T(8,128)(2,1)S(1)} collective-permute-done((bf16[256,1024]{1,0:T(8,128)(2,1)S(1)}, bf16[256,1024]{1,0:T(8,128)(2,1)S(1)}, u32[]{:S(2)}, u32[]{:S(2)}) %collective-permute-start.21) | collective-permute-done | bytes 524320 | tf_op jit(solution)/shard_map/ppermute | solution.py:516
  421.9 10.0 %attention_backward.4 = (bf16[256,512]{1,0:T(8,128)(2,1)S(1)}, f32[1024,512]{1,0:T(8,128)S(1)}, f32[1024,512]{1,0:T(8,128)}) custom-call(bf16[256,1536]{1,0:T(8,128)(2,1)S(1)} %copy-done.8, bf16[1024,1024]{1,0:T(8,128)(2,1)} %copy-done.1, bf16[1024,1024]{1,0:T(8,128)(2,1)} %copy-done.1, bf16[256,512]{1,0:T(8,128)(2,1)S(1)} %convolution_convert_fusion.15.g_ref, ...), custom_call_target="tpu_custom_call" | custom-call | flops 2684354560 | bytes 5242880 | tf_op jit(solution)/shard_map/attention_backward/pallas_call | solution.py:731
  434.7 10.4 %attention_backward.5 = (bf16[256,512]{1,0:T(8,128)(2,1)S(1)}, f32[1024,512]{1,0:T(8,128)S(1)}, f32[1024,512]{1,0:T(8,128)}) custom-call(bf16[256,1536]{1,0:T(8,128)(2,1)S(1)} %copy-done.3, bf16[1024,1024]{1,0:T(8,128)(2,1)} %copy-done.1, bf16[1024,1024]{1,0:T(8,128)(2,1)} %copy-done.1, bf16[256,512]{1,0:T(8,128)(2,1)S(1)} %convolution_convert_fusion.14.g_ref, ...), custom_call_target="tpu_custom_call" | custom-call | flops 2684354560 | bytes 5242880 | tf_op jit(solution)/shard_map/attention_backward/pallas_call | solution.py:731
  479.6 10.7 %collective-permute-done.24 = bf16[256,1024]{1,0:T(8,128)(2,1)S(1)} collective-permute-done((bf16[256,1024]{1,0:T(8,128)(2,1)S(1)}, bf16[256,1024]{1,0:T(8,128)(2,1)S(1)}, u32[]{:S(2)}, u32[]{:S(2)}) %collective-permute-start.24) | collective-permute-done | bytes 524320 | tf_op jit(solution)/shard_map/ppermute | solution.py:516
  536.7 10.2 %attention_backward.6 = (bf16[256,512]{1,0:T(8,128)(2,1)S(1)}, f32[1024,512]{1,0:T(8,128)S(1)}, f32[1024,512]{1,0:T(8,128)}) custom-call(bf16[256,1536]{1,0:T(8,128)(2,1)S(1)} %copy-done.6, bf16[1024,1024]{1,0:T(8,128)(2,1)} %copy-done, bf16[1024,1024]{1,0:T(8,128)(2,1)} %copy-done, bf16[256,512]{1,0:T(8,128)(2,1)S(1)} %convolution_convert_fusion.13.g_ref, ...), custom_call_target="tpu_custom_call" | custom-call | flops 2684354560 | bytes 5242880 | tf_op jit(solution)/shard_map/attention_backward/pallas_call | solution.py:731
  549.4 10.8 %attention_backward.7 = (bf16[256,512]{1,0:T(8,128)(2,1)S(1)}, f32[1024,512]{1,0:T(8,128)S(1)}, f32[1024,512]{1,0:T(8,128)}) custom-call(bf16[256,1536]{1,0:T(8,128)(2,1)S(1)} %convolution_convert_fusion.4.q_ref, bf16[1024,1024]{1,0:T(8,128)(2,1)} %copy-done, bf16[1024,1024]{1,0:T(8,128)(2,1)} %copy-done, ...), custom_call_target="tpu_custom_call" | custom-call | flops 2684354560 | bytes 5242880 | tf_op jit(solution)/shard_map/attention_backward/pallas_call | solution.py:731
  597.7 10.7 %collective-permute-done.29 = bf16[256,1024]{1,0:T(8,128)(2,1)S(1)} collective-permute-done((bf16[256,1024]{1,0:T(8,128)(2,1)S(1)}, bf16[256,1024]{1,0:T(8,128)(2,1)S(1)}, u32[]{:S(2)}, u32[]{:S(2)}) %collective-permute-start.29) | collective-permute-done | bytes 524320 | tf_op jit(solution)/shard_map/ppermute | solution.py:516
  621.0 19.5 %collective-permute-done.30 = bf16[256,1024]{1,0:T(8,128)(2,1)} collective-permute-done((bf16[256,1024]{1,0:T(8,128)(2,1)}, bf16[256,1024]{1,0:T(8,128)(2,1)}, u32[]{:S(2)}, u32[]{:S(2)}) %collective-permute-start.30) | collective-permute-done | bytes 524320 | tf_op jit(solution)/shard_map/ppermute | solution.py:516
  640.5 11.2 %collective-permute-done.31 = bf16[256,1024]{1,0:T(8,128)(2,1)} collective-permute-done((bf16[256,1024]{1,0:T(8,128)(2,1)}, bf16[256,1024]{1,0:T(8,128)(2,1)}, u32[]{:S(2)}, u32[]{:S(2)}) %collective-permute-start.31) | collective-permute-done | bytes 524320 | tf_op jit(solution)/shard_map/ppermute | solution.py:516
  674.0 8.7 %fusion.395 = f32[33,256,256]{2,1,0:T(8,128)} fusion(bf16[2,256,256]{2,1,0:T(8,128)(2,1)S(1)} %copy-done.130, bf16[2,256,256]{2,1,0:T(8,128)(2,1)S(1)} %reshape.686), kind=kOutput, calls=%fused_computation.665 | convolution fusion | flops 2143289344 | bytes 9175040 | tf_op jit(solution)/shard_map/conv_general_dilated | solution.py:829
  697.3 10.7 %all-to-all-start.4 = ((bf16[8,2,256,128]{3,2,1,0:T(8,128)(2,1)}), bf16[8,2,256,128]{3,2,1,0:T(8,128)(2,1)S(1)}, u32[]{:S(2)}, u32[]{:S(2)}) async-start(bf16[8,2,256,128]{3,2,1,0:T(8,128)(2,1)} %copy.417), calls=%async_computation.5 | async-start | bytes 2097152 | tf_op jit(solution)/shard_map/all_to_all | solution.py:1123
  708.0 8.8 %fusion.22 = bf16[8192,64]{1,0:T(8,128)(2,1)S(1)} fusion(f32[8448,256]{1,0:T(8,128)} %bitcast.288), kind=kLoop, calls=%fused_computation.35 | loop fusion | flops 2097152 | bytes 9437184 | tf_op jit(solution)/shard_map/convert.32
  734.6 28.4 %reduce-scatter.8.cloned.1.call-done = bf16[64,2176]{1,0:T(8,128)(2,1)} async-done(((bf16[1024,2176]{1,0:T(8,128)(2,1)}), bf16[64,2176]{1,0:T(8,128)(2,1)}) %reduce-scatter.8.cloned.1.call-update) | async-done | bytes 278544 | tf_op jit(solution)/shard_map/reduce_scatter | solution.py:592
  786.0 13.9 %collective-permute-done.35 = bf16[2,4,272,128]{3,2,1,0:T(8,128)(2,1)} collective-permute-done((bf16[2,4,272,128]{3,2,1,0:T(8,128)(2,1)}, bf16[2,4,272,128]{3,2,1,0:T(8,128)(2,1)}, u32[]{:S(2)}, u32[]{:S(2)}) %collective-permute-start.35) | collective-permute-done | bytes 557088 | tf_op jit(solution)/shard_map/ppermute | solution.py:572
  (868 shorter events, 509.9 us)
Async XLA Ops:
  7.2 208.1 %all-gather.3.cloned.1.call-start = ((), (), s32[]{:S(2)}) async-start(), calls=%async_computation.9 | async-start | bytes 13926400 | tf_op jit(solution)/shard_map/all_gather | solution.py:586
  34.0 279.0 %all-gather.5.cloned.1.call-start = ((), (), s32[]{:S(2)}) async-start(), calls=%async_computation.10 | async-start | bytes 13926400 | tf_op jit(solution)/shard_map/all_gather | solution.py:586
  49.2 34.4 %collective-permute-start.3 = (bf16[8,272,128]{2,1,0:T(8,128)(2,1)S(1)}, bf16[8,272,128]{2,1,0:T(8,128)(2,1)}, u32[]{:S(2)}, u32[]{:S(2)}) collective-permute-start(bf16[8,272,128]{2,1,0:T(8,128)(2,1)S(1)} %all_to_all.30), channel_id=1, source_target_pairs={{0,4},{4,8},{8,12},{1,5},{5,9},{9,13},{2,6},{6,10},{10,14},{3,7},{... | collective-permute-start | bytes 1671176 | tf_op jit(solution)/shard_map/ppermute | solution.py:538
  52.5 38.9 %collective-permute-start.2 = (bf16[8,272,128]{2,1,0:T(8,128)(2,1)S(1)}, bf16[8,272,128]{2,1,0:T(8,128)(2,1)}, u32[]{:S(2)}, u32[]{:S(2)}) collective-permute-start(bf16[8,272,128]{2,1,0:T(8,128)(2,1)S(1)} %all_to_all.30), channel_id=1, source_target_pairs={{4,0},{8,4},{12,8},{5,1},{9,5},{13,9},{6,2},{10,6},{14,10},{7,3},{... | collective-permute-start | bytes 1671176 | tf_op jit(solution)/shard_map/ppermute | solution.py:539
  83.6 31.8 %collective-permute-start.4 = (bf16[8,272,128]{2,1,0:T(8,128)(2,1)}, bf16[8,272,128]{2,1,0:T(8,128)(2,1)S(1)}, u32[]{:S(2)}, u32[]{:S(2)}) collective-permute-start(bf16[8,272,128]{2,1,0:T(8,128)(2,1)} %collective-permute-done.3), channel_id=1, source_target_pairs={{0,4},{4,8},{8,12},{1,5},{5,9},{9,13},{2,6},{6,10},{10,14},{3,7},{... | collective-permute-start | bytes 1671176 | tf_op jit(solution)/shard_map/ppermute | solution.py:538
  87.9 29.9 %all-to-all-start = ((bf16[4,2,256,128]{2,3,1,0:T(8,128)(2,1)}), bf16[4,2,256,128]{2,3,1,0:T(8,128)(2,1)S(1)}, u32[]{:S(2)}, u32[]{:S(2)}) async-start(bf16[4,2,256,128]{2,3,1,0:T(8,128)(2,1)} %copy.367), calls=%async_computation | async-start | bytes 1048576 | tf_op jit(solution)/shard_map/all_to_all | solution.py:880
  91.4 34.4 %collective-permute-start.6 = (bf16[8,272,128]{2,1,0:T(8,128)(2,1)}, bf16[8,272,128]{2,1,0:T(8,128)(2,1)}, u32[]{:S(2)}, u32[]{:S(2)}) collective-permute-start(bf16[8,272,128]{2,1,0:T(8,128)(2,1)} %collective-permute-done.2), channel_id=1, source_target_pairs={{4,0},{8,4},{12,8},{5,1},{9,5},{13,9},{6,2},{10,6},{14,10},{7,3},{... | collective-permute-start | bytes 1671176 | tf_op jit(solution)/shard_map/ppermute | solution.py:539
  115.4 38.4 %collective-permute-start.5 = (bf16[8,272,128]{2,1,0:T(8,128)(2,1)S(1)}, bf16[8,272,128]{2,1,0:T(8,128)(2,1)}, u32[]{:S(2)}, u32[]{:S(2)}) collective-permute-start(bf16[8,272,128]{2,1,0:T(8,128)(2,1)S(1)} %collective-permute-done.4), channel_id=1, source_target_pairs={{0,4},{4,8},{8,12},{1,5},{5,9},{9,13},{2,6},{6,10},{10,14},{3,7},{... | collective-permute-start | bytes 1671176 | tf_op jit(solution)/shard_map/ppermute | solution.py:538
  125.8 38.7 %collective-permute-start.7 = (bf16[8,272,128]{2,1,0:T(8,128)(2,1)}, bf16[8,272,128]{2,1,0:T(8,128)(2,1)S(1)}, u32[]{:S(2)}, u32[]{:S(2)}) collective-permute-start(bf16[8,272,128]{2,1,0:T(8,128)(2,1)} %collective-permute-done.6), channel_id=1, source_target_pairs={{4,0},{8,4},{12,8},{5,1},{9,5},{13,9},{6,2},{10,6},{14,10},{7,3},{... | collective-permute-start | bytes 1671176 | tf_op jit(solution)/shard_map/ppermute | solution.py:539
  192.9 21.8 %all-to-all-start.2 = ((bf16[8,512,128]{2,1,0:T(8,128)(2,1)}), bf16[8,512,128]{2,1,0:T(8,128)(2,1)S(1)}, u32[]{:S(2)}, u32[]{:S(2)}) async-start(bf16[8,512,128]{2,1,0:T(8,128)(2,1)} %bitcast.21), calls=%async_computation.2 | async-start | bytes 2097152 | tf_op jit(solution)/shard_map/all_to_all | solution.py:961
  199.9 361.0 %reduce-scatter.4.cloned.1.call-start = ((), (), s32[]{:S(2)}) async-start(), calls=%async_computation.11 | async-start | bytes 9191424 | tf_op jit(solution)/shard_map/reduce_scatter | solution.py:592
  200.8 38.6 %collective-permute-start = (bf16[256,1024]{1,0:T(8,128)(2,1)}, bf16[256,1024]{1,0:T(8,128)(2,1)}, u32[]{:S(2)}, u32[]{:S(2)}) collective-permute-start(bf16[256,1024]{1,0:T(8,128)(2,1)} %select_bitcast_fusion.2), channel_id=1, source_target_pairs={{0,0},{1,1},{2,16},{3,17},{16,2},{17,3},{18,18},{19,19},{4,4},{5,5... | collective-permute-start | bytes 1572872 | tf_op jit(solution)/shard_map/ppermute | solution.py:944
  239.4 84.8 %collective-permute-start.1 = (bf16[256,1024]{1,0:T(8,128)(2,1)}, bf16[256,1024]{1,0:T(8,128)(2,1)}, u32[]{:S(2)}, u32[]{:S(2)}) collective-permute-start(bf16[256,1024]{1,0:T(8,128)(2,1)} %collective-permute-done), channel_id=1, source_target_pairs={{0,1},{1,0},{2,3},{3,2},{4,5},{5,4},{6,7},{7,6},{8,9},{9,8},{10,11... | collective-permute-start | bytes 1572872 | tf_op jit(solution)/shard_map/ppermute | solution.py:516
  247.4 27.3 %collective-permute-start.13 = (bf16[256,1024]{1,0:T(8,128)(2,1)S(1)}, bf16[256,1024]{1,0:T(8,128)(2,1)S(1)}, u32[]{:S(2)}, u32[]{:S(2)}) collective-permute-start(bf16[256,1024]{1,0:T(8,128)(2,1)S(1)} %convolution_convert_fusion.10), channel_id=1, source_target_pairs={{0,1},{1,0},{2,3},{3,2},{4,5},{5,4},{6,7},{7,6},{8,9},{9,8},{10,11... | collective-permute-start | bytes 1572872 | tf_op jit(solution)/shard_map/ppermute | solution.py:516
  402.8 331.8 %reduce-scatter.6.cloned.1.call-start = ((), (), s32[]{:S(2)}) async-start(), calls=%async_computation.12 | async-start | bytes 13647872 | tf_op jit(solution)/shard_map/reduce_scatter | solution.py:592
  611.4 47.7 %all-to-all-start.3 = ((bf16[8,512,128]{2,1,0:T(8,128)(2,1)}), bf16[8,512,128]{2,1,0:T(8,128)(2,1)S(1)}, u32[]{:S(2)}, u32[]{:S(2)}) async-start(bf16[8,512,128]{2,1,0:T(8,128)(2,1)} %bitcast_bitcast_fusion), calls=%async_computation.4 | async-start | bytes 2097152 | tf_op jit(solution)/shard_map/all_to_all | solution.py:1113
  615.5 147.5 %reduce-scatter.8.cloned.1.call-start = ((), (), s32[]{:S(2)}) async-start(), calls=%async_computation.13 | async-start | bytes 4734976 | tf_op jit(solution)/shard_map/reduce_scatter | solution.py:592
  615.7 24.7 %collective-permute-start.30 = (bf16[256,1024]{1,0:T(8,128)(2,1)}, bf16[256,1024]{1,0:T(8,128)(2,1)}, u32[]{:S(2)}, u32[]{:S(2)}) collective-permute-start(bf16[256,1024]{1,0:T(8,128)(2,1)} %fusion.132), channel_id=1, source_target_pairs={{0,1},{1,0},{2,3},{3,2},{4,5},{5,4},{6,7},{7,6},{8,9},{9,8},{10,11... | collective-permute-start | bytes 1572872 | tf_op jit(solution)/shard_map/ppermute | solution.py:516
  617.2 34.5 %collective-permute-start.31 = (bf16[256,1024]{1,0:T(8,128)(2,1)}, bf16[256,1024]{1,0:T(8,128)(2,1)}, u32[]{:S(2)}, u32[]{:S(2)}) collective-permute-start(bf16[256,1024]{1,0:T(8,128)(2,1)} %fusion.159), channel_id=1, source_target_pairs={{0,1},{1,0},{2,3},{3,2},{4,5},{5,4},{6,7},{7,6},{8,9},{9,8},{10,11... | collective-permute-start | bytes 1572872 | tf_op jit(solution)/shard_map/ppermute | solution.py:516
  654.7 64.4 %collective-permute-start.32 = (f32[256,1024]{1,0:T(8,128)}, f32[256,1024]{1,0:T(8,128)}, u32[]{:S(2)}, u32[]{:S(2)}) collective-permute-start(f32[256,1024]{1,0:T(8,128)} %add_select_fusion), channel_id=1, source_target_pairs={{0,0},{1,1},{2,16},{3,17},{16,2},{17,3},{18,18},{19,19},{4,4},{5,5... | collective-permute-start | bytes 3145736 | tf_op jit(solution)/shard_map/ppermute | solution.py:1151
  697.3 27.9 %all-to-all-start.4 = ((bf16[8,2,256,128]{3,2,1,0:T(8,128)(2,1)}), bf16[8,2,256,128]{3,2,1,0:T(8,128)(2,1)S(1)}, u32[]{:S(2)}, u32[]{:S(2)}) async-start(bf16[8,2,256,128]{3,2,1,0:T(8,128)(2,1)} %copy.417), calls=%async_computation.5 | async-start | bytes 2097152 | tf_op jit(solution)/shard_map/all_to_all | solution.py:1123
  768.0 36.5 %collective-permute-start.42 = (bf16[64,4096]{1,0:T(8,128)(2,1)}, bf16[64,4096]{1,0:T(8,128)(2,1)}, u32[]{:S(2)}, u32[]{:S(2)}) collective-permute-start(bf16[64,4096]{1,0:T(8,128)(2,1)} %broadcast_select_fusion.8), channel_id=1, source_target_pairs={{0,16},{16,0},{1,17},{17,1},{2,18},{18,2},{3,19},{19,3},{4,20},{20... | collective-permute-start | bytes 1572872 | tf_op jit(solution)/shard_map/ppermute | solution.py:512
  775.5 24.3 %collective-permute-start.35 = (bf16[2,4,272,128]{3,2,1,0:T(8,128)(2,1)}, bf16[2,4,272,128]{3,2,1,0:T(8,128)(2,1)}, u32[]{:S(2)}, u32[]{:S(2)}) collective-permute-start(bf16[2,4,272,128]{3,2,1,0:T(8,128)(2,1)} %fusion.166), channel_id=1, source_target_pairs={{0,4},{4,8},{1,5},{5,9},{2,6},{6,10},{3,7},{7,11},{16,20},{20,24},... | collective-permute-start | bytes 1671176 | tf_op jit(solution)/shard_map/ppermute | solution.py:572
  806.4 31.2 %collective-permute-start.43 = (bf16[64,2048]{1,0:T(8,128)(2,1)}, bf16[64,2048]{1,0:T(8,128)(2,1)S(1)}, u32[]{:S(2)}, u32[]{:S(2)}) collective-permute-start(bf16[64,2048]{1,0:T(8,128)(2,1)} %broadcast_select_fusion.23), channel_id=1, source_target_pairs={{0,1},{1,0},{2,3},{3,2},{4,5},{5,4},{6,7},{7,6},{8,9},{9,8},{10,11... | collective-permute-start | bytes 786440 | tf_op jit(solution)/shard_map/ppermute | solution.py:516
  (240 other events, 2051.7 us)
Sparse Core Ops, SparseCore 0:
  34.1 137.6 all-gather.2
  174.6 103.0 all-gather.4
  402.9 107.6 reduce-scatter.3
  530.8 147.1 reduce-scatter.5
  681.8 81.1 reduce-scatter.7

commit v4 on v3

--- a/solution.py
+++ b/solution.py
@@ -516,8 +516,11 @@
     return lax.ppermute(value, "seq", [(q, q ^ 1) for q in range(4)])
 
 
-def pair_sum(low):
-    return low.astype(jnp.float32) + swap_x(low).astype(jnp.float32)
+def pair_sum(low, behind=None):
+    other = swap_x(low)
+    if behind is not None:
+        other, _ = lax.optimization_barrier((other, behind))
+    return low.astype(jnp.float32) + other.astype(jnp.float32)
 
 
 def after(first, second):
@@ -526,31 +529,6 @@
 
 def choose(flag, first, second):
     return jnp.where(flag, first, second), jnp.where(flag, second, first)
-
-
-def chain_steps(value):
-    count = lax.axis_size("dp")
-    upward = [(i, i + 1) for i in range(count - 1)]
-    downward = [(i + 1, i) for i in range(count - 1)]
-    low, high = value, value
-    lows, highs = [], []
-    for _ in range(count - 1):
-        low = lax.ppermute(low, "dp", upward)
-        high = lax.ppermute(high, "dp", downward)
-        lows.append(low)
-        highs.append(high)
-    return lows, highs
-
-
-def place_dp(value, dp):
-    count = lax.axis_size("dp")
-    lows, highs = chain_steps(value)
-    whole = jnp.zeros((count, *value.shape), value.dtype)
-    whole = lax.dynamic_update_index_in_dim(whole, value, dp, 0)
-    for turn in range(1, count):
-        piece = jnp.where(dp + turn < count, highs[turn - 1], lows[count - turn - 1])
-        whole = lax.dynamic_update_index_in_dim(whole, piece, (dp + turn) % count, 0)
-    return whole
 
 
 def sum_dp(blocks, dp):
@@ -593,6 +571,278 @@
         partial, ("section", "dp", "seq"), scatter_dimension=0, tiled=True,
         axis_index_groups=line_groups(),
     )
+
+
+MESH = pl.DeviceIdType.MESH
+
+
+def opening_kernel(
+    dp_count, parts, conv_ref, signal_ref, keep_ref, send_ref, rest_ref, conv_out, signal_out, whole_out,
+    local_sem, a2a_send, a2a_recv, sig_send, sig_recv, line_send, line_recv, own_send, own_recv,
+    up_send, up_recv, y_send, y_recv, core_send, core_recv,
+):
+    sec, dp, seq = (lax.axis_index(name) for name in ("section", "dp", "seq"))
+    me = sec * 4 + seq
+    x, y = seq % 2, seq // 2
+    partner_x = (seq + 1 - 2 * x) % 4
+    partner_y = {"seq": (seq + 2) % 4}
+    sibling = {"section": 1 - sec}
+    has_up, has_down = dp < dp_count - 1, dp > 0
+    split = keep_ref.shape[1]
+    rows = keep_ref.shape[0] // parts
+
+    barrier = pltpu.get_barrier_semaphore()
+    for turn in range(1, 8):
+        other = (me + turn) % 8
+        pl.semaphore_signal(
+            barrier, inc=1, device_id={"section": other // 4, "seq": other % 4}, device_id_type=MESH
+        )
+    for there, step in ((has_up, 1), (has_down, -1)):
+
+        @pl.when(there)
+        def _(step=step):
+            pl.semaphore_signal(barrier, inc=1, device_id={"dp": dp + step}, device_id_type=MESH)
+
+    pl.semaphore_wait(barrier, 7 + jnp.where(has_up, 1, 0) + jnp.where(has_down, 1, 0))
+
+    def remote(source, target, send, recv, device):
+        return pltpu.make_async_remote_copy(
+            src_ref=source, dst_ref=target, send_sem=send, recv_sem=recv,
+            device_id=device, device_id_type=MESH,
+        )
+
+    def a2a(target, source):
+        return remote(
+            conv_ref.at[target], conv_out.at[dp, source], a2a_send.at[target], a2a_recv.at[source],
+            {"section": target // 4, "seq": target % 4},
+        )
+
+    def sig(target, source):
+        return remote(
+            signal_ref.at[target], signal_out.at[source], sig_send.at[target], sig_recv.at[source],
+            {"seq": target},
+        )
+
+    for turn in range(1, 8):
+        a2a((me + turn) % 8, me).start()
+    conv_local = pltpu.make_async_copy(conv_ref.at[me], conv_out.at[dp, me], local_sem.at[0])
+    signal_local = pltpu.make_async_copy(signal_ref.at[seq], signal_out.at[seq], local_sem.at[1])
+    conv_local.start()
+    signal_local.start()
+
+    def columns(half):
+        return whole_out.at[dp, y, half, :, pl.ds(0, split)]
+
+    def others(half):
+        return whole_out.at[dp, y, half, :, pl.ds(split, rest_ref.shape[2])]
+
+    keep_local = pltpu.make_async_copy(keep_ref, columns(0), local_sem.at[2])
+    rest_local = pltpu.make_async_copy(rest_ref.at[0], others(0), local_sem.at[3])
+    keep_far = remote(keep_ref, columns(1), own_send.at[0], own_recv.at[0], {"section": 1})
+    send_same = remote(send_ref, columns(0), own_send.at[1], own_recv.at[0], {"seq": partner_x})
+    send_cross = remote(
+        send_ref, columns(1), own_send.at[1], own_recv.at[0], {"section": 1, "seq": partner_x}
+    )
+    rest_far = remote(rest_ref.at[1], others(1), own_send.at[2], own_recv.at[1], {"section": 1})
+    first, second = sec == 0, sec == 1
+
+    @pl.when(first & (x == 0))
+    def _():
+        send_same.start()
+        keep_local.start()
+
+    @pl.when(first & (x == 1))
+    def _():
+        send_cross.start()
+        keep_far.start()
+
+    @pl.when(first)
+    def _():
+        rest_far.start()
+        rest_local.start()
+
+    for turn in range(1, 4):
+        sig((seq + turn) % 4, seq).start()
+
+    def line(slot, direction):
+        index = (direction + 1) // 2
+        return remote(
+            conv_out.at[slot], conv_out.at[slot], line_send.at[index, slot], line_recv.at[slot],
+            {"dp": dp + direction},
+        )
+
+    def place(slot, row, half, part):
+        return whole_out.at[slot, row, half, pl.ds(part * rows, rows)]
+
+    def along(slot, direction, part):
+        index = (direction + 1) // 2
+        ref = place(slot, y, sec, part)
+        return remote(
+            ref, ref, up_send.at[index, slot, part], up_recv.at[slot, part], {"dp": dp + direction}
+        )
+
+    def across(slot, row, part):
+        ref = place(slot, row, sec, part)
+        return remote(ref, ref, y_send.at[slot, part], y_recv.at[slot, part], partner_y)
+
+    def to_core(slot, row, half, part):
+        ref = place(slot, row, half, part)
+        return remote(
+            ref, ref, core_send.at[slot, row, part], core_recv.at[slot, row, part], sibling
+        )
+
+    for turn in range(1, 8):
+        a2a((me + turn) % 8, (me + turn) % 8).wait_recv()
+    conv_local.wait()
+    for there, direction in ((has_up, 1), (has_down, -1)):
+
+        @pl.when(there)
+        def _(direction=direction):
+            line(dp, direction).start()
+
+    @pl.when(first & (x == 0))
+    def _():
+        keep_local.wait()
+
+    @pl.when(first & (x == 1))
+    def _():
+        send_same.wait_recv()
+
+    @pl.when(first)
+    def _():
+        rest_local.wait()
+
+    @pl.when(second & (x == 0))
+    def _():
+        send_cross.wait_recv()
+
+    @pl.when(second & (x == 1))
+    def _():
+        keep_far.wait_recv()
+
+    @pl.when(second)
+    def _():
+        rest_far.wait_recv()
+
+    for part in range(parts):
+        for there, direction in ((has_up, 1), (has_down, -1)):
+
+            @pl.when(there)
+            def _(direction=direction, part=part):
+                along(dp, direction, part).start()
+
+        across(dp, y, part).start()
+        to_core(dp, y, sec, part).start()
+
+    def stage(distance):
+        arrivals = []
+        for direction in (1, -1):
+            slot = dp - direction * distance
+            arrives = (slot >= 0) & (slot < dp_count)
+            goes_on = arrives & (has_up if direction == 1 else has_down)
+            arrivals.append((direction, slot, arrives, goes_on))
+
+            @pl.when(arrives)
+            def _(slot=slot, direction=direction):
+                line(slot, direction).wait_recv()
+
+            @pl.when(goes_on)
+            def _(slot=slot, direction=direction):
+                line(slot, direction).start()
+
+        for part in range(parts):
+            for direction, slot, arrives, goes_on in arrivals:
+
+                @pl.when(arrives)
+                def _(slot=slot, direction=direction, part=part):
+                    along(slot, direction, part).wait_recv()
+
+                @pl.when(goes_on)
+                def _(slot=slot, direction=direction, part=part):
+                    along(slot, direction, part).start()
+
+                @pl.when(arrives)
+                def _(slot=slot, part=part):
+                    across(slot, y, part).start()
+                    to_core(slot, y, sec, part).start()
+
+    def pass_crossed(distance):
+        for part in range(parts):
+            for sign in (1, -1) if distance else (1,):
+                slot = dp - sign * distance
+
+                @pl.when((slot >= 0) & (slot < dp_count))
+                def _(slot=slot, part=part):
+                    across(slot, 1 - y, part).wait_recv()
+                    to_core(slot, 1 - y, sec, part).start()
+
+    for distance in range(1, dp_count):
+        stage(distance)
+        pass_crossed(distance - 1)
+    pass_crossed(dp_count - 1)
+
+    for slot in range(dp_count):
+        for part in range(parts):
+            for row in range(2):
+                to_core(slot, row, 1 - sec, part).wait_recv()
+                to_core(slot, row, sec, part).wait_send()
+            across(slot, y, part).wait_send()
+        for direction in (1, -1):
+            sent = (slot <= dp if direction == 1 else slot >= dp) & (has_up if direction == 1 else has_down)
+
+            @pl.when(sent)
+            def _(slot=slot, direction=direction):
+                line(slot, direction).wait_send()
+                for part in range(parts):
+                    along(slot, direction, part).wait_send()
+
+    @pl.when(first & (x == 0))
+    def _():
+        send_same.wait_send()
+
+    @pl.when(first & (x == 1))
+    def _():
+        send_cross.wait_send()
+        keep_far.wait_send()
+
+    @pl.when(first)
+    def _():
+        rest_far.wait_send()
+
+    for turn in range(1, 8):
+        a2a((me + turn) % 8, me).wait_send()
+    for turn in range(1, 4):
+        sig((seq + turn) % 4, (seq + turn) % 4).wait_recv()
+        sig((seq + turn) % 4, seq).wait_send()
+    signal_local.wait()
+
+
+def opening(conv_send, signal_send, keep, send, rest):
+    count = lax.axis_size("dp")
+    parts = 2
+    rows, columns = keep.shape[0], keep.shape[1] + rest.shape[2]
+    anywhere = pl.BlockSpec(memory_space=pl.ANY)
+    dma = pltpu.SemaphoreType.DMA
+    conv_all, signal_all, whole = pl.pallas_call(
+        functools.partial(opening_kernel, count, parts),
+        in_specs=[anywhere] * 5,
+        out_specs=[anywhere] * 3,
+        out_shape=[
+            jax.ShapeDtypeStruct((count, *conv_send.shape), conv_send.dtype),
+            jax.ShapeDtypeStruct(signal_send.shape, signal_send.dtype),
+            jax.ShapeDtypeStruct((count, 2, 2, rows, columns), keep.dtype),
+        ],
+        scratch_shapes=[
+            dma((4,)), dma((8,)), dma((8,)), dma((4,)), dma((4,)), dma((2, count)), dma((count,)),
+            dma((3,)), dma((2,)), dma((2, count, parts)), dma((count, parts)), dma((count, parts)),
+            dma((count, parts)), dma((count, 2, parts)), dma((count, 2, parts)),
+        ],
+        compiler_params=pltpu.CompilerParams(
+            collective_id=0, has_side_effects=True, vmem_limit_bytes=4 * 1024 * 1024
+        ),
+        name="opening",
+    )(conv_send, signal_send, keep, send, rest)
+    return conv_all, signal_all, whole.reshape(-1, columns)
 
 
 def norm_stats(values):
@@ -873,21 +1123,9 @@
         jnp.broadcast_to(bias_low[None, None, :], (1, 8, block_width)), ((0, 15), (0, 0), (0, 0))
     )
     conv_send = jnp.transpose(jnp.concatenate([conv_low, bias_rows], axis=0), (1, 0, 2))
-    conv_got = lax.all_to_all(conv_send, both, 0, 0, tiled=True)
 
     own_half = jnp.where(sec0, signal[:, :, : width // 2], signal[:, :, width // 2 :])
     sig_send = jnp.transpose(own_half.reshape(micro_count, frames, 4, block_width), (2, 0, 1, 3))
-    sig_got = lax.all_to_all(sig_send, "seq", 0, 0, tiled=True)
-    sig_all = jnp.transpose(sig_got, (1, 0, 2, 3)).reshape(micro_count, row_frames, block_width)
-
-    conv_all = place_dp(conv_got, dp)
-    conv_all = conv_all.reshape(dp_count, 2, 4, rows_here + 16, block_width)
-    conv_all = jnp.transpose(conv_all, (1, 0, 2, 3, 4))
-    bias_all = conv_all[:, :, :, rows_here, : conv_bias.shape[0]].reshape(width)
-    bias_own = lax.dynamic_slice_in_dim(bias_all, (sec * 4 + seq) * block_width, block_width, 0)
-    kernel_own = conv_all[:, :, :, :rows_here].reshape(TAPS * per_group, block_width)
-    bands = conv_bands(kernel_own, per_group)
-
     in_rows = qkv_weight.shape[1]
     unit = down_weight.shape[1] // 4
     qkv_view = qkv_weight[0].astype(bf16).reshape(in_rows, -1, 2, HEAD_DIM)
@@ -904,32 +1142,39 @@
         jnp.concatenate([a, col_one, b, col_two], axis=1)
         for a, b in zip(choose(x0, *qkv_parity), choose(x0, *up_parity))
     ]
-    row_sets = choose(x0, keep_cols, swap_x(send_cols))
     out_low = out_weight[0].astype(bf16)
     down_low = down_weight[0].astype(bf16).reshape(2, 2, unit, width)
-    out_at, up_at = cut, cut + width // 2
+    rest = jnp.stack(
+        [
+            jnp.concatenate(
+                [out_low[:, h * width // 2 : (h + 1) * width // 2], down_low[h, 0], down_low[h, 1]], axis=1
+            )
+            for h in range(2)
+        ]
+    )
+    up_at = cut
     two_at = up_at + up_cols
-    down_at = two_at + 128
-    row_parts = [
-        jnp.concatenate(
-            [
-                row_sets[h][:, :cut],
-                out_low[:, h * width // 2 : (h + 1) * width // 2],
-                row_sets[h][:, cut:],
-                down_low[h, 0],
-                down_low[h, 1],
-            ],
-            axis=1,
-        )
-        for h in range(2)
-    ]
+    out_at = two_at + 128
+    down_at = out_at + width // 2
+    conv_all, sig_got, whole = opening(conv_send, sig_send, keep_cols, send_cols, rest)
+    whole, (keep_cols, send_cols) = after(whole, (keep_cols, send_cols))
+    row_sets = choose(x0, keep_cols, swap_x(send_cols))
+    row_parts = [jnp.concatenate([row_sets[h], rest[h]], axis=1) for h in range(2)]
     keep, send = choose(sec0, *row_parts)
-    layer_pieces = choose(sec0, keep, swap_section(send))
-    gathered = [gather_rows(layer_pieces[layer]) for layer in range(2)]
+    _, second_piece = choose(sec0, keep, swap_section(send))
+    gathered = [whole, gather_rows(second_piece)]
+    sig_all = jnp.transpose(sig_got, (1, 0, 2, 3)).reshape(micro_count, row_frames, block_width)
+    conv_all = conv_all.reshape(dp_count, 2, 4, rows_here + 16, block_width)
+    conv_all = jnp.transpose(conv_all, (1, 0, 2, 3, 4))
+    bias_all = conv_all[:, :, :, rows_here, : conv_bias.shape[0]].reshape(width)
+    bias_own = lax.dynamic_slice_in_dim(bias_all, (sec * 4 + seq) * block_width, block_width, 0)
+    kernel_own = conv_all[:, :, :, :rows_here].reshape(TAPS * per_group, block_width)
+    bands = conv_bands(kernel_own, per_group)
+
 
     def views(whole):
         w_out = jnp.transpose(
-            whole[:, out_at:up_at].reshape(-1, 2, in_rows, width // 2), (0, 2, 1, 3)
+            whole[:, out_at:down_at].reshape(-1, 2, in_rows, width // 2), (0, 2, 1, 3)
         ).reshape(-1, width)
         gain_one = whole[:, qkv_cols].astype(f32)[None, :]
         gain_two = whole[:, two_at].astype(f32)[None, :]
@@ -967,36 +1212,36 @@
     chunk_segs = [query_segs[c * rows : (c + 1) * rows] for c in range(chunks)]
     kept = []
     for layer in range(2):
-        layer_in, whole = after(layer_in, gathered[layer])
+        whole = gathered[layer]
+        if layer:
+            layer_in = []
+            previous_lows[0], whole = after(previous_lows[0], whole)
         layer_weights.append(views(whole))
         gain_one, w_qkv, w_out, gain_two, w_up, w_down = layer_weights[layer]
         normed_one, packed, kv_own, kv_other = [], [], [], []
         for c in range(chunks):
+            if layer:
+                total = previous[c] + pair_sum(previous_lows[c], packed[-1] if c else None)
+                layer_in.append(total.astype(bf16).astype(f32))
             centred, inv = norm_stats(layer_in[c])
             normed_one.append((centred * inv * gain_one).astype(bf16))
             packed.append(jnp.dot(normed_one[c], w_qkv, preferred_element_type=f32).astype(bf16))
             kv_own.append(packed[c][:, width // 2 :])
             kv_other.append(swap_section(kv_own[c]))
         kv_all = jnp.concatenate(kv_own + kv_other, axis=0)
-        attended, lse, resid_two, normed_two, hidden, hidden_slope, result = [], [], [], [], [], [], []
-        low = None
+        attended, lse, resid_two, normed_two, hidden, hidden_slope = [], [], [], [], [], []
+        attn_lows, lows = [], []
         for c in range(chunks):
             own = packed[c]
-            if low is not None:
-                low, own = after(low, own)
-                resid_two.append(layer_in[c - 1] + pair_sum(low))
+            if c:
+                attn_lows[-1], own = after(attn_lows[-1], own)
             mixed, log_total = attention_forward(own, kv_all, chunk_segs[c], key_segs, factor)
             attended.append(mixed)
             lse.append(log_total)
-            low = jnp.dot(mixed, w_out, preferred_element_type=f32).astype(bf16)
-        resid_two.append(layer_in[-1] + pair_sum(low))
-        low, lows = None, []
+            attn_lows.append(jnp.dot(mixed, w_out, preferred_element_type=f32).astype(bf16))
         for c in range(chunks):
-            values = resid_two[c]
-            if low is not None:
-                low, values = after(low, values)
-                lows.append(low)
-            centred, inv = norm_stats(values)
+            resid_two.append(layer_in[c] + pair_sum(attn_lows[c], lows[-1] if c else None))
+            centred, inv = norm_stats(resid_two[c])
             normed_two.append((centred * inv * gain_two).astype(bf16))
             down_sum, own_hidden, own_slope = None, [], []
             for part in range(2):
@@ -1008,17 +1253,11 @@
                 down_sum = term if down_sum is None else down_sum + term
             hidden.append(own_hidden)
             hidden_slope.append(own_slope)
-            low = down_sum.astype(bf16)
-        lows.append(low)
-
-        def joined(members):
-            return jnp.concatenate(members, axis=0)
+            lows.append(down_sum.astype(bf16))
 
         resid_two_last = resid_two
         kept.append((layer_in, normed_one, packed, kv_all, attended, lse, resid_two, normed_two, hidden, hidden_slope))
-        if layer == 0:
-            result = [member + pair_sum(low) for member, low in zip(resid_two, lows)]
-            layer_in = [member.astype(bf16).astype(f32) for member in result]
+        previous, previous_lows = resid_two, lows
 
     def outer(left, right):
         return lax.dot_general(
@@ -1070,6 +1309,9 @@
             resid_grad.append(in_part + grad_out[c])
             attn_branch.append(resid_grad[c].astype(bf16))
             attended_grad = back(attn_branch[c], w_out).astype(bf16)
+            if layer == 1 and c == 0:
+                attended_grad, lows = after(attended_grad, lows)
+                output = [member + pair_sum(low) for member, low in zip(resid_two_last, lows)]
             own_dq, *dkv = attention_backward(
                 packed[c], kv_all, attended_grad, attended[c], lse[c], chunk_segs[c], key_segs, factor,
                 None if c == 0 else dkv,
@@ -1077,6 +1319,8 @@
             dq.append(own_dq)
         if layer == 0:
             dkv, scattered[0] = after(dkv, scattered[0])
+        else:
+            dkv, output = after(dkv, output)
         dkv = jnp.concatenate(dkv, axis=1)
         other_dkv = swap_section(dkv[half_frames:].astype(bf16))
         dkv_own = (dkv[:half_frames] + other_dkv.astype(f32)).astype(bf16)
@@ -1106,8 +1350,7 @@
         grad_out = [member.astype(f32) for member in next_grad]
     grad_in_low = jnp.concatenate(next_grad)
     scattered.append(scatter_rows(jnp.concatenate(attn_members, axis=1)))
-    grad_in_low, lows = after(grad_in_low, lows)
-    output = jnp.concatenate([member + pair_sum(low) for member, low in zip(resid_two_last, lows)])
+    output = jnp.concatenate(output)
 
     lig_send = jnp.transpose(grad_in_low.reshape(half_frames, 8, block_width), (1, 0, 2))
     lig_got = lax.all_to_all(lig_send, both, 0, 0, tiled=True).reshape(2, 2, 2, half_frames, block_width)
@@ -1121,6 +1364,7 @@
     )
     gs_send = jnp.concatenate([gs_send, gs_send], axis=0)
     gs_got = lax.all_to_all(gs_send, both, 0, 0, tiled=True)
+    gs_got, scattered[1] = after(gs_got, scattered[1])
     gs_rows = jnp.transpose(gs_got, (1, 2, 0, 3)).reshape(micro_count, frames, width).astype(f32)
 
     taps_grad = conv_taps_grad(sig_views, grad_views, per_group)
@@ -1133,7 +1377,6 @@
         ((0, 0), (0, 0), (0, 0), (0, 15), (0, 0)),
     )
     taps_send = jnp.concatenate([taps_view, bias_view], axis=3)
-    taps_send, scattered[1] = after(taps_send, scattered[1])
     taps_sum = sum_dp(taps_send, dp)
     taps_got = lax.all_to_all(
         taps_sum.reshape(8, rows_here + 16, block_width), both, 0, 0, tiled=True
@@ -1153,7 +1396,7 @@
     output_rows = jnp.stack(choose(sec0, row_block, other_row))
     ends = jnp.where(sec0, gs_rows, output_rows)[None]
 
-    attn_cols = up_at
+    attn_cols = cut + width // 2
     attn_sums = (scattered[2], scattered[1][:, :attn_cols])
     ff_sums = (scattered[1][:, attn_cols:], scattered[0][:, :-128])
     half_sets = []
@@ -1161,7 +1404,7 @@
         keep, send = choose(sec0, *sums)
         half_sets.append(choose(sec0, keep, swap_section(send)))
     attn_sets, ff_sets = half_sets
-    out_grad = jnp.concatenate([member[:, out_at:up_at] for member in attn_sets], axis=1).astype(f32)[None]
+    out_grad = jnp.concatenate([member[:, cut:attn_cols] for member in attn_sets], axis=1).astype(f32)[None]
     down_grad = jnp.concatenate(
         [member[:, up_cols + at : up_cols + at + width] for member in ff_sets for at in (0, width)],
         axis=0,

time: 870 us -> 820 us (0.943)
  waiting for transfers between devices: 305 us -> 201 us
  Pallas kernels: 68.3 us -> 165 us
  starting transfers between devices: 101 us -> 72 us
  matrix products: 169 us -> 155 us
  blocking collectives: 13.5 us -> 0 us
    pallas_call x0 -> x1, Pallas kernels: none -> 96.6 us  [opening(): pl.pallas_call(functools.partial(opening_kernel, count, parts), in_specs=...]
    ppermute x6 -> x0, waiting for transfers between devices: 86.8 us -> none  [the longest x3 71.4 us: chain_steps(): low = lax.ppermute(low, 'dp', upward)]
    ppermute x20, waiting for transfers between devices: 142 us -> 87.3 us  [swap_x(): return lax.ppermute(value, 'seq', [(q, q ^ 1) for q in range(4)])]
    ppermute x6, waiting for transfers between devices: 28.6 us -> 73.5 us  [sum_dp(): running = lax.ppermute(own, 'dp', live)]
    reduce_scatter x3, waiting for transfers between devices: 28.4 us -> 0.01 us  [scatter_rows(): lax.psum_scatter(partial, ('section', 'dp', 'seq'), scatter_dimension=0,...]
    ppermute x6 -> x0, starting transfers between devices: 19.8 us -> none  [the longest x3 10.8 us: chain_steps(): high = lax.ppermute(high, 'dp', downward)]
    all_to_all x1 -> x0, blocking collectives: 13.5 us -> none  [per_device_pairs(): conv_got = lax.all_to_all(conv_send, both, 0, 0, tiled=True)]
    all_to_all x1, waiting for transfers between devices: 0.01 us -> 12.5 us  [per_device_pairs(): lax.all_to_all(lig_send, both, 0, 0, tiled=True)]
  transfers between devices with their start and end apart: 54 -> 46, of which waited for: 31 -> 26; matrix products, arithmetic and copies ran while one was open for 34% -> 35% of each run, Pallas kernels for 7% -> 8%
where the time goes in v4:
time: 820 us; the launch traced here: 807 us
  waiting for transfers between devices  201 us (25%)
  Pallas kernels  165 us (20%)
  matrix products  155 us (19%)
  other arithmetic  107 us (13%)
  local copies, waits for them, and re-layouts  88.3 us (11%)
  starting transfers between devices  72 us (9%)
  between operations  17.9 us (2%)
    pallas_call x1, Pallas kernels, opening(): pl.pallas_call(functools.partial(opening_kernel, count, parts), in_specs=...  96.6 us
    ppermute x20, waiting for transfers between devices, swap_x(): return lax.ppermute(value, 'seq', [(q, q ^ 1) for q in range(4)])  87.3 us
    ppermute x6, waiting for transfers between devices, sum_dp(): running = lax.ppermute(own, 'dp', live)  73.5 us
    pallas_call x4, Pallas kernels, attention_backward(): pl.pallas_call(functools.partial(attention_backward_kernel, factor), grid...  41.6 us
    dot_general x24, matrix products, back(): lax.dot_general(left, right, (((1,), (1,)), ((), ())), preferred_element_...  35.4 us
    dot_general x8, matrix products, per_device_pairs(): hidden_pre = jnp.dot(normed_two[c], w_up[part], preferred_element_type=f32)  31.7 us
    dot_general x12, matrix products, outer(): lax.dot_general(left, right, (((0,), (0,)), ((), ())), preferred_element_...  31.4 us
    pallas_call x4, Pallas kernels, attention_forward(): pl.pallas_call(functools.partial(attention_forward_kernel, factor), grid=...  26.9 us
  transfers between devices with their start and end apart: 46, of which 26 were waited for; matrix products, arithmetic and copies ran while one was open for 35% of the time, Pallas kernels for 8%

profile of v4, /device:TPU:17, one launch (start us, length us, event | category | flops | bytes accessed | tf_op | source)
XLA Modules:
  0.0 806.7 jit_solution(11143046602924106499)
XLA Ops:
  26.2 96.6 %opening.1 = (bf16[4,8,272,128]{3,2,1,0:T(8,128)(2,1)S(1)}, bf16[4,2,256,128]{3,2,1,0:T(8,128)(2,1)S(1)}, bf16[4,2,2,64,6400]{4,3,2,1,0:T(8,128)(2,1)S(1)}) custom-call(bf16[8,272,128]{2,1,0:T(8,128)(2,1)S(1)} %fusion.402.conv_ref, bf16[4,2,256,128]{3,2,1,0:T(8,128)(2,1)S(1)} %bitcast.286, bf16[64,3840]{1,0:T(8,128)(2,1)S(1)} %get-tuple-element.74.keep_ref, ...), custom_call_target="tpu_custom_call" | custom-call | tf_op jit(solution)/shard_map/opening/pallas_call | solution.py:826
  151.7 6.2 fusion.429
  164.2 6.2 fusion.425
  175.9 7.1 all-to-all-start
  190.0 7.8 all-to-all-done
  211.1 6.8 attention_forward.4
  220.8 6.6 attention_forward.5
  247.0 8.2 %collective-permute-done.8 = bf16[256,1024]{1,0:T(8,128)(2,1)S(1)} collective-permute-done((bf16[256,1024]{1,0:T(8,128)(2,1)S(1)}, bf16[256,1024]{1,0:T(8,128)(2,1)S(1)}, u32[]{:S(2)}, u32[]{:S(2)}) %collective-permute-start.8) | collective-permute-done | bytes 524320 | tf_op jit(solution)/shard_map/ppermute | solution.py:516
  264.0 10.5 %all-gather.2.cloned.1.call-done = bf16[1024,6400]{1,0:T(8,128)(2,1)} async-done(((bf16[64,6400]{1,0:T(8,128)(2,1)}), bf16[1024,6400]{1,0:T(8,128)(2,1)}) %all-gather.2.cloned.1.call-update) | async-done | bytes 13107216 | tf_op jit(solution)/shard_map/all_gather | solution.py:564
  291.6 7.4 collective-permute-done.9
  306.4 6.6 attention_forward.6
  315.8 7.0 attention_forward.7
  343.0 7.9 collective-permute-done.13
  385.8 10.2 %attention_backward.4 = (bf16[256,512]{1,0:T(8,128)(2,1)S(1)}, f32[1024,512]{1,0:T(8,128)S(1)}, f32[1024,512]{1,0:T(8,128)}) custom-call(bf16[256,1536]{1,0:T(8,128)(2,1)S(1)} %copy-done.8, bf16[1024,1024]{1,0:T(8,128)(2,1)} %copy-done.1, bf16[1024,1024]{1,0:T(8,128)(2,1)} %copy-done.1, bf16[256,512]{1,0:T(8,128)(2,1)S(1)} %convolution_convert_fusion.15.g_ref, ...), custom_call_target="tpu_custom_call" | custom-call | flops 2684354560 | bytes 5242880 | tf_op jit(solution)/shard_map/attention_backward/pallas_call | solution.py:981
  398.9 10.5 %attention_backward.5 = (bf16[256,512]{1,0:T(8,128)(2,1)S(1)}, f32[1024,512]{1,0:T(8,128)S(1)}, f32[1024,512]{1,0:T(8,128)}) custom-call(bf16[256,1536]{1,0:T(8,128)(2,1)S(1)} %copy-done.3, bf16[1024,1024]{1,0:T(8,128)(2,1)} %copy-done.1, bf16[1024,1024]{1,0:T(8,128)(2,1)} %copy-done.1, bf16[256,512]{1,0:T(8,128)(2,1)S(1)} %convolution_convert_fusion.14.g_ref, ...), custom_call_target="tpu_custom_call" | custom-call | flops 2684354560 | bytes 5242880 | tf_op jit(solution)/shard_map/attention_backward/pallas_call | solution.py:981
  444.9 10.7 %collective-permute-done.20 = bf16[256,1024]{1,0:T(8,128)(2,1)S(1)} collective-permute-done((bf16[256,1024]{1,0:T(8,128)(2,1)S(1)}, bf16[256,1024]{1,0:T(8,128)(2,1)S(1)}, u32[]{:S(2)}, u32[]{:S(2)}) %collective-permute-start.20) | collective-permute-done | bytes 524320 | tf_op jit(solution)/shard_map/ppermute | solution.py:516
  504.8 10.1 %attention_backward.6 = (bf16[256,512]{1,0:T(8,128)(2,1)S(1)}, f32[1024,512]{1,0:T(8,128)S(1)}, f32[1024,512]{1,0:T(8,128)}) custom-call(bf16[256,1536]{1,0:T(8,128)(2,1)S(1)} %copy-done.6, bf16[1024,1024]{1,0:T(8,128)(2,1)} %copy-done, bf16[1024,1024]{1,0:T(8,128)(2,1)} %copy-done, bf16[256,512]{1,0:T(8,128)(2,1)S(1)} %convolution_convert_fusion.13.g_ref, ...), custom_call_target="tpu_custom_call" | custom-call | flops 2684354560 | bytes 5242880 | tf_op jit(solution)/shard_map/attention_backward/pallas_call | solution.py:981
  517.4 10.8 %attention_backward.7 = (bf16[256,512]{1,0:T(8,128)(2,1)S(1)}, f32[1024,512]{1,0:T(8,128)S(1)}, f32[1024,512]{1,0:T(8,128)}) custom-call(bf16[256,1536]{1,0:T(8,128)(2,1)S(1)} %convolution_convert_fusion.4.q_ref, bf16[1024,1024]{1,0:T(8,128)(2,1)} %copy-done, bf16[1024,1024]{1,0:T(8,128)(2,1)} %copy-done, ...), custom_call_target="tpu_custom_call" | custom-call | flops 2684354560 | bytes 5242880 | tf_op jit(solution)/shard_map/attention_backward/pallas_call | solution.py:981
  561.2 10.7 %collective-permute-done.25 = bf16[256,1024]{1,0:T(8,128)(2,1)S(1)} collective-permute-done((bf16[256,1024]{1,0:T(8,128)(2,1)S(1)}, bf16[256,1024]{1,0:T(8,128)(2,1)S(1)}, u32[]{:S(2)}, u32[]{:S(2)}) %collective-permute-start.25) | collective-permute-done | bytes 524320 | tf_op jit(solution)/shard_map/ppermute | solution.py:516
  583.1 12.5 %all-to-all-done.1 = bf16[8,512,128]{2,1,0:T(8,128)(2,1)S(1)} async-done(((bf16[8,512,128]{2,1,0:T(8,128)(2,1)}), bf16[8,512,128]{2,1,0:T(8,128)(2,1)S(1)}, u32[]{:S(2)}, u32[]{:S(2)}) %all-to-all-start.1) | async-done | bytes 1048608 | tf_op jit(solution)/shard_map/all_to_all | solution.py:1356
  628.3 32.1 %collective-permute-done.31 = bf16[2,4,272,128]{3,2,1,0:T(8,128)(2,1)} collective-permute-done((bf16[2,4,272,128]{3,2,1,0:T(8,128)(2,1)}, bf16[2,4,272,128]{3,2,1,0:T(8,128)(2,1)}, u32[]{:S(2)}, u32[]{:S(2)}) %collective-permute-start.31) | collective-permute-done | bytes 557088 | tf_op jit(solution)/shard_map/ppermute | solution.py:550
  660.4 14.8 %collective-permute-done.29 = bf16[2,4,272,128]{3,2,1,0:T(8,128)(2,1)} collective-permute-done((bf16[2,4,272,128]{3,2,1,0:T(8,128)(2,1)S(1)}, bf16[2,4,272,128]{3,2,1,0:T(8,128)(2,1)}, u32[]{:S(2)}, u32[]{:S(2)}) %collective-permute-start.29) | collective-permute-done | bytes 557088 | tf_op jit(solution)/shard_map/ppermute | solution.py:550
  707.5 16.0 %collective-permute-done.33 = bf16[2,4,272,128]{3,2,1,0:T(8,128)(2,1)S(1)} collective-permute-done((bf16[2,4,272,128]{3,2,1,0:T(8,128)(2,1)S(1)}, bf16[2,4,272,128]{3,2,1,0:T(8,128)(2,1)S(1)}, u32[]{:S(2)}, u32[]{:S(2)}) %collective-permute-start.33) | collective-permute-done | bytes 557088 | tf_op jit(solution)/shard_map/ppermute | solution.py:550
  724.5 7.5 all-to-all-start.3
  (791 shorter events, 458.2 us)
Async XLA Ops:
  7.2 267.4 %all-gather.2.cloned.1.call-start = ((), (), s32[]{:S(2)}) async-start(), calls=%async_computation.7 | async-start | bytes 13926400 | tf_op jit(solution)/shard_map/all_gather | solution.py:564
  175.9 21.9 %all-to-all-start = ((bf16[8,512,128]{2,1,0:T(8,128)(2,1)}), bf16[8,512,128]{2,1,0:T(8,128)(2,1)S(1)}, u32[]{:S(2)}, u32[]{:S(2)}) async-start(bf16[8,512,128]{2,1,0:T(8,128)(2,1)} %bitcast.29), calls=%async_computation | async-start | bytes 2097152 | tf_op jit(solution)/shard_map/all_to_all | solution.py:1206
  183.0 345.9 %reduce-scatter.4.cloned.1.call-start = ((), (), s32[]{:S(2)}) async-start(), calls=%async_computation.8 | async-start | bytes 9191424 | tf_op jit(solution)/shard_map/reduce_scatter | solution.py:570
  183.9 36.3 %collective-permute-start = (bf16[256,1024]{1,0:T(8,128)(2,1)}, bf16[256,1024]{1,0:T(8,128)(2,1)}, u32[]{:S(2)}, u32[]{:S(2)}) collective-permute-start(bf16[256,1024]{1,0:T(8,128)(2,1)} %select_bitcast_fusion.2), channel_id=1, source_target_pairs={{0,0},{1,1},{2,16},{3,17},{16,2},{17,3},{18,18},{19,19},{4,4},{5,5... | collective-permute-start | bytes 1572872 | tf_op jit(solution)/shard_map/ppermute | solution.py:1189
  220.2 82.0 %collective-permute-start.1 = (bf16[256,1024]{1,0:T(8,128)(2,1)}, bf16[256,1024]{1,0:T(8,128)(2,1)}, u32[]{:S(2)}, u32[]{:S(2)}) collective-permute-start(bf16[256,1024]{1,0:T(8,128)(2,1)} %collective-permute-done), channel_id=1, source_target_pairs={{0,1},{1,0},{2,3},{3,2},{4,5},{5,4},{6,7},{7,6},{8,9},{9,8},{10,11... | collective-permute-start | bytes 1572872 | tf_op jit(solution)/shard_map/ppermute | solution.py:516
  227.9 27.3 %collective-permute-start.8 = (bf16[256,1024]{1,0:T(8,128)(2,1)S(1)}, bf16[256,1024]{1,0:T(8,128)(2,1)S(1)}, u32[]{:S(2)}, u32[]{:S(2)}) collective-permute-start(bf16[256,1024]{1,0:T(8,128)(2,1)S(1)} %convolution_convert_fusion.10), channel_id=1, source_target_pairs={{0,1},{1,0},{2,3},{3,2},{4,5},{5,4},{6,7},{7,6},{8,9},{9,8},{10,11... | collective-permute-start | bytes 1572872 | tf_op jit(solution)/shard_map/ppermute | solution.py:516
  323.3 19.2 %collective-permute-start.14 = (bf16[256,1024]{1,0:T(8,128)(2,1)S(1)}, bf16[256,1024]{1,0:T(8,128)(2,1)S(1)}, u32[]{:S(2)}, u32[]{:S(2)}) collective-permute-start(bf16[256,1024]{1,0:T(8,128)(2,1)S(1)} %convolution_convert_fusion.8), channel_id=1, source_target_pairs={{0,1},{1,0},{2,3},{3,2},{4,5},{5,4},{6,7},{7,6},{8,9},{9,8},{10,11... | collective-permute-start | bytes 1572872 | tf_op jit(solution)/shard_map/ppermute | solution.py:516
  377.3 384.4 %reduce-scatter.6.cloned.1.call-start = ((), (), s32[]{:S(2)}) async-start(), calls=%async_computation.9 | async-start | bytes 13647872 | tf_op jit(solution)/shard_map/reduce_scatter | solution.py:570
  384.2 25.2 %collective-permute-start.16 = (bf16[256,1024]{1,0:T(8,128)(2,1)S(1)}, bf16[256,1024]{1,0:T(8,128)(2,1)S(1)}, u32[]{:S(2)}, u32[]{:S(2)}) collective-permute-start(bf16[256,1024]{1,0:T(8,128)(2,1)S(1)} %copy-done.134), channel_id=1, source_target_pairs={{0,1},{1,0},{2,3},{3,2},{4,5},{5,4},{6,7},{7,6},{8,9},{9,8},{10,11... | collective-permute-start | bytes 1572872 | tf_op jit(solution)/shard_map/ppermute | solution.py:516
  384.6 26.1 %collective-permute-start.17 = (bf16[256,1024]{1,0:T(8,128)(2,1)S(1)}, bf16[256,1024]{1,0:T(8,128)(2,1)S(1)}, u32[]{:S(2)}, u32[]{:S(2)}) collective-permute-start(bf16[256,1024]{1,0:T(8,128)(2,1)S(1)} %copy-done.137), channel_id=1, source_target_pairs={{0,1},{1,0},{2,3},{3,2},{4,5},{5,4},{6,7},{7,6},{8,9},{9,8},{10,11... | collective-permute-start | bytes 1572872 | tf_op jit(solution)/shard_map/ppermute | solution.py:516
  433.8 21.7 %collective-permute-start.20 = (bf16[256,1024]{1,0:T(8,128)(2,1)S(1)}, bf16[256,1024]{1,0:T(8,128)(2,1)S(1)}, u32[]{:S(2)}, u32[]{:S(2)}) collective-permute-start(bf16[256,1024]{1,0:T(8,128)(2,1)S(1)} %fusion.110), channel_id=1, source_target_pairs={{0,1},{1,0},{2,3},{3,2},{4,5},{5,4},{6,7},{7,6},{8,9},{9,8},{10,11... | collective-permute-start | bytes 1572872 | tf_op jit(solution)/shard_map/ppermute | solution.py:516
  470.5 18.9 %collective-permute-start.21 = (bf16[256,1024]{1,0:T(8,128)(2,1)}, bf16[256,1024]{1,0:T(8,128)(2,1)}, u32[]{:S(2)}, u32[]{:S(2)}) collective-permute-start(bf16[256,1024]{1,0:T(8,128)(2,1)} %fusion.149), channel_id=1, source_target_pairs={{0,1},{1,0},{2,3},{3,2},{4,5},{5,4},{6,7},{7,6},{8,9},{9,8},{10,11... | collective-permute-start | bytes 1572872 | tf_op jit(solution)/shard_map/ppermute | solution.py:516
  475.3 19.5 %collective-permute-start.22 = (bf16[256,1024]{1,0:T(8,128)(2,1)}, bf16[256,1024]{1,0:T(8,128)(2,1)S(1)}, u32[]{:S(2)}, u32[]{:S(2)}) collective-permute-start(bf16[256,1024]{1,0:T(8,128)(2,1)} %fusion.158), channel_id=1, source_target_pairs={{0,1},{1,0},{2,3},{3,2},{4,5},{5,4},{6,7},{7,6},{8,9},{9,8},{10,11... | collective-permute-start | bytes 1572872 | tf_op jit(solution)/shard_map/ppermute | solution.py:516
  549.8 22.0 %collective-permute-start.25 = (bf16[256,1024]{1,0:T(8,128)(2,1)S(1)}, bf16[256,1024]{1,0:T(8,128)(2,1)S(1)}, u32[]{:S(2)}, u32[]{:S(2)}) collective-permute-start(bf16[256,1024]{1,0:T(8,128)(2,1)S(1)} %fusion.104), channel_id=1, source_target_pairs={{0,1},{1,0},{2,3},{3,2},{4,5},{5,4},{6,7},{7,6},{8,9},{9,8},{10,11... | collective-permute-start | bytes 1572872 | tf_op jit(solution)/shard_map/ppermute | solution.py:516
  574.7 20.9 %all-to-all-start.1 = ((bf16[8,512,128]{2,1,0:T(8,128)(2,1)}), bf16[8,512,128]{2,1,0:T(8,128)(2,1)S(1)}, u32[]{:S(2)}, u32[]{:S(2)}) async-start(bf16[8,512,128]{2,1,0:T(8,128)(2,1)} %bitcast_bitcast_fusion), calls=%async_computation.2 | async-start | bytes 2097152 | tf_op jit(solution)/shard_map/all_to_all | solution.py:1356
  578.7 183.1 %reduce-scatter.8.cloned.1.call-start = ((), (), s32[]{:S(2)}) async-start(), calls=%async_computation.10 | async-start | bytes 4734976 | tf_op jit(solution)/shard_map/reduce_scatter | solution.py:570
  622.4 58.4 %collective-permute-start.26 = (f32[256,1024]{1,0:T(8,128)}, f32[256,1024]{1,0:T(8,128)}, u32[]{:S(2)}, u32[]{:S(2)}) collective-permute-start(f32[256,1024]{1,0:T(8,128)} %broadcast_select_fusion.8), channel_id=1, source_target_pairs={{0,0},{1,1},{2,16},{3,17},{16,2},{17,3},{18,18},{19,19},{4,4},{5,5... | collective-permute-start | bytes 3145736 | tf_op jit(solution)/shard_map/ppermute | solution.py:1394
  624.4 36.1 %collective-permute-start.31 = (bf16[2,4,272,128]{3,2,1,0:T(8,128)(2,1)}, bf16[2,4,272,128]{3,2,1,0:T(8,128)(2,1)}, u32[]{:S(2)}, u32[]{:S(2)}) collective-permute-start(bf16[2,4,272,128]{3,2,1,0:T(8,128)(2,1)} %get-tuple-element.207), channel_id=1, source_target_pairs={{12,8},{13,9},{14,10},{15,11},{28,24},{29,25},{30,26},{31,27}} | collective-permute-start | bytes 1671176 | tf_op jit(solution)/shard_map/ppermute | solution.py:550
  626.9 48.3 %collective-permute-start.29 = (bf16[2,4,272,128]{3,2,1,0:T(8,128)(2,1)S(1)}, bf16[2,4,272,128]{3,2,1,0:T(8,128)(2,1)}, u32[]{:S(2)}, u32[]{:S(2)}) collective-permute-start(bf16[2,4,272,128]{3,2,1,0:T(8,128)(2,1)S(1)} %fusion.177), channel_id=1, source_target_pairs={{0,4},{4,8},{1,5},{5,9},{2,6},{6,10},{3,7},{7,11},{16,20},{20,24},... | collective-permute-start | bytes 1671176 | tf_op jit(solution)/shard_map/ppermute | solution.py:550
  680.9 66.3 %collective-permute-start.27 = (f32[256,1024]{1,0:T(8,128)}, f32[256,1024]{1,0:T(8,128)}, u32[]{:S(2)}, u32[]{:S(2)}) collective-permute-start(f32[256,1024]{1,0:T(8,128)} %collective-permute-done.26), channel_id=1, source_target_pairs={{0,16},{16,0},{1,17},{17,1},{2,18},{18,2},{3,19},{19,3},{4,20},{20... | collective-permute-start | bytes 3145736 | tf_op jit(solution)/shard_map/ppermute | solution.py:512
  684.9 22.6 %collective-permute-start.30 = (bf16[2,4,272,128]{3,2,1,0:T(8,128)(2,1)S(1)}, bf16[2,4,272,128]{3,2,1,0:T(8,128)(2,1)S(1)}, u32[]{:S(2)}, u32[]{:S(2)}) collective-permute-start(bf16[2,4,272,128]{3,2,1,0:T(8,128)(2,1)S(1)} %copy-done.120), channel_id=1, source_target_pairs={{0,4},{4,8},{8,12},{1,5},{5,9},{9,13},{2,6},{6,10},{10,14},{3,7},{... | collective-permute-start | bytes 1671176 | tf_op jit(solution)/shard_map/ppermute | solution.py:550
  694.3 29.2 %collective-permute-start.33 = (bf16[2,4,272,128]{3,2,1,0:T(8,128)(2,1)S(1)}, bf16[2,4,272,128]{3,2,1,0:T(8,128)(2,1)S(1)}, u32[]{:S(2)}, u32[]{:S(2)}) collective-permute-start(bf16[2,4,272,128]{3,2,1,0:T(8,128)(2,1)S(1)} %fusion.176), channel_id=1, source_target_pairs={{4,0},{8,4},{12,8},{5,1},{9,5},{13,9},{6,2},{10,6},{14,10},{7,3},{... | collective-permute-start | bytes 1671176 | tf_op jit(solution)/shard_map/ppermute | solution.py:550
  724.5 18.9 %all-to-all-start.3 = ((bf16[8,272,128]{2,1,0:T(8,128)(2,1)}), bf16[8,272,128]{2,1,0:T(8,128)(2,1)}, u32[]{:S(2)}, u32[]{:S(2)}) async-start(bf16[8,272,128]{2,1,0:T(8,128)(2,1)} %bitcast.69), calls=%async_computation.5 | async-start | bytes 1114112 | tf_op jit(solution)/shard_map/all_to_all | solution.py:1381
  765.7 20.1 %collective-permute-start.36 = (bf16[64,4096]{1,0:T(8,128)(2,1)}, bf16[64,4096]{1,0:T(8,128)(2,1)}, u32[]{:S(2)}, u32[]{:S(2)}) collective-permute-start(bf16[64,4096]{1,0:T(8,128)(2,1)} %broadcast_select_fusion.5), channel_id=1, source_target_pairs={{0,16},{16,0},{1,17},{17,1},{2,18},{18,2},{3,19},{19,3},{4,20},{20... | collective-permute-start | bytes 1572872 | tf_op jit(solution)/shard_map/ppermute | solution.py:512
  (212 other events, 1959.4 us)
Sparse Core Ops, SparseCore 0:
  140.9 133.5 all-gather.1
  377.5 116.6 reduce-scatter.3
  498.2 164.0 reduce-scatter.5
  666.0 84.0 reduce-scatter.7

commit v5 on v4

--- a/solution.py
+++ b/solution.py
@@ -531,25 +531,27 @@
     return jnp.where(flag, first, second), jnp.where(flag, second, first)
 
 
-def sum_dp(blocks, dp):
+def sum_dp(blocks, dp, meanwhile):
     count = lax.axis_size("dp")
     f32, bf16 = jnp.float32, jnp.bfloat16
+    meanwhile = list(meanwhile)
 
     def block(index):
         return lax.dynamic_index_in_dim(blocks, jnp.clip(index, 0, count - 1), 0, keepdims=False)
 
-    total = block(dp).astype(f32)
-    for sign in (1, -1):
-        pairs = [(i, i + sign) for i in range(count) if 0 <= i + sign < count]
-        running = None
-        for distance in range(count - 1, 0, -1):
+    running = [None, None]
+    for turn, distance in enumerate(range(count - 1, 0, -1)):
+        for way, sign in enumerate((1, -1)):
             own = block(dp + sign * distance)
-            if running is not None:
-                own = (own.astype(f32) + running.astype(f32)).astype(bf16)
-            live = [(a, b) for a, b in pairs if 0 <= a + sign * distance < count]
-            running = lax.ppermute(own, "dp", live)
-        total = total + running.astype(f32)
-    return total.astype(bf16)
+            if running[way] is not None:
+                own = (own.astype(f32) + running[way].astype(f32)).astype(bf16)
+            live = [(i, i + sign) for i in range(count) if 0 <= i + sign < count and 0 <= i + sign * distance < count]
+            running[way] = lax.ppermute(own, "dp", live)
+        if turn < len(meanwhile):
+            running, meanwhile[turn] = after(running, meanwhile[turn])
+            running = list(running)
+    total = block(dp).astype(f32) + running[0].astype(f32) + running[1].astype(f32)
+    return total.astype(bf16), meanwhile
 
 
 def line_groups():
@@ -577,8 +579,9 @@
 
 
 def opening_kernel(
-    dp_count, parts, conv_ref, signal_ref, keep_ref, send_ref, rest_ref, conv_out, signal_out, whole_out,
-    local_sem, a2a_send, a2a_recv, sig_send, sig_recv, line_send, line_recv, own_send, own_recv,
+    dp_count, parts, conv_ref, signal_ref, keep_ref, send_ref, rest_ref,
+    conv_out, signal_out, whole_out, second_out,
+    local_sem, a2a_send, a2a_recv, sig_send, sig_recv, line_send, line_recv, own_send, column_recv, rest_recv,
     up_send, up_recv, y_send, y_recv, core_send, core_recv,
 ):
     sec, dp, seq = (lax.axis_index(name) for name in ("section", "dp", "seq"))
@@ -630,37 +633,92 @@
     conv_local.start()
     signal_local.start()
 
-    def columns(half):
-        return whole_out.at[dp, y, half, :, pl.ds(0, split)]
-
-    def others(half):
-        return whole_out.at[dp, y, half, :, pl.ds(split, rest_ref.shape[2])]
-
-    keep_local = pltpu.make_async_copy(keep_ref, columns(0), local_sem.at[2])
-    rest_local = pltpu.make_async_copy(rest_ref.at[0], others(0), local_sem.at[3])
-    keep_far = remote(keep_ref, columns(1), own_send.at[0], own_recv.at[0], {"section": 1})
-    send_same = remote(send_ref, columns(0), own_send.at[1], own_recv.at[0], {"seq": partner_x})
-    send_cross = remote(
-        send_ref, columns(1), own_send.at[1], own_recv.at[0], {"section": 1, "seq": partner_x}
-    )
-    rest_far = remote(rest_ref.at[1], others(1), own_send.at[2], own_recv.at[1], {"section": 1})
-    first, second = sec == 0, sec == 1
-
-    @pl.when(first & (x == 0))
-    def _():
-        send_same.start()
-        keep_local.start()
-
-    @pl.when(first & (x == 1))
-    def _():
-        send_cross.start()
-        keep_far.start()
-
-    @pl.when(first)
-    def _():
-        rest_far.start()
-        rest_local.start()
-
+    def columns(layer, half):
+        return (second_out if layer else whole_out.at[dp, y, half]).at[:, pl.ds(0, split)]
+
+    def others(layer, half):
+        return (second_out if layer else whole_out.at[dp, y, half]).at[:, pl.ds(split, rest_ref.shape[2])]
+
+    class Layer:
+        def __init__(self, layer):
+            far = {"section": 1 - layer}
+            self.mine = sec == layer
+            self.even = x == layer
+            received = column_recv.at[layer]
+            self.keep_local = pltpu.make_async_copy(keep_ref, columns(layer, layer), local_sem.at[2])
+            self.rest_local = pltpu.make_async_copy(rest_ref.at[layer], others(layer, layer), local_sem.at[3])
+            self.keep_far = remote(keep_ref, columns(layer, 1 - layer), own_send.at[0], received, far)
+            self.send_same = remote(
+                send_ref, columns(layer, layer), own_send.at[1], received, {"seq": partner_x}
+            )
+            self.send_cross = remote(
+                send_ref, columns(layer, 1 - layer), own_send.at[1], received, {**far, "seq": partner_x}
+            )
+            self.rest_far = remote(
+                rest_ref.at[1 - layer], others(layer, 1 - layer), own_send.at[2], rest_recv.at[layer], far
+            )
+
+        def start(self):
+            @pl.when(self.mine & self.even)
+            def _():
+                self.send_same.start()
+                self.keep_local.start()
+
+            @pl.when(self.mine & jnp.logical_not(self.even))
+            def _():
+                self.send_cross.start()
+                self.keep_far.start()
+
+            @pl.when(self.mine)
+            def _():
+                self.rest_far.start()
+                self.rest_local.start()
+
+        def wait(self):
+            other = jnp.logical_not(self.mine)
+            odd = jnp.logical_not(self.even)
+
+            @pl.when(self.mine & self.even)
+            def _():
+                self.keep_local.wait()
+
+            @pl.when(self.mine & odd)
+            def _():
+                self.send_same.wait_recv()
+
+            @pl.when(self.mine)
+            def _():
+                self.rest_local.wait()
+
+            @pl.when(other & self.even)
+            def _():
+                self.send_cross.wait_recv()
+
+            @pl.when(other & odd)
+            def _():
+                self.keep_far.wait_recv()
+
+            @pl.when(other)
+            def _():
+                self.rest_far.wait_recv()
+
+        def finish(self):
+            @pl.when(self.mine & self.even)
+            def _():
+                self.send_same.wait_send()
+
+            @pl.when(self.mine & jnp.logical_not(self.even))
+            def _():
+                self.send_cross.wait_send()
+                self.keep_far.wait_send()
+
+            @pl.when(self.mine)
+            def _():
+                self.rest_far.wait_send()
+
+    layers = [Layer(0), Layer(1)]
+    for layer in layers:
+        layer.start()
     for turn in range(1, 4):
         sig((seq + turn) % 4, seq).start()
 
@@ -700,30 +758,7 @@
         def _(direction=direction):
             line(dp, direction).start()
 
-    @pl.when(first & (x == 0))
-    def _():
-        keep_local.wait()
-
-    @pl.when(first & (x == 1))
-    def _():
-        send_same.wait_recv()
-
-    @pl.when(first)
-    def _():
-        rest_local.wait()
-
-    @pl.when(second & (x == 0))
-    def _():
-        send_cross.wait_recv()
-
-    @pl.when(second & (x == 1))
-    def _():
-        keep_far.wait_recv()
-
-    @pl.when(second)
-    def _():
-        rest_far.wait_recv()
-
+    layers[0].wait()
     for part in range(parts):
         for there, direction in ((has_up, 1), (has_down, -1)):
 
@@ -796,19 +831,9 @@
                 for part in range(parts):
                     along(slot, direction, part).wait_send()
 
-    @pl.when(first & (x == 0))
-    def _():
-        send_same.wait_send()
-
-    @pl.when(first & (x == 1))
-    def _():
-        send_cross.wait_send()
-        keep_far.wait_send()
-
-    @pl.when(first)
-    def _():
-        rest_far.wait_send()
-
+    layers[1].wait()
+    for layer in layers:
+        layer.finish()
     for turn in range(1, 8):
         a2a((me + turn) % 8, me).wait_send()
     for turn in range(1, 4):
@@ -823,18 +848,19 @@
     rows, columns = keep.shape[0], keep.shape[1] + rest.shape[2]
     anywhere = pl.BlockSpec(memory_space=pl.ANY)
     dma = pltpu.SemaphoreType.DMA
-    conv_all, signal_all, whole = pl.pallas_call(
+    conv_all, signal_all, whole, second = pl.pallas_call(
         functools.partial(opening_kernel, count, parts),
         in_specs=[anywhere] * 5,
-        out_specs=[anywhere] * 3,
+        out_specs=[anywhere] * 4,
         out_shape=[
             jax.ShapeDtypeStruct((count, *conv_send.shape), conv_send.dtype),
             jax.ShapeDtypeStruct(signal_send.shape, signal_send.dtype),
             jax.ShapeDtypeStruct((count, 2, 2, rows, columns), keep.dtype),
+            jax.ShapeDtypeStruct((rows, columns), keep.dtype),
         ],
         scratch_shapes=[
             dma((4,)), dma((8,)), dma((8,)), dma((4,)), dma((4,)), dma((2, count)), dma((count,)),
-            dma((3,)), dma((2,)), dma((2, count, parts)), dma((count, parts)), dma((count, parts)),
+            dma((3,)), dma((2,)), dma((2,)), dma((2, count, parts)), dma((count, parts)), dma((count, parts)),
             dma((count, parts)), dma((count, 2, parts)), dma((count, 2, parts)),
         ],
         compiler_params=pltpu.CompilerParams(
@@ -842,7 +868,7 @@
         ),
         name="opening",
     )(conv_send, signal_send, keep, send, rest)
-    return conv_all, signal_all, whole.reshape(-1, columns)
+    return conv_all, signal_all, whole.reshape(-1, columns), second
 
 
 def norm_stats(values):
@@ -1156,12 +1182,7 @@
     two_at = up_at + up_cols
     out_at = two_at + 128
     down_at = out_at + width // 2
-    conv_all, sig_got, whole = opening(conv_send, sig_send, keep_cols, send_cols, rest)
-    whole, (keep_cols, send_cols) = after(whole, (keep_cols, send_cols))
-    row_sets = choose(x0, keep_cols, swap_x(send_cols))
-    row_parts = [jnp.concatenate([row_sets[h], rest[h]], axis=1) for h in range(2)]
-    keep, send = choose(sec0, *row_parts)
-    _, second_piece = choose(sec0, keep, swap_section(send))
+    conv_all, sig_got, whole, second_piece = opening(conv_send, sig_send, keep_cols, send_cols, rest)
     gathered = [whole, gather_rows(second_piece)]
     sig_all = jnp.transpose(sig_got, (1, 0, 2, 3)).reshape(micro_count, row_frames, block_width)
     conv_all = conv_all.reshape(dp_count, 2, 4, rows_here + 16, block_width)
@@ -1299,7 +1320,7 @@
             ff_members.append(jnp.zeros((width, 128), bf16))
         partial = jnp.concatenate(attn_members + ff_members, axis=1)
         if layer == 0:
-            sums, partial = after(sums, partial)
+            sums, (partial, output_rows) = after(sums, (partial, output_rows))
         scattered.append(scatter_rows(partial))
         resid_grad, attn_branch, dq, gain_two_grad = [], [], [], None
         dkv = None
@@ -1312,6 +1333,8 @@
             if layer == 1 and c == 0:
                 attended_grad, lows = after(attended_grad, lows)
                 output = [member + pair_sum(low) for member, low in zip(resid_two_last, lows)]
+                row_block = lax.ppermute(jnp.where(x0, output[0], output[1]), both, across)
+                output_rows = jnp.stack(choose(sec0, row_block, swap_section(row_block)))
             own_dq, *dkv = attention_backward(
                 packed[c], kv_all, attended_grad, attended[c], lse[c], chunk_segs[c], key_segs, factor,
                 None if c == 0 else dkv,
@@ -1350,7 +1373,6 @@
         grad_out = [member.astype(f32) for member in next_grad]
     grad_in_low = jnp.concatenate(next_grad)
     scattered.append(scatter_rows(jnp.concatenate(attn_members, axis=1)))
-    output = jnp.concatenate(output)
 
     lig_send = jnp.transpose(grad_in_low.reshape(half_frames, 8, block_width), (1, 0, 2))
     lig_got = lax.all_to_all(lig_send, both, 0, 0, tiled=True).reshape(2, 2, 2, half_frames, block_width)
@@ -1363,10 +1385,6 @@
         grad_signal.reshape(micro_count, 4, frames, block_width), (1, 0, 2, 3)
     )
     gs_send = jnp.concatenate([gs_send, gs_send], axis=0)
-    gs_got = lax.all_to_all(gs_send, both, 0, 0, tiled=True)
-    gs_got, scattered[1] = after(gs_got, scattered[1])
-    gs_rows = jnp.transpose(gs_got, (1, 2, 0, 3)).reshape(micro_count, frames, width).astype(f32)
-
     taps_grad = conv_taps_grad(sig_views, grad_views, per_group)
     bias_grad = jnp.sum(conv_grad.astype(f32), axis=(0, 1))
     taps_view = jnp.transpose(
@@ -1377,10 +1395,24 @@
         ((0, 0), (0, 0), (0, 0), (0, 15), (0, 0)),
     )
     taps_send = jnp.concatenate([taps_view, bias_view], axis=3)
-    taps_sum = sum_dp(taps_send, dp)
+    gs_got = lax.all_to_all(gs_send, both, 0, 0, tiled=True)
+    attn_cols = cut + width // 2
+
+    def over_section(first, second):
+        keep, send = choose(sec0, first, second)
+        return choose(sec0, keep, swap_section(send))
+
+    def over_x(first, second):
+        keep, send = choose(x0, first, second)
+        return keep, choose(x0, keep, swap_x(send))
+
+    taps_sum, (_, gs_got) = sum_dp(taps_send, dp, (gs_send, gs_got))
+    gs_rows = jnp.transpose(gs_got, (1, 2, 0, 3)).reshape(micro_count, frames, width).astype(f32)
+    ends = jnp.where(sec0, gs_rows, output_rows)[None]
     taps_got = lax.all_to_all(
         taps_sum.reshape(8, rows_here + 16, block_width), both, 0, 0, tiled=True
     )
+    taps_got, scattered[1] = after(taps_got, scattered[1])
     conv_weight_grad = jnp.transpose(taps_got[:, :rows_here], (1, 0, 2)).reshape(rows_here, width).astype(f32)
     bias_count = conv_bias.shape[0]
     conv_bias_grad = lax.dynamic_slice_in_dim(
@@ -1390,43 +1422,27 @@
         0,
     ).astype(f32)
 
-    own_block = jnp.where(x0, output[:frames], output[frames:])
-    row_block = lax.ppermute(own_block, both, across)
-    other_row = swap_section(row_block)
-    output_rows = jnp.stack(choose(sec0, row_block, other_row))
-    ends = jnp.where(sec0, gs_rows, output_rows)[None]
-
-    attn_cols = cut + width // 2
-    attn_sums = (scattered[2], scattered[1][:, :attn_cols])
-    ff_sums = (scattered[1][:, attn_cols:], scattered[0][:, :-128])
-    half_sets = []
-    for sums in (attn_sums, ff_sums):
-        keep, send = choose(sec0, *sums)
-        half_sets.append(choose(sec0, keep, swap_section(send)))
-    attn_sets, ff_sets = half_sets
-    out_grad = jnp.concatenate([member[:, cut:attn_cols] for member in attn_sets], axis=1).astype(f32)[None]
+    ff_sets = over_section(scattered[1][:, attn_cols:], scattered[0][:, :-128])
     down_grad = jnp.concatenate(
         [member[:, up_cols + at : up_cols + at + width] for member in ff_sets for at in (0, width)],
         axis=0,
     ).astype(f32)[None]
-
-    def finish_columns(first, second, gains):
-        keep, send = choose(x0, first, second)
-        return keep[:, : keep.shape[1] - gains], keep[:, keep.shape[1] - gains :], choose(x0, keep, swap_x(send))
-
-    qkv_own, gain_own, qkv_sets = finish_columns(attn_sets[0][:, :cut], attn_sets[1][:, :cut], 128)
-    _, _, up_sets = finish_columns(ff_sets[0][:, :up_cols], ff_sets[1][:, :up_cols], 0)
-    norm1_grad = gain_own[:, 0].astype(f32)[None]
-    norm2_grad = gain_own[:, 1].astype(f32)[None]
-    qkv_grad = jnp.stack(
-        [member[:, :qkv_cols].reshape(in_rows, -1, HEAD_DIM) for member in qkv_sets], axis=2
-    ).reshape(in_rows, -1).astype(f32)[None]
+    _, up_sets = over_x(*(member[:, :up_cols] for member in ff_sets))
     up_grad = jnp.stack(
         [
             jnp.transpose(member.reshape(in_rows, 2, -1, 2, unit), (0, 2, 3, 1, 4))
             for member in up_sets
         ],
         axis=2,
+    ).reshape(in_rows, -1).astype(f32)[None]
+
+    attn_sets = over_section(scattered[2], scattered[1][:, :attn_cols])
+    out_grad = jnp.concatenate([member[:, cut:attn_cols] for member in attn_sets], axis=1).astype(f32)[None]
+    keep, qkv_sets = over_x(*(member[:, :cut] for member in attn_sets))
+    norm1_grad = keep[:, qkv_cols].astype(f32)[None]
+    norm2_grad = keep[:, qkv_cols + 1].astype(f32)[None]
+    qkv_grad = jnp.stack(
+        [member[:, :qkv_cols].reshape(in_rows, -1, HEAD_DIM) for member in qkv_sets], axis=2
     ).reshape(in_rows, -1).astype(f32)[None]
     return (ends, conv_weight_grad, conv_bias_grad, norm1_grad, qkv_grad, out_grad, norm2_grad, up_grad, down_grad)
 

time: 820 us -> 768 us (0.937)
  waiting for transfers between devices: 201 us -> 145 us
  starting transfers between devices: 72 us -> 84 us
  other arithmetic: 107 us -> 97.6 us
    ppermute x7, waiting for transfers between devices: 73.5 us -> 41.1 us  [the longest x6 40.9 us: sum_dp(): running[way] = lax.ppermute(own, 'dp', live)]
    ppermute x20 -> x19, waiting for transfers between devices: 87.3 us -> 63.2 us  [swap_x(): return lax.ppermute(value, 'seq', [(q, q ^ 1) for q in range(4)])]
    unnamed x392 -> x372, local copies, waits for them, and re-layouts: 26.8 us -> 33.1 us
    ppermute x10 -> x9, starting transfers between devices: 14 us -> 17.8 us  [swap_section(): return lax.ppermute(value, 'section', [(0, 1), (1, 0)])]
    ppermute x20 -> x19, starting transfers between devices: 17.6 us -> 14 us  [swap_x(): return lax.ppermute(value, 'seq', [(q, q ^ 1) for q in range(4)])]
  transfers between devices with their start and end apart: 46 -> 44, of which waited for: 26 -> 24; matrix products, arithmetic and copies ran while one was open for 35% -> 36% of each run, Pallas kernels for 8% -> 8%
where the time goes in v5:
time: 768 us; the launch traced here: 754 us
  Pallas kernels  168 us (22%)
  matrix products  151 us (20%)
  waiting for transfers between devices  145 us (19%)
  other arithmetic  97.6 us (13%)
  local copies, waits for them, and re-layouts  91.7 us (12%)
  starting transfers between devices  84 us (11%)
  between operations  17.4 us (2%)
    pallas_call x1, Pallas kernels, opening(): pl.pallas_call(functools.partial(opening_kernel, count, parts), in_specs=...  99.8 us
    ppermute x19, waiting for transfers between devices, swap_x(): return lax.ppermute(value, 'seq', [(q, q ^ 1) for q in range(4)])  63.2 us
    pallas_call x4, Pallas kernels, attention_backward(): pl.pallas_call(functools.partial(attention_backward_kernel, factor), grid...  41.3 us
    ppermute x6, waiting for transfers between devices, sum_dp(): running[way] = lax.ppermute(own, 'dp', live)  40.9 us
    dot_general x12, matrix products, outer(): lax.dot_general(left, right, (((0,), (0,)), ((), ())), preferred_element_...  35.7 us
    unnamed x372, local copies, waits for them, and re-layouts  33.1 us
    dot_general x8, matrix products, per_device_pairs(): hidden_pre = jnp.dot(normed_two[c], w_up[part], preferred_element_type=f32)  31.7 us
    dot_general x24, matrix products, back(): lax.dot_general(left, right, (((1,), (1,)), ((), ())), preferred_element_...  28.1 us
  transfers between devices with their start and end apart: 44, of which 24 were waited for; matrix products, arithmetic and copies ran while one was open for 36% of the time, Pallas kernels for 8%

profile of v5, /device:TPU:17, one launch (start us, length us, event | category | flops | bytes accessed | tf_op | source)
XLA Modules:
  0.0 754.4 jit_solution(17686999814893746877)
XLA Ops:
  22.4 99.8 %opening.1 = (bf16[4,8,272,128]{3,2,1,0:T(8,128)(2,1)S(1)}, bf16[4,2,256,128]{3,2,1,0:T(8,128)(2,1)S(1)}, bf16[4,2,2,64,6400]{4,3,2,1,0:T(8,128)(2,1)S(1)}, bf16[64,6400]{1,0:T(8,128)(2,1)S(1)}) custom-call(bf16[8,272,128]{2,1,0:T(8,128)(2,1)S(1)} %fusion.403.conv_ref, bf16[4,2,256,128]{3,2,1,0:T(8,128)(2,1)S(1)} %bitcast.291, ...), custom_call_target="tpu_custom_call" | custom-call | tf_op jit(solution)/shard_map/opening/pallas_call | solution.py:851
  143.4 6.8 fusion.17
  174.3 7.7 %all-to-all-done = bf16[8,512,128]{2,1,0:T(8,128)(2,1)S(1)} async-done(((bf16[8,512,128]{2,1,0:T(8,128)(2,1)}), bf16[8,512,128]{2,1,0:T(8,128)(2,1)S(1)}, u32[]{:S(2)}, u32[]{:S(2)}) %all-to-all-start) | async-done | bytes 1048608 | tf_op jit(solution)/shard_map/all_to_all | solution.py:1227
  195.4 6.8 attention_forward.4
  231.4 8.2 %collective-permute-done.6 = bf16[256,1024]{1,0:T(8,128)(2,1)S(1)} collective-permute-done((bf16[256,1024]{1,0:T(8,128)(2,1)S(1)}, bf16[256,1024]{1,0:T(8,128)(2,1)S(1)}, u32[]{:S(2)}, u32[]{:S(2)}) %collective-permute-start.6) | collective-permute-done | bytes 524320 | tf_op jit(solution)/shard_map/ppermute | solution.py:516
  249.4 8.7 %all-gather.2.cloned.1.call-done = bf16[1024,6400]{1,0:T(8,128)(2,1)} async-done(((bf16[64,6400]{1,0:T(8,128)(2,1)}), bf16[1024,6400]{1,0:T(8,128)(2,1)}) %all-gather.2.cloned.1.call-update) | async-done | bytes 13107216 | tf_op jit(solution)/shard_map/all_gather | solution.py:566
  274.6 8.3 %collective-permute-done.7 = bf16[256,1024]{1,0:T(8,128)(2,1)S(1)} collective-permute-done((bf16[256,1024]{1,0:T(8,128)(2,1)S(1)}, bf16[256,1024]{1,0:T(8,128)(2,1)S(1)}, u32[]{:S(2)}, u32[]{:S(2)}) %collective-permute-start.7) | collective-permute-done | bytes 524320 | tf_op jit(solution)/shard_map/ppermute | solution.py:516
  290.3 6.6 attention_forward.6
  299.7 6.7 attention_forward.7
  356.4 7.5 %collective-permute-done.11 = bf16[256,1024]{1,0:T(8,128)(2,1)} collective-permute-done((bf16[256,1024]{1,0:T(8,128)(2,1)S(1)}, bf16[256,1024]{1,0:T(8,128)(2,1)}, u32[]{:S(2)}, u32[]{:S(2)}) %collective-permute-start.11) | collective-permute-done | bytes 524320 | tf_op jit(solution)/shard_map/ppermute | solution.py:516
  372.5 10.1 %attention_backward.4 = (bf16[256,512]{1,0:T(8,128)(2,1)S(1)}, f32[1024,512]{1,0:T(8,128)S(1)}, f32[1024,512]{1,0:T(8,128)}) custom-call(bf16[256,1536]{1,0:T(8,128)(2,1)S(1)} %copy-done.8, bf16[1024,1024]{1,0:T(8,128)(2,1)} %copy-done.1, bf16[1024,1024]{1,0:T(8,128)(2,1)} %copy-done.1, bf16[256,512]{1,0:T(8,128)(2,1)S(1)} %convolution_convert_fusion.15.g_ref, ...), custom_call_target="tpu_custom_call" | custom-call | flops 2684354560 | bytes 5242880 | tf_op jit(solution)/shard_map/attention_backward/pallas_call | solution.py:1007
  385.4 10.4 %attention_backward.5 = (bf16[256,512]{1,0:T(8,128)(2,1)S(1)}, f32[1024,512]{1,0:T(8,128)S(1)}, f32[1024,512]{1,0:T(8,128)}) custom-call(bf16[256,1536]{1,0:T(8,128)(2,1)S(1)} %copy-done.3, bf16[1024,1024]{1,0:T(8,128)(2,1)} %copy-done.1, bf16[1024,1024]{1,0:T(8,128)(2,1)} %copy-done.1, bf16[256,512]{1,0:T(8,128)(2,1)S(1)} %convolution_convert_fusion.14.g_ref, ...), custom_call_target="tpu_custom_call" | custom-call | flops 2684354560 | bytes 5242880 | tf_op jit(solution)/shard_map/attention_backward/pallas_call | solution.py:1007
  418.8 7.9 %collective-permute-start.22 = (f32[256,1024]{1,0:T(8,128)}, f32[256,1024]{1,0:T(8,128)}, u32[]{:S(2)}, u32[]{:S(2)}) collective-permute-start(f32[256,1024]{1,0:T(8,128)} %collective-permute-done.21), channel_id=1, source_target_pairs={{0,16},{16,0},{1,17},{17,1},{2,18},{18,2},{3,19},{19,3},{4,20},{20... | collective-permute-start | bytes 3145736 | tf_op jit(solution)/shard_map/ppermute | solution.py:512
  475.6 10.0 %attention_backward.6 = (bf16[256,512]{1,0:T(8,128)(2,1)S(1)}, f32[1024,512]{1,0:T(8,128)S(1)}, f32[1024,512]{1,0:T(8,128)}) custom-call(bf16[256,1536]{1,0:T(8,128)(2,1)S(1)} %copy-done.6, bf16[1024,1024]{1,0:T(8,128)(2,1)} %copy-done, bf16[1024,1024]{1,0:T(8,128)(2,1)} %copy-done, bf16[256,512]{1,0:T(8,128)(2,1)S(1)} %convolution_convert_fusion.13.g_ref, ...), custom_call_target="tpu_custom_call" | custom-call | flops 2684354560 | bytes 5242880 | tf_op jit(solution)/shard_map/attention_backward/pallas_call | solution.py:1007
  487.8 10.8 %attention_backward.7 = (bf16[256,512]{1,0:T(8,128)(2,1)S(1)}, f32[1024,512]{1,0:T(8,128)S(1)}, f32[1024,512]{1,0:T(8,128)}) custom-call(bf16[256,1536]{1,0:T(8,128)(2,1)S(1)} %convolution_convert_fusion.4.q_ref, bf16[1024,1024]{1,0:T(8,128)(2,1)} %copy-done, bf16[1024,1024]{1,0:T(8,128)(2,1)} %copy-done, ...), custom_call_target="tpu_custom_call" | custom-call | flops 2684354560 | bytes 5242880 | tf_op jit(solution)/shard_map/attention_backward/pallas_call | solution.py:1007
  536.5 10.6 %collective-permute-done.25 = bf16[256,1024]{1,0:T(8,128)(2,1)S(1)} collective-permute-done((bf16[256,1024]{1,0:T(8,128)(2,1)S(1)}, bf16[256,1024]{1,0:T(8,128)(2,1)S(1)}, u32[]{:S(2)}, u32[]{:S(2)}) %collective-permute-start.25) | collective-permute-done | bytes 524320 | tf_op jit(solution)/shard_map/ppermute | solution.py:516
  558.4 10.6 %all-to-all-done.1 = bf16[8,512,128]{2,1,0:T(8,128)(2,1)S(1)} async-done(((bf16[8,512,128]{2,1,0:T(8,128)(2,1)}), bf16[8,512,128]{2,1,0:T(8,128)(2,1)S(1)}, u32[]{:S(2)}, u32[]{:S(2)}) %all-to-all-start.1) | async-done | bytes 1048608 | tf_op jit(solution)/shard_map/all_to_all | solution.py:1378
  618.4 7.9 %all-to-all-start.2 = ((bf16[8,2,256,128]{3,2,1,0:T(8,128)(2,1)}), bf16[8,2,256,128]{3,2,1,0:T(8,128)(2,1)S(1)}, u32[]{:S(2)}, u32[]{:S(2)}) async-start(bf16[8,2,256,128]{3,2,1,0:T(8,128)(2,1)} %copy.421), calls=%async_computation.3 | async-start | bytes 2097152 | tf_op jit(solution)/shard_map/all_to_all | solution.py:1398
  626.2 12.2 %collective-permute-done.27 = bf16[2,4,272,128]{3,2,1,0:T(8,128)(2,1)} collective-permute-done((bf16[2,4,272,128]{3,2,1,0:T(8,128)(2,1)}, bf16[2,4,272,128]{3,2,1,0:T(8,128)(2,1)}, u32[]{:S(2)}, u32[]{:S(2)}) %collective-permute-start.27) | collective-permute-done | bytes 557088 | tf_op jit(solution)/shard_map/ppermute | solution.py:549
  646.3 10.7 %collective-permute-done.28 = bf16[2,4,272,128]{3,2,1,0:T(8,128)(2,1)} collective-permute-done((bf16[2,4,272,128]{3,2,1,0:T(8,128)(2,1)}, bf16[2,4,272,128]{3,2,1,0:T(8,128)(2,1)}, u32[]{:S(2)}, u32[]{:S(2)}) %collective-permute-start.28) | collective-permute-done | bytes 557088 | tf_op jit(solution)/shard_map/ppermute | solution.py:549
  666.9 9.0 %collective-permute-done.31 = bf16[2,4,272,128]{3,2,1,0:T(8,128)(2,1)} collective-permute-done((bf16[2,4,272,128]{3,2,1,0:T(8,128)(2,1)}, bf16[2,4,272,128]{3,2,1,0:T(8,128)(2,1)}, u32[]{:S(2)}, u32[]{:S(2)}) %collective-permute-start.31) | collective-permute-done | bytes 557088 | tf_op jit(solution)/shard_map/ppermute | solution.py:549
  676.0 7.6 %collective-permute-done.30 = bf16[2,4,272,128]{3,2,1,0:T(8,128)(2,1)} collective-permute-done((bf16[2,4,272,128]{3,2,1,0:T(8,128)(2,1)}, bf16[2,4,272,128]{3,2,1,0:T(8,128)(2,1)}, u32[]{:S(2)}, u32[]{:S(2)}) %collective-permute-start.30) | collective-permute-done | bytes 557088 | tf_op jit(solution)/shard_map/ppermute | solution.py:549
  685.9 14.8 %all-to-all-start.3 = ((bf16[8,272,128]{2,1,0:T(8,128)(2,1)}), bf16[8,272,128]{2,1,0:T(8,128)(2,1)S(1)}, u32[]{:S(2)}, u32[]{:S(2)}) async-start(bf16[8,272,128]{2,1,0:T(8,128)(2,1)} %bitcast.367), calls=%async_computation.4 | async-start | bytes 1114112 | tf_op jit(solution)/shard_map/all_to_all | solution.py:1412
  712.9 7.3 reduce-scatter.8.cloned.1.call-done
  (765 shorter events, 429.8 us)
Async XLA Ops:
  7.2 250.9 %all-gather.2.cloned.1.call-start = ((), (), s32[]{:S(2)}) async-start(), calls=%async_computation.7 | async-start | bytes 13926400 | tf_op jit(solution)/shard_map/all_gather | solution.py:566
  162.9 19.2 %all-to-all-start = ((bf16[8,512,128]{2,1,0:T(8,128)(2,1)}), bf16[8,512,128]{2,1,0:T(8,128)(2,1)S(1)}, u32[]{:S(2)}, u32[]{:S(2)}) async-start(bf16[8,512,128]{2,1,0:T(8,128)(2,1)} %bitcast.29), calls=%async_computation | async-start | bytes 2097152 | tf_op jit(solution)/shard_map/all_to_all | solution.py:1227
  167.3 332.0 %reduce-scatter.4.cloned.1.call-start = ((), (), s32[]{:S(2)}) async-start(), calls=%async_computation.8 | async-start | bytes 9191424 | tf_op jit(solution)/shard_map/reduce_scatter | solution.py:572
  168.2 36.5 %collective-permute-start = (bf16[256,1024]{1,0:T(8,128)(2,1)}, bf16[256,1024]{1,0:T(8,128)(2,1)}, u32[]{:S(2)}, u32[]{:S(2)}) collective-permute-start(bf16[256,1024]{1,0:T(8,128)(2,1)} %select_bitcast_fusion.2), channel_id=1, source_target_pairs={{0,0},{1,1},{2,16},{3,17},{16,2},{17,3},{18,18},{19,19},{4,4},{5,5... | collective-permute-start | bytes 1572872 | tf_op jit(solution)/shard_map/ppermute | solution.py:1210
  204.7 81.4 %collective-permute-start.1 = (bf16[256,1024]{1,0:T(8,128)(2,1)}, bf16[256,1024]{1,0:T(8,128)(2,1)}, u32[]{:S(2)}, u32[]{:S(2)}) collective-permute-start(bf16[256,1024]{1,0:T(8,128)(2,1)} %collective-permute-done), channel_id=1, source_target_pairs={{0,1},{1,0},{2,3},{3,2},{4,5},{5,4},{6,7},{7,6},{8,9},{9,8},{10,11... | collective-permute-start | bytes 1572872 | tf_op jit(solution)/shard_map/ppermute | solution.py:516
  212.3 27.3 %collective-permute-start.6 = (bf16[256,1024]{1,0:T(8,128)(2,1)S(1)}, bf16[256,1024]{1,0:T(8,128)(2,1)S(1)}, u32[]{:S(2)}, u32[]{:S(2)}) collective-permute-start(bf16[256,1024]{1,0:T(8,128)(2,1)S(1)} %convolution_convert_fusion.10), channel_id=1, source_target_pairs={{0,1},{1,0},{2,3},{3,2},{4,5},{5,4},{6,7},{7,6},{8,9},{9,8},{10,11... | collective-permute-start | bytes 1572872 | tf_op jit(solution)/shard_map/ppermute | solution.py:516
  264.9 17.9 %collective-permute-start.7 = (bf16[256,1024]{1,0:T(8,128)(2,1)S(1)}, bf16[256,1024]{1,0:T(8,128)(2,1)S(1)}, u32[]{:S(2)}, u32[]{:S(2)}) collective-permute-start(bf16[256,1024]{1,0:T(8,128)(2,1)S(1)} %fusion.120), channel_id=1, source_target_pairs={{0,1},{1,0},{2,3},{3,2},{4,5},{5,4},{6,7},{7,6},{8,9},{9,8},{10,11... | collective-permute-start | bytes 1572872 | tf_op jit(solution)/shard_map/ppermute | solution.py:516
  341.5 22.5 %collective-permute-start.11 = (bf16[256,1024]{1,0:T(8,128)(2,1)S(1)}, bf16[256,1024]{1,0:T(8,128)(2,1)}, u32[]{:S(2)}, u32[]{:S(2)}) collective-permute-start(bf16[256,1024]{1,0:T(8,128)(2,1)S(1)} %fusion.126), channel_id=1, source_target_pairs={{0,1},{1,0},{2,3},{3,2},{4,5},{5,4},{6,7},{7,6},{8,9},{9,8},{10,11... | collective-permute-start | bytes 1572872 | tf_op jit(solution)/shard_map/ppermute | solution.py:516
  350.9 359.2 %reduce-scatter.6.cloned.1.call-start = ((), (), s32[]{:S(2)}) async-start(), calls=%async_computation.9 | async-start | bytes 13647872 | tf_op jit(solution)/shard_map/reduce_scatter | solution.py:572
  370.9 24.9 %collective-permute-start.15 = (bf16[256,1024]{1,0:T(8,128)(2,1)S(1)}, bf16[256,1024]{1,0:T(8,128)(2,1)S(1)}, u32[]{:S(2)}, u32[]{:S(2)}) collective-permute-start(bf16[256,1024]{1,0:T(8,128)(2,1)S(1)} %fusion.132), channel_id=1, source_target_pairs={{0,1},{1,0},{2,3},{3,2},{4,5},{5,4},{6,7},{7,6},{8,9},{9,8},{10,11... | collective-permute-start | bytes 1572872 | tf_op jit(solution)/shard_map/ppermute | solution.py:516
  372.2 23.6 %collective-permute-start.14 = (bf16[256,1024]{1,0:T(8,128)(2,1)S(1)}, bf16[256,1024]{1,0:T(8,128)(2,1)S(1)}, u32[]{:S(2)}, u32[]{:S(2)}) collective-permute-start(bf16[256,1024]{1,0:T(8,128)(2,1)S(1)} %copy-done.111), channel_id=1, source_target_pairs={{0,1},{1,0},{2,3},{3,2},{4,5},{5,4},{6,7},{7,6},{8,9},{9,8},{10,11... | collective-permute-start | bytes 1572872 | tf_op jit(solution)/shard_map/ppermute | solution.py:516
  402.1 16.7 %collective-permute-start.21 = (f32[256,1024]{1,0:T(8,128)}, f32[256,1024]{1,0:T(8,128)}, u32[]{:S(2)}, u32[]{:S(2)}) collective-permute-start(f32[256,1024]{1,0:T(8,128)} %broadcast_select_fusion.6), channel_id=1, source_target_pairs={{0,0},{1,1},{2,16},{3,17},{16,2},{17,3},{18,18},{19,19},{4,4},{5,5... | collective-permute-start | bytes 3145736 | tf_op jit(solution)/shard_map/ppermute | solution.py:1336
  410.2 21.8 %collective-permute-start.18 = (bf16[256,1024]{1,0:T(8,128)(2,1)S(1)}, bf16[256,1024]{1,0:T(8,128)(2,1)}, u32[]{:S(2)}, u32[]{:S(2)}) collective-permute-start(bf16[256,1024]{1,0:T(8,128)(2,1)S(1)} %fusion.105), channel_id=1, source_target_pairs={{0,1},{1,0},{2,3},{3,2},{4,5},{5,4},{6,7},{7,6},{8,9},{9,8},{10,11... | collective-permute-start | bytes 1572872 | tf_op jit(solution)/shard_map/ppermute | solution.py:516
  418.8 43.2 %collective-permute-start.22 = (f32[256,1024]{1,0:T(8,128)}, f32[256,1024]{1,0:T(8,128)}, u32[]{:S(2)}, u32[]{:S(2)}) collective-permute-start(f32[256,1024]{1,0:T(8,128)} %collective-permute-done.21), channel_id=1, source_target_pairs={{0,16},{16,0},{1,17},{17,1},{2,18},{18,2},{3,19},{19,3},{4,20},{20... | collective-permute-start | bytes 3145736 | tf_op jit(solution)/shard_map/ppermute | solution.py:512
  442.2 23.0 %collective-permute-start.19 = (bf16[256,1024]{1,0:T(8,128)(2,1)}, bf16[256,1024]{1,0:T(8,128)(2,1)}, u32[]{:S(2)}, u32[]{:S(2)}) collective-permute-start(bf16[256,1024]{1,0:T(8,128)(2,1)} %fusion.150), channel_id=1, source_target_pairs={{0,1},{1,0},{2,3},{3,2},{4,5},{5,4},{6,7},{7,6},{8,9},{9,8},{10,11... | collective-permute-start | bytes 1572872 | tf_op jit(solution)/shard_map/ppermute | solution.py:516
  448.2 18.4 %collective-permute-start.20 = (bf16[256,1024]{1,0:T(8,128)(2,1)}, bf16[256,1024]{1,0:T(8,128)(2,1)}, u32[]{:S(2)}, u32[]{:S(2)}) collective-permute-start(bf16[256,1024]{1,0:T(8,128)(2,1)} %fusion.159), channel_id=1, source_target_pairs={{0,1},{1,0},{2,3},{3,2},{4,5},{5,4},{6,7},{7,6},{8,9},{9,8},{10,11... | collective-permute-start | bytes 1572872 | tf_op jit(solution)/shard_map/ppermute | solution.py:516
  526.0 21.1 %collective-permute-start.25 = (bf16[256,1024]{1,0:T(8,128)(2,1)S(1)}, bf16[256,1024]{1,0:T(8,128)(2,1)S(1)}, u32[]{:S(2)}, u32[]{:S(2)}) collective-permute-start(bf16[256,1024]{1,0:T(8,128)(2,1)S(1)} %fusion.111), channel_id=1, source_target_pairs={{0,1},{1,0},{2,3},{3,2},{4,5},{5,4},{6,7},{7,6},{8,9},{9,8},{10,11... | collective-permute-start | bytes 1572872 | tf_op jit(solution)/shard_map/ppermute | solution.py:516
  549.9 19.1 %all-to-all-start.1 = ((bf16[8,512,128]{2,1,0:T(8,128)(2,1)}), bf16[8,512,128]{2,1,0:T(8,128)(2,1)S(1)}, u32[]{:S(2)}, u32[]{:S(2)}) async-start(bf16[8,512,128]{2,1,0:T(8,128)(2,1)} %bitcast_bitcast_fusion), calls=%async_computation.2 | async-start | bytes 2097152 | tf_op jit(solution)/shard_map/all_to_all | solution.py:1378
  554.2 166.0 %reduce-scatter.8.cloned.1.call-start = ((), (), s32[]{:S(2)}) async-start(), calls=%async_computation.10 | async-start | bytes 4734976 | tf_op jit(solution)/shard_map/reduce_scatter | solution.py:572
  593.9 32.4 %collective-permute-start.26 = (bf16[2,4,272,128]{3,2,1,0:T(8,128)(2,1)}, bf16[2,4,272,128]{3,2,1,0:T(8,128)(2,1)}, u32[]{:S(2)}, u32[]{:S(2)}) collective-permute-start(bf16[2,4,272,128]{3,2,1,0:T(8,128)(2,1)} %get-tuple-element.216), channel_id=1, source_target_pairs={{0,4},{1,5},{2,6},{3,7},{16,20},{17,21},{18,22},{19,23}} | collective-permute-start | bytes 1671176 | tf_op jit(solution)/shard_map/ppermute | solution.py:549
  595.6 42.9 %collective-permute-start.27 = (bf16[2,4,272,128]{3,2,1,0:T(8,128)(2,1)}, bf16[2,4,272,128]{3,2,1,0:T(8,128)(2,1)}, u32[]{:S(2)}, u32[]{:S(2)}) collective-permute-start(bf16[2,4,272,128]{3,2,1,0:T(8,128)(2,1)} %get-tuple-element.215), channel_id=1, source_target_pairs={{12,8},{13,9},{14,10},{15,11},{28,24},{29,25},{30,26},{31,27}} | collective-permute-start | bytes 1671176 | tf_op jit(solution)/shard_map/ppermute | solution.py:549
  618.4 27.9 %all-to-all-start.2 = ((bf16[8,2,256,128]{3,2,1,0:T(8,128)(2,1)}), bf16[8,2,256,128]{3,2,1,0:T(8,128)(2,1)S(1)}, u32[]{:S(2)}, u32[]{:S(2)}) async-start(bf16[8,2,256,128]{3,2,1,0:T(8,128)(2,1)} %copy.421), calls=%async_computation.3 | async-start | bytes 2097152 | tf_op jit(solution)/shard_map/all_to_all | solution.py:1398
  664.5 19.1 %collective-permute-start.30 = (bf16[2,4,272,128]{3,2,1,0:T(8,128)(2,1)}, bf16[2,4,272,128]{3,2,1,0:T(8,128)(2,1)}, u32[]{:S(2)}, u32[]{:S(2)}) collective-permute-start(bf16[2,4,272,128]{3,2,1,0:T(8,128)(2,1)} %get-tuple-element.211), channel_id=1, source_target_pairs={{0,4},{4,8},{8,12},{1,5},{5,9},{9,13},{2,6},{6,10},{10,14},{3,7},{... | collective-permute-start | bytes 1671176 | tf_op jit(solution)/shard_map/ppermute | solution.py:549
  685.9 24.3 %all-to-all-start.3 = ((bf16[8,272,128]{2,1,0:T(8,128)(2,1)}), bf16[8,272,128]{2,1,0:T(8,128)(2,1)S(1)}, u32[]{:S(2)}, u32[]{:S(2)}) async-start(bf16[8,272,128]{2,1,0:T(8,128)(2,1)} %bitcast.367), calls=%async_computation.4 | async-start | bytes 1114112 | tf_op jit(solution)/shard_map/all_to_all | solution.py:1412
  (202 other events, 1382.3 us)
Sparse Core Ops, SparseCore 0:
  128.1 129.9 all-gather.1
  351.1 119.5 reduce-scatter.3
  474.8 166.9 reduce-scatter.5
  645.5 74.7 reduce-scatter.7

commit v6 on v5

--- a/solution.py
+++ b/solution.py
@@ -869,6 +869,63 @@
         name="opening",
     )(conv_send, signal_send, keep, send, rest)
     return conv_all, signal_all, whole.reshape(-1, columns), second
+
+
+def slice_exchange_kernel(same_x, send_ref, got_ref, local_sem, send_sem, recv_sem):
+    sec, seq = lax.axis_index("section"), lax.axis_index("seq")
+    x, y = seq % 2, seq // 2
+    if same_x:
+        peers = [((sec + a) % 2, 2 * ((y + b) % 2) + x) for a, b in ((0, 1), (1, 0), (1, 1))]
+    else:
+        peers = [
+            ((sec + a) % 2, 2 * ((y + b) % 2) + (x + c) % 2)
+            for a in range(2) for b in range(2) for c in range(2) if a + b + c
+        ]
+
+    def place(section, seq):
+        return section * 2 + seq // 2 if same_x else section * 4 + seq
+
+    barrier = pltpu.get_barrier_semaphore()
+    for section, other in peers:
+        pl.semaphore_signal(
+            barrier, inc=1, device_id={"section": section, "seq": other}, device_id_type=MESH
+        )
+    pl.semaphore_wait(barrier, len(peers))
+
+    def copy(index, landing):
+        section, other = peers[index]
+        return pltpu.make_async_remote_copy(
+            src_ref=send_ref.at[section * 4 + other], dst_ref=got_ref.at[landing],
+            send_sem=send_sem.at[index], recv_sem=recv_sem.at[index],
+            device_id={"section": section, "seq": other}, device_id_type=MESH,
+        )
+
+    for index in range(len(peers)):
+        copy(index, place(sec, seq)).start()
+    own = pltpu.make_async_copy(send_ref.at[sec * 4 + seq], got_ref.at[place(sec, seq)], local_sem.at[0])
+    own.start()
+    for index, peer in enumerate(peers):
+        copy(index, place(*peer)).wait_recv()
+        copy(index, place(sec, seq)).wait_send()
+    own.wait()
+
+
+def slice_exchange(value, same_x):
+    anywhere = pl.BlockSpec(memory_space=pl.ANY)
+    dma = pltpu.SemaphoreType.DMA
+    count = 4 if same_x else 8
+    return pl.pallas_call(
+        functools.partial(slice_exchange_kernel, same_x),
+        in_specs=[anywhere],
+        out_specs=anywhere,
+        out_shape=jax.ShapeDtypeStruct((count, *value.shape[1:]), value.dtype),
+        scratch_shapes=[dma((1,)), dma((count - 1,)), dma((count - 1,))],
+        compiler_params=pltpu.CompilerParams(
+            collective_id=2 if same_x else 1, has_side_effects=True, vmem_limit_bytes=4 * 1024 * 1024
+        ),
+        cost_estimate=pl.CostEstimate(flops=0, bytes_accessed=value.size, transcendentals=0),
+        name="slice_exchange",
+    )(value)
 
 
 def norm_stats(values):
@@ -1207,7 +1264,12 @@
 
     picked = jnp.where(sec0, cotangent[0], cotangent[1])
     across = [(s * 4 + 2 * yy + xx, yy * 4 + 2 * s + xx) for s in range(2) for yy in range(2) for xx in range(2)]
-    cot_own = lax.ppermute(picked, both, across)
+    across = [(a, b) for a, b in across if a != b]
+
+    def over_rows(value):
+        return jnp.where(sec == y, value, lax.ppermute(value, both, across))
+
+    cot_own = over_rows(picked)
     cot_other = swap_x(cot_own)
     cot_pair = choose(x0, cot_own, cot_other)
     top_grad = jnp.concatenate(cot_pair, axis=0).astype(f32)
@@ -1224,7 +1286,7 @@
     stream_send = stream.reshape(2, 2, half_frames, block_width)
     stream_send = jnp.transpose(stream_send, (1, 0, 2, 3))
     stream_send = jnp.repeat(stream_send.reshape(4, half_frames, block_width), 2, axis=0)
-    stream_got = lax.all_to_all(stream_send, both, 0, 0, tiled=True)
+    stream_got = slice_exchange(stream_send, False)
     layer_in = jnp.transpose(stream_got, (1, 0, 2)).reshape(half_frames, width).astype(f32)
 
     chunks = 2
@@ -1333,7 +1395,7 @@
             if layer == 1 and c == 0:
                 attended_grad, lows = after(attended_grad, lows)
                 output = [member + pair_sum(low) for member, low in zip(resid_two_last, lows)]
-                row_block = lax.ppermute(jnp.where(x0, output[0], output[1]), both, across)
+                row_block = over_rows(jnp.where(x0, output[0], output[1]))
                 output_rows = jnp.stack(choose(sec0, row_block, swap_section(row_block)))
             own_dq, *dkv = attention_backward(
                 packed[c], kv_all, attended_grad, attended[c], lse[c], chunk_segs[c], key_segs, factor,
@@ -1375,8 +1437,8 @@
     scattered.append(scatter_rows(jnp.concatenate(attn_members, axis=1)))
 
     lig_send = jnp.transpose(grad_in_low.reshape(half_frames, 8, block_width), (1, 0, 2))
-    lig_got = lax.all_to_all(lig_send, both, 0, 0, tiled=True).reshape(2, 2, 2, half_frames, block_width)
-    lig = jnp.transpose(lig_got[:, :, 0], (1, 0, 2, 3)).reshape(micro_count, row_frames, block_width)
+    lig_got = lax.all_to_all(lig_send, both, 0, 0, tiled=True).reshape(2, 2, 2, half_frames, block_width)[:, :, 0]
+    lig = jnp.transpose(lig_got, (1, 0, 2, 3)).reshape(micro_count, row_frames, block_width)
     conv_grad = (lig.astype(f32) * slope.astype(f32)).astype(bf16)
     grad_views = group_view(conv_grad, per_group)
     back = ungroup(conv_back(grad_views, bands), per_group)
@@ -1402,9 +1464,6 @@
         keep, send = choose(sec0, first, second)
         return choose(sec0, keep, swap_section(send))
 
-    def over_x(first, second):
-        keep, send = choose(x0, first, second)
-        return keep, choose(x0, keep, swap_x(send))
 
     taps_sum, (_, gs_got) = sum_dp(taps_send, dp, (gs_send, gs_got))
     gs_rows = jnp.transpose(gs_got, (1, 2, 0, 3)).reshape(micro_count, frames, width).astype(f32)
@@ -1422,25 +1481,34 @@
         0,
     ).astype(f32)
 
-    ff_sets = over_section(scattered[1][:, attn_cols:], scattered[0][:, :-128])
+    turned = [(t * 4 + 2 * r + c, c * 4 + 2 * r + t) for t in range(2) for r in range(2) for c in range(2) if t != c]
+    crossed = [(t * 4 + 2 * r + c, (1 - c) * 4 + 2 * r + t) for t in range(2) for r in range(2) for c in range(2)]
+
+    def home(first, second):
+        straight, other = choose(x0, first, second)
+        straight = jnp.where(sec == x, straight, lax.ppermute(straight, both, turned))
+        other = lax.ppermute(other, both, crossed)
+        return choose(sec0, straight, other)
+
+    ff_layers = (scattered[1][:, attn_cols:], scattered[0][:, :-128])
+    ff_sets = over_section(*(member[:, up_cols:] for member in ff_layers))
     down_grad = jnp.concatenate(
-        [member[:, up_cols + at : up_cols + at + width] for member in ff_sets for at in (0, width)],
-        axis=0,
+        [member[:, at : at + width] for member in ff_sets for at in (0, width)], axis=0
     ).astype(f32)[None]
-    _, up_sets = over_x(*(member[:, :up_cols] for member in ff_sets))
     up_grad = jnp.stack(
         [
             jnp.transpose(member.reshape(in_rows, 2, -1, 2, unit), (0, 2, 3, 1, 4))
-            for member in up_sets
+            for member in home(*(member[:, :up_cols] for member in ff_layers))
         ],
         axis=2,
     ).reshape(in_rows, -1).astype(f32)[None]
-
-    attn_sets = over_section(scattered[2], scattered[1][:, :attn_cols])
-    out_grad = jnp.concatenate([member[:, cut:attn_cols] for member in attn_sets], axis=1).astype(f32)[None]
-    keep, qkv_sets = over_x(*(member[:, :cut] for member in attn_sets))
-    norm1_grad = keep[:, qkv_cols].astype(f32)[None]
-    norm2_grad = keep[:, qkv_cols + 1].astype(f32)[None]
+    scattered[2], (up_grad, down_grad) = after(scattered[2], (up_grad, down_grad))
+    attn_layers = (scattered[2], scattered[1][:, :attn_cols])
+    attn_sets = over_section(*(member[:, cut:] for member in attn_layers))
+    out_grad = jnp.concatenate(attn_sets, axis=1).astype(f32)[None]
+    qkv_sets = home(*(member[:, :cut] for member in attn_layers))
+    norm1_grad = qkv_sets[0][:, qkv_cols].astype(f32)[None]
+    norm2_grad = qkv_sets[0][:, qkv_cols + 1].astype(f32)[None]
     qkv_grad = jnp.stack(
         [member[:, :qkv_cols].reshape(in_rows, -1, HEAD_DIM) for member in qkv_sets], axis=2
     ).reshape(in_rows, -1).astype(f32)[None]

time: 768 us -> 781 us (1.017)
  Pallas kernels: 168 us -> 182 us
  starting transfers between devices: 84 us -> 72.7 us
  other arithmetic: 97.6 us -> 106 us
    ppermute x6, waiting for transfers between devices: 40.9 us -> 58.2 us  [sum_dp(): running[way] = lax.ppermute(own, 'dp', live)]
    pallas_call x0 -> x1, Pallas kernels: none -> 14.8 us  [slice_exchange(): pl.pallas_call(functools.partial(slice_exchange_kernel, same_x), in_specs...]
    ppermute x9, starting transfers between devices: 17.8 us -> 6.12 us  [swap_section(): return lax.ppermute(value, 'section', [(0, 1), (1, 0)])]
    ppermute x2 -> x6, waiting for transfers between devices: 0.19 us -> 11.4 us  [the longest x2 6.35 us: home(): lax.ppermute(straight, both, turned)]
    ppermute x2 -> x6, starting transfers between devices: 5.67 us -> 14.4 us  [the longest x2 6.39 us: over_rows(): return jnp.where(sec == y, value, lax.ppermute(value, both, across))]
    all_gather x1, waiting for transfers between devices: 8.69 us -> 0.02 us  [gather_rows(): lax.all_gather(piece, ('section', 'dp', 'seq'), axis=0, tiled=True, axis_...]
    ppermute x19 -> x17, waiting for transfers between devices: 63.2 us -> 60.8 us  [swap_x(): return lax.ppermute(value, 'seq', [(q, q ^ 1) for q in range(4)])]
    unnamed x372 -> x346, local copies, waits for them, and re-layouts: 33.1 us -> 31 us
  transfers between devices with their start and end apart: 44 -> 45, of which waited for: 24 -> 21; matrix products, arithmetic and copies ran while one was open for 36% -> 37% of each run, Pallas kernels for 8% -> 10%
where the time goes in v6:
time: 781 us; the launch traced here: 772 us
  Pallas kernels  182 us (23%)
  matrix products  150 us (19%)
  waiting for transfers between devices  149 us (19%)
  other arithmetic  106 us (14%)
  local copies, waits for them, and re-layouts  95.3 us (12%)
  starting transfers between devices  72.7 us (9%)
  between operations  17.5 us (2%)
    pallas_call x1, Pallas kernels, opening(): pl.pallas_call(functools.partial(opening_kernel, count, parts), in_specs=...  99.8 us
    ppermute x17, waiting for transfers between devices, swap_x(): return lax.ppermute(value, 'seq', [(q, q ^ 1) for q in range(4)])  60.8 us
    ppermute x6, waiting for transfers between devices, sum_dp(): running[way] = lax.ppermute(own, 'dp', live)  58.2 us
    pallas_call x4, Pallas kernels, attention_backward(): pl.pallas_call(functools.partial(attention_backward_kernel, factor), grid...  41.2 us
    dot_general x12, matrix products, outer(): lax.dot_general(left, right, (((0,), (0,)), ((), ())), preferred_element_...  32.8 us
    dot_general x8, matrix products, per_device_pairs(): hidden_pre = jnp.dot(normed_two[c], w_up[part], preferred_element_type=f32)  31.9 us
    unnamed x346, local copies, waits for them, and re-layouts  31 us
    dot_general x24, matrix products, back(): lax.dot_general(left, right, (((1,), (1,)), ((), ())), preferred_element_...  29 us
  transfers between devices with their start and end apart: 45, of which 21 were waited for; matrix products, arithmetic and copies ran while one was open for 37% of the time, Pallas kernels for 10%

profile of v6, /device:TPU:17, one launch (start us, length us, event | category | flops | bytes accessed | tf_op | source)
XLA Modules:
  0.0 772.2 jit_solution(17428627216407661715)
XLA Ops:
  22.4 99.8 %opening.1 = (bf16[4,8,272,128]{3,2,1,0:T(8,128)(2,1)S(1)}, bf16[4,2,256,128]{3,2,1,0:T(8,128)(2,1)S(1)}, bf16[4,2,2,64,6400]{4,3,2,1,0:T(8,128)(2,1)S(1)}, bf16[64,6400]{1,0:T(8,128)(2,1)S(1)}) custom-call(bf16[8,272,128]{2,1,0:T(8,128)(2,1)S(1)} %fusion.401.conv_ref, bf16[4,2,256,128]{3,2,1,0:T(8,128)(2,1)S(1)} %bitcast.260, ...), custom_call_target="tpu_custom_call" | custom-call | tf_op jit(solution)/shard_map/opening/pallas_call | solution.py:851
  143.1 6.2 fusion.428
  149.9 6.8 fusion.17
  156.8 6.2 fusion.422
  168.5 14.8 %slice_exchange.1 = bf16[8,512,128]{2,1,0:T(8,128)(2,1)S(1)} custom-call(bf16[8,512,128]{2,1,0:T(8,128)(2,1)S(1)} %bitcast.257), custom_call_target="tpu_custom_call" | custom-call | bytes 524288 | tf_op jit(solution)/shard_map/slice_exchange/pallas_call | solution.py:917
  203.8 6.6 attention_forward.4
  213.6 6.7 attention_forward.5
  237.4 9.5 %collective-permute-done.6 = bf16[256,1024]{1,0:T(8,128)(2,1)S(1)} collective-permute-done((bf16[256,1024]{1,0:T(8,128)(2,1)S(1)}, bf16[256,1024]{1,0:T(8,128)(2,1)S(1)}, u32[]{:S(2)}, u32[]{:S(2)}) %collective-permute-start.6) | collective-permute-done | bytes 524320 | tf_op jit(solution)/shard_map/ppermute | solution.py:516
  287.4 6.6 attention_forward.6
  296.3 6.6 attention_forward.7
  353.3 8.0 %collective-permute-done.11 = bf16[256,1024]{1,0:T(8,128)(2,1)} collective-permute-done((bf16[256,1024]{1,0:T(8,128)(2,1)S(1)}, bf16[256,1024]{1,0:T(8,128)(2,1)}, u32[]{:S(2)}, u32[]{:S(2)}) %collective-permute-start.11) | collective-permute-done | bytes 524320 | tf_op jit(solution)/shard_map/ppermute | solution.py:516
  369.5 9.9 %attention_backward.4 = (bf16[256,512]{1,0:T(8,128)(2,1)S(1)}, f32[1024,512]{1,0:T(8,128)S(1)}, f32[1024,512]{1,0:T(8,128)}) custom-call(bf16[256,1536]{1,0:T(8,128)(2,1)S(1)} %copy-done.7, bf16[1024,1024]{1,0:T(8,128)(2,1)} %copy-done.1, bf16[1024,1024]{1,0:T(8,128)(2,1)} %copy-done.1, bf16[256,512]{1,0:T(8,128)(2,1)S(1)} %convolution_convert_fusion.15.g_ref, ...), custom_call_target="tpu_custom_call" | custom-call | flops 2684354560 | bytes 5242880 | tf_op jit(solution)/shard_map/attention_backward/pallas_call | solution.py:1064
  382.0 10.5 %attention_backward.5 = (bf16[256,512]{1,0:T(8,128)(2,1)S(1)}, f32[1024,512]{1,0:T(8,128)S(1)}, f32[1024,512]{1,0:T(8,128)}) custom-call(bf16[256,1536]{1,0:T(8,128)(2,1)S(1)} %convolution_convert_fusion.2.q_ref, bf16[1024,1024]{1,0:T(8,128)(2,1)} %copy-done.1, bf16[1024,1024]{1,0:T(8,128)(2,1)} %copy-done.1, ...), custom_call_target="tpu_custom_call" | custom-call | flops 2684354560 | bytes 5242880 | tf_op jit(solution)/shard_map/attention_backward/pallas_call | solution.py:1064
  428.8 10.2 %collective-permute-done.18 = bf16[256,1024]{1,0:T(8,128)(2,1)S(1)} collective-permute-done((bf16[256,1024]{1,0:T(8,128)(2,1)S(1)}, bf16[256,1024]{1,0:T(8,128)(2,1)S(1)}, u32[]{:S(2)}, u32[]{:S(2)}) %collective-permute-start.18) | collective-permute-done | bytes 524320 | tf_op jit(solution)/shard_map/ppermute | solution.py:516
  483.6 10.5 %attention_backward.6 = (bf16[256,512]{1,0:T(8,128)(2,1)S(1)}, f32[1024,512]{1,0:T(8,128)S(1)}, f32[1024,512]{1,0:T(8,128)}) custom-call(bf16[256,1536]{1,0:T(8,128)(2,1)S(1)} %copy-done.5, bf16[1024,1024]{1,0:T(8,128)(2,1)} %copy-done, bf16[1024,1024]{1,0:T(8,128)(2,1)} %copy-done, bf16[256,512]{1,0:T(8,128)(2,1)S(1)} %convolution_convert_fusion.13.g_ref, ...), custom_call_target="tpu_custom_call" | custom-call | flops 2684354560 | bytes 5242880 | tf_op jit(solution)/shard_map/attention_backward/pallas_call | solution.py:1064
  496.9 10.3 %attention_backward.7 = (bf16[256,512]{1,0:T(8,128)(2,1)S(1)}, f32[1024,512]{1,0:T(8,128)S(1)}, f32[1024,512]{1,0:T(8,128)}) custom-call(bf16[256,1536]{1,0:T(8,128)(2,1)S(1)} %copy-done.3, bf16[1024,1024]{1,0:T(8,128)(2,1)} %copy-done, bf16[1024,1024]{1,0:T(8,128)(2,1)} %copy-done, bf16[256,512]{1,0:T(8,128)(2,1)S(1)} %convolution_convert_fusion.12.g_ref, ...), custom_call_target="tpu_custom_call" | custom-call | flops 2684354560 | bytes 5242880 | tf_op jit(solution)/shard_map/attention_backward/pallas_call | solution.py:1064
  538.8 10.7 %collective-permute-done.25 = bf16[256,1024]{1,0:T(8,128)(2,1)S(1)} collective-permute-done((bf16[256,1024]{1,0:T(8,128)(2,1)S(1)}, bf16[256,1024]{1,0:T(8,128)(2,1)S(1)}, u32[]{:S(2)}, u32[]{:S(2)}) %collective-permute-start.25) | collective-permute-done | bytes 524320 | tf_op jit(solution)/shard_map/ppermute | solution.py:516
  561.9 10.5 %all-to-all-done = bf16[8,512,128]{2,1,0:T(8,128)(2,1)} async-done(((bf16[8,512,128]{2,1,0:T(8,128)(2,1)}), bf16[8,512,128]{2,1,0:T(8,128)(2,1)}, u32[]{:S(2)}, u32[]{:S(2)}) %all-to-all-start) | async-done | bytes 1048608 | tf_op jit(solution)/shard_map/all_to_all | solution.py:1440
  627.4 25.8 %collective-permute-done.27 = bf16[2,4,272,128]{3,2,1,0:T(8,128)(2,1)} collective-permute-done((bf16[2,4,272,128]{3,2,1,0:T(8,128)(2,1)}, bf16[2,4,272,128]{3,2,1,0:T(8,128)(2,1)}, u32[]{:S(2)}, u32[]{:S(2)}) %collective-permute-start.27) | collective-permute-done | bytes 557088 | tf_op jit(solution)/shard_map/ppermute | solution.py:549
  661.0 10.7 %collective-permute-done.28 = bf16[2,4,272,128]{3,2,1,0:T(8,128)(2,1)} collective-permute-done((bf16[2,4,272,128]{3,2,1,0:T(8,128)(2,1)}, bf16[2,4,272,128]{3,2,1,0:T(8,128)(2,1)}, u32[]{:S(2)}, u32[]{:S(2)}) %collective-permute-start.28) | collective-permute-done | bytes 557088 | tf_op jit(solution)/shard_map/ppermute | solution.py:549
  681.6 10.2 %collective-permute-done.31 = bf16[2,4,272,128]{3,2,1,0:T(8,128)(2,1)} collective-permute-done((bf16[2,4,272,128]{3,2,1,0:T(8,128)(2,1)}, bf16[2,4,272,128]{3,2,1,0:T(8,128)(2,1)}, u32[]{:S(2)}, u32[]{:S(2)}) %collective-permute-start.31) | collective-permute-done | bytes 557088 | tf_op jit(solution)/shard_map/ppermute | solution.py:549
  691.8 10.2 %collective-permute-done.30 = bf16[2,4,272,128]{3,2,1,0:T(8,128)(2,1)} collective-permute-done((bf16[2,4,272,128]{3,2,1,0:T(8,128)(2,1)}, bf16[2,4,272,128]{3,2,1,0:T(8,128)(2,1)}, u32[]{:S(2)}, u32[]{:S(2)}) %collective-permute-start.30) | collective-permute-done | bytes 557088 | tf_op jit(solution)/shard_map/ppermute | solution.py:549
  704.3 15.5 %all-to-all-start.2 = ((bf16[8,272,128]{2,1,0:T(8,128)(2,1)}), bf16[8,272,128]{2,1,0:T(8,128)(2,1)S(1)}, u32[]{:S(2)}, u32[]{:S(2)}) async-start(bf16[8,272,128]{2,1,0:T(8,128)(2,1)} %bitcast.334), calls=%async_computation.3 | async-start | bytes 1114112 | tf_op jit(solution)/shard_map/all_to_all | solution.py:1471
  723.2 7.8 %all-to-all-done.2 = bf16[8,272,128]{2,1,0:T(8,128)(2,1)S(1)} async-done(((bf16[8,272,128]{2,1,0:T(8,128)(2,1)}), bf16[8,272,128]{2,1,0:T(8,128)(2,1)S(1)}, u32[]{:S(2)}, u32[]{:S(2)}) %all-to-all-start.2) | async-done | bytes 557088 | tf_op jit(solution)/shard_map/all_to_all | solution.py:1471
  (746 shorter events, 424.1 us)
Async XLA Ops:
  7.2 248.4 %all-gather.2.cloned.1.call-start = ((), (), s32[]{:S(2)}) async-start(), calls=%async_computation.6 | async-start | bytes 13926400 | tf_op jit(solution)/shard_map/all_gather | solution.py:566
  127.9 379.3 %reduce-scatter.4.cloned.1.call-start = ((), (), s32[]{:S(2)}) async-start(), calls=%async_computation.7 | async-start | bytes 9191424 | tf_op jit(solution)/shard_map/reduce_scatter | solution.py:572
  130.0 81.5 %collective-permute-start = (bf16[256,1024]{1,0:T(8,128)(2,1)}, bf16[256,1024]{1,0:T(8,128)(2,1)}, u32[]{:S(2)}, u32[]{:S(2)}) collective-permute-start(bf16[256,1024]{1,0:T(8,128)(2,1)} %select_bitcast_fusion.2), channel_id=1, source_target_pairs={{2,16},{3,17},{16,2},{17,3},{6,20},{7,21},{20,6},{21,7},{10,24},{1... | collective-permute-start | bytes 1572872 | tf_op jit(solution)/shard_map/ppermute | solution.py:1270
  212.7 71.7 %collective-permute-start.1 = (bf16[256,1024]{1,0:T(8,128)(2,1)S(1)}, bf16[256,1024]{1,0:T(8,128)(2,1)S(1)}, u32[]{:S(2)}, u32[]{:S(2)}) collective-permute-start(bf16[256,1024]{1,0:T(8,128)(2,1)S(1)} %broadcast_select_fusion.3), channel_id=1, source_target_pairs={{0,1},{1,0},{2,3},{3,2},{4,5},{5,4},{6,7},{7,6},{8,9},{9,8},{10,11... | collective-permute-start | bytes 1572872 | tf_op jit(solution)/shard_map/ppermute | solution.py:516
  220.8 26.1 %collective-permute-start.6 = (bf16[256,1024]{1,0:T(8,128)(2,1)S(1)}, bf16[256,1024]{1,0:T(8,128)(2,1)S(1)}, u32[]{:S(2)}, u32[]{:S(2)}) collective-permute-start(bf16[256,1024]{1,0:T(8,128)(2,1)S(1)} %convolution_convert_fusion.10), channel_id=1, source_target_pairs={{0,1},{1,0},{2,3},{3,2},{4,5},{5,4},{6,7},{7,6},{8,9},{9,8},{10,11... | collective-permute-start | bytes 1572872 | tf_op jit(solution)/shard_map/ppermute | solution.py:516
  261.3 18.4 %collective-permute-start.7 = (bf16[256,1024]{1,0:T(8,128)(2,1)S(1)}, bf16[256,1024]{1,0:T(8,128)(2,1)S(1)}, u32[]{:S(2)}, u32[]{:S(2)}) collective-permute-start(bf16[256,1024]{1,0:T(8,128)(2,1)S(1)} %fusion.120), channel_id=1, source_target_pairs={{0,1},{1,0},{2,3},{3,2},{4,5},{5,4},{6,7},{7,6},{8,9},{9,8},{10,11... | collective-permute-start | bytes 1572872 | tf_op jit(solution)/shard_map/ppermute | solution.py:516
  338.3 23.0 %collective-permute-start.11 = (bf16[256,1024]{1,0:T(8,128)(2,1)S(1)}, bf16[256,1024]{1,0:T(8,128)(2,1)}, u32[]{:S(2)}, u32[]{:S(2)}) collective-permute-start(bf16[256,1024]{1,0:T(8,128)(2,1)S(1)} %fusion.126), channel_id=1, source_target_pairs={{0,1},{1,0},{2,3},{3,2},{4,5},{5,4},{6,7},{7,6},{8,9},{9,8},{10,11... | collective-permute-start | bytes 1572872 | tf_op jit(solution)/shard_map/ppermute | solution.py:516
  348.1 383.0 %reduce-scatter.6.cloned.1.call-start = ((), (), s32[]{:S(2)}) async-start(), calls=%async_computation.8 | async-start | bytes 13647872 | tf_op jit(solution)/shard_map/reduce_scatter | solution.py:572
  367.9 24.6 %collective-permute-start.15 = (bf16[256,1024]{1,0:T(8,128)(2,1)S(1)}, bf16[256,1024]{1,0:T(8,128)(2,1)S(1)}, u32[]{:S(2)}, u32[]{:S(2)}) collective-permute-start(bf16[256,1024]{1,0:T(8,128)(2,1)S(1)} %fusion.132), channel_id=1, source_target_pairs={{0,1},{1,0},{2,3},{3,2},{4,5},{5,4},{6,7},{7,6},{8,9},{9,8},{10,11... | collective-permute-start | bytes 1572872 | tf_op jit(solution)/shard_map/ppermute | solution.py:516
  368.6 23.9 %collective-permute-start.14 = (bf16[256,1024]{1,0:T(8,128)(2,1)S(1)}, bf16[256,1024]{1,0:T(8,128)(2,1)S(1)}, u32[]{:S(2)}, u32[]{:S(2)}) collective-permute-start(bf16[256,1024]{1,0:T(8,128)(2,1)S(1)} %copy-done.101), channel_id=1, source_target_pairs={{0,1},{1,0},{2,3},{3,2},{4,5},{5,4},{6,7},{7,6},{8,9},{9,8},{10,11... | collective-permute-start | bytes 1572872 | tf_op jit(solution)/shard_map/ppermute | solution.py:516
  406.9 17.0 %collective-permute-start.21 = (f32[256,1024]{1,0:T(8,128)}, f32[256,1024]{1,0:T(8,128)S(1)}, u32[]{:S(2)}, u32[]{:S(2)}) collective-permute-start(f32[256,1024]{1,0:T(8,128)} %broadcast_select_fusion.4), channel_id=1, source_target_pairs={{2,16},{3,17},{16,2},{17,3},{6,20},{7,21},{20,6},{21,7},{10,24},{1... | collective-permute-start | bytes 3145736 | tf_op jit(solution)/shard_map/ppermute | solution.py:1270
  414.3 25.2 %collective-permute-start.17 = (bf16[256,1024]{1,0:T(8,128)(2,1)S(1)}, bf16[256,1024]{1,0:T(8,128)(2,1)S(1)}, u32[]{:S(2)}, u32[]{:S(2)}) collective-permute-start(bf16[256,1024]{1,0:T(8,128)(2,1)S(1)} %fusion.102), channel_id=1, source_target_pairs={{0,1},{1,0},{2,3},{3,2},{4,5},{5,4},{6,7},{7,6},{8,9},{9,8},{10,11... | collective-permute-start | bytes 1572872 | tf_op jit(solution)/shard_map/ppermute | solution.py:516
  418.0 20.9 %collective-permute-start.18 = (bf16[256,1024]{1,0:T(8,128)(2,1)S(1)}, bf16[256,1024]{1,0:T(8,128)(2,1)S(1)}, u32[]{:S(2)}, u32[]{:S(2)}) collective-permute-start(bf16[256,1024]{1,0:T(8,128)(2,1)S(1)} %fusion.105), channel_id=1, source_target_pairs={{0,1},{1,0},{2,3},{3,2},{4,5},{5,4},{6,7},{7,6},{8,9},{9,8},{10,11... | collective-permute-start | bytes 1572872 | tf_op jit(solution)/shard_map/ppermute | solution.py:516
  425.1 43.4 %collective-permute-start.22 = (f32[256,1024]{1,0:T(8,128)}, f32[256,1024]{1,0:T(8,128)}, u32[]{:S(2)}, u32[]{:S(2)}) collective-permute-start(f32[256,1024]{1,0:T(8,128)} %broadcast_select_fusion.2), channel_id=1, source_target_pairs={{0,16},{16,0},{1,17},{17,1},{2,18},{18,2},{3,19},{19,3},{4,20},{20... | collective-permute-start | bytes 3145736 | tf_op jit(solution)/shard_map/ppermute | solution.py:512
  447.2 24.5 %collective-permute-start.19 = (bf16[256,1024]{1,0:T(8,128)(2,1)}, bf16[256,1024]{1,0:T(8,128)(2,1)}, u32[]{:S(2)}, u32[]{:S(2)}) collective-permute-start(bf16[256,1024]{1,0:T(8,128)(2,1)} %fusion.150), channel_id=1, source_target_pairs={{0,1},{1,0},{2,3},{3,2},{4,5},{5,4},{6,7},{7,6},{8,9},{9,8},{10,11... | collective-permute-start | bytes 1572872 | tf_op jit(solution)/shard_map/ppermute | solution.py:516
  452.4 21.7 %collective-permute-start.20 = (bf16[256,1024]{1,0:T(8,128)(2,1)}, bf16[256,1024]{1,0:T(8,128)(2,1)}, u32[]{:S(2)}, u32[]{:S(2)}) collective-permute-start(bf16[256,1024]{1,0:T(8,128)(2,1)} %fusion.159), channel_id=1, source_target_pairs={{0,1},{1,0},{2,3},{3,2},{4,5},{5,4},{6,7},{7,6},{8,9},{9,8},{10,11... | collective-permute-start | bytes 1572872 | tf_op jit(solution)/shard_map/ppermute | solution.py:516
  528.4 21.1 %collective-permute-start.25 = (bf16[256,1024]{1,0:T(8,128)(2,1)S(1)}, bf16[256,1024]{1,0:T(8,128)(2,1)S(1)}, u32[]{:S(2)}, u32[]{:S(2)}) collective-permute-start(bf16[256,1024]{1,0:T(8,128)(2,1)S(1)} %fusion.111), channel_id=1, source_target_pairs={{0,1},{1,0},{2,3},{3,2},{4,5},{5,4},{6,7},{7,6},{8,9},{9,8},{10,11... | collective-permute-start | bytes 1572872 | tf_op jit(solution)/shard_map/ppermute | solution.py:516
  552.4 20.0 %all-to-all-start = ((bf16[8,512,128]{2,1,0:T(8,128)(2,1)}), bf16[8,512,128]{2,1,0:T(8,128)(2,1)}, u32[]{:S(2)}, u32[]{:S(2)}) async-start(bf16[8,512,128]{2,1,0:T(8,128)(2,1)} %bitcast_bitcast_fusion), calls=%async_computation.1 | async-start | bytes 2097152 | tf_op jit(solution)/shard_map/all_to_all | solution.py:1440
  557.6 192.6 %reduce-scatter.8.cloned.1.call-start = ((), (), s32[]{:S(2)}) async-start(), calls=%async_computation.9 | async-start | bytes 4734976 | tf_op jit(solution)/shard_map/reduce_scatter | solution.py:572
  599.2 28.1 %collective-permute-start.26 = (bf16[2,4,272,128]{3,2,1,0:T(8,128)(2,1)}, bf16[2,4,272,128]{3,2,1,0:T(8,128)(2,1)}, u32[]{:S(2)}, u32[]{:S(2)}) collective-permute-start(bf16[2,4,272,128]{3,2,1,0:T(8,128)(2,1)} %get-tuple-element.224), channel_id=1, source_target_pairs={{0,4},{1,5},{2,6},{3,7},{16,20},{17,21},{18,22},{19,23}} | collective-permute-start | bytes 1671176 | tf_op jit(solution)/shard_map/ppermute | solution.py:549
  600.7 52.4 %collective-permute-start.27 = (bf16[2,4,272,128]{3,2,1,0:T(8,128)(2,1)}, bf16[2,4,272,128]{3,2,1,0:T(8,128)(2,1)}, u32[]{:S(2)}, u32[]{:S(2)}) collective-permute-start(bf16[2,4,272,128]{3,2,1,0:T(8,128)(2,1)} %get-tuple-element.223), channel_id=1, source_target_pairs={{12,8},{13,9},{14,10},{15,11},{28,24},{29,25},{30,26},{31,27}} | collective-permute-start | bytes 1671176 | tf_op jit(solution)/shard_map/ppermute | solution.py:549
  623.7 37.3 %all-to-all-start.1 = ((bf16[8,2,256,128]{3,2,1,0:T(8,128)(2,1)}), bf16[8,2,256,128]{3,2,1,0:T(8,128)(2,1)S(1)}, u32[]{:S(2)}, u32[]{:S(2)}) async-start(bf16[8,2,256,128]{3,2,1,0:T(8,128)(2,1)} %copy.449), calls=%async_computation.2 | async-start | bytes 2097152 | tf_op jit(solution)/shard_map/all_to_all | solution.py:1460
  679.2 22.8 %collective-permute-start.30 = (bf16[2,4,272,128]{3,2,1,0:T(8,128)(2,1)}, bf16[2,4,272,128]{3,2,1,0:T(8,128)(2,1)}, u32[]{:S(2)}, u32[]{:S(2)}) collective-permute-start(bf16[2,4,272,128]{3,2,1,0:T(8,128)(2,1)} %get-tuple-element.219), channel_id=1, source_target_pairs={{0,4},{4,8},{8,12},{1,5},{5,9},{9,13},{2,6},{6,10},{10,14},{3,7},{... | collective-permute-start | bytes 1671176 | tf_op jit(solution)/shard_map/ppermute | solution.py:549
  704.3 26.8 %all-to-all-start.2 = ((bf16[8,272,128]{2,1,0:T(8,128)(2,1)}), bf16[8,272,128]{2,1,0:T(8,128)(2,1)S(1)}, u32[]{:S(2)}, u32[]{:S(2)}) async-start(bf16[8,272,128]{2,1,0:T(8,128)(2,1)} %bitcast.334), calls=%async_computation.3 | async-start | bytes 1114112 | tf_op jit(solution)/shard_map/all_to_all | solution.py:1471
  (190 other events, 1292.2 us)
Sparse Core Ops, SparseCore 0:
  128.1 126.3 all-gather.1
  348.2 131.4 reduce-scatter.3
  483.7 170.4 reduce-scatter.5
  657.9 78.5 reduce-scatter.7

commit v7 on v5

--- a/solution.py
+++ b/solution.py
@@ -1207,7 +1207,12 @@
 
     picked = jnp.where(sec0, cotangent[0], cotangent[1])
     across = [(s * 4 + 2 * yy + xx, yy * 4 + 2 * s + xx) for s in range(2) for yy in range(2) for xx in range(2)]
-    cot_own = lax.ppermute(picked, both, across)
+    across = [(a, b) for a, b in across if a != b]
+
+    def over_rows(value):
+        return jnp.where(sec == y, value, lax.ppermute(value, both, across))
+
+    cot_own = over_rows(picked)
     cot_other = swap_x(cot_own)
     cot_pair = choose(x0, cot_own, cot_other)
     top_grad = jnp.concatenate(cot_pair, axis=0).astype(f32)
@@ -1320,7 +1325,7 @@
             ff_members.append(jnp.zeros((width, 128), bf16))
         partial = jnp.concatenate(attn_members + ff_members, axis=1)
         if layer == 0:
-            sums, (partial, output_rows) = after(sums, (partial, output_rows))
+            sums, partial = after(sums, partial)
         scattered.append(scatter_rows(partial))
         resid_grad, attn_branch, dq, gain_two_grad = [], [], [], None
         dkv = None
@@ -1333,8 +1338,6 @@
             if layer == 1 and c == 0:
                 attended_grad, lows = after(attended_grad, lows)
                 output = [member + pair_sum(low) for member, low in zip(resid_two_last, lows)]
-                row_block = lax.ppermute(jnp.where(x0, output[0], output[1]), both, across)
-                output_rows = jnp.stack(choose(sec0, row_block, swap_section(row_block)))
             own_dq, *dkv = attention_backward(
                 packed[c], kv_all, attended_grad, attended[c], lse[c], chunk_segs[c], key_segs, factor,
                 None if c == 0 else dkv,
@@ -1375,8 +1378,8 @@
     scattered.append(scatter_rows(jnp.concatenate(attn_members, axis=1)))
 
     lig_send = jnp.transpose(grad_in_low.reshape(half_frames, 8, block_width), (1, 0, 2))
-    lig_got = lax.all_to_all(lig_send, both, 0, 0, tiled=True).reshape(2, 2, 2, half_frames, block_width)
-    lig = jnp.transpose(lig_got[:, :, 0], (1, 0, 2, 3)).reshape(micro_count, row_frames, block_width)
+    lig_got = lax.all_to_all(lig_send, both, 0, 0, tiled=True).reshape(2, 2, 2, half_frames, block_width)[:, :, 0]
+    lig = jnp.transpose(lig_got, (1, 0, 2, 3)).reshape(micro_count, row_frames, block_width)
     conv_grad = (lig.astype(f32) * slope.astype(f32)).astype(bf16)
     grad_views = group_view(conv_grad, per_group)
     back = ungroup(conv_back(grad_views, bands), per_group)
@@ -1402,11 +1405,10 @@
         keep, send = choose(sec0, first, second)
         return choose(sec0, keep, swap_section(send))
 
-    def over_x(first, second):
-        keep, send = choose(x0, first, second)
-        return keep, choose(x0, keep, swap_x(send))
-
-    taps_sum, (_, gs_got) = sum_dp(taps_send, dp, (gs_send, gs_got))
+
+    row_block = over_rows(jnp.where(x0, output[0], output[1]).astype(bf16))
+    output_rows = jnp.stack(choose(sec0, row_block, swap_section(row_block))).astype(f32)
+    taps_sum, (_, gs_got, output_rows) = sum_dp(taps_send, dp, (gs_send, gs_got, output_rows))
     gs_rows = jnp.transpose(gs_got, (1, 2, 0, 3)).reshape(micro_count, frames, width).astype(f32)
     ends = jnp.where(sec0, gs_rows, output_rows)[None]
     taps_got = lax.all_to_all(
@@ -1422,25 +1424,34 @@
         0,
     ).astype(f32)
 
-    ff_sets = over_section(scattered[1][:, attn_cols:], scattered[0][:, :-128])
+    turned = [(t * 4 + 2 * r + c, c * 4 + 2 * r + t) for t in range(2) for r in range(2) for c in range(2) if t != c]
+    crossed = [(t * 4 + 2 * r + c, (1 - c) * 4 + 2 * r + t) for t in range(2) for r in range(2) for c in range(2)]
+
+    def home(first, second):
+        straight, other = choose(x0, first, second)
+        straight = jnp.where(sec == x, straight, lax.ppermute(straight, both, turned))
+        other = lax.ppermute(other, both, crossed)
+        return choose(sec0, straight, other)
+
+    ff_layers = (scattered[1][:, attn_cols:], scattered[0][:, :-128])
+    ff_sets = over_section(*(member[:, up_cols:] for member in ff_layers))
     down_grad = jnp.concatenate(
-        [member[:, up_cols + at : up_cols + at + width] for member in ff_sets for at in (0, width)],
-        axis=0,
+        [member[:, at : at + width] for member in ff_sets for at in (0, width)], axis=0
     ).astype(f32)[None]
-    _, up_sets = over_x(*(member[:, :up_cols] for member in ff_sets))
     up_grad = jnp.stack(
         [
             jnp.transpose(member.reshape(in_rows, 2, -1, 2, unit), (0, 2, 3, 1, 4))
-            for member in up_sets
+            for member in home(*(member[:, :up_cols] for member in ff_layers))
         ],
         axis=2,
     ).reshape(in_rows, -1).astype(f32)[None]
-
-    attn_sets = over_section(scattered[2], scattered[1][:, :attn_cols])
-    out_grad = jnp.concatenate([member[:, cut:attn_cols] for member in attn_sets], axis=1).astype(f32)[None]
-    keep, qkv_sets = over_x(*(member[:, :cut] for member in attn_sets))
-    norm1_grad = keep[:, qkv_cols].astype(f32)[None]
-    norm2_grad = keep[:, qkv_cols + 1].astype(f32)[None]
+    scattered[2], (up_grad, down_grad) = after(scattered[2], (up_grad, down_grad))
+    attn_layers = (scattered[2], scattered[1][:, :attn_cols])
+    attn_sets = over_section(*(member[:, cut:] for member in attn_layers))
+    out_grad = jnp.concatenate(attn_sets, axis=1).astype(f32)[None]
+    qkv_sets = home(*(member[:, :cut] for member in attn_layers))
+    norm1_grad = qkv_sets[0][:, qkv_cols].astype(f32)[None]
+    norm2_grad = qkv_sets[0][:, qkv_cols + 1].astype(f32)[None]
     qkv_grad = jnp.stack(
         [member[:, :qkv_cols].reshape(in_rows, -1, HEAD_DIM) for member in qkv_sets], axis=2
     ).reshape(in_rows, -1).astype(f32)[None]

time: 768 us -> 806 us (1.049); the launches traced: 754 us -> 802 us
  waiting for transfers between devices: 145 us -> 170 us
  other arithmetic: 97.6 us -> 117 us
  matrix products: 151 us -> 167 us
  starting transfers between devices: 84 us -> 72.2 us
    ppermute x6, waiting for transfers between devices: 40.9 us -> 63.7 us  [sum_dp(): running[way] = lax.ppermute(own, 'dp', live)]
    dot_general x24, matrix products: 28.1 us -> 43.9 us  [back(): lax.dot_general(left, right, (((1,), (1,)), ((), ())), preferred_element_...]
    all_to_all x1, starting transfers between devices: 14.8 us -> 4.4 us  [per_device_pairs(): lax.all_to_all(taps_sum.reshape(8, rows_here + 16, block_width), both, 0,...]
    ppermute x9, starting transfers between devices: 17.8 us -> 8.29 us  [swap_section(): return lax.ppermute(value, 'section', [(0, 1), (1, 0)])]
    ppermute x2 -> x6, starting transfers between devices: 5.67 us -> 15.1 us  [the longest x2 7.06 us: over_rows(): return jnp.where(sec == y, value, lax.ppermute(value, both, across))]
    unnamed x372 -> x340, local copies, waits for them, and re-layouts: 33.1 us -> 25.2 us
    ppermute x19 -> x17, waiting for transfers between devices: 63.2 us -> 71 us  [swap_x(): return lax.ppermute(value, 'seq', [(q, q ^ 1) for q in range(4)])]
  transfers between devices with their start and end apart: 44 -> 46, of which waited for: 24 -> 21; matrix products, arithmetic and copies ran while one was open for 36% -> 39% of each run, Pallas kernels for 8% -> 8%
where the time goes in v7:
time: 806 us; the launch traced here: 802 us
  waiting for transfers between devices  170 us (21%)
  Pallas kernels  168 us (21%)
  matrix products  167 us (21%)
  other arithmetic  117 us (15%)
  local copies, waits for them, and re-layouts  90.1 us (11%)
  starting transfers between devices  72.2 us (9%)
  between operations  17.2 us (2%)
    pallas_call x1, Pallas kernels, opening(): pl.pallas_call(functools.partial(opening_kernel, count, parts), in_specs=...  99.8 us
    ppermute x17, waiting for transfers between devices, swap_x(): return lax.ppermute(value, 'seq', [(q, q ^ 1) for q in range(4)])  71 us
    ppermute x6, waiting for transfers between devices, sum_dp(): running[way] = lax.ppermute(own, 'dp', live)  63.7 us
    dot_general x24, matrix products, back(): lax.dot_general(left, right, (((1,), (1,)), ((), ())), preferred_element_...  43.9 us
    pallas_call x4, Pallas kernels, attention_backward(): pl.pallas_call(functools.partial(attention_backward_kernel, factor), grid...  41.9 us
    dot_general x12, matrix products, outer(): lax.dot_general(left, right, (((0,), (0,)), ((), ())), preferred_element_...  32.2 us
    dot_general x8, matrix products, per_device_pairs(): hidden_pre = jnp.dot(normed_two[c], w_up[part], preferred_element_type=f32)  29.5 us
    pallas_call x4, Pallas kernels, attention_forward(): pl.pallas_call(functools.partial(attention_forward_kernel, factor), grid=...  26.7 us
  transfers between devices with their start and end apart: 46, of which 21 were waited for; matrix products, arithmetic and copies ran while one was open for 39% of the time, Pallas kernels for 8%

profile of v7, /device:TPU:17, one launch (start us, length us, event | category | flops | bytes accessed | tf_op | source)
XLA Modules:
  0.0 801.8 jit_solution(219473985001829627)
XLA Ops:
  26.9 99.8 %opening.1 = (bf16[4,8,272,128]{3,2,1,0:T(8,128)(2,1)S(1)}, bf16[4,2,256,128]{3,2,1,0:T(8,128)(2,1)S(1)}, bf16[4,2,2,64,6400]{4,3,2,1,0:T(8,128)(2,1)S(1)}, bf16[64,6400]{1,0:T(8,128)(2,1)S(1)}) custom-call(bf16[8,272,128]{2,1,0:T(8,128)(2,1)S(1)} %fusion.403.conv_ref, bf16[4,2,256,128]{3,2,1,0:T(8,128)(2,1)S(1)} %bitcast.293, ...), custom_call_target="tpu_custom_call" | custom-call | tf_op jit(solution)/shard_map/opening/pallas_call | solution.py:851
  143.2 6.2 fusion.424
  151.6 12.9 %fusion.20 = bf16[8448,256]{1,0:T(8,128)(2,1)S(1)} fusion(bf16[8192,64]{1,0:T(8,128)(2,1)S(1)} %copy-done.56), kind=kLoop, calls=%fused_computation.29 | loop fusion | flops 43253760 | bytes 5373952 | tf_op jit(solution)/shard_map/concatenate | solution.py:1054
  187.7 7.8 all-to-all-done
  209.1 7.0 attention_forward.4
  220.8 6.6 attention_forward.5
  241.8 11.9 %collective-permute-done.6 = bf16[256,1024]{1,0:T(8,128)(2,1)S(1)} collective-permute-done((bf16[256,1024]{1,0:T(8,128)(2,1)S(1)}, bf16[256,1024]{1,0:T(8,128)(2,1)S(1)}, u32[]{:S(2)}, u32[]{:S(2)}) %collective-permute-start.6) | collective-permute-done | bytes 524320 | tf_op jit(solution)/shard_map/ppermute | solution.py:516
  285.4 6.4 collective-permute-done.7
  297.9 6.6 attention_forward.6
  306.4 6.6 attention_forward.7
  333.8 8.2 %collective-permute-done.11 = bf16[256,1024]{1,0:T(8,128)(2,1)S(1)} collective-permute-done((bf16[256,1024]{1,0:T(8,128)(2,1)S(1)}, bf16[256,1024]{1,0:T(8,128)(2,1)S(1)}, u32[]{:S(2)}, u32[]{:S(2)}) %collective-permute-start.11) | collective-permute-done | bytes 524320 | tf_op jit(solution)/shard_map/ppermute | solution.py:516
  378.8 10.4 %attention_backward.4 = (bf16[256,512]{1,0:T(8,128)(2,1)S(1)}, f32[1024,512]{1,0:T(8,128)S(1)}, f32[1024,512]{1,0:T(8,128)}) custom-call(bf16[256,1536]{1,0:T(8,128)(2,1)S(1)} %copy-done.7, bf16[1024,1024]{1,0:T(8,128)(2,1)} %copy-done.1, bf16[1024,1024]{1,0:T(8,128)(2,1)} %copy-done.1, bf16[256,512]{1,0:T(8,128)(2,1)S(1)} %convolution_convert_fusion.15.g_ref, ...), custom_call_target="tpu_custom_call" | custom-call | flops 2684354560 | bytes 5242880 | tf_op jit(solution)/shard_map/attention_backward/pallas_call | solution.py:1007
  391.8 10.5 %attention_backward.5 = (bf16[256,512]{1,0:T(8,128)(2,1)S(1)}, f32[1024,512]{1,0:T(8,128)S(1)}, f32[1024,512]{1,0:T(8,128)}) custom-call(bf16[256,1536]{1,0:T(8,128)(2,1)S(1)} %convolution_convert_fusion.2.q_ref, bf16[1024,1024]{1,0:T(8,128)(2,1)} %copy-done.1, bf16[1024,1024]{1,0:T(8,128)(2,1)} %copy-done.1, ...), custom_call_target="tpu_custom_call" | custom-call | flops 2684354560 | bytes 5242880 | tf_op jit(solution)/shard_map/attention_backward/pallas_call | solution.py:1007
  437.1 10.7 %collective-permute-done.18 = bf16[256,1024]{1,0:T(8,128)(2,1)S(1)} collective-permute-done((bf16[256,1024]{1,0:T(8,128)(2,1)S(1)}, bf16[256,1024]{1,0:T(8,128)(2,1)S(1)}, u32[]{:S(2)}, u32[]{:S(2)}) %collective-permute-start.18) | collective-permute-done | bytes 524320 | tf_op jit(solution)/shard_map/ppermute | solution.py:516
  500.8 10.1 %attention_backward.6 = (bf16[256,512]{1,0:T(8,128)(2,1)S(1)}, f32[1024,512]{1,0:T(8,128)S(1)}, f32[1024,512]{1,0:T(8,128)}) custom-call(bf16[256,1536]{1,0:T(8,128)(2,1)S(1)} %copy-done.5, bf16[1024,1024]{1,0:T(8,128)(2,1)} %copy-done, bf16[1024,1024]{1,0:T(8,128)(2,1)} %copy-done, bf16[256,512]{1,0:T(8,128)(2,1)S(1)} %convolution_convert_fusion.13.g_ref, ...), custom_call_target="tpu_custom_call" | custom-call | flops 2684354560 | bytes 5242880 | tf_op jit(solution)/shard_map/attention_backward/pallas_call | solution.py:1007
  513.8 11.0 %attention_backward.7 = (bf16[256,512]{1,0:T(8,128)(2,1)S(1)}, f32[1024,512]{1,0:T(8,128)S(1)}, f32[1024,512]{1,0:T(8,128)}) custom-call(bf16[256,1536]{1,0:T(8,128)(2,1)S(1)} %copy-done.3, bf16[1024,1024]{1,0:T(8,128)(2,1)} %copy-done, bf16[1024,1024]{1,0:T(8,128)(2,1)} %copy-done, bf16[256,512]{1,0:T(8,128)(2,1)S(1)} %convolution_convert_fusion.12.g_ref, ...), custom_call_target="tpu_custom_call" | custom-call | flops 2684354560 | bytes 5242880 | tf_op jit(solution)/shard_map/attention_backward/pallas_call | solution.py:1007
  556.9 10.6 %collective-permute-done.23 = bf16[256,1024]{1,0:T(8,128)(2,1)S(1)} collective-permute-done((bf16[256,1024]{1,0:T(8,128)(2,1)S(1)}, bf16[256,1024]{1,0:T(8,128)(2,1)S(1)}, u32[]{:S(2)}, u32[]{:S(2)}) %collective-permute-start.23) | collective-permute-done | bytes 524320 | tf_op jit(solution)/shard_map/ppermute | solution.py:516
  578.7 10.6 %all-to-all-done.1 = bf16[8,512,128]{2,1,0:T(8,128)(2,1)S(1)} async-done(((bf16[8,512,128]{2,1,0:T(8,128)(2,1)}), bf16[8,512,128]{2,1,0:T(8,128)(2,1)S(1)}, u32[]{:S(2)}, u32[]{:S(2)}) %all-to-all-start.1) | async-done | bytes 1048608 | tf_op jit(solution)/shard_map/all_to_all | solution.py:1381
  592.6 8.7 %fusion.426 = f32[33,256,256]{2,1,0:T(8,128)} fusion(bf16[2,256,256]{2,1,0:T(8,128)(2,1)S(1)} %copy-done.120, bf16[2,256,256]{2,1,0:T(8,128)(2,1)S(1)} %reshape.624), kind=kOutput, calls=%fused_computation.680 | convolution fusion | flops 2143289344 | bytes 9175040 | tf_op jit(solution)/shard_map/conv_general_dilated | solution.py:1105
  609.9 8.3 %fusion.22 = bf16[8192,64]{1,0:T(8,128)(2,1)S(1)} fusion(f32[8448,256]{1,0:T(8,128)} %bitcast.326), kind=kLoop, calls=%fused_computation.35 | loop fusion | flops 2097152 | bytes 9437184 | tf_op jit(solution)/shard_map/convert.32
  658.7 17.0 %collective-permute-done.25 = bf16[2,4,272,128]{3,2,1,0:T(8,128)(2,1)} collective-permute-done((bf16[2,4,272,128]{3,2,1,0:T(8,128)(2,1)}, bf16[2,4,272,128]{3,2,1,0:T(8,128)(2,1)}, u32[]{:S(2)}, u32[]{:S(2)}) %collective-permute-start.25) | collective-permute-done | bytes 557088 | tf_op jit(solution)/shard_map/ppermute | solution.py:549
  686.3 20.0 %collective-permute-done.27 = bf16[2,4,272,128]{3,2,1,0:T(8,128)(2,1)} collective-permute-done((bf16[2,4,272,128]{3,2,1,0:T(8,128)(2,1)}, bf16[2,4,272,128]{3,2,1,0:T(8,128)(2,1)}, u32[]{:S(2)}, u32[]{:S(2)}) %collective-permute-start.27) | collective-permute-done | bytes 557088 | tf_op jit(solution)/shard_map/ppermute | solution.py:549
  706.2 10.3 %collective-permute-done.26 = bf16[2,4,272,128]{3,2,1,0:T(8,128)(2,1)} collective-permute-done((bf16[2,4,272,128]{3,2,1,0:T(8,128)(2,1)}, bf16[2,4,272,128]{3,2,1,0:T(8,128)(2,1)}, u32[]{:S(2)}, u32[]{:S(2)}) %collective-permute-start.26) | collective-permute-done | bytes 557088 | tf_op jit(solution)/shard_map/ppermute | solution.py:549
  727.9 16.4 %collective-permute-done.29 = bf16[2,4,272,128]{3,2,1,0:T(8,128)(2,1)} collective-permute-done((bf16[2,4,272,128]{3,2,1,0:T(8,128)(2,1)}, bf16[2,4,272,128]{3,2,1,0:T(8,128)(2,1)}, u32[]{:S(2)}, u32[]{:S(2)}) %collective-permute-start.29) | collective-permute-done | bytes 557088 | tf_op jit(solution)/shard_map/ppermute | solution.py:549
  (737 shorter events, 450.2 us)
Async XLA Ops:
  7.2 259.9 %all-gather.2.cloned.1.call-start = ((), (), s32[]{:S(2)}) async-start(), calls=%async_computation.7 | async-start | bytes 13926400 | tf_op jit(solution)/shard_map/all_gather | solution.py:566
  176.3 19.2 %all-to-all-start = ((bf16[8,512,128]{2,1,0:T(8,128)(2,1)}), bf16[8,512,128]{2,1,0:T(8,128)(2,1)S(1)}, u32[]{:S(2)}, u32[]{:S(2)}) async-start(bf16[8,512,128]{2,1,0:T(8,128)(2,1)} %bitcast.29), calls=%async_computation | async-start | bytes 2097152 | tf_op jit(solution)/shard_map/all_to_all | solution.py:1232
  180.7 344.1 %reduce-scatter.4.cloned.1.call-start = ((), (), s32[]{:S(2)}) async-start(), calls=%async_computation.8 | async-start | bytes 9191424 | tf_op jit(solution)/shard_map/reduce_scatter | solution.py:572
  181.5 37.6 %collective-permute-start = (bf16[256,1024]{1,0:T(8,128)(2,1)}, bf16[256,1024]{1,0:T(8,128)(2,1)}, u32[]{:S(2)}, u32[]{:S(2)}) collective-permute-start(bf16[256,1024]{1,0:T(8,128)(2,1)} %select_bitcast_fusion.2), channel_id=1, source_target_pairs={{2,16},{3,17},{16,2},{17,3},{6,20},{7,21},{20,6},{21,7},{10,24},{1... | collective-permute-start | bytes 1572872 | tf_op jit(solution)/shard_map/ppermute | solution.py:1213
  220.3 74.7 %collective-permute-start.1 = (bf16[256,1024]{1,0:T(8,128)(2,1)S(1)}, bf16[256,1024]{1,0:T(8,128)(2,1)S(1)}, u32[]{:S(2)}, u32[]{:S(2)}) collective-permute-start(bf16[256,1024]{1,0:T(8,128)(2,1)S(1)} %broadcast_select_fusion.3), channel_id=1, source_target_pairs={{0,1},{1,0},{2,3},{3,2},{4,5},{5,4},{6,7},{7,6},{8,9},{9,8},{10,11... | collective-permute-start | bytes 1572872 | tf_op jit(solution)/shard_map/ppermute | solution.py:516
  227.9 25.7 %collective-permute-start.6 = (bf16[256,1024]{1,0:T(8,128)(2,1)S(1)}, bf16[256,1024]{1,0:T(8,128)(2,1)S(1)}, u32[]{:S(2)}, u32[]{:S(2)}) collective-permute-start(bf16[256,1024]{1,0:T(8,128)(2,1)S(1)} %convolution_convert_fusion.10), channel_id=1, source_target_pairs={{0,1},{1,0},{2,3},{3,2},{4,5},{5,4},{6,7},{7,6},{8,9},{9,8},{10,11... | collective-permute-start | bytes 1572872 | tf_op jit(solution)/shard_map/ppermute | solution.py:516
  313.5 19.7 %collective-permute-start.12 = (bf16[256,1024]{1,0:T(8,128)(2,1)S(1)}, bf16[256,1024]{1,0:T(8,128)(2,1)S(1)}, u32[]{:S(2)}, u32[]{:S(2)}) collective-permute-start(bf16[256,1024]{1,0:T(8,128)(2,1)S(1)} %convolution_convert_fusion.8), channel_id=1, source_target_pairs={{0,1},{1,0},{2,3},{3,2},{4,5},{5,4},{6,7},{7,6},{8,9},{9,8},{10,11... | collective-permute-start | bytes 1572872 | tf_op jit(solution)/shard_map/ppermute | solution.py:516
  368.3 392.0 %reduce-scatter.6.cloned.1.call-start = ((), (), s32[]{:S(2)}) async-start(), calls=%async_computation.9 | async-start | bytes 13647872 | tf_op jit(solution)/shard_map/reduce_scatter | solution.py:572
  377.3 25.0 %collective-permute-start.14 = (bf16[256,1024]{1,0:T(8,128)(2,1)S(1)}, bf16[256,1024]{1,0:T(8,128)(2,1)S(1)}, u32[]{:S(2)}, u32[]{:S(2)}) collective-permute-start(bf16[256,1024]{1,0:T(8,128)(2,1)S(1)} %copy-done.102), channel_id=1, source_target_pairs={{0,1},{1,0},{2,3},{3,2},{4,5},{5,4},{6,7},{7,6},{8,9},{9,8},{10,11... | collective-permute-start | bytes 1572872 | tf_op jit(solution)/shard_map/ppermute | solution.py:516
  377.6 25.7 %collective-permute-start.15 = (bf16[256,1024]{1,0:T(8,128)(2,1)S(1)}, bf16[256,1024]{1,0:T(8,128)(2,1)S(1)}, u32[]{:S(2)}, u32[]{:S(2)}) collective-permute-start(bf16[256,1024]{1,0:T(8,128)(2,1)S(1)} %fusion.132), channel_id=1, source_target_pairs={{0,1},{1,0},{2,3},{3,2},{4,5},{5,4},{6,7},{7,6},{8,9},{9,8},{10,11... | collective-permute-start | bytes 1572872 | tf_op jit(solution)/shard_map/ppermute | solution.py:516
  426.0 21.7 %collective-permute-start.18 = (bf16[256,1024]{1,0:T(8,128)(2,1)S(1)}, bf16[256,1024]{1,0:T(8,128)(2,1)S(1)}, u32[]{:S(2)}, u32[]{:S(2)}) collective-permute-start(bf16[256,1024]{1,0:T(8,128)(2,1)S(1)} %fusion.105), channel_id=1, source_target_pairs={{0,1},{1,0},{2,3},{3,2},{4,5},{5,4},{6,7},{7,6},{8,9},{9,8},{10,11... | collective-permute-start | bytes 1572872 | tf_op jit(solution)/shard_map/ppermute | solution.py:516
  463.3 25.7 %collective-permute-start.19 = (bf16[256,1024]{1,0:T(8,128)(2,1)}, bf16[256,1024]{1,0:T(8,128)(2,1)}, u32[]{:S(2)}, u32[]{:S(2)}) collective-permute-start(bf16[256,1024]{1,0:T(8,128)(2,1)} %fusion.150), channel_id=1, source_target_pairs={{0,1},{1,0},{2,3},{3,2},{4,5},{5,4},{6,7},{7,6},{8,9},{9,8},{10,11... | collective-permute-start | bytes 1572872 | tf_op jit(solution)/shard_map/ppermute | solution.py:516
  545.8 21.7 %collective-permute-start.23 = (bf16[256,1024]{1,0:T(8,128)(2,1)S(1)}, bf16[256,1024]{1,0:T(8,128)(2,1)S(1)}, u32[]{:S(2)}, u32[]{:S(2)}) collective-permute-start(bf16[256,1024]{1,0:T(8,128)(2,1)S(1)} %fusion.111), channel_id=1, source_target_pairs={{0,1},{1,0},{2,3},{3,2},{4,5},{5,4},{6,7},{7,6},{8,9},{9,8},{10,11... | collective-permute-start | bytes 1572872 | tf_op jit(solution)/shard_map/ppermute | solution.py:516
  570.4 18.9 %all-to-all-start.1 = ((bf16[8,512,128]{2,1,0:T(8,128)(2,1)}), bf16[8,512,128]{2,1,0:T(8,128)(2,1)S(1)}, u32[]{:S(2)}, u32[]{:S(2)}) async-start(bf16[8,512,128]{2,1,0:T(8,128)(2,1)} %bitcast_bitcast_fusion), calls=%async_computation.2 | async-start | bytes 2097152 | tf_op jit(solution)/shard_map/all_to_all | solution.py:1381
  574.5 205.5 %reduce-scatter.8.cloned.1.call-start = ((), (), s32[]{:S(2)}) async-start(), calls=%async_computation.10 | async-start | bytes 4734976 | tf_op jit(solution)/shard_map/reduce_scatter | solution.py:572
  643.2 32.5 %collective-permute-start.25 = (bf16[2,4,272,128]{3,2,1,0:T(8,128)(2,1)}, bf16[2,4,272,128]{3,2,1,0:T(8,128)(2,1)}, u32[]{:S(2)}, u32[]{:S(2)}) collective-permute-start(bf16[2,4,272,128]{3,2,1,0:T(8,128)(2,1)} %get-tuple-element.228), channel_id=1, source_target_pairs={{12,8},{13,9},{14,10},{15,11},{28,24},{29,25},{30,26},{31,27}} | collective-permute-start | bytes 1671176 | tf_op jit(solution)/shard_map/ppermute | solution.py:549
  644.5 31.2 %collective-permute-start.24 = (bf16[2,4,272,128]{3,2,1,0:T(8,128)(2,1)}, bf16[2,4,272,128]{3,2,1,0:T(8,128)(2,1)}, u32[]{:S(2)}, u32[]{:S(2)}) collective-permute-start(bf16[2,4,272,128]{3,2,1,0:T(8,128)(2,1)} %get-tuple-element.229), channel_id=1, source_target_pairs={{0,4},{1,5},{2,6},{3,7},{16,20},{17,21},{18,22},{19,23}} | collective-permute-start | bytes 1671176 | tf_op jit(solution)/shard_map/ppermute | solution.py:549
  647.5 38.8 %all-to-all-start.2 = ((bf16[8,2,256,128]{3,2,1,0:T(8,128)(2,1)}), bf16[8,2,256,128]{3,2,1,0:T(8,128)(2,1)S(1)}, u32[]{:S(2)}, u32[]{:S(2)}) async-start(bf16[8,2,256,128]{3,2,1,0:T(8,128)(2,1)} %copy.421), calls=%async_computation.3 | async-start | bytes 2097152 | tf_op jit(solution)/shard_map/all_to_all | solution.py:1401
  655.2 28.5 %collective-permute-start.30 = (bf16[256,1024]{1,0:T(8,128)(2,1)}, bf16[256,1024]{1,0:T(8,128)(2,1)}, u32[]{:S(2)}, u32[]{:S(2)}) collective-permute-start(bf16[256,1024]{1,0:T(8,128)(2,1)} %select_convert_fusion), channel_id=1, source_target_pairs={{2,16},{3,17},{16,2},{17,3},{6,20},{7,21},{20,6},{21,7},{10,24},{1... | collective-permute-start | bytes 1572872 | tf_op jit(solution)/shard_map/ppermute | solution.py:1213
  678.2 28.0 %collective-permute-start.27 = (bf16[2,4,272,128]{3,2,1,0:T(8,128)(2,1)}, bf16[2,4,272,128]{3,2,1,0:T(8,128)(2,1)}, u32[]{:S(2)}, u32[]{:S(2)}) collective-permute-start(bf16[2,4,272,128]{3,2,1,0:T(8,128)(2,1)} %get-tuple-element.226), channel_id=1, source_target_pairs={{8,4},{12,8},{9,5},{13,9},{10,6},{14,10},{11,7},{15,11},{24,20},{2... | collective-permute-start | bytes 1671176 | tf_op jit(solution)/shard_map/ppermute | solution.py:549
  682.3 34.3 %collective-permute-start.26 = (bf16[2,4,272,128]{3,2,1,0:T(8,128)(2,1)}, bf16[2,4,272,128]{3,2,1,0:T(8,128)(2,1)}, u32[]{:S(2)}, u32[]{:S(2)}) collective-permute-start(bf16[2,4,272,128]{3,2,1,0:T(8,128)(2,1)} %get-tuple-element.227), channel_id=1, source_target_pairs={{0,4},{4,8},{1,5},{5,9},{2,6},{6,10},{3,7},{7,11},{16,20},{20,24},... | collective-permute-start | bytes 1671176 | tf_op jit(solution)/shard_map/ppermute | solution.py:549
  685.5 39.6 %collective-permute-start.31 = (bf16[256,1024]{1,0:T(8,128)(2,1)}, bf16[256,1024]{1,0:T(8,128)(2,1)}, u32[]{:S(2)}, u32[]{:S(2)}) collective-permute-start(bf16[256,1024]{1,0:T(8,128)(2,1)} %broadcast_select_fusion.2), channel_id=1, source_target_pairs={{0,16},{16,0},{1,17},{17,1},{2,18},{18,2},{3,19},{19,3},{4,20},{20... | collective-permute-start | bytes 1572872 | tf_op jit(solution)/shard_map/ppermute | solution.py:512
  719.1 25.3 %collective-permute-start.29 = (bf16[2,4,272,128]{3,2,1,0:T(8,128)(2,1)}, bf16[2,4,272,128]{3,2,1,0:T(8,128)(2,1)}, u32[]{:S(2)}, u32[]{:S(2)}) collective-permute-start(bf16[2,4,272,128]{3,2,1,0:T(8,128)(2,1)} %get-tuple-element.224), channel_id=1, source_target_pairs={{4,0},{8,4},{12,8},{5,1},{9,5},{13,9},{6,2},{10,6},{14,10},{7,3},{... | collective-permute-start | bytes 1671176 | tf_op jit(solution)/shard_map/ppermute | solution.py:549
  721.0 23.3 %collective-permute-start.28 = (bf16[2,4,272,128]{3,2,1,0:T(8,128)(2,1)}, bf16[2,4,272,128]{3,2,1,0:T(8,128)(2,1)}, u32[]{:S(2)}, u32[]{:S(2)}) collective-permute-start(bf16[2,4,272,128]{3,2,1,0:T(8,128)(2,1)} %get-tuple-element.225), channel_id=1, source_target_pairs={{0,4},{4,8},{8,12},{1,5},{5,9},{9,13},{2,6},{6,10},{10,14},{3,7},{... | collective-permute-start | bytes 1671176 | tf_op jit(solution)/shard_map/ppermute | solution.py:549
  (188 other events, 1507.9 us)
Sparse Core Ops, SparseCore 0:
  132.5 134.5 all-gather.1
  368.5 120.6 reduce-scatter.3
  493.8 159.2 reduce-scatter.5
  656.8 86.0 reduce-scatter.7

commit v8 on v7

--- a/solution.py
+++ b/solution.py
@@ -1207,12 +1207,7 @@
 
     picked = jnp.where(sec0, cotangent[0], cotangent[1])
     across = [(s * 4 + 2 * yy + xx, yy * 4 + 2 * s + xx) for s in range(2) for yy in range(2) for xx in range(2)]
-    across = [(a, b) for a, b in across if a != b]
-
-    def over_rows(value):
-        return jnp.where(sec == y, value, lax.ppermute(value, both, across))
-
-    cot_own = over_rows(picked)
+    cot_own = lax.ppermute(picked, both, across)
     cot_other = swap_x(cot_own)
     cot_pair = choose(x0, cot_own, cot_other)
     top_grad = jnp.concatenate(cot_pair, axis=0).astype(f32)
@@ -1325,7 +1320,7 @@
             ff_members.append(jnp.zeros((width, 128), bf16))
         partial = jnp.concatenate(attn_members + ff_members, axis=1)
         if layer == 0:
-            sums, partial = after(sums, partial)
+            sums, (partial, output_rows) = after(sums, (partial, output_rows))
         scattered.append(scatter_rows(partial))
         resid_grad, attn_branch, dq, gain_two_grad = [], [], [], None
         dkv = None
@@ -1338,6 +1333,8 @@
             if layer == 1 and c == 0:
                 attended_grad, lows = after(attended_grad, lows)
                 output = [member + pair_sum(low) for member, low in zip(resid_two_last, lows)]
+                row_block = lax.ppermute(jnp.where(x0, output[0], output[1]), both, across)
+                output_rows = jnp.stack(choose(sec0, row_block, swap_section(row_block)))
             own_dq, *dkv = attention_backward(
                 packed[c], kv_all, attended_grad, attended[c], lse[c], chunk_segs[c], key_segs, factor,
                 None if c == 0 else dkv,
@@ -1378,8 +1375,8 @@
     scattered.append(scatter_rows(jnp.concatenate(attn_members, axis=1)))
 
     lig_send = jnp.transpose(grad_in_low.reshape(half_frames, 8, block_width), (1, 0, 2))
-    lig_got = lax.all_to_all(lig_send, both, 0, 0, tiled=True).reshape(2, 2, 2, half_frames, block_width)[:, :, 0]
-    lig = jnp.transpose(lig_got, (1, 0, 2, 3)).reshape(micro_count, row_frames, block_width)
+    lig_got = lax.all_to_all(lig_send, both, 0, 0, tiled=True).reshape(2, 2, 2, half_frames, block_width)
+    lig = jnp.transpose(lig_got[:, :, 0], (1, 0, 2, 3)).reshape(micro_count, row_frames, block_width)
     conv_grad = (lig.astype(f32) * slope.astype(f32)).astype(bf16)
     grad_views = group_view(conv_grad, per_group)
     back = ungroup(conv_back(grad_views, bands), per_group)
@@ -1406,9 +1403,7 @@
         return choose(sec0, keep, swap_section(send))
 
 
-    row_block = over_rows(jnp.where(x0, output[0], output[1]).astype(bf16))
-    output_rows = jnp.stack(choose(sec0, row_block, swap_section(row_block))).astype(f32)
-    taps_sum, (_, gs_got, output_rows) = sum_dp(taps_send, dp, (gs_send, gs_got, output_rows))
+    taps_sum, (_, gs_got) = sum_dp(taps_send, dp, (gs_send, gs_got))
     gs_rows = jnp.transpose(gs_got, (1, 2, 0, 3)).reshape(micro_count, frames, width).astype(f32)
     ends = jnp.where(sec0, gs_rows, output_rows)[None]
     taps_got = lax.all_to_all(

time: 806 us -> 767 us (0.952)
  waiting for transfers between devices: 170 us -> 139 us
  other arithmetic: 117 us -> 99.7 us
  matrix products: 167 us -> 151 us
  starting transfers between devices: 72.2 us -> 84.7 us
    ppermute x6, waiting for transfers between devices: 63.7 us -> 43.7 us  [sum_dp(): running[way] = lax.ppermute(own, 'dp', live)]
    ppermute x17, waiting for transfers between devices: 71 us -> 54.8 us  [swap_x(): return lax.ppermute(value, 'seq', [(q, q ^ 1) for q in range(4)])]
    dot_general x24, matrix products: 43.9 us -> 28.2 us  [back(): lax.dot_general(left, right, (((1,), (1,)), ((), ())), preferred_element_...]
    ppermute x9, starting transfers between devices: 8.29 us -> 17.9 us  [swap_section(): return lax.ppermute(value, 'section', [(0, 1), (1, 0)])]
    unnamed x340 -> x372, local copies, waits for them, and re-layouts: 25.2 us -> 32.5 us
  transfers between devices with their start and end apart: 46 -> 46, of which waited for: 21 -> 24; matrix products, arithmetic and copies ran while one was open for 39% -> 37% of each run, Pallas kernels for 8% -> 8%
where the time goes in v8:
time: 767 us; the launch traced here: 756 us
  Pallas kernels  167 us (22%)
  matrix products  151 us (20%)
  waiting for transfers between devices  139 us (18%)
  other arithmetic  99.7 us (13%)
  local copies, waits for them, and re-layouts  96.2 us (13%)
  starting transfers between devices  84.7 us (11%)
  between operations  17.4 us (2%)
    pallas_call x1, Pallas kernels, opening(): pl.pallas_call(functools.partial(opening_kernel, count, parts), in_specs=...  99.8 us
    ppermute x17, waiting for transfers between devices, swap_x(): return lax.ppermute(value, 'seq', [(q, q ^ 1) for q in range(4)])  54.8 us
    ppermute x6, waiting for transfers between devices, sum_dp(): running[way] = lax.ppermute(own, 'dp', live)  43.7 us
    pallas_call x4, Pallas kernels, attention_backward(): pl.pallas_call(functools.partial(attention_backward_kernel, factor), grid...  40.9 us
    dot_general x12, matrix products, outer(): lax.dot_general(left, right, (((0,), (0,)), ((), ())), preferred_element_...  34.6 us
    unnamed x372, local copies, waits for them, and re-layouts  32.5 us
    dot_general x8, matrix products, per_device_pairs(): hidden_pre = jnp.dot(normed_two[c], w_up[part], preferred_element_type=f32)  31.7 us
    dot_general x24, matrix products, back(): lax.dot_general(left, right, (((1,), (1,)), ((), ())), preferred_element_...  28.2 us
  transfers between devices with their start and end apart: 46, of which 24 were waited for; matrix products, arithmetic and copies ran while one was open for 37% of the time, Pallas kernels for 8%

profile of v8, /device:TPU:17, one launch (start us, length us, event | category | flops | bytes accessed | tf_op | source)
XLA Modules:
  0.0 755.9 jit_solution(7411435477101408725)
XLA Ops:
  22.4 99.8 %opening.1 = (bf16[4,8,272,128]{3,2,1,0:T(8,128)(2,1)S(1)}, bf16[4,2,256,128]{3,2,1,0:T(8,128)(2,1)S(1)}, bf16[4,2,2,64,6400]{4,3,2,1,0:T(8,128)(2,1)S(1)}, bf16[64,6400]{1,0:T(8,128)(2,1)S(1)}) custom-call(bf16[8,272,128]{2,1,0:T(8,128)(2,1)S(1)} %fusion.403.conv_ref, bf16[4,2,256,128]{3,2,1,0:T(8,128)(2,1)S(1)} %bitcast.291, ...), custom_call_target="tpu_custom_call" | custom-call | tf_op jit(solution)/shard_map/opening/pallas_call | solution.py:851
  144.6 6.8 fusion.17
  175.5 7.8 %all-to-all-done = bf16[8,512,128]{2,1,0:T(8,128)(2,1)S(1)} async-done(((bf16[8,512,128]{2,1,0:T(8,128)(2,1)}), bf16[8,512,128]{2,1,0:T(8,128)(2,1)S(1)}, u32[]{:S(2)}, u32[]{:S(2)}) %all-to-all-start) | async-done | bytes 1048608 | tf_op jit(solution)/shard_map/all_to_all | solution.py:1227
  197.3 6.8 attention_forward.4
  207.1 6.6 attention_forward.5
  233.3 8.2 %collective-permute-done.6 = bf16[256,1024]{1,0:T(8,128)(2,1)S(1)} collective-permute-done((bf16[256,1024]{1,0:T(8,128)(2,1)S(1)}, bf16[256,1024]{1,0:T(8,128)(2,1)S(1)}, u32[]{:S(2)}, u32[]{:S(2)}) %collective-permute-start.6) | collective-permute-done | bytes 524320 | tf_op jit(solution)/shard_map/ppermute | solution.py:516
  251.3 7.9 %all-gather.2.cloned.1.call-done = bf16[1024,6400]{1,0:T(8,128)(2,1)} async-done(((bf16[64,6400]{1,0:T(8,128)(2,1)}), bf16[1024,6400]{1,0:T(8,128)(2,1)}) %all-gather.2.cloned.1.call-update) | async-done | bytes 13107216 | tf_op jit(solution)/shard_map/all_gather | solution.py:566
  275.7 8.3 %collective-permute-done.7 = bf16[256,1024]{1,0:T(8,128)(2,1)S(1)} collective-permute-done((bf16[256,1024]{1,0:T(8,128)(2,1)S(1)}, bf16[256,1024]{1,0:T(8,128)(2,1)S(1)}, u32[]{:S(2)}, u32[]{:S(2)}) %collective-permute-start.7) | collective-permute-done | bytes 524320 | tf_op jit(solution)/shard_map/ppermute | solution.py:516
  291.4 6.6 attention_forward.6
  300.9 6.7 attention_forward.7
  357.7 7.6 %collective-permute-done.11 = bf16[256,1024]{1,0:T(8,128)(2,1)} collective-permute-done((bf16[256,1024]{1,0:T(8,128)(2,1)S(1)}, bf16[256,1024]{1,0:T(8,128)(2,1)}, u32[]{:S(2)}, u32[]{:S(2)}) %collective-permute-start.11) | collective-permute-done | bytes 524320 | tf_op jit(solution)/shard_map/ppermute | solution.py:516
  373.8 10.0 %attention_backward.4 = (bf16[256,512]{1,0:T(8,128)(2,1)S(1)}, f32[1024,512]{1,0:T(8,128)S(1)}, f32[1024,512]{1,0:T(8,128)}) custom-call(bf16[256,1536]{1,0:T(8,128)(2,1)S(1)} %copy-done.8, bf16[1024,1024]{1,0:T(8,128)(2,1)} %copy-done.1, bf16[1024,1024]{1,0:T(8,128)(2,1)} %copy-done.1, bf16[256,512]{1,0:T(8,128)(2,1)S(1)} %convolution_convert_fusion.15.g_ref, ...), custom_call_target="tpu_custom_call" | custom-call | flops 2684354560 | bytes 5242880 | tf_op jit(solution)/shard_map/attention_backward/pallas_call | solution.py:1007
  386.7 10.4 %attention_backward.5 = (bf16[256,512]{1,0:T(8,128)(2,1)S(1)}, f32[1024,512]{1,0:T(8,128)S(1)}, f32[1024,512]{1,0:T(8,128)}) custom-call(bf16[256,1536]{1,0:T(8,128)(2,1)S(1)} %copy-done.3, bf16[1024,1024]{1,0:T(8,128)(2,1)} %copy-done.1, bf16[1024,1024]{1,0:T(8,128)(2,1)} %copy-done.1, bf16[256,512]{1,0:T(8,128)(2,1)S(1)} %convolution_convert_fusion.14.g_ref, ...), custom_call_target="tpu_custom_call" | custom-call | flops 2684354560 | bytes 5242880 | tf_op jit(solution)/shard_map/attention_backward/pallas_call | solution.py:1007
  420.1 8.0 %collective-permute-start.22 = (f32[256,1024]{1,0:T(8,128)}, f32[256,1024]{1,0:T(8,128)}, u32[]{:S(2)}, u32[]{:S(2)}) collective-permute-start(f32[256,1024]{1,0:T(8,128)} %collective-permute-done.21), channel_id=1, source_target_pairs={{0,16},{16,0},{1,17},{17,1},{2,18},{18,2},{3,19},{19,3},{4,20},{20... | collective-permute-start | bytes 3145736 | tf_op jit(solution)/shard_map/ppermute | solution.py:512
  477.8 10.0 %attention_backward.6 = (bf16[256,512]{1,0:T(8,128)(2,1)S(1)}, f32[1024,512]{1,0:T(8,128)S(1)}, f32[1024,512]{1,0:T(8,128)}) custom-call(bf16[256,1536]{1,0:T(8,128)(2,1)S(1)} %copy-done.6, bf16[1024,1024]{1,0:T(8,128)(2,1)} %copy-done, bf16[1024,1024]{1,0:T(8,128)(2,1)} %copy-done, bf16[256,512]{1,0:T(8,128)(2,1)S(1)} %convolution_convert_fusion.13.g_ref, ...), custom_call_target="tpu_custom_call" | custom-call | flops 2684354560 | bytes 5242880 | tf_op jit(solution)/shard_map/attention_backward/pallas_call | solution.py:1007
  490.1 10.5 %attention_backward.7 = (bf16[256,512]{1,0:T(8,128)(2,1)S(1)}, f32[1024,512]{1,0:T(8,128)S(1)}, f32[1024,512]{1,0:T(8,128)}) custom-call(bf16[256,1536]{1,0:T(8,128)(2,1)S(1)} %convolution_convert_fusion.4.q_ref, bf16[1024,1024]{1,0:T(8,128)(2,1)} %copy-done, bf16[1024,1024]{1,0:T(8,128)(2,1)} %copy-done, ...), custom_call_target="tpu_custom_call" | custom-call | flops 2684354560 | bytes 5242880 | tf_op jit(solution)/shard_map/attention_backward/pallas_call | solution.py:1007
  539.0 10.5 %collective-permute-done.25 = bf16[256,1024]{1,0:T(8,128)(2,1)S(1)} collective-permute-done((bf16[256,1024]{1,0:T(8,128)(2,1)S(1)}, bf16[256,1024]{1,0:T(8,128)(2,1)S(1)}, u32[]{:S(2)}, u32[]{:S(2)}) %collective-permute-start.25) | collective-permute-done | bytes 524320 | tf_op jit(solution)/shard_map/ppermute | solution.py:516
  560.7 11.6 %all-to-all-done.1 = bf16[8,512,128]{2,1,0:T(8,128)(2,1)S(1)} async-done(((bf16[8,512,128]{2,1,0:T(8,128)(2,1)}), bf16[8,512,128]{2,1,0:T(8,128)(2,1)S(1)}, u32[]{:S(2)}, u32[]{:S(2)}) %all-to-all-start.1) | async-done | bytes 1048608 | tf_op jit(solution)/shard_map/all_to_all | solution.py:1378
  624.5 6.8 all-to-all-start.2
  631.3 9.4 %collective-permute-done.27 = bf16[2,4,272,128]{3,2,1,0:T(8,128)(2,1)} collective-permute-done((bf16[2,4,272,128]{3,2,1,0:T(8,128)(2,1)}, bf16[2,4,272,128]{3,2,1,0:T(8,128)(2,1)}, u32[]{:S(2)}, u32[]{:S(2)}) %collective-permute-start.27) | collective-permute-done | bytes 557088 | tf_op jit(solution)/shard_map/ppermute | solution.py:549
  648.6 10.7 %collective-permute-done.28 = bf16[2,4,272,128]{3,2,1,0:T(8,128)(2,1)} collective-permute-done((bf16[2,4,272,128]{3,2,1,0:T(8,128)(2,1)}, bf16[2,4,272,128]{3,2,1,0:T(8,128)(2,1)}, u32[]{:S(2)}, u32[]{:S(2)}) %collective-permute-start.28) | collective-permute-done | bytes 557088 | tf_op jit(solution)/shard_map/ppermute | solution.py:549
  670.7 11.0 %collective-permute-done.31 = bf16[2,4,272,128]{3,2,1,0:T(8,128)(2,1)} collective-permute-done((bf16[2,4,272,128]{3,2,1,0:T(8,128)(2,1)}, bf16[2,4,272,128]{3,2,1,0:T(8,128)(2,1)}, u32[]{:S(2)}, u32[]{:S(2)}) %collective-permute-start.31) | collective-permute-done | bytes 557088 | tf_op jit(solution)/shard_map/ppermute | solution.py:549
  681.7 10.0 %collective-permute-done.30 = bf16[2,4,272,128]{3,2,1,0:T(8,128)(2,1)} collective-permute-done((bf16[2,4,272,128]{3,2,1,0:T(8,128)(2,1)}, bf16[2,4,272,128]{3,2,1,0:T(8,128)(2,1)}, u32[]{:S(2)}, u32[]{:S(2)}) %collective-permute-start.30) | collective-permute-done | bytes 557088 | tf_op jit(solution)/shard_map/ppermute | solution.py:549
  694.0 10.1 %all-to-all-start.3 = ((bf16[8,272,128]{2,1,0:T(8,128)(2,1)}), bf16[8,272,128]{2,1,0:T(8,128)(2,1)S(1)}, u32[]{:S(2)}, u32[]{:S(2)}) async-start(bf16[8,272,128]{2,1,0:T(8,128)(2,1)} %bitcast.367), calls=%async_computation.4 | async-start | bytes 1114112 | tf_op jit(solution)/shard_map/all_to_all | solution.py:1409
  (768 shorter events, 436.4 us)
Async XLA Ops:
  7.2 252.1 %all-gather.2.cloned.1.call-start = ((), (), s32[]{:S(2)}) async-start(), calls=%async_computation.7 | async-start | bytes 13926400 | tf_op jit(solution)/shard_map/all_gather | solution.py:566
  164.1 19.2 %all-to-all-start = ((bf16[8,512,128]{2,1,0:T(8,128)(2,1)}), bf16[8,512,128]{2,1,0:T(8,128)(2,1)S(1)}, u32[]{:S(2)}, u32[]{:S(2)}) async-start(bf16[8,512,128]{2,1,0:T(8,128)(2,1)} %bitcast.29), calls=%async_computation | async-start | bytes 2097152 | tf_op jit(solution)/shard_map/all_to_all | solution.py:1227
  168.5 332.7 %reduce-scatter.4.cloned.1.call-start = ((), (), s32[]{:S(2)}) async-start(), calls=%async_computation.8 | async-start | bytes 9191424 | tf_op jit(solution)/shard_map/reduce_scatter | solution.py:572
  169.4 36.2 %collective-permute-start = (bf16[256,1024]{1,0:T(8,128)(2,1)}, bf16[256,1024]{1,0:T(8,128)(2,1)}, u32[]{:S(2)}, u32[]{:S(2)}) collective-permute-start(bf16[256,1024]{1,0:T(8,128)(2,1)} %select_bitcast_fusion.2), channel_id=1, source_target_pairs={{0,0},{1,1},{2,16},{3,17},{16,2},{17,3},{18,18},{19,19},{4,4},{5,5... | collective-permute-start | bytes 1572872 | tf_op jit(solution)/shard_map/ppermute | solution.py:1210
  205.6 81.6 %collective-permute-start.1 = (bf16[256,1024]{1,0:T(8,128)(2,1)}, bf16[256,1024]{1,0:T(8,128)(2,1)}, u32[]{:S(2)}, u32[]{:S(2)}) collective-permute-start(bf16[256,1024]{1,0:T(8,128)(2,1)} %collective-permute-done), channel_id=1, source_target_pairs={{0,1},{1,0},{2,3},{3,2},{4,5},{5,4},{6,7},{7,6},{8,9},{9,8},{10,11... | collective-permute-start | bytes 1572872 | tf_op jit(solution)/shard_map/ppermute | solution.py:516
  214.2 27.4 %collective-permute-start.6 = (bf16[256,1024]{1,0:T(8,128)(2,1)S(1)}, bf16[256,1024]{1,0:T(8,128)(2,1)S(1)}, u32[]{:S(2)}, u32[]{:S(2)}) collective-permute-start(bf16[256,1024]{1,0:T(8,128)(2,1)S(1)} %convolution_convert_fusion.10), channel_id=1, source_target_pairs={{0,1},{1,0},{2,3},{3,2},{4,5},{5,4},{6,7},{7,6},{8,9},{9,8},{10,11... | collective-permute-start | bytes 1572872 | tf_op jit(solution)/shard_map/ppermute | solution.py:516
  266.0 17.9 %collective-permute-start.7 = (bf16[256,1024]{1,0:T(8,128)(2,1)S(1)}, bf16[256,1024]{1,0:T(8,128)(2,1)S(1)}, u32[]{:S(2)}, u32[]{:S(2)}) collective-permute-start(bf16[256,1024]{1,0:T(8,128)(2,1)S(1)} %fusion.120), channel_id=1, source_target_pairs={{0,1},{1,0},{2,3},{3,2},{4,5},{5,4},{6,7},{7,6},{8,9},{9,8},{10,11... | collective-permute-start | bytes 1572872 | tf_op jit(solution)/shard_map/ppermute | solution.py:516
  342.8 22.5 %collective-permute-start.11 = (bf16[256,1024]{1,0:T(8,128)(2,1)S(1)}, bf16[256,1024]{1,0:T(8,128)(2,1)}, u32[]{:S(2)}, u32[]{:S(2)}) collective-permute-start(bf16[256,1024]{1,0:T(8,128)(2,1)S(1)} %fusion.126), channel_id=1, source_target_pairs={{0,1},{1,0},{2,3},{3,2},{4,5},{5,4},{6,7},{7,6},{8,9},{9,8},{10,11... | collective-permute-start | bytes 1572872 | tf_op jit(solution)/shard_map/ppermute | solution.py:516
  352.2 361.5 %reduce-scatter.6.cloned.1.call-start = ((), (), s32[]{:S(2)}) async-start(), calls=%async_computation.9 | async-start | bytes 13647872 | tf_op jit(solution)/shard_map/reduce_scatter | solution.py:572
  372.3 24.8 %collective-permute-start.15 = (bf16[256,1024]{1,0:T(8,128)(2,1)S(1)}, bf16[256,1024]{1,0:T(8,128)(2,1)S(1)}, u32[]{:S(2)}, u32[]{:S(2)}) collective-permute-start(bf16[256,1024]{1,0:T(8,128)(2,1)S(1)} %fusion.132), channel_id=1, source_target_pairs={{0,1},{1,0},{2,3},{3,2},{4,5},{5,4},{6,7},{7,6},{8,9},{9,8},{10,11... | collective-permute-start | bytes 1572872 | tf_op jit(solution)/shard_map/ppermute | solution.py:516
  373.6 23.5 %collective-permute-start.14 = (bf16[256,1024]{1,0:T(8,128)(2,1)S(1)}, bf16[256,1024]{1,0:T(8,128)(2,1)S(1)}, u32[]{:S(2)}, u32[]{:S(2)}) collective-permute-start(bf16[256,1024]{1,0:T(8,128)(2,1)S(1)} %copy-done.111), channel_id=1, source_target_pairs={{0,1},{1,0},{2,3},{3,2},{4,5},{5,4},{6,7},{7,6},{8,9},{9,8},{10,11... | collective-permute-start | bytes 1572872 | tf_op jit(solution)/shard_map/ppermute | solution.py:516
  411.5 22.0 %collective-permute-start.18 = (bf16[256,1024]{1,0:T(8,128)(2,1)S(1)}, bf16[256,1024]{1,0:T(8,128)(2,1)}, u32[]{:S(2)}, u32[]{:S(2)}) collective-permute-start(bf16[256,1024]{1,0:T(8,128)(2,1)S(1)} %fusion.105), channel_id=1, source_target_pairs={{0,1},{1,0},{2,3},{3,2},{4,5},{5,4},{6,7},{7,6},{8,9},{9,8},{10,11... | collective-permute-start | bytes 1572872 | tf_op jit(solution)/shard_map/ppermute | solution.py:516
  420.1 44.1 %collective-permute-start.22 = (f32[256,1024]{1,0:T(8,128)}, f32[256,1024]{1,0:T(8,128)}, u32[]{:S(2)}, u32[]{:S(2)}) collective-permute-start(f32[256,1024]{1,0:T(8,128)} %collective-permute-done.21), channel_id=1, source_target_pairs={{0,16},{16,0},{1,17},{17,1},{2,18},{18,2},{3,19},{19,3},{4,20},{20... | collective-permute-start | bytes 3145736 | tf_op jit(solution)/shard_map/ppermute | solution.py:512
  443.7 23.8 %collective-permute-start.19 = (bf16[256,1024]{1,0:T(8,128)(2,1)}, bf16[256,1024]{1,0:T(8,128)(2,1)}, u32[]{:S(2)}, u32[]{:S(2)}) collective-permute-start(bf16[256,1024]{1,0:T(8,128)(2,1)} %fusion.150), channel_id=1, source_target_pairs={{0,1},{1,0},{2,3},{3,2},{4,5},{5,4},{6,7},{7,6},{8,9},{9,8},{10,11... | collective-permute-start | bytes 1572872 | tf_op jit(solution)/shard_map/ppermute | solution.py:516
  450.4 18.4 %collective-permute-start.20 = (bf16[256,1024]{1,0:T(8,128)(2,1)}, bf16[256,1024]{1,0:T(8,128)(2,1)}, u32[]{:S(2)}, u32[]{:S(2)}) collective-permute-start(bf16[256,1024]{1,0:T(8,128)(2,1)} %fusion.159), channel_id=1, source_target_pairs={{0,1},{1,0},{2,3},{3,2},{4,5},{5,4},{6,7},{7,6},{8,9},{9,8},{10,11... | collective-permute-start | bytes 1572872 | tf_op jit(solution)/shard_map/ppermute | solution.py:516
  527.7 21.8 %collective-permute-start.25 = (bf16[256,1024]{1,0:T(8,128)(2,1)S(1)}, bf16[256,1024]{1,0:T(8,128)(2,1)S(1)}, u32[]{:S(2)}, u32[]{:S(2)}) collective-permute-start(bf16[256,1024]{1,0:T(8,128)(2,1)S(1)} %fusion.111), channel_id=1, source_target_pairs={{0,1},{1,0},{2,3},{3,2},{4,5},{5,4},{6,7},{7,6},{8,9},{9,8},{10,11... | collective-permute-start | bytes 1572872 | tf_op jit(solution)/shard_map/ppermute | solution.py:516
  552.4 19.9 %all-to-all-start.1 = ((bf16[8,512,128]{2,1,0:T(8,128)(2,1)}), bf16[8,512,128]{2,1,0:T(8,128)(2,1)S(1)}, u32[]{:S(2)}, u32[]{:S(2)}) async-start(bf16[8,512,128]{2,1,0:T(8,128)(2,1)} %bitcast_bitcast_fusion), calls=%async_computation.2 | async-start | bytes 2097152 | tf_op jit(solution)/shard_map/all_to_all | solution.py:1378
  556.5 177.3 %reduce-scatter.8.cloned.1.call-start = ((), (), s32[]{:S(2)}) async-start(), calls=%async_computation.10 | async-start | bytes 4734976 | tf_op jit(solution)/shard_map/reduce_scatter | solution.py:572
  597.9 33.3 %collective-permute-start.26 = (bf16[2,4,272,128]{3,2,1,0:T(8,128)(2,1)}, bf16[2,4,272,128]{3,2,1,0:T(8,128)(2,1)}, u32[]{:S(2)}, u32[]{:S(2)}) collective-permute-start(bf16[2,4,272,128]{3,2,1,0:T(8,128)(2,1)} %get-tuple-element.224), channel_id=1, source_target_pairs={{0,4},{1,5},{2,6},{3,7},{16,20},{17,21},{18,22},{19,23}} | collective-permute-start | bytes 1671176 | tf_op jit(solution)/shard_map/ppermute | solution.py:549
  599.5 41.2 %collective-permute-start.27 = (bf16[2,4,272,128]{3,2,1,0:T(8,128)(2,1)}, bf16[2,4,272,128]{3,2,1,0:T(8,128)(2,1)}, u32[]{:S(2)}, u32[]{:S(2)}) collective-permute-start(bf16[2,4,272,128]{3,2,1,0:T(8,128)(2,1)} %get-tuple-element.223), channel_id=1, source_target_pairs={{12,8},{13,9},{14,10},{15,11},{28,24},{29,25},{30,26},{31,27}} | collective-permute-start | bytes 1671176 | tf_op jit(solution)/shard_map/ppermute | solution.py:549
  624.5 24.1 %all-to-all-start.2 = ((bf16[8,2,256,128]{3,2,1,0:T(8,128)(2,1)}), bf16[8,2,256,128]{3,2,1,0:T(8,128)(2,1)S(1)}, u32[]{:S(2)}, u32[]{:S(2)}) async-start(bf16[8,2,256,128]{3,2,1,0:T(8,128)(2,1)} %copy.421), calls=%async_computation.3 | async-start | bytes 2097152 | tf_op jit(solution)/shard_map/all_to_all | solution.py:1398
  644.5 17.4 %collective-permute-start.29 = (bf16[2,4,272,128]{3,2,1,0:T(8,128)(2,1)}, bf16[2,4,272,128]{3,2,1,0:T(8,128)(2,1)}, u32[]{:S(2)}, u32[]{:S(2)}) collective-permute-start(bf16[2,4,272,128]{3,2,1,0:T(8,128)(2,1)} %get-tuple-element.221), channel_id=1, source_target_pairs={{8,4},{12,8},{9,5},{13,9},{10,6},{14,10},{11,7},{15,11},{24,20},{2... | collective-permute-start | bytes 1671176 | tf_op jit(solution)/shard_map/ppermute | solution.py:549
  666.8 24.8 %collective-permute-start.30 = (bf16[2,4,272,128]{3,2,1,0:T(8,128)(2,1)}, bf16[2,4,272,128]{3,2,1,0:T(8,128)(2,1)}, u32[]{:S(2)}, u32[]{:S(2)}) collective-permute-start(bf16[2,4,272,128]{3,2,1,0:T(8,128)(2,1)} %get-tuple-element.219), channel_id=1, source_target_pairs={{0,4},{4,8},{8,12},{1,5},{5,9},{9,13},{2,6},{6,10},{10,14},{3,7},{... | collective-permute-start | bytes 1671176 | tf_op jit(solution)/shard_map/ppermute | solution.py:549
  694.0 19.6 %all-to-all-start.3 = ((bf16[8,272,128]{2,1,0:T(8,128)(2,1)}), bf16[8,272,128]{2,1,0:T(8,128)(2,1)S(1)}, u32[]{:S(2)}, u32[]{:S(2)}) async-start(bf16[8,272,128]{2,1,0:T(8,128)(2,1)} %bitcast.367), calls=%async_computation.4 | async-start | bytes 1114112 | tf_op jit(solution)/shard_map/all_to_all | solution.py:1409
  (204 other events, 1441.7 us)
Sparse Core Ops, SparseCore 0:
  128.1 131.1 all-gather.1
  352.3 119.7 reduce-scatter.3
  476.1 167.1 reduce-scatter.5
  647.0 77.1 reduce-scatter.7

commit v9 on v8

--- a/solution.py
+++ b/solution.py
@@ -1375,8 +1375,18 @@
     scattered.append(scatter_rows(jnp.concatenate(attn_members, axis=1)))
 
     lig_send = jnp.transpose(grad_in_low.reshape(half_frames, 8, block_width), (1, 0, 2))
-    lig_got = lax.all_to_all(lig_send, both, 0, 0, tiled=True).reshape(2, 2, 2, half_frames, block_width)
-    lig = jnp.transpose(lig_got[:, :, 0], (1, 0, 2, 3)).reshape(micro_count, row_frames, block_width)
+    def gradient_block(section, place):
+        return lax.dynamic_index_in_dim(lig_send, section * 4 + place, 0, keepdims=False)
+
+    beyond = (seq + 2) % 4
+    corner = [(t * 4 + q, (1 - t) * 4 + (q ^ 2)) for t in range(2) for q in range(4)]
+    near = choose(sec0, gradient_block(sec, seq), swap_section(gradient_block(1 - sec, seq)))
+    far = choose(
+        sec0,
+        lax.ppermute(gradient_block(sec, beyond), "seq", [(q, q ^ 2) for q in range(4)]),
+        lax.ppermute(gradient_block(1 - sec, beyond), both, corner),
+    )
+    lig = jnp.stack(choose(y == 0, jnp.concatenate(near), jnp.concatenate(far)))
     conv_grad = (lig.astype(f32) * slope.astype(f32)).astype(bf16)
     grad_views = group_view(conv_grad, per_group)
     back = ungroup(conv_back(grad_views, bands), per_group)

time: 767 us -> 749 us (0.977)
  waiting for transfers between devices: 139 us -> 129 us
    all_to_all x1 -> x0, waiting for transfers between devices: 11.6 us -> none  [per_device_pairs(): lax.all_to_all(lig_send, both, 0, 0, tiled=True)]
    unnamed x372 -> x368, local copies, waits for them, and re-layouts: 32.5 us -> 30.1 us
    ppermute x9 -> x10, starting transfers between devices: 17.9 us -> 18.2 us  [swap_section(): return lax.ppermute(value, 'section', [(0, 1), (1, 0)])]
  transfers between devices with their start and end apart: 46 -> 48, of which waited for: 24 -> 23; matrix products, arithmetic and copies ran while one was open for 37% -> 38% of each run, Pallas kernels for 8% -> 8%
where the time goes in v9:
time: 749 us; the launch traced here: 740 us
  Pallas kernels  168 us (22%)
  matrix products  151 us (20%)
  waiting for transfers between devices  129 us (17%)
  other arithmetic  95.9 us (13%)
  local copies, waits for them, and re-layouts  95.9 us (13%)
  starting transfers between devices  81.8 us (11%)
  between operations  17.5 us (2%)
    pallas_call x1, Pallas kernels, opening(): pl.pallas_call(functools.partial(opening_kernel, count, parts), in_specs=...  99.8 us
    ppermute x17, waiting for transfers between devices, swap_x(): return lax.ppermute(value, 'seq', [(q, q ^ 1) for q in range(4)])  54.5 us
    ppermute x6, waiting for transfers between devices, sum_dp(): running[way] = lax.ppermute(own, 'dp', live)  42.4 us
    pallas_call x4, Pallas kernels, attention_backward(): pl.pallas_call(functools.partial(attention_backward_kernel, factor), grid...  41.2 us
    dot_general x12, matrix products, outer(): lax.dot_general(left, right, (((0,), (0,)), ((), ())), preferred_element_...  35.6 us
    dot_general x8, matrix products, per_device_pairs(): hidden_pre = jnp.dot(normed_two[c], w_up[part], preferred_element_type=f32)  31.8 us
    unnamed x368, local copies, waits for them, and re-layouts  30.1 us
    dot_general x24, matrix products, back(): lax.dot_general(left, right, (((1,), (1,)), ((), ())), preferred_element_...  28 us
  transfers between devices with their start and end apart: 48, of which 23 were waited for; matrix products, arithmetic and copies ran while one was open for 38% of the time, Pallas kernels for 8%

profile of v9, /device:TPU:17, one launch (start us, length us, event | category | flops | bytes accessed | tf_op | source)
XLA Modules:
  0.0 739.7 jit_solution(5946434381170497259)
XLA Ops:
  22.4 99.8 %opening.1 = (bf16[4,8,272,128]{3,2,1,0:T(8,128)(2,1)S(1)}, bf16[4,2,256,128]{3,2,1,0:T(8,128)(2,1)S(1)}, bf16[4,2,2,64,6400]{4,3,2,1,0:T(8,128)(2,1)S(1)}, bf16[64,6400]{1,0:T(8,128)(2,1)S(1)}) custom-call(bf16[8,272,128]{2,1,0:T(8,128)(2,1)S(1)} %fusion.396.conv_ref, bf16[4,2,256,128]{3,2,1,0:T(8,128)(2,1)S(1)} %bitcast.291, ...), custom_call_target="tpu_custom_call" | custom-call | tf_op jit(solution)/shard_map/opening/pallas_call | solution.py:851
  135.6 6.2 fusion.421
  148.3 6.2 fusion.415
  172.6 7.8 %all-to-all-done = bf16[8,512,128]{2,1,0:T(8,128)(2,1)S(1)} async-done(((bf16[8,512,128]{2,1,0:T(8,128)(2,1)}), bf16[8,512,128]{2,1,0:T(8,128)(2,1)S(1)}, u32[]{:S(2)}, u32[]{:S(2)}) %all-to-all-start) | async-done | bytes 1048608 | tf_op jit(solution)/shard_map/all_to_all | solution.py:1227
  194.6 6.8 attention_forward.4
  204.4 6.6 attention_forward.5
  218.3 6.2 fusion.205
  230.6 8.1 %collective-permute-done.6 = bf16[256,1024]{1,0:T(8,128)(2,1)S(1)} collective-permute-done((bf16[256,1024]{1,0:T(8,128)(2,1)S(1)}, bf16[256,1024]{1,0:T(8,128)(2,1)S(1)}, u32[]{:S(2)}, u32[]{:S(2)}) %collective-permute-start.6) | collective-permute-done | bytes 524320 | tf_op jit(solution)/shard_map/ppermute | solution.py:516
  248.5 8.0 %all-gather.2.cloned.1.call-done = bf16[1024,6400]{1,0:T(8,128)(2,1)} async-done(((bf16[64,6400]{1,0:T(8,128)(2,1)}), bf16[1024,6400]{1,0:T(8,128)(2,1)}) %all-gather.2.cloned.1.call-update) | async-done | bytes 13107216 | tf_op jit(solution)/shard_map/all_gather | solution.py:566
  272.9 8.2 %collective-permute-done.7 = bf16[256,1024]{1,0:T(8,128)(2,1)S(1)} collective-permute-done((bf16[256,1024]{1,0:T(8,128)(2,1)S(1)}, bf16[256,1024]{1,0:T(8,128)(2,1)S(1)}, u32[]{:S(2)}, u32[]{:S(2)}) %collective-permute-start.7) | collective-permute-done | bytes 524320 | tf_op jit(solution)/shard_map/ppermute | solution.py:516
  288.6 6.6 attention_forward.6
  298.1 6.7 attention_forward.7
  354.8 7.7 %collective-permute-done.11 = bf16[256,1024]{1,0:T(8,128)(2,1)} collective-permute-done((bf16[256,1024]{1,0:T(8,128)(2,1)S(1)}, bf16[256,1024]{1,0:T(8,128)(2,1)}, u32[]{:S(2)}, u32[]{:S(2)}) %collective-permute-start.11) | collective-permute-done | bytes 524320 | tf_op jit(solution)/shard_map/ppermute | solution.py:516
  370.7 10.0 %attention_backward.4 = (bf16[256,512]{1,0:T(8,128)(2,1)S(1)}, f32[1024,512]{1,0:T(8,128)S(1)}, f32[1024,512]{1,0:T(8,128)}) custom-call(bf16[256,1536]{1,0:T(8,128)(2,1)S(1)} %copy-done.8, bf16[1024,1024]{1,0:T(8,128)(2,1)} %copy-done.1, bf16[1024,1024]{1,0:T(8,128)(2,1)} %copy-done.1, bf16[256,512]{1,0:T(8,128)(2,1)S(1)} %convolution_convert_fusion.15.g_ref, ...), custom_call_target="tpu_custom_call" | custom-call | flops 2684354560 | bytes 5242880 | tf_op jit(solution)/shard_map/attention_backward/pallas_call | solution.py:1007
  383.5 10.4 %attention_backward.5 = (bf16[256,512]{1,0:T(8,128)(2,1)S(1)}, f32[1024,512]{1,0:T(8,128)S(1)}, f32[1024,512]{1,0:T(8,128)}) custom-call(bf16[256,1536]{1,0:T(8,128)(2,1)S(1)} %copy-done.3, bf16[1024,1024]{1,0:T(8,128)(2,1)} %copy-done.1, bf16[1024,1024]{1,0:T(8,128)(2,1)} %copy-done.1, bf16[256,512]{1,0:T(8,128)(2,1)S(1)} %convolution_convert_fusion.14.g_ref, ...), custom_call_target="tpu_custom_call" | custom-call | flops 2684354560 | bytes 5242880 | tf_op jit(solution)/shard_map/attention_backward/pallas_call | solution.py:1007
  417.3 8.2 %collective-permute-start.22 = (f32[256,1024]{1,0:T(8,128)}, f32[256,1024]{1,0:T(8,128)}, u32[]{:S(2)}, u32[]{:S(2)}) collective-permute-start(f32[256,1024]{1,0:T(8,128)} %collective-permute-done.21), channel_id=1, source_target_pairs={{0,16},{16,0},{1,17},{17,1},{2,18},{18,2},{3,19},{19,3},{4,20},{20... | collective-permute-start | bytes 3145736 | tf_op jit(solution)/shard_map/ppermute | solution.py:512
  475.9 10.1 %attention_backward.6 = (bf16[256,512]{1,0:T(8,128)(2,1)S(1)}, f32[1024,512]{1,0:T(8,128)S(1)}, f32[1024,512]{1,0:T(8,128)}) custom-call(bf16[256,1536]{1,0:T(8,128)(2,1)S(1)} %copy-done.6, bf16[1024,1024]{1,0:T(8,128)(2,1)} %copy-done, bf16[1024,1024]{1,0:T(8,128)(2,1)} %copy-done, bf16[256,512]{1,0:T(8,128)(2,1)S(1)} %convolution_convert_fusion.13.g_ref, ...), custom_call_target="tpu_custom_call" | custom-call | flops 2684354560 | bytes 5242880 | tf_op jit(solution)/shard_map/attention_backward/pallas_call | solution.py:1007
  488.4 10.7 %attention_backward.7 = (bf16[256,512]{1,0:T(8,128)(2,1)S(1)}, f32[1024,512]{1,0:T(8,128)S(1)}, f32[1024,512]{1,0:T(8,128)}) custom-call(bf16[256,1536]{1,0:T(8,128)(2,1)S(1)} %convolution_convert_fusion.4.q_ref, bf16[1024,1024]{1,0:T(8,128)(2,1)} %copy-done, bf16[1024,1024]{1,0:T(8,128)(2,1)} %copy-done, ...), custom_call_target="tpu_custom_call" | custom-call | flops 2684354560 | bytes 5242880 | tf_op jit(solution)/shard_map/attention_backward/pallas_call | solution.py:1007
  539.1 10.6 %collective-permute-done.25 = bf16[256,1024]{1,0:T(8,128)(2,1)S(1)} collective-permute-done((bf16[256,1024]{1,0:T(8,128)(2,1)S(1)}, bf16[256,1024]{1,0:T(8,128)(2,1)S(1)}, u32[]{:S(2)}, u32[]{:S(2)}) %collective-permute-start.25) | collective-permute-done | bytes 524320 | tf_op jit(solution)/shard_map/ppermute | solution.py:516
  616.1 13.4 %collective-permute-done.30 = bf16[2,4,272,128]{3,2,1,0:T(8,128)(2,1)} collective-permute-done((bf16[2,4,272,128]{3,2,1,0:T(8,128)(2,1)}, bf16[2,4,272,128]{3,2,1,0:T(8,128)(2,1)}, u32[]{:S(2)}, u32[]{:S(2)}) %collective-permute-start.30) | collective-permute-done | bytes 557088 | tf_op jit(solution)/shard_map/ppermute | solution.py:549
  637.2 11.2 %collective-permute-done.31 = bf16[2,4,272,128]{3,2,1,0:T(8,128)(2,1)} collective-permute-done((bf16[2,4,272,128]{3,2,1,0:T(8,128)(2,1)}, bf16[2,4,272,128]{3,2,1,0:T(8,128)(2,1)}, u32[]{:S(2)}, u32[]{:S(2)}) %collective-permute-start.31) | collective-permute-done | bytes 557088 | tf_op jit(solution)/shard_map/ppermute | solution.py:549
  658.4 9.6 %collective-permute-done.34 = bf16[2,4,272,128]{3,2,1,0:T(8,128)(2,1)} collective-permute-done((bf16[2,4,272,128]{3,2,1,0:T(8,128)(2,1)}, bf16[2,4,272,128]{3,2,1,0:T(8,128)(2,1)}, u32[]{:S(2)}, u32[]{:S(2)}) %collective-permute-start.34) | collective-permute-done | bytes 557088 | tf_op jit(solution)/shard_map/ppermute | solution.py:549
  667.9 7.0 collective-permute-done.33
  677.1 12.3 %all-to-all-start.2 = ((bf16[8,272,128]{2,1,0:T(8,128)(2,1)}), bf16[8,272,128]{2,1,0:T(8,128)(2,1)S(1)}, u32[]{:S(2)}, u32[]{:S(2)}) async-start(bf16[8,272,128]{2,1,0:T(8,128)(2,1)} %bitcast.367), calls=%async_computation.3 | async-start | bytes 1114112 | tf_op jit(solution)/shard_map/all_to_all | solution.py:1419
  (770 shorter events, 423.9 us)
Async XLA Ops:
  7.2 249.3 %all-gather.2.cloned.1.call-start = ((), (), s32[]{:S(2)}) async-start(), calls=%async_computation.6 | async-start | bytes 13926400 | tf_op jit(solution)/shard_map/all_gather | solution.py:566
  161.2 19.2 %all-to-all-start = ((bf16[8,512,128]{2,1,0:T(8,128)(2,1)}), bf16[8,512,128]{2,1,0:T(8,128)(2,1)S(1)}, u32[]{:S(2)}, u32[]{:S(2)}) async-start(bf16[8,512,128]{2,1,0:T(8,128)(2,1)} %bitcast.29), calls=%async_computation | async-start | bytes 2097152 | tf_op jit(solution)/shard_map/all_to_all | solution.py:1227
  165.6 334.2 %reduce-scatter.4.cloned.1.call-start = ((), (), s32[]{:S(2)}) async-start(), calls=%async_computation.7 | async-start | bytes 9191424 | tf_op jit(solution)/shard_map/reduce_scatter | solution.py:572
  166.5 36.5 %collective-permute-start = (bf16[256,1024]{1,0:T(8,128)(2,1)}, bf16[256,1024]{1,0:T(8,128)(2,1)}, u32[]{:S(2)}, u32[]{:S(2)}) collective-permute-start(bf16[256,1024]{1,0:T(8,128)(2,1)} %select_bitcast_fusion.2), channel_id=1, source_target_pairs={{0,0},{1,1},{2,16},{3,17},{16,2},{17,3},{18,18},{19,19},{4,4},{5,5... | collective-permute-start | bytes 1572872 | tf_op jit(solution)/shard_map/ppermute | solution.py:1210
  203.0 81.5 %collective-permute-start.1 = (bf16[256,1024]{1,0:T(8,128)(2,1)}, bf16[256,1024]{1,0:T(8,128)(2,1)}, u32[]{:S(2)}, u32[]{:S(2)}) collective-permute-start(bf16[256,1024]{1,0:T(8,128)(2,1)} %collective-permute-done), channel_id=1, source_target_pairs={{0,1},{1,0},{2,3},{3,2},{4,5},{5,4},{6,7},{7,6},{8,9},{9,8},{10,11... | collective-permute-start | bytes 1572872 | tf_op jit(solution)/shard_map/ppermute | solution.py:516
  211.5 27.3 %collective-permute-start.6 = (bf16[256,1024]{1,0:T(8,128)(2,1)S(1)}, bf16[256,1024]{1,0:T(8,128)(2,1)S(1)}, u32[]{:S(2)}, u32[]{:S(2)}) collective-permute-start(bf16[256,1024]{1,0:T(8,128)(2,1)S(1)} %convolution_convert_fusion.10), channel_id=1, source_target_pairs={{0,1},{1,0},{2,3},{3,2},{4,5},{5,4},{6,7},{7,6},{8,9},{9,8},{10,11... | collective-permute-start | bytes 1572872 | tf_op jit(solution)/shard_map/ppermute | solution.py:516
  263.2 17.9 %collective-permute-start.7 = (bf16[256,1024]{1,0:T(8,128)(2,1)S(1)}, bf16[256,1024]{1,0:T(8,128)(2,1)S(1)}, u32[]{:S(2)}, u32[]{:S(2)}) collective-permute-start(bf16[256,1024]{1,0:T(8,128)(2,1)S(1)} %fusion.120), channel_id=1, source_target_pairs={{0,1},{1,0},{2,3},{3,2},{4,5},{5,4},{6,7},{7,6},{8,9},{9,8},{10,11... | collective-permute-start | bytes 1572872 | tf_op jit(solution)/shard_map/ppermute | solution.py:516
  339.9 22.5 %collective-permute-start.11 = (bf16[256,1024]{1,0:T(8,128)(2,1)S(1)}, bf16[256,1024]{1,0:T(8,128)(2,1)}, u32[]{:S(2)}, u32[]{:S(2)}) collective-permute-start(bf16[256,1024]{1,0:T(8,128)(2,1)S(1)} %fusion.126), channel_id=1, source_target_pairs={{0,1},{1,0},{2,3},{3,2},{4,5},{5,4},{6,7},{7,6},{8,9},{9,8},{10,11... | collective-permute-start | bytes 1572872 | tf_op jit(solution)/shard_map/ppermute | solution.py:516
  349.3 349.6 %reduce-scatter.6.cloned.1.call-start = ((), (), s32[]{:S(2)}) async-start(), calls=%async_computation.8 | async-start | bytes 13647872 | tf_op jit(solution)/shard_map/reduce_scatter | solution.py:572
  369.1 24.8 %collective-permute-start.15 = (bf16[256,1024]{1,0:T(8,128)(2,1)S(1)}, bf16[256,1024]{1,0:T(8,128)(2,1)S(1)}, u32[]{:S(2)}, u32[]{:S(2)}) collective-permute-start(bf16[256,1024]{1,0:T(8,128)(2,1)S(1)} %fusion.132), channel_id=1, source_target_pairs={{0,1},{1,0},{2,3},{3,2},{4,5},{5,4},{6,7},{7,6},{8,9},{9,8},{10,11... | collective-permute-start | bytes 1572872 | tf_op jit(solution)/shard_map/ppermute | solution.py:516
  370.3 23.6 %collective-permute-start.14 = (bf16[256,1024]{1,0:T(8,128)(2,1)S(1)}, bf16[256,1024]{1,0:T(8,128)(2,1)S(1)}, u32[]{:S(2)}, u32[]{:S(2)}) collective-permute-start(bf16[256,1024]{1,0:T(8,128)(2,1)S(1)} %copy-done.107), channel_id=1, source_target_pairs={{0,1},{1,0},{2,3},{3,2},{4,5},{5,4},{6,7},{7,6},{8,9},{9,8},{10,11... | collective-permute-start | bytes 1572872 | tf_op jit(solution)/shard_map/ppermute | solution.py:516
  400.7 16.5 %collective-permute-start.21 = (f32[256,1024]{1,0:T(8,128)}, f32[256,1024]{1,0:T(8,128)}, u32[]{:S(2)}, u32[]{:S(2)}) collective-permute-start(f32[256,1024]{1,0:T(8,128)} %broadcast_select_fusion.2), channel_id=1, source_target_pairs={{0,0},{1,1},{2,16},{3,17},{16,2},{17,3},{18,18},{19,19},{4,4},{5,5... | collective-permute-start | bytes 3145736 | tf_op jit(solution)/shard_map/ppermute | solution.py:1336
  408.8 22.1 %collective-permute-start.18 = (bf16[256,1024]{1,0:T(8,128)(2,1)S(1)}, bf16[256,1024]{1,0:T(8,128)(2,1)}, u32[]{:S(2)}, u32[]{:S(2)}) collective-permute-start(bf16[256,1024]{1,0:T(8,128)(2,1)S(1)} %fusion.105), channel_id=1, source_target_pairs={{0,1},{1,0},{2,3},{3,2},{4,5},{5,4},{6,7},{7,6},{8,9},{9,8},{10,11... | collective-permute-start | bytes 1572872 | tf_op jit(solution)/shard_map/ppermute | solution.py:516
  417.3 43.4 %collective-permute-start.22 = (f32[256,1024]{1,0:T(8,128)}, f32[256,1024]{1,0:T(8,128)}, u32[]{:S(2)}, u32[]{:S(2)}) collective-permute-start(f32[256,1024]{1,0:T(8,128)} %collective-permute-done.21), channel_id=1, source_target_pairs={{0,16},{16,0},{1,17},{17,1},{2,18},{18,2},{3,19},{19,3},{4,20},{20... | collective-permute-start | bytes 3145736 | tf_op jit(solution)/shard_map/ppermute | solution.py:512
  441.1 22.8 %collective-permute-start.19 = (bf16[256,1024]{1,0:T(8,128)(2,1)}, bf16[256,1024]{1,0:T(8,128)(2,1)}, u32[]{:S(2)}, u32[]{:S(2)}) collective-permute-start(bf16[256,1024]{1,0:T(8,128)(2,1)} %fusion.150), channel_id=1, source_target_pairs={{0,1},{1,0},{2,3},{3,2},{4,5},{5,4},{6,7},{7,6},{8,9},{9,8},{10,11... | collective-permute-start | bytes 1572872 | tf_op jit(solution)/shard_map/ppermute | solution.py:516
  447.0 19.3 %collective-permute-start.20 = (bf16[256,1024]{1,0:T(8,128)(2,1)}, bf16[256,1024]{1,0:T(8,128)(2,1)}, u32[]{:S(2)}, u32[]{:S(2)}) collective-permute-start(bf16[256,1024]{1,0:T(8,128)(2,1)} %fusion.159), channel_id=1, source_target_pairs={{0,1},{1,0},{2,3},{3,2},{4,5},{5,4},{6,7},{7,6},{8,9},{9,8},{10,11... | collective-permute-start | bytes 1572872 | tf_op jit(solution)/shard_map/ppermute | solution.py:516
  468.7 249.2 %reduce-scatter.8.cloned.1.call-start = ((), (), s32[]{:S(2)}) async-start(), calls=%async_computation.9 | async-start | bytes 4734976 | tf_op jit(solution)/shard_map/reduce_scatter | solution.py:572
  528.4 21.2 %collective-permute-start.25 = (bf16[256,1024]{1,0:T(8,128)(2,1)S(1)}, bf16[256,1024]{1,0:T(8,128)(2,1)S(1)}, u32[]{:S(2)}, u32[]{:S(2)}) collective-permute-start(bf16[256,1024]{1,0:T(8,128)(2,1)S(1)} %fusion.111), channel_id=1, source_target_pairs={{0,1},{1,0},{2,3},{3,2},{4,5},{5,4},{6,7},{7,6},{8,9},{9,8},{10,11... | collective-permute-start | bytes 1572872 | tf_op jit(solution)/shard_map/ppermute | solution.py:516
  587.4 28.7 %collective-permute-start.29 = (bf16[2,4,272,128]{3,2,1,0:T(8,128)(2,1)}, bf16[2,4,272,128]{3,2,1,0:T(8,128)(2,1)}, u32[]{:S(2)}, u32[]{:S(2)}) collective-permute-start(bf16[2,4,272,128]{3,2,1,0:T(8,128)(2,1)} %get-tuple-element.226), channel_id=1, source_target_pairs={{0,4},{1,5},{2,6},{3,7},{16,20},{17,21},{18,22},{19,23}} | collective-permute-start | bytes 1671176 | tf_op jit(solution)/shard_map/ppermute | solution.py:549
  588.9 40.6 %collective-permute-start.30 = (bf16[2,4,272,128]{3,2,1,0:T(8,128)(2,1)}, bf16[2,4,272,128]{3,2,1,0:T(8,128)(2,1)}, u32[]{:S(2)}, u32[]{:S(2)}) collective-permute-start(bf16[2,4,272,128]{3,2,1,0:T(8,128)(2,1)} %get-tuple-element.225), channel_id=1, source_target_pairs={{12,8},{13,9},{14,10},{15,11},{28,24},{29,25},{30,26},{31,27}} | collective-permute-start | bytes 1671176 | tf_op jit(solution)/shard_map/ppermute | solution.py:549
  612.5 24.7 %all-to-all-start.1 = ((bf16[8,2,256,128]{3,2,1,0:T(8,128)(2,1)}), bf16[8,2,256,128]{3,2,1,0:T(8,128)(2,1)S(1)}, u32[]{:S(2)}, u32[]{:S(2)}) async-start(bf16[8,2,256,128]{3,2,1,0:T(8,128)(2,1)} %copy.435), calls=%async_computation.2 | async-start | bytes 2097152 | tf_op jit(solution)/shard_map/all_to_all | solution.py:1408
  633.2 16.5 %collective-permute-start.32 = (bf16[2,4,272,128]{3,2,1,0:T(8,128)(2,1)}, bf16[2,4,272,128]{3,2,1,0:T(8,128)(2,1)}, u32[]{:S(2)}, u32[]{:S(2)}) collective-permute-start(bf16[2,4,272,128]{3,2,1,0:T(8,128)(2,1)} %get-tuple-element.223), channel_id=1, source_target_pairs={{8,4},{12,8},{9,5},{13,9},{10,6},{14,10},{11,7},{15,11},{24,20},{2... | collective-permute-start | bytes 1671176 | tf_op jit(solution)/shard_map/ppermute | solution.py:549
  656.0 18.9 %collective-permute-start.33 = (bf16[2,4,272,128]{3,2,1,0:T(8,128)(2,1)}, bf16[2,4,272,128]{3,2,1,0:T(8,128)(2,1)}, u32[]{:S(2)}, u32[]{:S(2)}) collective-permute-start(bf16[2,4,272,128]{3,2,1,0:T(8,128)(2,1)} %get-tuple-element.221), channel_id=1, source_target_pairs={{0,4},{4,8},{8,12},{1,5},{5,9},{9,13},{2,6},{6,10},{10,14},{3,7},{... | collective-permute-start | bytes 1671176 | tf_op jit(solution)/shard_map/ppermute | solution.py:549
  677.1 21.8 %all-to-all-start.2 = ((bf16[8,272,128]{2,1,0:T(8,128)(2,1)}), bf16[8,272,128]{2,1,0:T(8,128)(2,1)S(1)}, u32[]{:S(2)}, u32[]{:S(2)}) async-start(bf16[8,272,128]{2,1,0:T(8,128)(2,1)} %bitcast.367), calls=%async_computation.3 | async-start | bytes 1114112 | tf_op jit(solution)/shard_map/all_to_all | solution.py:1419
  (202 other events, 1366.8 us)
Sparse Core Ops, SparseCore 0:
  128.1 128.3 all-gather.1
  349.4 118.7 reduce-scatter.3
  472.3 161.6 reduce-scatter.5
  637.8 71.8 reduce-scatter.7

commit v10 on v9

--- a/solution.py
+++ b/solution.py
@@ -1413,7 +1413,7 @@
         return choose(sec0, keep, swap_section(send))
 
 
-    taps_sum, (_, gs_got) = sum_dp(taps_send, dp, (gs_send, gs_got))
+    taps_sum, (_, _, gs_got) = sum_dp(taps_send, dp, (gs_send, (), gs_got))
     gs_rows = jnp.transpose(gs_got, (1, 2, 0, 3)).reshape(micro_count, frames, width).astype(f32)
     ends = jnp.where(sec0, gs_rows, output_rows)[None]
     taps_got = lax.all_to_all(

time: 749 us -> 762 us (1.017)
    unnamed x368 -> x366, local copies, waits for them, and re-layouts: 30.1 us -> 30.1 us
  transfers between devices with their start and end apart: 48 -> 48, of which waited for: 23 -> 24; matrix products, arithmetic and copies ran while one was open for 38% -> 38% of each run, Pallas kernels for 8% -> 8%
where the time goes in v10:
time: 762 us; the launch traced here: 751 us
  Pallas kernels  168 us (22%)
  matrix products  155 us (20%)
  waiting for transfers between devices  129 us (17%)
  other arithmetic  101 us (13%)
  local copies, waits for them, and re-layouts  95.9 us (13%)
  starting transfers between devices  84.2 us (11%)
  between operations  17.5 us (2%)
    pallas_call x1, Pallas kernels, opening(): pl.pallas_call(functools.partial(opening_kernel, count, parts), in_specs=...  99.8 us
    ppermute x17, waiting for transfers between devices, swap_x(): return lax.ppermute(value, 'seq', [(q, q ^ 1) for q in range(4)])  54.5 us
    pallas_call x4, Pallas kernels, attention_backward(): pl.pallas_call(functools.partial(attention_backward_kernel, factor), grid...  41.2 us
    ppermute x6, waiting for transfers between devices, sum_dp(): running[way] = lax.ppermute(own, 'dp', live)  39.9 us
    dot_general x12, matrix products, outer(): lax.dot_general(left, right, (((0,), (0,)), ((), ())), preferred_element_...  35.5 us
    dot_general x8, matrix products, per_device_pairs(): hidden_pre = jnp.dot(normed_two[c], w_up[part], preferred_element_type=f32)  31.8 us
    unnamed x366, local copies, waits for them, and re-layouts  30.1 us
    dot_general x24, matrix products, back(): lax.dot_general(left, right, (((1,), (1,)), ((), ())), preferred_element_...  28 us
  transfers between devices with their start and end apart: 48, of which 24 were waited for; matrix products, arithmetic and copies ran while one was open for 38% of the time, Pallas kernels for 8%

profile of v10, /device:TPU:17, one launch (start us, length us, event | category | flops | bytes accessed | tf_op | source)
XLA Modules:
  0.0 750.5 jit_solution(2964629229669041156)
XLA Ops:
  22.4 99.8 %opening.1 = (bf16[4,8,272,128]{3,2,1,0:T(8,128)(2,1)S(1)}, bf16[4,2,256,128]{3,2,1,0:T(8,128)(2,1)S(1)}, bf16[4,2,2,64,6400]{4,3,2,1,0:T(8,128)(2,1)S(1)}, bf16[64,6400]{1,0:T(8,128)(2,1)S(1)}) custom-call(bf16[8,272,128]{2,1,0:T(8,128)(2,1)S(1)} %fusion.396.conv_ref, bf16[4,2,256,128]{3,2,1,0:T(8,128)(2,1)S(1)} %bitcast.291, ...), custom_call_target="tpu_custom_call" | custom-call | tf_op jit(solution)/shard_map/opening/pallas_call | solution.py:851
  135.5 6.2 fusion.421
  148.3 6.2 fusion.415
  172.6 7.8 %all-to-all-done = bf16[8,512,128]{2,1,0:T(8,128)(2,1)S(1)} async-done(((bf16[8,512,128]{2,1,0:T(8,128)(2,1)}), bf16[8,512,128]{2,1,0:T(8,128)(2,1)S(1)}, u32[]{:S(2)}, u32[]{:S(2)}) %all-to-all-start) | async-done | bytes 1048608 | tf_op jit(solution)/shard_map/all_to_all | solution.py:1227
  194.6 6.8 attention_forward.4
  204.4 6.6 attention_forward.5
  230.6 8.1 %collective-permute-done.6 = bf16[256,1024]{1,0:T(8,128)(2,1)S(1)} collective-permute-done((bf16[256,1024]{1,0:T(8,128)(2,1)S(1)}, bf16[256,1024]{1,0:T(8,128)(2,1)S(1)}, u32[]{:S(2)}, u32[]{:S(2)}) %collective-permute-start.6) | collective-permute-done | bytes 524320 | tf_op jit(solution)/shard_map/ppermute | solution.py:516
  248.5 7.9 %all-gather.2.cloned.1.call-done = bf16[1024,6400]{1,0:T(8,128)(2,1)} async-done(((bf16[64,6400]{1,0:T(8,128)(2,1)}), bf16[1024,6400]{1,0:T(8,128)(2,1)}) %all-gather.2.cloned.1.call-update) | async-done | bytes 13107216 | tf_op jit(solution)/shard_map/all_gather | solution.py:566
  272.9 8.3 %collective-permute-done.7 = bf16[256,1024]{1,0:T(8,128)(2,1)S(1)} collective-permute-done((bf16[256,1024]{1,0:T(8,128)(2,1)S(1)}, bf16[256,1024]{1,0:T(8,128)(2,1)S(1)}, u32[]{:S(2)}, u32[]{:S(2)}) %collective-permute-start.7) | collective-permute-done | bytes 524320 | tf_op jit(solution)/shard_map/ppermute | solution.py:516
  288.6 6.6 attention_forward.6
  298.1 6.7 attention_forward.7
  354.8 7.7 %collective-permute-done.11 = bf16[256,1024]{1,0:T(8,128)(2,1)} collective-permute-done((bf16[256,1024]{1,0:T(8,128)(2,1)S(1)}, bf16[256,1024]{1,0:T(8,128)(2,1)}, u32[]{:S(2)}, u32[]{:S(2)}) %collective-permute-start.11) | collective-permute-done | bytes 524320 | tf_op jit(solution)/shard_map/ppermute | solution.py:516
  370.7 10.0 %attention_backward.4 = (bf16[256,512]{1,0:T(8,128)(2,1)S(1)}, f32[1024,512]{1,0:T(8,128)S(1)}, f32[1024,512]{1,0:T(8,128)}) custom-call(bf16[256,1536]{1,0:T(8,128)(2,1)S(1)} %copy-done.8, bf16[1024,1024]{1,0:T(8,128)(2,1)} %copy-done.1, bf16[1024,1024]{1,0:T(8,128)(2,1)} %copy-done.1, bf16[256,512]{1,0:T(8,128)(2,1)S(1)} %convolution_convert_fusion.15.g_ref, ...), custom_call_target="tpu_custom_call" | custom-call | flops 2684354560 | bytes 5242880 | tf_op jit(solution)/shard_map/attention_backward/pallas_call | solution.py:1007
  383.5 10.4 %attention_backward.5 = (bf16[256,512]{1,0:T(8,128)(2,1)S(1)}, f32[1024,512]{1,0:T(8,128)S(1)}, f32[1024,512]{1,0:T(8,128)}) custom-call(bf16[256,1536]{1,0:T(8,128)(2,1)S(1)} %copy-done.3, bf16[1024,1024]{1,0:T(8,128)(2,1)} %copy-done.1, bf16[1024,1024]{1,0:T(8,128)(2,1)} %copy-done.1, bf16[256,512]{1,0:T(8,128)(2,1)S(1)} %convolution_convert_fusion.14.g_ref, ...), custom_call_target="tpu_custom_call" | custom-call | flops 2684354560 | bytes 5242880 | tf_op jit(solution)/shard_map/attention_backward/pallas_call | solution.py:1007
  417.4 8.1 %collective-permute-start.22 = (f32[256,1024]{1,0:T(8,128)}, f32[256,1024]{1,0:T(8,128)}, u32[]{:S(2)}, u32[]{:S(2)}) collective-permute-start(f32[256,1024]{1,0:T(8,128)} %collective-permute-done.21), channel_id=1, source_target_pairs={{0,16},{16,0},{1,17},{17,1},{2,18},{18,2},{3,19},{19,3},{4,20},{20... | collective-permute-start | bytes 3145736 | tf_op jit(solution)/shard_map/ppermute | solution.py:512
  475.8 10.1 %attention_backward.6 = (bf16[256,512]{1,0:T(8,128)(2,1)S(1)}, f32[1024,512]{1,0:T(8,128)S(1)}, f32[1024,512]{1,0:T(8,128)}) custom-call(bf16[256,1536]{1,0:T(8,128)(2,1)S(1)} %copy-done.6, bf16[1024,1024]{1,0:T(8,128)(2,1)} %copy-done, bf16[1024,1024]{1,0:T(8,128)(2,1)} %copy-done, bf16[256,512]{1,0:T(8,128)(2,1)S(1)} %convolution_convert_fusion.13.g_ref, ...), custom_call_target="tpu_custom_call" | custom-call | flops 2684354560 | bytes 5242880 | tf_op jit(solution)/shard_map/attention_backward/pallas_call | solution.py:1007
  488.3 10.7 %attention_backward.7 = (bf16[256,512]{1,0:T(8,128)(2,1)S(1)}, f32[1024,512]{1,0:T(8,128)S(1)}, f32[1024,512]{1,0:T(8,128)}) custom-call(bf16[256,1536]{1,0:T(8,128)(2,1)S(1)} %convolution_convert_fusion.4.q_ref, bf16[1024,1024]{1,0:T(8,128)(2,1)} %copy-done, bf16[1024,1024]{1,0:T(8,128)(2,1)} %copy-done, ...), custom_call_target="tpu_custom_call" | custom-call | flops 2684354560 | bytes 5242880 | tf_op jit(solution)/shard_map/attention_backward/pallas_call | solution.py:1007
  539.0 10.6 %collective-permute-done.25 = bf16[256,1024]{1,0:T(8,128)(2,1)S(1)} collective-permute-done((bf16[256,1024]{1,0:T(8,128)(2,1)S(1)}, bf16[256,1024]{1,0:T(8,128)(2,1)S(1)}, u32[]{:S(2)}, u32[]{:S(2)}) %collective-permute-start.25) | collective-permute-done | bytes 524320 | tf_op jit(solution)/shard_map/ppermute | solution.py:516
  566.5 8.7 %fusion.419 = f32[33,256,256]{2,1,0:T(8,128)} fusion(bf16[2,256,256]{2,1,0:T(8,128)(2,1)S(1)} %copy-done.108, bf16[2,256,256]{2,1,0:T(8,128)(2,1)S(1)} %reshape.754), kind=kOutput, calls=%fused_computation.671 | convolution fusion | flops 2143289344 | bytes 9175040 | tf_op jit(solution)/shard_map/conv_general_dilated | solution.py:1105
  582.3 8.5 %fusion.21 = bf16[8192,64]{1,0:T(8,128)(2,1)S(1)} fusion(f32[8448,256]{1,0:T(8,128)} %bitcast.326), kind=kLoop, calls=%fused_computation.31 | loop fusion | flops 2097152 | bytes 9437184 | tf_op jit(solution)/shard_map/convert.25
  620.0 12.6 %collective-permute-done.30 = bf16[2,4,272,128]{3,2,1,0:T(8,128)(2,1)} collective-permute-done((bf16[2,4,272,128]{3,2,1,0:T(8,128)(2,1)}, bf16[2,4,272,128]{3,2,1,0:T(8,128)(2,1)}, u32[]{:S(2)}, u32[]{:S(2)}) %collective-permute-start.30) | collective-permute-done | bytes 557088 | tf_op jit(solution)/shard_map/ppermute | solution.py:549
  661.0 18.5 %collective-permute-done.33 = bf16[2,4,272,128]{3,2,1,0:T(8,128)(2,1)} collective-permute-done((bf16[2,4,272,128]{3,2,1,0:T(8,128)(2,1)}, bf16[2,4,272,128]{3,2,1,0:T(8,128)(2,1)}, u32[]{:S(2)}, u32[]{:S(2)}) %collective-permute-start.33) | collective-permute-done | bytes 557088 | tf_op jit(solution)/shard_map/ppermute | solution.py:549
  683.9 13.8 %all-to-all-start.2 = ((bf16[8,272,128]{2,1,0:T(8,128)(2,1)}), bf16[8,272,128]{2,1,0:T(8,128)(2,1)S(1)}, u32[]{:S(2)}, u32[]{:S(2)}) async-start(bf16[8,272,128]{2,1,0:T(8,128)(2,1)} %bitcast.367), calls=%async_computation.3 | async-start | bytes 1114112 | tf_op jit(solution)/shard_map/all_to_all | solution.py:1419
  701.2 8.2 %all-to-all-done.2 = bf16[8,272,128]{2,1,0:T(8,128)(2,1)S(1)} async-done(((bf16[8,272,128]{2,1,0:T(8,128)(2,1)}), bf16[8,272,128]{2,1,0:T(8,128)(2,1)S(1)}, u32[]{:S(2)}, u32[]{:S(2)}) %all-to-all-start.2) | async-done | bytes 557088 | tf_op jit(solution)/shard_map/all_to_all | solution.py:1419
  (768 shorter events, 424.2 us)
Async XLA Ops:
  7.2 249.2 %all-gather.2.cloned.1.call-start = ((), (), s32[]{:S(2)}) async-start(), calls=%async_computation.6 | async-start | bytes 13926400 | tf_op jit(solution)/shard_map/all_gather | solution.py:566
  161.2 19.2 %all-to-all-start = ((bf16[8,512,128]{2,1,0:T(8,128)(2,1)}), bf16[8,512,128]{2,1,0:T(8,128)(2,1)S(1)}, u32[]{:S(2)}, u32[]{:S(2)}) async-start(bf16[8,512,128]{2,1,0:T(8,128)(2,1)} %bitcast.29), calls=%async_computation | async-start | bytes 2097152 | tf_op jit(solution)/shard_map/all_to_all | solution.py:1227
  165.6 334.1 %reduce-scatter.4.cloned.1.call-start = ((), (), s32[]{:S(2)}) async-start(), calls=%async_computation.7 | async-start | bytes 9191424 | tf_op jit(solution)/shard_map/reduce_scatter | solution.py:572
  166.5 36.4 %collective-permute-start = (bf16[256,1024]{1,0:T(8,128)(2,1)}, bf16[256,1024]{1,0:T(8,128)(2,1)}, u32[]{:S(2)}, u32[]{:S(2)}) collective-permute-start(bf16[256,1024]{1,0:T(8,128)(2,1)} %select_bitcast_fusion.2), channel_id=1, source_target_pairs={{0,0},{1,1},{2,16},{3,17},{16,2},{17,3},{18,18},{19,19},{4,4},{5,5... | collective-permute-start | bytes 1572872 | tf_op jit(solution)/shard_map/ppermute | solution.py:1210
  202.9 81.5 %collective-permute-start.1 = (bf16[256,1024]{1,0:T(8,128)(2,1)}, bf16[256,1024]{1,0:T(8,128)(2,1)}, u32[]{:S(2)}, u32[]{:S(2)}) collective-permute-start(bf16[256,1024]{1,0:T(8,128)(2,1)} %collective-permute-done), channel_id=1, source_target_pairs={{0,1},{1,0},{2,3},{3,2},{4,5},{5,4},{6,7},{7,6},{8,9},{9,8},{10,11... | collective-permute-start | bytes 1572872 | tf_op jit(solution)/shard_map/ppermute | solution.py:516
  211.5 27.3 %collective-permute-start.6 = (bf16[256,1024]{1,0:T(8,128)(2,1)S(1)}, bf16[256,1024]{1,0:T(8,128)(2,1)S(1)}, u32[]{:S(2)}, u32[]{:S(2)}) collective-permute-start(bf16[256,1024]{1,0:T(8,128)(2,1)S(1)} %convolution_convert_fusion.10), channel_id=1, source_target_pairs={{0,1},{1,0},{2,3},{3,2},{4,5},{5,4},{6,7},{7,6},{8,9},{9,8},{10,11... | collective-permute-start | bytes 1572872 | tf_op jit(solution)/shard_map/ppermute | solution.py:516
  263.2 17.9 %collective-permute-start.7 = (bf16[256,1024]{1,0:T(8,128)(2,1)S(1)}, bf16[256,1024]{1,0:T(8,128)(2,1)S(1)}, u32[]{:S(2)}, u32[]{:S(2)}) collective-permute-start(bf16[256,1024]{1,0:T(8,128)(2,1)S(1)} %fusion.120), channel_id=1, source_target_pairs={{0,1},{1,0},{2,3},{3,2},{4,5},{5,4},{6,7},{7,6},{8,9},{9,8},{10,11... | collective-permute-start | bytes 1572872 | tf_op jit(solution)/shard_map/ppermute | solution.py:516
  340.0 22.5 %collective-permute-start.11 = (bf16[256,1024]{1,0:T(8,128)(2,1)S(1)}, bf16[256,1024]{1,0:T(8,128)(2,1)}, u32[]{:S(2)}, u32[]{:S(2)}) collective-permute-start(bf16[256,1024]{1,0:T(8,128)(2,1)S(1)} %fusion.126), channel_id=1, source_target_pairs={{0,1},{1,0},{2,3},{3,2},{4,5},{5,4},{6,7},{7,6},{8,9},{9,8},{10,11... | collective-permute-start | bytes 1572872 | tf_op jit(solution)/shard_map/ppermute | solution.py:516
  349.3 360.2 %reduce-scatter.6.cloned.1.call-start = ((), (), s32[]{:S(2)}) async-start(), calls=%async_computation.8 | async-start | bytes 13647872 | tf_op jit(solution)/shard_map/reduce_scatter | solution.py:572
  369.1 24.8 %collective-permute-start.15 = (bf16[256,1024]{1,0:T(8,128)(2,1)S(1)}, bf16[256,1024]{1,0:T(8,128)(2,1)S(1)}, u32[]{:S(2)}, u32[]{:S(2)}) collective-permute-start(bf16[256,1024]{1,0:T(8,128)(2,1)S(1)} %fusion.132), channel_id=1, source_target_pairs={{0,1},{1,0},{2,3},{3,2},{4,5},{5,4},{6,7},{7,6},{8,9},{9,8},{10,11... | collective-permute-start | bytes 1572872 | tf_op jit(solution)/shard_map/ppermute | solution.py:516
  370.4 23.5 %collective-permute-start.14 = (bf16[256,1024]{1,0:T(8,128)(2,1)S(1)}, bf16[256,1024]{1,0:T(8,128)(2,1)S(1)}, u32[]{:S(2)}, u32[]{:S(2)}) collective-permute-start(bf16[256,1024]{1,0:T(8,128)(2,1)S(1)} %copy-done.106), channel_id=1, source_target_pairs={{0,1},{1,0},{2,3},{3,2},{4,5},{5,4},{6,7},{7,6},{8,9},{9,8},{10,11... | collective-permute-start | bytes 1572872 | tf_op jit(solution)/shard_map/ppermute | solution.py:516
  408.9 21.9 %collective-permute-start.18 = (bf16[256,1024]{1,0:T(8,128)(2,1)S(1)}, bf16[256,1024]{1,0:T(8,128)(2,1)}, u32[]{:S(2)}, u32[]{:S(2)}) collective-permute-start(bf16[256,1024]{1,0:T(8,128)(2,1)S(1)} %fusion.105), channel_id=1, source_target_pairs={{0,1},{1,0},{2,3},{3,2},{4,5},{5,4},{6,7},{7,6},{8,9},{9,8},{10,11... | collective-permute-start | bytes 1572872 | tf_op jit(solution)/shard_map/ppermute | solution.py:516
  417.4 43.3 %collective-permute-start.22 = (f32[256,1024]{1,0:T(8,128)}, f32[256,1024]{1,0:T(8,128)}, u32[]{:S(2)}, u32[]{:S(2)}) collective-permute-start(f32[256,1024]{1,0:T(8,128)} %collective-permute-done.21), channel_id=1, source_target_pairs={{0,16},{16,0},{1,17},{17,1},{2,18},{18,2},{3,19},{19,3},{4,20},{20... | collective-permute-start | bytes 3145736 | tf_op jit(solution)/shard_map/ppermute | solution.py:512
  441.1 22.8 %collective-permute-start.19 = (bf16[256,1024]{1,0:T(8,128)(2,1)}, bf16[256,1024]{1,0:T(8,128)(2,1)}, u32[]{:S(2)}, u32[]{:S(2)}) collective-permute-start(bf16[256,1024]{1,0:T(8,128)(2,1)} %fusion.150), channel_id=1, source_target_pairs={{0,1},{1,0},{2,3},{3,2},{4,5},{5,4},{6,7},{7,6},{8,9},{9,8},{10,11... | collective-permute-start | bytes 1572872 | tf_op jit(solution)/shard_map/ppermute | solution.py:516
  447.0 19.2 %collective-permute-start.20 = (bf16[256,1024]{1,0:T(8,128)(2,1)}, bf16[256,1024]{1,0:T(8,128)(2,1)}, u32[]{:S(2)}, u32[]{:S(2)}) collective-permute-start(bf16[256,1024]{1,0:T(8,128)(2,1)} %fusion.159), channel_id=1, source_target_pairs={{0,1},{1,0},{2,3},{3,2},{4,5},{5,4},{6,7},{7,6},{8,9},{9,8},{10,11... | collective-permute-start | bytes 1572872 | tf_op jit(solution)/shard_map/ppermute | solution.py:516
  468.6 260.0 %reduce-scatter.8.cloned.1.call-start = ((), (), s32[]{:S(2)}) async-start(), calls=%async_computation.9 | async-start | bytes 4734976 | tf_op jit(solution)/shard_map/reduce_scatter | solution.py:572
  528.4 21.2 %collective-permute-start.25 = (bf16[256,1024]{1,0:T(8,128)(2,1)S(1)}, bf16[256,1024]{1,0:T(8,128)(2,1)S(1)}, u32[]{:S(2)}, u32[]{:S(2)}) collective-permute-start(bf16[256,1024]{1,0:T(8,128)(2,1)S(1)} %fusion.111), channel_id=1, source_target_pairs={{0,1},{1,0},{2,3},{3,2},{4,5},{5,4},{6,7},{7,6},{8,9},{9,8},{10,11... | collective-permute-start | bytes 1572872 | tf_op jit(solution)/shard_map/ppermute | solution.py:516
  596.1 23.9 %collective-permute-start.29 = (bf16[2,4,272,128]{3,2,1,0:T(8,128)(2,1)}, bf16[2,4,272,128]{3,2,1,0:T(8,128)(2,1)}, u32[]{:S(2)}, u32[]{:S(2)}) collective-permute-start(bf16[2,4,272,128]{3,2,1,0:T(8,128)(2,1)} %get-tuple-element.230), channel_id=1, source_target_pairs={{0,4},{1,5},{2,6},{3,7},{16,20},{17,21},{18,22},{19,23}} | collective-permute-start | bytes 1671176 | tf_op jit(solution)/shard_map/ppermute | solution.py:549
  597.7 34.9 %collective-permute-start.30 = (bf16[2,4,272,128]{3,2,1,0:T(8,128)(2,1)}, bf16[2,4,272,128]{3,2,1,0:T(8,128)(2,1)}, u32[]{:S(2)}, u32[]{:S(2)}) collective-permute-start(bf16[2,4,272,128]{3,2,1,0:T(8,128)(2,1)} %get-tuple-element.229), channel_id=1, source_target_pairs={{12,8},{13,9},{14,10},{15,11},{28,24},{29,25},{30,26},{31,27}} | collective-permute-start | bytes 1671176 | tf_op jit(solution)/shard_map/ppermute | solution.py:549
  636.4 16.5 %collective-permute-start.32 = (bf16[2,4,272,128]{3,2,1,0:T(8,128)(2,1)}, bf16[2,4,272,128]{3,2,1,0:T(8,128)(2,1)}, u32[]{:S(2)}, u32[]{:S(2)}) collective-permute-start(bf16[2,4,272,128]{3,2,1,0:T(8,128)(2,1)} %get-tuple-element.227), channel_id=1, source_target_pairs={{8,4},{12,8},{9,5},{13,9},{10,6},{14,10},{11,7},{15,11},{24,20},{2... | collective-permute-start | bytes 1671176 | tf_op jit(solution)/shard_map/ppermute | solution.py:549
  641.5 19.5 %all-to-all-start.1 = ((bf16[8,2,256,128]{3,2,1,0:T(8,128)(2,1)}), bf16[8,2,256,128]{3,2,1,0:T(8,128)(2,1)S(1)}, u32[]{:S(2)}, u32[]{:S(2)}) async-start(bf16[8,2,256,128]{3,2,1,0:T(8,128)(2,1)} %copy.435), calls=%async_computation.2 | async-start | bytes 2097152 | tf_op jit(solution)/shard_map/all_to_all | solution.py:1408
  655.5 24.0 %collective-permute-start.33 = (bf16[2,4,272,128]{3,2,1,0:T(8,128)(2,1)}, bf16[2,4,272,128]{3,2,1,0:T(8,128)(2,1)}, u32[]{:S(2)}, u32[]{:S(2)}) collective-permute-start(bf16[2,4,272,128]{3,2,1,0:T(8,128)(2,1)} %get-tuple-element.226), channel_id=1, source_target_pairs={{0,4},{4,8},{8,12},{1,5},{5,9},{9,13},{2,6},{6,10},{10,14},{3,7},{... | collective-permute-start | bytes 1671176 | tf_op jit(solution)/shard_map/ppermute | solution.py:549
  657.4 24.2 %collective-permute-start.34 = (bf16[2,4,272,128]{3,2,1,0:T(8,128)(2,1)}, bf16[2,4,272,128]{3,2,1,0:T(8,128)(2,1)}, u32[]{:S(2)}, u32[]{:S(2)}) collective-permute-start(bf16[2,4,272,128]{3,2,1,0:T(8,128)(2,1)} %get-tuple-element.225), channel_id=1, source_target_pairs={{4,0},{8,4},{12,8},{5,1},{9,5},{13,9},{6,2},{10,6},{14,10},{7,3},{... | collective-permute-start | bytes 1671176 | tf_op jit(solution)/shard_map/ppermute | solution.py:549
  683.9 25.5 %all-to-all-start.2 = ((bf16[8,272,128]{2,1,0:T(8,128)(2,1)}), bf16[8,272,128]{2,1,0:T(8,128)(2,1)S(1)}, u32[]{:S(2)}, u32[]{:S(2)}) async-start(bf16[8,272,128]{2,1,0:T(8,128)(2,1)} %bitcast.367), calls=%async_computation.3 | async-start | bytes 1114112 | tf_op jit(solution)/shard_map/all_to_all | solution.py:1419
  (201 other events, 1376.6 us)
Sparse Core Ops, SparseCore 0:
  128.1 128.3 all-gather.1
  349.4 118.8 reduce-scatter.3
  472.4 156.1 reduce-scatter.5
  632.3 83.5 reduce-scatter.7
